TPU v7x, 256 devices: a whole 4x4x8 slice. The times are simulated.
256 devices in a mesh: dp: 2 (over z_lo), ctx: 32 (over z_hi, y, core), tensor: 4 (over x).
Axes of the slice: x: 4, y: 4, z: 8 (z_hi: 4, z_lo: 2; z = z_hi * 2 + z_lo), core: 2. Of those that a mesh axis runs over, the one named last changes fastest.
Arguments:
- queries: bfloat16 [8192, 3072], P(('dp', 'ctx'), 'tensor'), parts along dimension 0, may hold values from -6 to 6
- keys: bfloat16 [8192, 512], P(('dp', 'ctx'), 'tensor'), parts along dimension 0, may hold values from -6 to 6
- values: bfloat16 [8192, 512], P(('dp', 'ctx'), 'tensor'), parts along dimension 0, may hold values from -6 to 6
- cache_keys: bfloat16 [8192, 512], P(('dp', 'ctx'), 'tensor'), parts along dimension 0, may hold values from -6 to 6
- cache_values: bfloat16 [8192, 512], P(('dp', 'ctx'), 'tensor'), parts along dimension 0, may hold values from -6 to 6
- residual: bfloat16 [8192, 3072], P(('dp', 'ctx'), 'tensor'), parts along dimension 0, may hold values from -36 to 36
- norm_gain: float32 [3072], replicated, may hold values from 0.1 to 1.9
- w_gate: bfloat16 [3072, 65536], P(None, ('ctx', 'tensor')), may hold values from -0.109375 to 0.109375
- w_up: bfloat16 [3072, 65536], P(None, ('ctx', 'tensor')), may hold values from -0.109375 to 0.109375
- w_down: bfloat16 [65536, 3072], P(('ctx', 'tensor')), may hold values from -0.0625 to 0.0625
- expert_ids: int32 [8192, 2], P(('dp', 'ctx')), parts along dimension 0, may hold values from 0 to 7, all different within a row; in each aligned block of 128 rows (0 to 127, 128 to 255, ...) at most 36 rows name the same one
- gate_weights: float32 [8192, 2], P(('dp', 'ctx')), parts along dimension 0, may hold values from 0.1 to 0.9
Outputs:
- layer_out: bfloat16 [8192, 3072], P(('dp', 'ctx'), 'tensor'), parts along dimension 0
There are 2 independent parts, one for each index of `dp`. A program takes and returns all parts, laid end to end along the dimension named above; an argument that names none is the same for every part. Nothing has to cross between parts.
Inputs may be any that keep to these rules, and one draw needn't show every extreme that they name: `expert_ids`: among the 128 rows of each index of ctx (aligned blocks of rows), no expert is named by more than 36 rows, a bound that some block reaches.
All inputs are finite; a program needn't handle non-finite values.
Results may differ from a plain program's by a relative error of at most 0.012.
Values may be sent and summed in bfloat16 or wider, within the bound.
No kernel may reach another device: no remote copies, remote signals or barrier semaphores. Data moves between devices by JAX's collectives and lax.ppermute only.
A program may use at most 192 MiB of HBM per device.

v0:
```python
import math

import jax
import jax.numpy as jnp
from jax import lax
from jax.experimental import pallas as pl
from jax.experimental.pallas import tpu as pltpu
from jax.sharding import Mesh, PartitionSpec as P

HEADS = 24
KV_HEADS = 4
HEAD_DIM = 128
EXPERTS = 8
TOP = 2
CAP = 36
PAD = 40
EPS = 1e-05
NZ, NY, NX, NC = 4, 4, 4, 2
SHIFTS = (1, 3, 2)
MB = 1024 * 1024

bf16 = jnp.bfloat16
f32 = jnp.float32
VM = pl.BlockSpec(memory_space=pltpu.VMEM)
SM = pl.BlockSpec(memory_space=pltpu.SMEM)
HBM = pl.BlockSpec(memory_space=pltpu.HBM)


def call(body, out_shape, args, name, scratch=(), limit=16, scalars=0, hbm=0):
    many = isinstance(out_shape, list)
    return pl.pallas_call(
        body,
        out_shape=out_shape,
        in_specs=[SM] * scalars + [VM] * (len(args) - scalars - hbm) + [HBM] * hbm,
        out_specs=[VM] * len(out_shape) if many else VM,
        scratch_shapes=list(scratch),
        compiler_params=pltpu.CompilerParams(vmem_limit_bytes=limit * MB),
        name=name,
    )(*args)


def group_expert(z, yh, g):
    return lax.rem(z + g // 2, NZ) * 2 + lax.rem(yh + g % 2, 2)


def pick_table(z, yh, ids_ref):
    n = ids_ref.shape[1]
    first, second = ids_ref[0:1, :], ids_ref[1:2, :]
    line = lax.broadcasted_iota(jnp.int32, (EXPERTS, n), 0)
    expert = jnp.zeros((EXPERTS, n), jnp.int32)
    for g in range(EXPERTS):
        expert = jnp.where(line == g, group_expert(z, yh, g), expert)
    named = (first == expert) | (second == expert)
    earlier = (
        lax.broadcasted_iota(jnp.int32, (n, n), 0) < lax.broadcasted_iota(jnp.int32, (n, n), 1)
    ).astype(bf16)
    rank = jnp.dot(named.astype(bf16), earlier, preferred_element_type=f32).astype(jnp.int32)
    rank = jnp.where(named, rank, -1)
    row = lax.broadcasted_iota(jnp.int32, (PAD, n), 0)
    return [rank[g : g + 1, :] == row for g in range(EXPERTS)]


def prep_kernel(where_ref, ids_ref, q_ref, res_ref, k_ref, v_ref, ck_ref, cv_ref, *outs):
    q_all, res_out, tract, cache, table = outs
    rows = q_ref.shape[0]
    for h in range(q_ref.shape[1] // HEAD_DIM):
        q_all[h * rows : (h + 1) * rows, :] = q_ref[:, h * HEAD_DIM : (h + 1) * HEAD_DIM]
    res_out[...] = res_ref[...]
    tract[0], tract[1] = k_ref[...], v_ref[...]
    cache[0], cache[1] = ck_ref[...], cv_ref[...]
    picks = pick_table(where_ref[0], lax.div(where_ref[1], 2), ids_ref)
    table[...] = jnp.concatenate([t.astype(f32) for t in picks], axis=0).astype(bf16)


def pack_kv_kernel(where_ref, tract, cache, *refs):
    from_z, outs = refs[: NZ - 1], refs[NZ - 1 :]
    n = tract.shape[1]
    y, core = where_ref[1], where_ref[2]
    later = [y + s < NY for s in SHIFTS] + [core == 0]
    for out, is_later in zip(outs, later):
        out[:, 0:n] = jnp.where(is_later, tract[...], cache[...])
        for i, ref in enumerate(from_z):
            out[:, (i + 1) * n : (i + 2) * n] = ref[...]


SCALE = math.log2(math.e) / math.sqrt(HEAD_DIM)
BY_ROWS = (((1,), (1,)), ((), ()))


def attend_piece(q, k, v, m, l, acc):
    s = lax.dot_general(q, k, BY_ROWS, preferred_element_type=f32) * SCALE
    m_new = jnp.maximum(m, jnp.max(s, axis=1, keepdims=True))
    fade = jnp.exp2(m - m_new)
    p = jnp.exp2(s - m_new)
    l = l * fade + jnp.sum(p, axis=1, keepdims=True)
    acc = acc * fade + jnp.dot(p.astype(bf16), v, preferred_element_type=f32)
    return m_new, l, acc


def attend_near_kernel(q_all, tract_ref, cache_ref, *refs):
    kv_refs, (m_ref, l_ref, acc_ref) = refs[:-3], refs[-3:]
    rows = tract_ref.shape[1]
    tile = 2 * rows
    row_at = lax.rem(lax.broadcasted_iota(jnp.int32, (tile, rows), 0), rows)
    col_at = lax.broadcasted_iota(jnp.int32, (tile, rows), 1)
    tract = col_at <= row_at

    def group(g, carry):
        at = pl.ds(pl.multiple_of(g * tile, tile), tile)
        q = q_all[at, :]
        s_tract = lax.dot_general(q, tract_ref[0], BY_ROWS, preferred_element_type=f32)
        s_cache = lax.dot_general(q, cache_ref[0], BY_ROWS, preferred_element_type=f32)
        s = jnp.where(tract, s_tract, s_cache) * SCALE
        m = jnp.max(s, axis=1, keepdims=True)
        p = jnp.exp2(s - m)
        l = jnp.sum(p, axis=1, keepdims=True)
        low = p.astype(bf16)
        zero = jnp.zeros_like(low)
        acc = jnp.dot(jnp.where(tract, low, zero), tract_ref[1], preferred_element_type=f32)
        acc += jnp.dot(jnp.where(tract, zero, low), cache_ref[1], preferred_element_type=f32)
        for i, ref in enumerate(kv_refs):
            keys = slice(0 if i else rows, ref.shape[1])
            m, l, acc = attend_piece(q, ref[0, keys], ref[1, keys], m, l, acc)
        m_ref[at, :] = jnp.broadcast_to(m, acc.shape)
        l_ref[at, :] = jnp.broadcast_to(l, acc.shape)
        acc_ref[at, :] = acc
        return carry

    lax.fori_loop(0, q_all.shape[0] // tile, group, 0)


def attend_kernel(q_all, res_ref, table, m_ref, l_ref, acc_ref, *refs):
    kv_refs, hid_ref, z_refs, o_all = refs[:NY], refs[NY], refs[NY + 1 : -1], refs[-1]
    rows, width = res_ref.shape
    heads = width // HEAD_DIM
    tile = 2 * rows

    def group(g, carry):
        at = pl.ds(pl.multiple_of(g * tile, tile), tile)
        q = q_all[at, :]
        m, l, acc = m_ref[at, :][:, :1], l_ref[at, :][:, :1], acc_ref[at, :]
        for ref in kv_refs:
            m, l, acc = attend_piece(q, ref[0], ref[1], m, l, acc)
        o_all[at, :] = acc / l
        return carry

    lax.fori_loop(0, heads * rows // tile, group, 0)
    for h in range(heads):
        cols = slice(h * HEAD_DIM, (h + 1) * HEAD_DIM)
        attended = o_all[h * rows : (h + 1) * rows, :]
        hid_ref[:, cols] = (res_ref[:, cols].astype(f32) + attended).astype(bf16)
    routed = jnp.dot(table[...], hid_ref[...], preferred_element_type=f32).astype(bf16)
    for g in range(EXPERTS):
        z_refs[g // 2][g % 2] = routed[g * PAD : g * PAD + CAP]


def merge_kernel(*refs):
    keep, away = refs[NZ:]
    for d, ref in enumerate(refs[:NZ]):
        keep[d * CAP : (d + 1) * CAP, :] = ref[0]
        away[d * CAP : (d + 1) * CAP, :] = ref[1]


def expert_kernel(where_ref, gain_ref, *refs):
    a_own, a_far, b_all = refs[0], refs[1], refs[2 : 2 + NX]
    weights = refs[2 + NX : 8 + NX]
    a_own_out, a_far_out = refs[8 + NX : 10 + NX]
    b_out = refs[10 + NX : 10 + 2 * NX]
    normed, act, gate_v, up_v, down_v, sems = refs[10 + 2 * NX :]
    rows, width = a_own.shape[1:]
    total, ff = weights[0].shape
    gate_loads, up_loads, down_loads = [
        [pltpu.make_async_copy(weights[3 * h + j], place(h), sems.at[h, j]) for h in range(2)]
        for j, place in enumerate(
            (
                lambda h: gate_v.at[h],
                lambda h: up_v.at[h],
                lambda h: down_v.at[pl.ds(h * ff, ff)],
            )
        )
    ]
    for c in (gate_loads[0], up_loads[0], gate_loads[1], up_loads[1], *down_loads):
        c.start()
    x = where_ref[3]
    order = (0,) + SHIFTS
    parts = [
        lambda i: a_own[i],
        lambda i: a_far[i],
        lambda i: b_all[i][0],
        lambda i: b_all[i][1],
    ]
    for r, part in enumerate(parts):
        sq = jnp.zeros((rows, 1), f32)
        for i in range(NX):
            v = part(i).astype(f32)
            sq = sq + jnp.sum(v * v, axis=1, keepdims=True)
        inverse = lax.rsqrt(sq * (1.0 / total) + EPS)
        for i, shift in enumerate(order):
            src = lax.rem(x - shift + NX, NX)
            cols = pl.ds(pl.multiple_of(src * width, width), width)
            v = part(i).astype(f32) * inverse * gain_ref[src]
            normed[r * rows : (r + 1) * rows, cols] = v.astype(bf16)

    def hidden_units(half, carry):
        for j, v in enumerate((gate_v, up_v)):
            pltpu.make_async_copy(v.at[half], v.at[half], sems.at[half, j]).wait()
        gate = jnp.dot(normed[...], gate_v[half], preferred_element_type=f32)
        up = jnp.dot(normed[...], up_v[half], preferred_element_type=f32)
        low = (gate / (1.0 + jnp.exp(-gate)) * up).astype(bf16)
        act[:, pl.ds(pl.multiple_of(half * ff, ff), ff)] = low
        return carry

    lax.fori_loop(0, 2, hidden_units, 0)
    for c in down_loads:
        c.wait()
    for i, shift in enumerate(order):
        cols = pl.ds(pl.multiple_of(lax.rem(x + shift, NX) * width, width), width)
        out = jnp.dot(act[...], down_v[:, cols], preferred_element_type=f32).astype(bf16)
        a_own_out[i] = out[0:rows]
        a_far_out[i] = out[rows : 2 * rows]
        b_out[i][0] = out[2 * rows : 3 * rows]
        b_out[i][1] = out[3 * rows :]


def experts(where, gain, a_own, a_far, b_all, own, other):
    rows, width = a_own.shape[1:]
    total, ff = own[0].shape
    out = call(
        expert_kernel,
        [jax.ShapeDtypeStruct((NX, rows, width), bf16)] * 2
        + [jax.ShapeDtypeStruct((2, rows, width), bf16)] * NX,
        [where, gain, a_own, a_far, *b_all, *own, *other],
        "experts",
        [pltpu.VMEM((4 * rows, total), bf16), pltpu.VMEM((4 * rows, 2 * ff), bf16)]
        + [pltpu.VMEM((2, total, ff), bf16)] * 2
        + [pltpu.VMEM((2 * ff, total), bf16), pltpu.SemaphoreType.DMA((2, 3))],
        limit=47,
        scalars=1,
        hbm=6,
    )
    return out[0], out[1], out[2:]


def first_sum_kernel(*refs):
    a_own, a_got, b_own, b_got = refs[0], refs[1], refs[2], refs[3 : 2 + NX]
    a_out, b_out = refs[2 + NX : 2 + 2 * NX], refs[2 + 2 * NX :]
    for i, out in enumerate(a_out):
        out[...] = (a_own[i].astype(f32) + a_got[i].astype(f32)).astype(bf16)
    for r in range(2):
        total = b_own[r].astype(f32)
        for got in b_got:
            total = total + got[r].astype(f32)
        b_out[r][...] = total.astype(bf16)


def last_sum_kernel(*refs):
    parts, back, outs = refs[:NX], refs[NX], refs[NX + 1 :]
    total = parts[0][...].astype(f32)
    for ref in parts[1:]:
        total = total + ref[...].astype(f32)
    total = total.astype(bf16)
    for d, out in enumerate(outs):
        out[0] = total[d * CAP : (d + 1) * CAP]
        out[1] = back[d * CAP : (d + 1) * CAP, :]


def mix_kernel(where_ref, ids_ref, gates_ref, hid_ref, *refs):
    part_refs, out_ref, held = refs[:NZ], refs[NZ], refs[NZ + 1]
    z, yh = where_ref[0], lax.div(where_ref[1], 2)
    weight = []
    for g, pick in enumerate(pick_table(z, yh, ids_ref)):
        e = group_expert(z, yh, g)
        gate = jnp.where(ids_ref[0:1, :] == e, gates_ref[0:1, :], 0.0)
        gate = gate + jnp.where(ids_ref[1:2, :] == e, gates_ref[1:2, :], 0.0)
        weight.append(jnp.where(pick, gate, 0.0))
    held[...] = jnp.zeros_like(held)
    for g in range(EXPERTS):
        held[g * PAD : g * PAD + CAP, :] = part_refs[g // 2][g % 2].astype(f32)
    mixture = lax.dot_general(
        jnp.concatenate(weight, axis=0),
        held[...],
        (((0,), (0,)), ((), ())),
        precision=lax.Precision.HIGHEST,
        preferred_element_type=f32,
    )
    out_ref[...] = (hid_ref[...].astype(f32) + mixture).astype(bf16)


SWAP = [(0, 1), (1, 0)]


def turn(v, axis, shift):
    n = 4
    return lax.ppermute(v, axis, [(i, (i + shift) % n) for i in range(n)])


def cross(v):
    return lax.ppermute(v, ("yh", "yl"), [(i, NY - 1 - i) for i in range(NY)])


def swap_y(v):
    return lax.ppermute(v, "yl", SWAP)


def swap_core(v):
    return lax.ppermute(v, "core", SWAP)


def per_device(
    queries, keys, values, cache_keys, cache_values, residual, norm_gain, w_gate, w_up, w_down, expert_ids, gate_weights
):
    rows, width = queries.shape
    heads = width // HEAD_DIM
    z = lax.axis_index("zh")
    y = lax.axis_index(("yh", "yl"))
    where = jnp.stack((z, y, lax.axis_index("core"), lax.axis_index("x"))).astype(jnp.int32)
    ids, gates = expert_ids.T, gate_weights.T
    shaped = lambda *dims: jax.ShapeDtypeStruct(dims, bf16)
    block = shaped(2, rows, HEAD_DIM)

    near, past = jnp.stack((keys, values)), jnp.stack((cache_keys, cache_values))
    from_z = [turn(jnp.where(z + s < NZ, near, past), "zh", s) for s in SHIFTS]
    q_all, res, tract, cache, table = call(
        prep_kernel,
        [shaped(heads * rows, HEAD_DIM), shaped(rows, width), block, block, shaped(EXPERTS * PAD, rows)],
        [where, ids, queries, residual, keys, values, cache_keys, cache_values],
        "prep",
        scalars=1,
    )
    packed = call(
        pack_kv_kernel,
        [shaped(2, NZ * rows, HEAD_DIM)] * 4,
        [where, tract, cache, *from_z],
        "pack_kv",
        scalars=1,
    )
    packed, other_gate = lax.optimization_barrier((packed, swap_core(w_gate)))
    held = lax.optimization_barrier((w_up, packed[0]))[0]
    y_1, y_3, partner = lax.optimization_barrier(
        [turn(packed[0], ("yh", "yl"), 1), turn(packed[1], ("yh", "yl"), 3), swap_core(packed[3])]
    )
    y_2 = turn(packed[2], ("yh", "yl"), 2)
    far_1, far_3 = swap_core(y_1), swap_core(y_3)
    state = [jax.ShapeDtypeStruct((heads * rows, HEAD_DIM), f32)] * 3
    carried = call(
        attend_near_kernel, state, [q_all, tract, cache, packed[3], partner, y_1, y_3], "attend_near"
    )
    carried, y_2, far_1, far_3, other_up = lax.optimization_barrier(
        (carried, y_2, far_1, far_3, swap_core(held))
    )
    far_2 = swap_core(y_2)
    held = lax.optimization_barrier((w_down, far_2))[0]
    own, other = (w_gate, w_up, w_down), (other_gate, other_up, swap_core(held))
    hidden, *sent = call(
        attend_kernel,
        [shaped(rows, width)] + [shaped(2, CAP, width)] * NZ,
        [q_all, res, table, *carried, y_2, far_1, far_3, far_2],
        "attend",
        [pltpu.VMEM((heads * rows, HEAD_DIM), f32)],
    )

    sent, other = lax.optimization_barrier((sent, other))
    arrived = [sent[0]] + [turn(sent[s], "zh", s) for s in (1, 2, 3)]
    rows_a = shaped(NZ * CAP, width)
    a, away = call(merge_kernel, [rows_a] * 2, arrived, "merge")
    b = cross(away)
    b_far = swap_y(b)
    *a_turned, b_far = lax.optimization_barrier([turn(a, "x", s) for s in SHIFTS] + [b_far])
    a_own = jnp.stack([a] + a_turned)
    b_pair = jnp.stack((b, b_far))
    *b_turned, a_far = lax.optimization_barrier(
        [turn(b_pair, "x", s) for s in SHIFTS] + [swap_y(a_own)]
    )
    gain = norm_gain.reshape(NX, 1, width)
    a_own, a_far, b_all = experts(where, gain, a_own, a_far, [b_pair] + b_turned, own, other)

    *b_turned, a_far = lax.optimization_barrier(
        [turn(v, "x", s) for v, s in zip(b_all[1:], SHIFTS)] + [swap_y(a_far)]
    )
    *a_sums, b_own, b_far = call(
        first_sum_kernel, [rows_a] * (NX + 2), [a_own, a_far, b_all[0], *b_turned], "first_sum"
    )
    b_sum = (b_own.astype(f32) + swap_y(b_far).astype(f32)).astype(bf16)
    moved = lax.optimization_barrier(
        [turn(v, "x", s) for v, s in zip(a_sums[1:], SHIFTS)] + [cross(b_sum)]
    )
    result = call(
        last_sum_kernel,
        [shaped(2, CAP, width)] * NZ,
        [a_sums[0], *moved],
        "last_sum",
    )
    back = [result[0]] + [turn(result[s], "zh", NZ - s) for s in (1, 2, 3)]
    return call(
        mix_kernel,
        shaped(rows, width),
        [where, ids, gates, hidden, *back],
        "mix",
        [pltpu.VMEM((EXPERTS * PAD, width), f32)],
        scalars=1,
    )


def solution(mesh):
    fine = Mesh(mesh.devices.reshape(2, 4, 2, 2, 2, 4), ("dp", "zh", "yh", "yl", "core", "x"))
    ctx = ("zh", "yh", "yl", "core")
    tok = P(("dp",) + ctx, "x")
    in_specs = (
        tok, tok, tok, tok, tok, tok,
        P(),
        P(None, ctx + ("x",)),
        P(None, ctx + ("x",)),
        P(ctx + ("x",), None),
        P(("dp",) + ctx, None),
        P(("dp",) + ctx, None),
    )
    return jax.shard_map(per_device, mesh=fine, in_specs=in_specs, out_specs=tok, check_vma=False)
```

profile of v0, /device:TPU:32, one launch (start us, length us, event | category | flops | bytes accessed | tf_op | source)
XLA Modules:
  0.0 178.1 jit_solution(8589719446899192791)
XLA Ops:
  0.0 0.8 broadcast_select_fusion
  0.8 6.4 %collective-permute-start.2 = (bf16[2,128,128]{2,1,0:T(8,128)(2,1)S(1)}, bf16[2,128,128]{2,1,0:T(8,128)(2,1)S(1)}, u32[]{:S(2)}, u32[]{:S(2)}) collective-permute-start(bf16[2,128,128]{2,1,0:T(8,128)(2,1)S(1)} %get-tuple-element.155), channel_id=1, source_target_pairs={{0,64},{32,96},{64,0},{96,32},{1,65},{33,97},{65,1},{97,33},{2,66}... | collective-permute-start | bytes 196616 | tf_op jit(solution)/shard_map/ppermute | solution.py:294
  7.8 2.4 %collective-permute-start = (bf16[2,128,128]{2,1,0:T(8,128)(2,1)S(1)}, bf16[2,128,128]{2,1,0:T(8,128)(2,1)S(1)}, u32[]{:S(2)}, u32[]{:S(2)}) collective-permute-start(bf16[2,128,128]{2,1,0:T(8,128)(2,1)S(1)} %get-tuple-element.157), channel_id=1, source_target_pairs={{0,32},{32,64},{64,96},{96,0},{1,33},{33,65},{65,97},{97,1},{2,34}... | collective-permute-start | bytes 196616 | tf_op jit(solution)/shard_map/ppermute | solution.py:294
  10.2 0.9 copy-done
  11.1 0.9 copy-done.1
  12.1 0.8 copy-done.2
  17.4 3.1 %collective-permute-start.5 = (bf16[2,512,128]{2,1,0:T(8,128)(2,1)S(1)}, bf16[2,512,128]{2,1,0:T(8,128)(2,1)S(1)}, u32[]{:S(2)}, u32[]{:S(2)}) collective-permute-start(bf16[2,512,128]{2,1,0:T(8,128)(2,1)S(1)} %get-tuple-element.91), channel_id=1, source_target_pairs={{0,24},{8,0},{16,8},{24,16},{1,25},{9,1},{17,9},{25,17},{2,26},{10... | collective-permute-start | bytes 786440 | tf_op jit(solution)/shard_map/ppermute | solution.py:294
  20.6 2.2 %collective-permute-start.7 = (bf16[2,512,128]{2,1,0:T(8,128)(2,1)S(1)}, bf16[2,512,128]{2,1,0:T(8,128)(2,1)S(1)}, u32[]{:S(2)}, u32[]{:S(2)}) collective-permute-start(bf16[2,512,128]{2,1,0:T(8,128)(2,1)S(1)} %get-tuple-element.98), channel_id=1, source_target_pairs={{0,16},{8,24},{16,0},{24,8},{1,17},{9,25},{17,1},{25,9},{2,18},{10... | collective-permute-start | bytes 786440 | tf_op jit(solution)/shard_map/ppermute | solution.py:294
  22.9 9.4 %collective-permute-done.5.refs_3_ = bf16[2,512,128]{2,1,0:T(8,128)(2,1)S(1)} collective-permute-done((bf16[2,512,128]{2,1,0:T(8,128)(2,1)S(1)}, bf16[2,512,128]{2,1,0:T(8,128)(2,1)S(1)}, u32[]{:S(2)}, u32[]{:S(2)}) %collective-permute-start.5) | collective-permute-done | bytes 262176 | tf_op jit(solution)/shard_map/ppermute | solution.py:294
  32.3 3.8 %collective-permute-done.4.refs_2_ = bf16[2,512,128]{2,1,0:T(8,128)(2,1)S(1)} collective-permute-done((bf16[2,512,128]{2,1,0:T(8,128)(2,1)S(1)}, bf16[2,512,128]{2,1,0:T(8,128)(2,1)S(1)}, u32[]{:S(2)}, u32[]{:S(2)}) %collective-permute-start.4) | collective-permute-done | bytes 262176 | tf_op jit(solution)/shard_map/ppermute | solution.py:294
  36.5 4.9 %attend_near.1 = (f32[768,128]{1,0:T(8,128)S(1)}, f32[768,128]{1,0:T(8,128)S(1)}, f32[768,128]{1,0:T(8,128)S(1)}) custom-call(bf16[768,128]{1,0:T(8,128)(2,1)S(1)} %get-tuple-element.80.q_all, bf16[2,128,128]{2,1,0:T(8,128)(2,1)S(1)} %get-tuple-element.83.tract.tract_ref, bf16[2,128,128]{2,1,0:T(8,128)(2,1)S(1)} %get-tuple-element.84.cache.cache_ref, ...), custom_call_target="tpu_custom_call" | custom-call | tf_op jit(solution)/shard_map/attend_near/pallas_call | solution.py:31
  41.7 1.5 collective-permute-done.11.refs_3_
  43.3 5.9 %attend.1 = (bf16[128,768]{1,0:T(8,128)(2,1)S(1)}, bf16[2,36,768]{2,1,0:T(8,128)(2,1)S(1)}, bf16[2,36,768]{2,1,0:T(8,128)(2,1)S(1)}, bf16[2,36,768]{2,1,0:T(8,128)(2,1)S(1)}, bf16[2,36,768]{2,1,0:T(8,128)(2,1)S(1)}) custom-call(bf16[768,128]{1,0:T(8,128)(2,1)S(1)} %get-tuple-element.80.q_all, bf16[128,768]{1,0:T(8,128)(2,1)S(1)} %get-tuple-element.81.res_ref, ...), custom_call_target="tpu_custom_call" | custom-call | tf_op jit(solution)/shard_map/attend/pallas_call | solution.py:31
  49.2 2.9 %collective-permute-start.13 = (bf16[2,36,768]{2,1,0:T(8,128)(2,1)S(1)}, bf16[2,36,768]{2,1,0:T(8,128)(2,1)S(1)}, u32[]{:S(2)}, u32[]{:S(2)}) collective-permute-start(bf16[2,36,768]{2,1,0:T(8,128)(2,1)S(1)} %get-tuple-element.115), channel_id=1, source_target_pairs={{0,32},{32,64},{64,96},{96,0},{1,33},{33,65},{65,97},{97,1},{2,34}... | collective-permute-start | bytes 331784 | tf_op jit(solution)/shard_map/ppermute | solution.py:294
  52.2 1.4 collective-permute-start.14
  53.6 2.8 %collective-permute-start.15 = (bf16[2,36,768]{2,1,0:T(8,128)(2,1)S(1)}, bf16[2,36,768]{2,1,0:T(8,128)(2,1)S(1)}, u32[]{:S(2)}, u32[]{:S(2)}) collective-permute-start(bf16[2,36,768]{2,1,0:T(8,128)(2,1)S(1)} %get-tuple-element.117), channel_id=1, source_target_pairs={{0,96},{32,0},{64,32},{96,64},{1,97},{33,1},{65,33},{97,65},{2,98}... | collective-permute-start | bytes 331784 | tf_op jit(solution)/shard_map/ppermute | solution.py:294
  56.5 3.3 %collective-permute-done.13.refs_1_ = bf16[2,36,768]{2,1,0:T(8,128)(2,1)S(1)} collective-permute-done((bf16[2,36,768]{2,1,0:T(8,128)(2,1)S(1)}, bf16[2,36,768]{2,1,0:T(8,128)(2,1)S(1)}, u32[]{:S(2)}, u32[]{:S(2)}) %collective-permute-start.13) | collective-permute-done | bytes 110624 | tf_op jit(solution)/shard_map/ppermute | solution.py:294
  59.8 4.6 %collective-permute-done.14.refs_2_ = bf16[2,36,768]{2,1,0:T(8,128)(2,1)S(1)} collective-permute-done((bf16[2,36,768]{2,1,0:T(8,128)(2,1)S(1)}, bf16[2,36,768]{2,1,0:T(8,128)(2,1)S(1)}, u32[]{:S(2)}, u32[]{:S(2)}) %collective-permute-start.14) | collective-permute-done | bytes 110624 | tf_op jit(solution)/shard_map/ppermute | solution.py:294
  64.9 3.1 %collective-permute-start.18 = (bf16[144,768]{1,0:T(8,128)(2,1)S(1)}, bf16[144,768]{1,0:T(8,128)(2,1)S(1)}, u32[]{:S(2)}, u32[]{:S(2)}) collective-permute-start(bf16[144,768]{1,0:T(8,128)(2,1)S(1)} %get-tuple-element.118), channel_id=1, source_target_pairs={{0,2},{1,3},{2,0},{3,1},{4,6},{5,7},{6,4},{7,5},{8,10},{9,11},{10,... | collective-permute-start | bytes 663560 | tf_op jit(solution)/shard_map/ppermute | solution.py:294
  68.0 1.1 collective-permute-start.17
  69.1 0.9 collective-permute-start.16
  70.0 2.5 %collective-permute-done.19 = bf16[144,768]{1,0:T(8,128)(2,1)S(1)} collective-permute-done((bf16[144,768]{1,0:T(8,128)(2,1)S(1)}, bf16[144,768]{1,0:T(8,128)(2,1)S(1)}, u32[]{:S(2)}, u32[]{:S(2)}) %collective-permute-start.19) | collective-permute-done | bytes 221216 | tf_op jit(solution)/shard_map/ppermute | solution.py:298
  72.6 2.3 %collective-permute-done.18 = bf16[144,768]{1,0:T(8,128)(2,1)S(1)} collective-permute-done((bf16[144,768]{1,0:T(8,128)(2,1)S(1)}, bf16[144,768]{1,0:T(8,128)(2,1)S(1)}, u32[]{:S(2)}, u32[]{:S(2)}) %collective-permute-start.18) | collective-permute-done | bytes 221216 | tf_op jit(solution)/shard_map/ppermute | solution.py:294
  74.8 3.0 %collective-permute-done.17 = bf16[144,768]{1,0:T(8,128)(2,1)S(1)} collective-permute-done((bf16[144,768]{1,0:T(8,128)(2,1)S(1)}, bf16[144,768]{1,0:T(8,128)(2,1)S(1)}, u32[]{:S(2)}, u32[]{:S(2)}) %collective-permute-start.17) | collective-permute-done | bytes 221216 | tf_op jit(solution)/shard_map/ppermute | solution.py:294
  78.8 3.1 %collective-permute-start.23 = (bf16[2,144,768]{2,1,0:T(8,128)(2,1)S(1)}, bf16[2,144,768]{2,1,0:T(8,128)(2,1)S(1)}, u32[]{:S(2)}, u32[]{:S(2)}) collective-permute-start(bf16[2,144,768]{2,1,0:T(8,128)(2,1)S(1)} %pad_maximum_fusion.1.refs_2_), channel_id=1, source_target_pairs={{0,2},{1,3},{2,0},{3,1},{4,6},{5,7},{6,4},{7,5},{8,10},{9,11},{10,... | collective-permute-start | bytes 1327112 | tf_op jit(solution)/shard_map/ppermute | solution.py:294
  81.9 1.1 collective-permute-start.22
  83.0 0.9 collective-permute-start.21
  83.9 9.6 %collective-permute-done.23.refs_5_ = bf16[2,144,768]{2,1,0:T(8,128)(2,1)S(1)} collective-permute-done((bf16[2,144,768]{2,1,0:T(8,128)(2,1)S(1)}, bf16[2,144,768]{2,1,0:T(8,128)(2,1)S(1)}, u32[]{:S(2)}, u32[]{:S(2)}) %collective-permute-start.23) | collective-permute-done | bytes 442400 | tf_op jit(solution)/shard_map/ppermute | solution.py:294
  93.5 7.8 %collective-permute-done.22.refs_4_ = bf16[2,144,768]{2,1,0:T(8,128)(2,1)S(1)} collective-permute-done((bf16[2,144,768]{2,1,0:T(8,128)(2,1)S(1)}, bf16[2,144,768]{2,1,0:T(8,128)(2,1)S(1)}, u32[]{:S(2)}, u32[]{:S(2)}) %collective-permute-start.22) | collective-permute-done | bytes 442400 | tf_op jit(solution)/shard_map/ppermute | solution.py:294
  101.3 16.2 %experts.1 = (bf16[4,144,768]{2,1,0:T(8,128)(2,1)S(1)}, bf16[4,144,768]{2,1,0:T(8,128)(2,1)S(1)}, bf16[2,144,768]{2,1,0:T(8,128)(2,1)S(1)}, bf16[2,144,768]{2,1,...) custom-call(s32[4]{0:T(128)S(1)} %pad_add_fusion.where_ref, ...), custom_call_target="tpu_custom_call" | custom-call | tf_op jit(solution)/shard_map/experts/pallas_call | solution.py:31
  117.6 1.8 %collective-permute-start.28 = (bf16[4,144,768]{2,1,0:T(8,128)(2,1)S(1)}, bf16[4,144,768]{2,1,0:T(8,128)(2,1)S(1)}, u32[]{:S(2)}, u32[]{:S(2)}) collective-permute-start(bf16[4,144,768]{2,1,0:T(8,128)(2,1)S(1)} %get-tuple-element.135), channel_id=1, source_target_pairs={{0,8},{8,0},{1,9},{9,1},{2,10},{10,2},{3,11},{11,3},{4,12},{12,4},... | collective-permute-start | bytes 2654216 | tf_op jit(solution)/shard_map/ppermute | solution.py:302
  119.4 1.4 collective-permute-start.25
  120.7 1.9 %collective-permute-start.26 = (bf16[2,144,768]{2,1,0:T(8,128)(2,1)S(1)}, bf16[2,144,768]{2,1,0:T(8,128)(2,1)S(1)}, u32[]{:S(2)}, u32[]{:S(2)}) collective-permute-start(bf16[2,144,768]{2,1,0:T(8,128)(2,1)S(1)} %get-tuple-element.133), channel_id=1, source_target_pairs={{0,3},{1,0},{2,1},{3,2},{4,7},{5,4},{6,5},{7,6},{8,11},{9,8},{10,9... | collective-permute-start | bytes 1327112 | tf_op jit(solution)/shard_map/ppermute | solution.py:294
  122.6 1.6 collective-permute-start.27
  124.2 7.9 %collective-permute-done.25.refs_3_ = bf16[2,144,768]{2,1,0:T(8,128)(2,1)S(1)} collective-permute-done((bf16[2,144,768]{2,1,0:T(8,128)(2,1)S(1)}, bf16[2,144,768]{2,1,0:T(8,128)(2,1)S(1)}, u32[]{:S(2)}, u32[]{:S(2)}) %collective-permute-start.25) | collective-permute-done | bytes 442400 | tf_op jit(solution)/shard_map/ppermute | solution.py:294
  132.1 1.7 collective-permute-done.26.refs_4_
  133.8 8.9 %collective-permute-done.27.refs_5_ = bf16[2,144,768]{2,1,0:T(8,128)(2,1)S(1)} collective-permute-done((bf16[2,144,768]{2,1,0:T(8,128)(2,1)S(1)}, bf16[2,144,768]{2,1,0:T(8,128)(2,1)S(1)}, u32[]{:S(2)}, u32[]{:S(2)}) %collective-permute-start.27) | collective-permute-done | bytes 442400 | tf_op jit(solution)/shard_map/ppermute | solution.py:294
  143.6 1.1 collective-permute-start.29
  144.7 2.1 %collective-permute-start.30 = (bf16[144,768]{1,0:T(8,128)(2,1)S(1)}, bf16[144,768]{1,0:T(8,128)(2,1)S(1)}, u32[]{:S(2)}, u32[]{:S(2)}) collective-permute-start(bf16[144,768]{1,0:T(8,128)(2,1)S(1)} %get-tuple-element.143), channel_id=1, source_target_pairs={{0,3},{1,0},{2,1},{3,2},{4,7},{5,4},{6,5},{7,6},{8,11},{9,8},{10,9... | collective-permute-start | bytes 663560 | tf_op jit(solution)/shard_map/ppermute | solution.py:294
  146.9 2.5 %collective-permute-done.32 = bf16[144,768]{1,0:T(8,128)(2,1)S(1)} collective-permute-done((bf16[144,768]{1,0:T(8,128)(2,1)S(1)}, bf16[144,768]{1,0:T(8,128)(2,1)S(1)}, u32[]{:S(2)}, u32[]{:S(2)}) %collective-permute-start.32) | collective-permute-done | bytes 221216 | tf_op jit(solution)/shard_map/ppermute | solution.py:302
  149.5 2.7 %collective-permute-start.33 = (bf16[144,768]{1,0:T(8,128)(2,1)S(1)}, bf16[144,768]{1,0:T(8,128)(2,1)S(1)}, u32[]{:S(2)}, u32[]{:S(2)}) collective-permute-start(bf16[144,768]{1,0:T(8,128)(2,1)S(1)} %add_convert_fusion), channel_id=1, source_target_pairs={{0,24},{8,16},{16,8},{24,0},{1,25},{9,17},{17,9},{25,1},{2,26},{10... | collective-permute-start | bytes 663560 | tf_op jit(solution)/shard_map/ppermute | solution.py:298
  152.6 2.2 %collective-permute-done.30.refs_2_ = bf16[144,768]{1,0:T(8,128)(2,1)S(1)} collective-permute-done((bf16[144,768]{1,0:T(8,128)(2,1)S(1)}, bf16[144,768]{1,0:T(8,128)(2,1)S(1)}, u32[]{:S(2)}, u32[]{:S(2)}) %collective-permute-start.30) | collective-permute-done | bytes 221216 | tf_op jit(solution)/shard_map/ppermute | solution.py:294
  155.6 1.1 collective-permute-done.33.refs_4_
  156.9 2.4 %collective-permute-start.34 = (bf16[2,36,768]{2,1,0:T(8,128)(2,1)S(1)}, bf16[2,36,768]{2,1,0:T(8,128)(2,1)S(1)}, u32[]{:S(2)}, u32[]{:S(2)}) collective-permute-start(bf16[2,36,768]{2,1,0:T(8,128)(2,1)S(1)} %get-tuple-element.152), channel_id=1, source_target_pairs={{0,96},{32,0},{64,32},{96,64},{1,97},{33,1},{65,33},{97,65},{2,98}... | collective-permute-start | bytes 331784 | tf_op jit(solution)/shard_map/ppermute | solution.py:294
  159.2 4.6 %collective-permute-start.35 = (bf16[2,36,768]{2,1,0:T(8,128)(2,1)S(1)}, bf16[2,36,768]{2,1,0:T(8,128)(2,1)S(1)}, u32[]{:S(2)}, u32[]{:S(2)}) collective-permute-start(bf16[2,36,768]{2,1,0:T(8,128)(2,1)S(1)} %get-tuple-element.153), channel_id=1, source_target_pairs={{0,64},{32,96},{64,0},{96,32},{1,65},{33,97},{65,1},{97,33},{2,66}... | collective-permute-start | bytes 331784 | tf_op jit(solution)/shard_map/ppermute | solution.py:294
  164.2 7.8 %collective-permute-done.35.refs_2_ = bf16[2,36,768]{2,1,0:T(8,128)(2,1)S(1)} collective-permute-done((bf16[2,36,768]{2,1,0:T(8,128)(2,1)S(1)}, bf16[2,36,768]{2,1,0:T(8,128)(2,1)S(1)}, u32[]{:S(2)}, u32[]{:S(2)}) %collective-permute-start.35) | collective-permute-done | bytes 110624 | tf_op jit(solution)/shard_map/ppermute | solution.py:294
  172.0 3.8 %collective-permute-done.36.refs_3_ = bf16[2,36,768]{2,1,0:T(8,128)(2,1)S(1)} collective-permute-done((bf16[2,36,768]{2,1,0:T(8,128)(2,1)S(1)}, bf16[2,36,768]{2,1,0:T(8,128)(2,1)S(1)}, u32[]{:S(2)}, u32[]{:S(2)}) %collective-permute-start.36) | collective-permute-done | bytes 110624 | tf_op jit(solution)/shard_map/ppermute | solution.py:294
  175.8 2.2 %mix.1 = bf16[128,768]{1,0:T(8,128)(2,1)} custom-call(s32[4]{0:T(128)S(1)} %pad_add_fusion.where_ref, s32[2,128]{1,0:T(2,128)S(1)} %bitcast.24, f32[2,128]{1,0:T(2,128)S(1)} %bitcast.25, bf16[128,768]{1,0:T(8,128)(2,1)S(1)} %get-tuple-element.106.hid_ref, bf16[2,36,768]{2,1,0:T(8,128)(2,1)S(1)} %get-tuple-element.151.refs_0_, ...), custom_call_target="tpu_custom_call" | custom-call | tf_op jit(solution)/shard_map/mix/pallas_call | solution.py:31
  (66 shorter events, 10.3 us)
Async XLA Ops:
  0.0 17.3 %collective-permute-start.3 = (bf16[3072,512]{1,0:T(8,128)(2,1)}, bf16[3072,512]{1,0:T(8,128)(2,1)S(1)}, u32[]{:S(2)}, u32[]{:S(2)}) collective-permute-start(bf16[3072,512]{1,0:T(8,128)(2,1)} %refs_6_.1), channel_id=1, source_target_pairs={{0,4},{4,0},{1,5},{5,1},{2,6},{6,2},{3,7},{7,3},{8,12},{12,8},{9,1... | collective-permute-start | bytes 9437192 | tf_op jit(solution)/shard_map/ppermute | solution.py:306
  0.8 15.7 %collective-permute-start.2 = (bf16[2,128,128]{2,1,0:T(8,128)(2,1)S(1)}, bf16[2,128,128]{2,1,0:T(8,128)(2,1)S(1)}, u32[]{:S(2)}, u32[]{:S(2)}) collective-permute-start(bf16[2,128,128]{2,1,0:T(8,128)(2,1)S(1)} %get-tuple-element.155), channel_id=1, source_target_pairs={{0,64},{32,96},{64,0},{96,32},{1,65},{33,97},{65,1},{97,33},{2,66}... | collective-permute-start | bytes 196616 | tf_op jit(solution)/shard_map/ppermute | solution.py:294
  7.2 9.3 %collective-permute-start.1 = (bf16[2,128,128]{2,1,0:T(8,128)(2,1)S(1)}, bf16[2,128,128]{2,1,0:T(8,128)(2,1)S(1)}, u32[]{:S(2)}, u32[]{:S(2)}) collective-permute-start(bf16[2,128,128]{2,1,0:T(8,128)(2,1)S(1)} %get-tuple-element.156), channel_id=1, source_target_pairs={{0,96},{32,0},{64,32},{96,64},{1,97},{33,1},{65,33},{97,65},{2,98}... | collective-permute-start | bytes 196616 | tf_op jit(solution)/shard_map/ppermute | solution.py:294
  7.8 8.8 %collective-permute-start = (bf16[2,128,128]{2,1,0:T(8,128)(2,1)S(1)}, bf16[2,128,128]{2,1,0:T(8,128)(2,1)S(1)}, u32[]{:S(2)}, u32[]{:S(2)}) collective-permute-start(bf16[2,128,128]{2,1,0:T(8,128)(2,1)S(1)} %get-tuple-element.157), channel_id=1, source_target_pairs={{0,32},{32,64},{64,96},{96,0},{1,33},{33,65},{65,97},{97,1},{2,34}... | collective-permute-start | bytes 196616 | tf_op jit(solution)/shard_map/ppermute | solution.py:294
  10.2 0.9 copy-start
  11.1 0.9 copy-start.1
  12.1 0.8 copy-start.2
  12.8 0.8 copy-start.3
  13.6 0.8 copy-start.4
  17.3 61.3 %copy-start.10 = (bf16[3072,512]{1,0:T(8,128)(2,1)}, bf16[3072,512]{1,0:T(8,128)(2,1)S(1)}, u32[]{:S(2)}) copy-start(bf16[3072,512]{1,0:T(8,128)(2,1)S(1)} %collective-permute-done.3.refs_9_) | copy-start | bytes 9437188
  17.3 24.2 %collective-permute-start.10 = (bf16[3072,512]{1,0:T(8,128)(2,1)}, bf16[3072,512]{1,0:T(8,128)(2,1)S(1)}, u32[]{:S(2)}, u32[]{:S(2)}) collective-permute-start(bf16[3072,512]{1,0:T(8,128)(2,1)} %refs_7_.1), channel_id=1, source_target_pairs={{0,4},{4,0},{1,5},{5,1},{2,6},{6,2},{3,7},{7,3},{8,12},{12,8},{9,1... | collective-permute-start | bytes 9437192 | tf_op jit(solution)/shard_map/ppermute | solution.py:306
  17.4 14.9 %collective-permute-start.5 = (bf16[2,512,128]{2,1,0:T(8,128)(2,1)S(1)}, bf16[2,512,128]{2,1,0:T(8,128)(2,1)S(1)}, u32[]{:S(2)}, u32[]{:S(2)}) collective-permute-start(bf16[2,512,128]{2,1,0:T(8,128)(2,1)S(1)} %get-tuple-element.91), channel_id=1, source_target_pairs={{0,24},{8,0},{16,8},{24,16},{1,25},{9,1},{17,9},{25,17},{2,26},{10... | collective-permute-start | bytes 786440 | tf_op jit(solution)/shard_map/ppermute | solution.py:294
  20.5 11.8 %collective-permute-start.6 = (bf16[2,512,128]{2,1,0:T(8,128)(2,1)S(1)}, bf16[2,512,128]{2,1,0:T(8,128)(2,1)S(1)}, u32[]{:S(2)}, u32[]{:S(2)}) collective-permute-start(bf16[2,512,128]{2,1,0:T(8,128)(2,1)S(1)} %get-tuple-element.89.refs_0_), channel_id=1, source_target_pairs={{0,4},{4,0},{1,5},{5,1},{2,6},{6,2},{3,7},{7,3},{8,12},{12,8},{9,1... | collective-permute-start | bytes 786440 | tf_op jit(solution)/shard_map/ppermute | solution.py:306
  20.6 15.4 %collective-permute-start.4 = (bf16[2,512,128]{2,1,0:T(8,128)(2,1)S(1)}, bf16[2,512,128]{2,1,0:T(8,128)(2,1)S(1)}, u32[]{:S(2)}, u32[]{:S(2)}) collective-permute-start(bf16[2,512,128]{2,1,0:T(8,128)(2,1)S(1)} %get-tuple-element.90), channel_id=1, source_target_pairs={{0,8},{8,16},{16,24},{24,0},{1,9},{9,17},{17,25},{25,1},{2,10},{10... | collective-permute-start | bytes 786440 | tf_op jit(solution)/shard_map/ppermute | solution.py:294
  20.6 20.9 %collective-permute-start.7 = (bf16[2,512,128]{2,1,0:T(8,128)(2,1)S(1)}, bf16[2,512,128]{2,1,0:T(8,128)(2,1)S(1)}, u32[]{:S(2)}, u32[]{:S(2)}) collective-permute-start(bf16[2,512,128]{2,1,0:T(8,128)(2,1)S(1)} %get-tuple-element.98), channel_id=1, source_target_pairs={{0,16},{8,24},{16,0},{24,8},{1,17},{9,25},{17,1},{25,9},{2,18},{10... | collective-permute-start | bytes 786440 | tf_op jit(solution)/shard_map/ppermute | solution.py:294
  36.0 5.5 %collective-permute-start.8 = (bf16[2,512,128]{2,1,0:T(8,128)(2,1)S(1)}, bf16[2,512,128]{2,1,0:T(8,128)(2,1)S(1)}, u32[]{:S(2)}, u32[]{:S(2)}) collective-permute-start(bf16[2,512,128]{2,1,0:T(8,128)(2,1)S(1)} %collective-permute-done.4.refs_2_), channel_id=1, source_target_pairs={{0,4},{4,0},{1,5},{5,1},{2,6},{6,2},{3,7},{7,3},{8,12},{12,8},{9,1... | collective-permute-start | bytes 786440 | tf_op jit(solution)/shard_map/ppermute | solution.py:306
  36.0 5.5 %collective-permute-start.9 = (bf16[2,512,128]{2,1,0:T(8,128)(2,1)S(1)}, bf16[2,512,128]{2,1,0:T(8,128)(2,1)S(1)}, u32[]{:S(2)}, u32[]{:S(2)}) collective-permute-start(bf16[2,512,128]{2,1,0:T(8,128)(2,1)S(1)} %collective-permute-done.5.refs_3_), channel_id=1, source_target_pairs={{0,4},{4,0},{1,5},{5,1},{2,6},{6,2},{3,7},{7,3},{8,12},{12,8},{9,1... | collective-permute-start | bytes 786440 | tf_op jit(solution)/shard_map/ppermute | solution.py:306
  41.5 59.8 %copy-start.6 = (f32[3072]{0:T(1024)S(1)}, f32[3072]{0:T(1024)}, u32[]{:S(2)}) copy-start(f32[3072]{0:T(1024)} %param.18) | copy-start | bytes 36868
  41.5 59.7 %copy-start.11 = (bf16[3072,512]{1,0:T(8,128)(2,1)}, bf16[3072,512]{1,0:T(8,128)(2,1)S(1)}, u32[]{:S(2)}) copy-start(bf16[3072,512]{1,0:T(8,128)(2,1)S(1)} %collective-permute-done.10.refs_10_) | copy-start | bytes 9437188
  41.6 1.6 collective-permute-start.11
  43.2 6.0 %collective-permute-start.12 = (bf16[512,3072]{1,0:T(8,128)(2,1)}, bf16[512,3072]{1,0:T(8,128)(2,1)S(1)}, u32[]{:S(2)}, u32[]{:S(2)}) collective-permute-start(bf16[512,3072]{1,0:T(8,128)(2,1)} %refs_8_.1), channel_id=1, source_target_pairs={{0,4},{4,0},{1,5},{5,1},{2,6},{6,2},{3,7},{7,3},{8,12},{12,8},{9,1... | collective-permute-start | bytes 9437192 | tf_op jit(solution)/shard_map/ppermute | solution.py:306
  49.2 29.5 %copy-start.12 = (bf16[512,3072]{1,0:T(8,128)(2,1)}, bf16[512,3072]{1,0:T(8,128)(2,1)S(1)}, u32[]{:S(2)}) copy-start(bf16[512,3072]{1,0:T(8,128)(2,1)S(1)} %collective-permute-done.12.refs_11_) | copy-start | bytes 9437188
  49.2 10.6 %collective-permute-start.13 = (bf16[2,36,768]{2,1,0:T(8,128)(2,1)S(1)}, bf16[2,36,768]{2,1,0:T(8,128)(2,1)S(1)}, u32[]{:S(2)}, u32[]{:S(2)}) collective-permute-start(bf16[2,36,768]{2,1,0:T(8,128)(2,1)S(1)} %get-tuple-element.115), channel_id=1, source_target_pairs={{0,32},{32,64},{64,96},{96,0},{1,33},{33,65},{65,97},{97,1},{2,34}... | collective-permute-start | bytes 331784 | tf_op jit(solution)/shard_map/ppermute | solution.py:294
  52.2 12.2 %collective-permute-start.14 = (bf16[2,36,768]{2,1,0:T(8,128)(2,1)S(1)}, bf16[2,36,768]{2,1,0:T(8,128)(2,1)S(1)}, u32[]{:S(2)}, u32[]{:S(2)}) collective-permute-start(bf16[2,36,768]{2,1,0:T(8,128)(2,1)S(1)} %get-tuple-element.116), channel_id=1, source_target_pairs={{0,64},{32,96},{64,0},{96,32},{1,65},{33,97},{65,1},{97,33},{2,66}... | collective-permute-start | bytes 331784 | tf_op jit(solution)/shard_map/ppermute | solution.py:294
  53.6 11.1 %collective-permute-start.15 = (bf16[2,36,768]{2,1,0:T(8,128)(2,1)S(1)}, bf16[2,36,768]{2,1,0:T(8,128)(2,1)S(1)}, u32[]{:S(2)}, u32[]{:S(2)}) collective-permute-start(bf16[2,36,768]{2,1,0:T(8,128)(2,1)S(1)} %get-tuple-element.117), channel_id=1, source_target_pairs={{0,96},{32,0},{64,32},{96,64},{1,97},{33,1},{65,33},{97,65},{2,98}... | collective-permute-start | bytes 331784 | tf_op jit(solution)/shard_map/ppermute | solution.py:294
  64.8 7.8 %collective-permute-start.19 = (bf16[144,768]{1,0:T(8,128)(2,1)S(1)}, bf16[144,768]{1,0:T(8,128)(2,1)S(1)}, u32[]{:S(2)}, u32[]{:S(2)}) collective-permute-start(bf16[144,768]{1,0:T(8,128)(2,1)S(1)} %get-tuple-element.119), channel_id=1, source_target_pairs={{0,24},{8,16},{16,8},{24,0},{1,25},{9,17},{17,9},{25,1},{2,26},{10... | collective-permute-start | bytes 663560 | tf_op jit(solution)/shard_map/ppermute | solution.py:298
  64.9 10.0 %collective-permute-start.18 = (bf16[144,768]{1,0:T(8,128)(2,1)S(1)}, bf16[144,768]{1,0:T(8,128)(2,1)S(1)}, u32[]{:S(2)}, u32[]{:S(2)}) collective-permute-start(bf16[144,768]{1,0:T(8,128)(2,1)S(1)} %get-tuple-element.118), channel_id=1, source_target_pairs={{0,2},{1,3},{2,0},{3,1},{4,6},{5,7},{6,4},{7,5},{8,10},{9,11},{10,... | collective-permute-start | bytes 663560 | tf_op jit(solution)/shard_map/ppermute | solution.py:294
  68.0 9.8 %collective-permute-start.17 = (bf16[144,768]{1,0:T(8,128)(2,1)S(1)}, bf16[144,768]{1,0:T(8,128)(2,1)S(1)}, u32[]{:S(2)}, u32[]{:S(2)}) collective-permute-start(bf16[144,768]{1,0:T(8,128)(2,1)S(1)} %get-tuple-element.118), channel_id=1, source_target_pairs={{0,3},{1,0},{2,1},{3,2},{4,7},{5,4},{6,5},{7,6},{8,11},{9,8},{10,9... | collective-permute-start | bytes 663560 | tf_op jit(solution)/shard_map/ppermute | solution.py:294
  69.1 8.8 %collective-permute-start.16 = (bf16[144,768]{1,0:T(8,128)(2,1)S(1)}, bf16[144,768]{1,0:T(8,128)(2,1)S(1)}, u32[]{:S(2)}, u32[]{:S(2)}) collective-permute-start(bf16[144,768]{1,0:T(8,128)(2,1)S(1)} %get-tuple-element.118), channel_id=1, source_target_pairs={{0,1},{1,2},{2,3},{3,0},{4,5},{5,6},{6,7},{7,4},{8,9},{9,10},{10,1... | collective-permute-start | bytes 663560 | tf_op jit(solution)/shard_map/ppermute | solution.py:294
  72.6 5.9 %collective-permute-start.20 = (bf16[144,768]{1,0:T(8,128)(2,1)S(1)}, bf16[144,768]{1,0:T(8,128)(2,1)S(1)}, u32[]{:S(2)}, u32[]{:S(2)}) collective-permute-start(bf16[144,768]{1,0:T(8,128)(2,1)S(1)} %collective-permute-done.19), channel_id=1, source_target_pairs={{0,8},{8,0},{1,9},{9,1},{2,10},{10,2},{3,11},{11,3},{4,12},{12,4},... | collective-permute-start | bytes 663560 | tf_op jit(solution)/shard_map/ppermute | solution.py:302
  78.6 22.7 %collective-permute-start.24 = (bf16[4,144,768]{2,1,0:T(8,128)(2,1)S(1)}, bf16[4,144,768]{2,1,0:T(8,128)(2,1)S(1)}, u32[]{:S(2)}, u32[]{:S(2)}) collective-permute-start(bf16[4,144,768]{2,1,0:T(8,128)(2,1)S(1)} %pad_maximum_fusion.refs_0_), channel_id=1, source_target_pairs={{0,8},{8,0},{1,9},{9,1},{2,10},{10,2},{3,11},{11,3},{4,12},{12,4},... | collective-permute-start | bytes 2654216 | tf_op jit(solution)/shard_map/ppermute | solution.py:302
  78.8 14.7 %collective-permute-start.23 = (bf16[2,144,768]{2,1,0:T(8,128)(2,1)S(1)}, bf16[2,144,768]{2,1,0:T(8,128)(2,1)S(1)}, u32[]{:S(2)}, u32[]{:S(2)}) collective-permute-start(bf16[2,144,768]{2,1,0:T(8,128)(2,1)S(1)} %pad_maximum_fusion.1.refs_2_), channel_id=1, source_target_pairs={{0,2},{1,3},{2,0},{3,1},{4,6},{5,7},{6,4},{7,5},{8,10},{9,11},{10,... | collective-permute-start | bytes 1327112 | tf_op jit(solution)/shard_map/ppermute | solution.py:294
  81.9 19.4 %collective-permute-start.22 = (bf16[2,144,768]{2,1,0:T(8,128)(2,1)S(1)}, bf16[2,144,768]{2,1,0:T(8,128)(2,1)S(1)}, u32[]{:S(2)}, u32[]{:S(2)}) collective-permute-start(bf16[2,144,768]{2,1,0:T(8,128)(2,1)S(1)} %pad_maximum_fusion.1.refs_2_), channel_id=1, source_target_pairs={{0,3},{1,0},{2,1},{3,2},{4,7},{5,4},{6,5},{7,6},{8,11},{9,8},{10,9... | collective-permute-start | bytes 1327112 | tf_op jit(solution)/shard_map/ppermute | solution.py:294
  83.0 18.3 %collective-permute-start.21 = (bf16[2,144,768]{2,1,0:T(8,128)(2,1)S(1)}, bf16[2,144,768]{2,1,0:T(8,128)(2,1)S(1)}, u32[]{:S(2)}, u32[]{:S(2)}) collective-permute-start(bf16[2,144,768]{2,1,0:T(8,128)(2,1)S(1)} %pad_maximum_fusion.1.refs_2_), channel_id=1, source_target_pairs={{0,1},{1,2},{2,3},{3,0},{4,5},{5,6},{6,7},{7,4},{8,9},{9,10},{10,1... | collective-permute-start | bytes 1327112 | tf_op jit(solution)/shard_map/ppermute | solution.py:294
  117.5 58.3 %copy-start.8 = (s32[128,2]{0,1:T(2,128)S(1)}, s32[128,2]{0,1:T(2,128)}, u32[]{:S(2)}) copy-start(s32[128,2]{0,1:T(2,128)} %param.22) | copy-start | bytes 3076
  117.5 58.3 %copy-start.9 = (f32[128,2]{0,1:T(2,128)S(1)}, f32[128,2]{0,1:T(2,128)}, u32[]{:S(2)}) copy-start(f32[128,2]{0,1:T(2,128)} %param.23) | copy-start | bytes 3076
  117.6 25.2 %collective-permute-start.28 = (bf16[4,144,768]{2,1,0:T(8,128)(2,1)S(1)}, bf16[4,144,768]{2,1,0:T(8,128)(2,1)S(1)}, u32[]{:S(2)}, u32[]{:S(2)}) collective-permute-start(bf16[4,144,768]{2,1,0:T(8,128)(2,1)S(1)} %get-tuple-element.135), channel_id=1, source_target_pairs={{0,8},{8,0},{1,9},{9,1},{2,10},{10,2},{3,11},{11,3},{4,12},{12,4},... | collective-permute-start | bytes 2654216 | tf_op jit(solution)/shard_map/ppermute | solution.py:302
  119.4 12.8 %collective-permute-start.25 = (bf16[2,144,768]{2,1,0:T(8,128)(2,1)S(1)}, bf16[2,144,768]{2,1,0:T(8,128)(2,1)S(1)}, u32[]{:S(2)}, u32[]{:S(2)}) collective-permute-start(bf16[2,144,768]{2,1,0:T(8,128)(2,1)S(1)} %get-tuple-element.132), channel_id=1, source_target_pairs={{0,1},{1,2},{2,3},{3,0},{4,5},{5,6},{6,7},{7,4},{8,9},{9,10},{10,1... | collective-permute-start | bytes 1327112 | tf_op jit(solution)/shard_map/ppermute | solution.py:294
  120.7 13.1 %collective-permute-start.26 = (bf16[2,144,768]{2,1,0:T(8,128)(2,1)S(1)}, bf16[2,144,768]{2,1,0:T(8,128)(2,1)S(1)}, u32[]{:S(2)}, u32[]{:S(2)}) collective-permute-start(bf16[2,144,768]{2,1,0:T(8,128)(2,1)S(1)} %get-tuple-element.133), channel_id=1, source_target_pairs={{0,3},{1,0},{2,1},{3,2},{4,7},{5,4},{6,5},{7,6},{8,11},{9,8},{10,9... | collective-permute-start | bytes 1327112 | tf_op jit(solution)/shard_map/ppermute | solution.py:294
  122.6 20.1 %collective-permute-start.27 = (bf16[2,144,768]{2,1,0:T(8,128)(2,1)S(1)}, bf16[2,144,768]{2,1,0:T(8,128)(2,1)S(1)}, u32[]{:S(2)}, u32[]{:S(2)}) collective-permute-start(bf16[2,144,768]{2,1,0:T(8,128)(2,1)S(1)} %get-tuple-element.134), channel_id=1, source_target_pairs={{0,2},{1,3},{2,0},{3,1},{4,6},{5,7},{6,4},{7,5},{8,10},{9,11},{10,... | collective-permute-start | bytes 1327112 | tf_op jit(solution)/shard_map/ppermute | solution.py:294
  143.1 6.3 %collective-permute-start.32 = (bf16[144,768]{1,0:T(8,128)(2,1)S(1)}, bf16[144,768]{1,0:T(8,128)(2,1)S(1)}, u32[]{:S(2)}, u32[]{:S(2)}) collective-permute-start(bf16[144,768]{1,0:T(8,128)(2,1)S(1)} %get-tuple-element.146), channel_id=1, source_target_pairs={{0,8},{8,0},{1,9},{9,1},{2,10},{10,2},{3,11},{11,3},{4,12},{12,4},... | collective-permute-start | bytes 663560 | tf_op jit(solution)/shard_map/ppermute | solution.py:302
  143.6 9.0 %collective-permute-start.29 = (bf16[144,768]{1,0:T(8,128)(2,1)S(1)}, bf16[144,768]{1,0:T(8,128)(2,1)S(1)}, u32[]{:S(2)}, u32[]{:S(2)}) collective-permute-start(bf16[144,768]{1,0:T(8,128)(2,1)S(1)} %get-tuple-element.142), channel_id=1, source_target_pairs={{0,1},{1,2},{2,3},{3,0},{4,5},{5,6},{6,7},{7,4},{8,9},{9,10},{10,1... | collective-permute-start | bytes 663560 | tf_op jit(solution)/shard_map/ppermute | solution.py:294
  144.7 10.1 %collective-permute-start.30 = (bf16[144,768]{1,0:T(8,128)(2,1)S(1)}, bf16[144,768]{1,0:T(8,128)(2,1)S(1)}, u32[]{:S(2)}, u32[]{:S(2)}) collective-permute-start(bf16[144,768]{1,0:T(8,128)(2,1)S(1)} %get-tuple-element.143), channel_id=1, source_target_pairs={{0,3},{1,0},{2,1},{3,2},{4,7},{5,4},{6,5},{7,6},{8,11},{9,8},{10,9... | collective-permute-start | bytes 663560 | tf_op jit(solution)/shard_map/ppermute | solution.py:294
  146.8 8.7 %collective-permute-start.31 = (bf16[144,768]{1,0:T(8,128)(2,1)S(1)}, bf16[144,768]{1,0:T(8,128)(2,1)S(1)}, u32[]{:S(2)}, u32[]{:S(2)}) collective-permute-start(bf16[144,768]{1,0:T(8,128)(2,1)S(1)} %get-tuple-element.144), channel_id=1, source_target_pairs={{0,2},{1,3},{2,0},{3,1},{4,6},{5,7},{6,4},{7,5},{8,10},{9,11},{10,... | collective-permute-start | bytes 663560 | tf_op jit(solution)/shard_map/ppermute | solution.py:294
  149.5 7.2 %collective-permute-start.33 = (bf16[144,768]{1,0:T(8,128)(2,1)S(1)}, bf16[144,768]{1,0:T(8,128)(2,1)S(1)}, u32[]{:S(2)}, u32[]{:S(2)}) collective-permute-start(bf16[144,768]{1,0:T(8,128)(2,1)S(1)} %add_convert_fusion), channel_id=1, source_target_pairs={{0,24},{8,16},{16,8},{24,0},{1,25},{9,17},{17,9},{25,1},{2,26},{10... | collective-permute-start | bytes 663560 | tf_op jit(solution)/shard_map/ppermute | solution.py:298
  156.9 7.4 %collective-permute-start.34 = (bf16[2,36,768]{2,1,0:T(8,128)(2,1)S(1)}, bf16[2,36,768]{2,1,0:T(8,128)(2,1)S(1)}, u32[]{:S(2)}, u32[]{:S(2)}) collective-permute-start(bf16[2,36,768]{2,1,0:T(8,128)(2,1)S(1)} %get-tuple-element.152), channel_id=1, source_target_pairs={{0,96},{32,0},{64,32},{96,64},{1,97},{33,1},{65,33},{97,65},{2,98}... | collective-permute-start | bytes 331784 | tf_op jit(solution)/shard_map/ppermute | solution.py:294
  159.2 12.8 %collective-permute-start.35 = (bf16[2,36,768]{2,1,0:T(8,128)(2,1)S(1)}, bf16[2,36,768]{2,1,0:T(8,128)(2,1)S(1)}, u32[]{:S(2)}, u32[]{:S(2)}) collective-permute-start(bf16[2,36,768]{2,1,0:T(8,128)(2,1)S(1)} %get-tuple-element.153), channel_id=1, source_target_pairs={{0,64},{32,96},{64,0},{96,32},{1,65},{33,97},{65,1},{97,33},{2,66}... | collective-permute-start | bytes 331784 | tf_op jit(solution)/shard_map/ppermute | solution.py:294
  163.8 12.0 %collective-permute-start.36 = (bf16[2,36,768]{2,1,0:T(8,128)(2,1)S(1)}, bf16[2,36,768]{2,1,0:T(8,128)(2,1)S(1)}, u32[]{:S(2)}, u32[]{:S(2)}) collective-permute-start(bf16[2,36,768]{2,1,0:T(8,128)(2,1)S(1)} %get-tuple-element.154), channel_id=1, source_target_pairs={{0,32},{32,64},{64,96},{96,0},{1,33},{33,65},{65,97},{97,1},{2,34}... | collective-permute-start | bytes 331784 | tf_op jit(solution)/shard_map/ppermute | solution.py:294
  (2 other events, 1.4 us)
where the time goes:
time: 179 us; the launch traced here: 178 us
  waiting for transfers between devices  86.4 us (48%)
  starting transfers between devices  53.4 us (30%)
  Pallas kernels  31.3 us (17%)
  local copies, waits for them, and re-layouts  5.59 us (3%)
    ppermute x24, waiting for transfers between devices, turn(): return lax.ppermute(v, axis, [(i, (i + shift) % n) for i in range(n)])  78.1 us
    ppermute x24, starting transfers between devices, turn(): return lax.ppermute(v, axis, [(i, (i + shift) % n) for i in range(n)])  47.3 us
    pallas_call x9, Pallas kernels, call(): pl.pallas_call(body, out_shape=out_shape, in_specs=[SM] * scalars + [VM]...  31.3 us
    unnamed x26, local copies, waits for them, and re-layouts  5.59 us
    ppermute x2, waiting for transfers between devices, cross(): return lax.ppermute(v, ('yh', 'yl'), [(i, NY - 1 - i) for i in range(NY)])  3.65 us
  transfers between devices with their start and end apart: 37, of which 24 were waited for; matrix products, arithmetic and copies ran while one was open for 1% of the time, Pallas kernels for 7%

commit v1 on v0

--- a/solution.py
+++ b/solution.py
@@ -60,14 +60,11 @@
     return [rank[g : g + 1, :] == row for g in range(EXPERTS)]
 
 
-def prep_kernel(where_ref, ids_ref, q_ref, res_ref, k_ref, v_ref, ck_ref, cv_ref, *outs):
-    q_all, res_out, tract, cache, table = outs
+def prep_kernel(where_ref, ids_ref, q_ref, res_ref, q_all, res_out, table):
     rows = q_ref.shape[0]
     for h in range(q_ref.shape[1] // HEAD_DIM):
         q_all[h * rows : (h + 1) * rows, :] = q_ref[:, h * HEAD_DIM : (h + 1) * HEAD_DIM]
     res_out[...] = res_ref[...]
-    tract[0], tract[1] = k_ref[...], v_ref[...]
-    cache[0], cache[1] = ck_ref[...], cv_ref[...]
     picks = pick_table(where_ref[0], lax.div(where_ref[1], 2), ids_ref)
     table[...] = jnp.concatenate([t.astype(f32) for t in picks], axis=0).astype(bf16)
 
@@ -97,7 +94,7 @@
     return m_new, l, acc
 
 
-def attend_near_kernel(q_all, tract_ref, cache_ref, *refs):
+def attend_own_kernel(q_all, tract_ref, cache_ref, *refs):
     kv_refs, (m_ref, l_ref, acc_ref) = refs[:-3], refs[-3:]
     rows = tract_ref.shape[1]
     tile = 2 * rows
@@ -129,8 +126,26 @@
     lax.fori_loop(0, q_all.shape[0] // tile, group, 0)
 
 
+def attend_more_kernel(q_all, m_ref, l_ref, acc_ref, *refs):
+    kv_refs, (m_out, l_out, acc_out) = refs[:-3], refs[-3:]
+    tile = 256
+
+    def group(g, carry):
+        at = pl.ds(pl.multiple_of(g * tile, tile), tile)
+        q = q_all[at, :]
+        m, l, acc = m_ref[at, :][:, :1], l_ref[at, :][:, :1], acc_ref[at, :]
+        for ref in kv_refs:
+            m, l, acc = attend_piece(q, ref[0], ref[1], m, l, acc)
+        m_out[at, :] = jnp.broadcast_to(m, acc.shape)
+        l_out[at, :] = jnp.broadcast_to(l, acc.shape)
+        acc_out[at, :] = acc
+        return carry
+
+    lax.fori_loop(0, q_all.shape[0] // tile, group, 0)
+
+
 def attend_kernel(q_all, res_ref, table, m_ref, l_ref, acc_ref, *refs):
-    kv_refs, hid_ref, z_refs, o_all = refs[:NY], refs[NY], refs[NY + 1 : -1], refs[-1]
+    kv_refs, hid_ref, z_refs, o_all = refs[:NC], refs[NC], refs[NC + 1 : -1], refs[-1]
     rows, width = res_ref.shape
     heads = width // HEAD_DIM
     tile = 2 * rows
@@ -151,14 +166,14 @@
         hid_ref[:, cols] = (res_ref[:, cols].astype(f32) + attended).astype(bf16)
     routed = jnp.dot(table[...], hid_ref[...], preferred_element_type=f32).astype(bf16)
     for g in range(EXPERTS):
-        z_refs[g // 2][g % 2] = routed[g * PAD : g * PAD + CAP]
+        z_refs[g // 2][(g % 2) * CAP : (g % 2 + 1) * CAP, :] = routed[g * PAD : g * PAD + CAP]
 
 
 def merge_kernel(*refs):
     keep, away = refs[NZ:]
     for d, ref in enumerate(refs[:NZ]):
-        keep[d * CAP : (d + 1) * CAP, :] = ref[0]
-        away[d * CAP : (d + 1) * CAP, :] = ref[1]
+        keep[d * CAP : (d + 1) * CAP, :] = ref[:CAP]
+        away[d * CAP : (d + 1) * CAP, :] = ref[CAP:]
 
 
 def expert_kernel(where_ref, gain_ref, *refs):
@@ -260,8 +275,8 @@
         total = total + ref[...].astype(f32)
     total = total.astype(bf16)
     for d, out in enumerate(outs):
-        out[0] = total[d * CAP : (d + 1) * CAP]
-        out[1] = back[d * CAP : (d + 1) * CAP, :]
+        out[:CAP] = total[d * CAP : (d + 1) * CAP]
+        out[CAP:] = back[d * CAP : (d + 1) * CAP, :]
 
 
 def mix_kernel(where_ref, ids_ref, gates_ref, hid_ref, *refs):
@@ -275,7 +290,8 @@
         weight.append(jnp.where(pick, gate, 0.0))
     held[...] = jnp.zeros_like(held)
     for g in range(EXPERTS):
-        held[g * PAD : g * PAD + CAP, :] = part_refs[g // 2][g % 2].astype(f32)
+        part = part_refs[g // 2][(g % 2) * CAP : (g % 2 + 1) * CAP, :]
+        held[g * PAD : g * PAD + CAP, :] = part.astype(f32)
     mixture = lax.dot_general(
         jnp.concatenate(weight, axis=0),
         held[...],
@@ -316,51 +332,49 @@
     where = jnp.stack((z, y, lax.axis_index("core"), lax.axis_index("x"))).astype(jnp.int32)
     ids, gates = expert_ids.T, gate_weights.T
     shaped = lambda *dims: jax.ShapeDtypeStruct(dims, bf16)
-    block = shaped(2, rows, HEAD_DIM)
 
     near, past = jnp.stack((keys, values)), jnp.stack((cache_keys, cache_values))
     from_z = [turn(jnp.where(z + s < NZ, near, past), "zh", s) for s in SHIFTS]
-    q_all, res, tract, cache, table = call(
+    q_all, res, table = call(
         prep_kernel,
-        [shaped(heads * rows, HEAD_DIM), shaped(rows, width), block, block, shaped(EXPERTS * PAD, rows)],
-        [where, ids, queries, residual, keys, values, cache_keys, cache_values],
+        [shaped(heads * rows, HEAD_DIM), shaped(rows, width), shaped(EXPERTS * PAD, rows)],
+        [where, ids, queries, residual],
         "prep",
         scalars=1,
     )
     packed = call(
         pack_kv_kernel,
         [shaped(2, NZ * rows, HEAD_DIM)] * 4,
-        [where, tract, cache, *from_z],
+        [where, near, past, *from_z],
         "pack_kv",
         scalars=1,
     )
     packed, other_gate = lax.optimization_barrier((packed, swap_core(w_gate)))
     held = lax.optimization_barrier((w_up, packed[0]))[0]
-    y_1, y_3, partner = lax.optimization_barrier(
-        [turn(packed[0], ("yh", "yl"), 1), turn(packed[1], ("yh", "yl"), 3), swap_core(packed[3])]
-    )
-    y_2 = turn(packed[2], ("yh", "yl"), 2)
+    partner = swap_core(packed[3])
+    y_1, y_3 = turn(packed[0], ("yh", "yl"), 1), turn(packed[1], ("yh", "yl"), 3)
+    state = [jax.ShapeDtypeStruct((heads * rows, HEAD_DIM), f32)] * 3
+    carried = call(attend_own_kernel, state, [q_all, near, past, packed[3], partner], "attend_own")
+    carried, y_1, y_3, last, other_up = lax.optimization_barrier(
+        (carried, y_1, y_3, packed[2], swap_core(held))
+    )
+    y_2 = turn(last, ("yh", "yl"), 2)
     far_1, far_3 = swap_core(y_1), swap_core(y_3)
-    state = [jax.ShapeDtypeStruct((heads * rows, HEAD_DIM), f32)] * 3
-    carried = call(
-        attend_near_kernel, state, [q_all, tract, cache, packed[3], partner, y_1, y_3], "attend_near"
-    )
-    carried, y_2, far_1, far_3, other_up = lax.optimization_barrier(
-        (carried, y_2, far_1, far_3, swap_core(held))
-    )
+    carried = call(attend_more_kernel, state, [q_all, *carried, y_1, y_3, far_1, far_3], "attend_more")
+    carried, y_2 = lax.optimization_barrier((carried, y_2))
     far_2 = swap_core(y_2)
     held = lax.optimization_barrier((w_down, far_2))[0]
     own, other = (w_gate, w_up, w_down), (other_gate, other_up, swap_core(held))
     hidden, *sent = call(
         attend_kernel,
-        [shaped(rows, width)] + [shaped(2, CAP, width)] * NZ,
-        [q_all, res, table, *carried, y_2, far_1, far_3, far_2],
+        [shaped(rows, width)] + [shaped(2 * CAP, width)] * NZ,
+        [q_all, res, table, *carried, y_2, far_2],
         "attend",
         [pltpu.VMEM((heads * rows, HEAD_DIM), f32)],
     )
 
-    sent, other = lax.optimization_barrier((sent, other))
     arrived = [sent[0]] + [turn(sent[s], "zh", s) for s in (1, 2, 3)]
+    arrived, other = lax.optimization_barrier((arrived, other))
     rows_a = shaped(NZ * CAP, width)
     a, away = call(merge_kernel, [rows_a] * 2, arrived, "merge")
     b = cross(away)
@@ -386,7 +400,7 @@
     )
     result = call(
         last_sum_kernel,
-        [shaped(2, CAP, width)] * NZ,
+        [shaped(2 * CAP, width)] * NZ,
         [a_sums[0], *moved],
         "last_sum",
     )

time: 179 us -> 173 us (0.966)
  waiting for transfers between devices: 86.4 us -> 80.5 us
  local copies, waits for them, and re-layouts: 5.59 us -> 2.57 us
    ppermute x24, waiting for transfers between devices: 78.1 us -> 71.6 us  [turn(): return lax.ppermute(v, axis, [(i, (i + shift) % n) for i in range(n)])]
    unnamed x26 -> x20, local copies, waits for them, and re-layouts: 5.59 us -> 2.57 us
    pallas_call x9 -> x10, Pallas kernels: 31.3 us -> 32.4 us  [call(): pl.pallas_call(body, out_shape=out_shape, in_specs=[SM] * scalars + [VM]...]
  transfers between devices with their start and end apart: 37 -> 37, of which waited for: 24 -> 28; matrix products, arithmetic and copies ran while one was open for 1% -> 1% of each run, Pallas kernels for 7% -> 8%
where the time goes in v1:
time: 173 us; the launch traced here: 171 us
  waiting for transfers between devices  80.5 us (47%)
  starting transfers between devices  53.6 us (31%)
  Pallas kernels  32.4 us (19%)
  local copies, waits for them, and re-layouts  2.57 us (1%)
  other arithmetic  1.77 us (1%)
    ppermute x24, waiting for transfers between devices, turn(): return lax.ppermute(v, axis, [(i, (i + shift) % n) for i in range(n)])  71.6 us
    ppermute x24, starting transfers between devices, turn(): return lax.ppermute(v, axis, [(i, (i + shift) % n) for i in range(n)])  46.6 us
    pallas_call x10, Pallas kernels, call(): pl.pallas_call(body, out_shape=out_shape, in_specs=[SM] * scalars + [VM]...  32.4 us
  transfers between devices with their start and end apart: 37, of which 28 were waited for; matrix products, arithmetic and copies ran while one was open for 1% of the time, Pallas kernels for 8%

profile of v1, /device:TPU:32, one launch (start us, length us, event | category | flops | bytes accessed | tf_op | source)
XLA Modules:
  0.0 171.1 jit_solution(9390469924786110030)
XLA Ops:
  0.0 1.5 broadcast_select_fusion
  1.5 6.3 %collective-permute-start.2 = (bf16[2,128,128]{2,1,0:T(8,128)(2,1)}, bf16[2,128,128]{2,1,0:T(8,128)(2,1)S(1)}, u32[]{:S(2)}, u32[]{:S(2)}) collective-permute-start(bf16[2,128,128]{2,1,0:T(8,128)(2,1)} %get-tuple-element.159), channel_id=1, source_target_pairs={{0,64},{32,96},{64,0},{96,32},{1,65},{33,97},{65,1},{97,33},{2,66}... | collective-permute-start | bytes 196616 | tf_op jit(solution)/shard_map/ppermute | solution.py:310
  7.8 1.5 collective-permute-start
  9.3 2.7 %collective-permute-start.1 = (bf16[2,128,128]{2,1,0:T(8,128)(2,1)S(1)}, bf16[2,128,128]{2,1,0:T(8,128)(2,1)S(1)}, u32[]{:S(2)}, u32[]{:S(2)}) collective-permute-start(bf16[2,128,128]{2,1,0:T(8,128)(2,1)S(1)} %get-tuple-element.161), channel_id=1, source_target_pairs={{0,96},{32,0},{64,32},{96,64},{1,97},{33,1},{65,33},{97,65},{2,98}... | collective-permute-start | bytes 196616 | tf_op jit(solution)/shard_map/ppermute | solution.py:310
  12.1 3.7 %collective-permute-done.refs_0_ = bf16[2,128,128]{2,1,0:T(8,128)(2,1)S(1)} collective-permute-done((bf16[2,128,128]{2,1,0:T(8,128)(2,1)}, bf16[2,128,128]{2,1,0:T(8,128)(2,1)S(1)}, u32[]{:S(2)}, u32[]{:S(2)}) %collective-permute-start) | collective-permute-done | bytes 65568 | tf_op jit(solution)/shard_map/ppermute | solution.py:310
  17.1 3.0 %collective-permute-start.6 = (bf16[2,512,128]{2,1,0:T(8,128)(2,1)S(1)}, bf16[2,512,128]{2,1,0:T(8,128)(2,1)S(1)}, u32[]{:S(2)}, u32[]{:S(2)}) collective-permute-start(bf16[2,512,128]{2,1,0:T(8,128)(2,1)S(1)} %get-tuple-element.94), channel_id=1, source_target_pairs={{0,24},{8,0},{16,8},{24,16},{1,25},{9,1},{17,9},{25,17},{2,26},{10... | collective-permute-start | bytes 786440 | tf_op jit(solution)/shard_map/ppermute | solution.py:310
  23.4 3.1 %attend_own.1 = (f32[768,128]{1,0:T(8,128)S(1)}, f32[768,128]{1,0:T(8,128)S(1)}, f32[768,128]{1,0:T(8,128)S(1)}) custom-call(bf16[768,128]{1,0:T(8,128)(2,1)S(1)} %get-tuple-element.82.q_all, bf16[2,128,128]{2,1,0:T(8,128)(2,1)S(1)} %get-tuple-element.162.tract.tract_ref, bf16[2,128,128]{2,1,0:T(8,128)(2,1)S(1)} %get-tuple-element.163.cache.cache_ref, ...), custom_call_target="tpu_custom_call" | custom-call | tf_op jit(solution)/shard_map/attend_own/pallas_call | solution.py:31
  26.5 2.8 %collective-permute-done.5.refs_0_ = bf16[2,512,128]{2,1,0:T(8,128)(2,1)S(1)} collective-permute-done((bf16[2,512,128]{2,1,0:T(8,128)(2,1)S(1)}, bf16[2,512,128]{2,1,0:T(8,128)(2,1)S(1)}, u32[]{:S(2)}, u32[]{:S(2)}) %collective-permute-start.5) | collective-permute-done | bytes 262176 | tf_op jit(solution)/shard_map/ppermute | solution.py:310
  29.8 1.0 collective-permute-done.8.refs_2_
  31.2 5.7 %attend_more.1 = (f32[768,128]{1,0:T(8,128)S(1)}, f32[768,128]{1,0:T(8,128)S(1)}, f32[768,128]{1,0:T(8,128)S(1)}) custom-call(bf16[768,128]{1,0:T(8,128)(2,1)S(1)} %get-tuple-element.82.q_all, f32[768,128]{1,0:T(8,128)S(1)} %get-tuple-element.97.m_ref, f32[768,128]{1,0:T(8,128)S(1)} %get-tuple-element.98.l_ref, f32[768,128]{1,0:T(8,128)S(1)} %get-tuple-element.99.acc_ref, ...), custom_call_target="tpu_custom_call" | custom-call | tf_op jit(solution)/shard_map/attend_more/pallas_call | solution.py:31
  36.9 2.7 %collective-permute-done.10.refs_0_ = bf16[2,512,128]{2,1,0:T(8,128)(2,1)S(1)} collective-permute-done((bf16[2,512,128]{2,1,0:T(8,128)(2,1)S(1)}, bf16[2,512,128]{2,1,0:T(8,128)(2,1)S(1)}, u32[]{:S(2)}, u32[]{:S(2)}) %collective-permute-start.10) | collective-permute-done | bytes 262176 | tf_op jit(solution)/shard_map/ppermute | solution.py:310
  39.7 1.5 collective-permute-done.11.refs_1_
  41.3 3.1 %attend.1 = (bf16[128,768]{1,0:T(8,128)(2,1)S(1)}, bf16[72,768]{1,0:T(8,128)(2,1)S(1)}, bf16[72,768]{1,0:T(8,128)(2,1)S(1)}, bf16[72,768]{1,0:T(8,128)(2,1)S(1)}, bf16[72,768]{1,0:T(8,128)(2,1)S(1)}) custom-call(bf16[768,128]{1,0:T(8,128)(2,1)S(1)} %get-tuple-element.82.q_all, bf16[128,768]{1,0:T(8,128)(2,1)S(1)} %get-tuple-element.83.res_ref, ...), custom_call_target="tpu_custom_call" | custom-call | tf_op jit(solution)/shard_map/attend/pallas_call | solution.py:31
  44.5 2.0 %collective-permute-start.12 = (bf16[72,768]{1,0:T(8,128)(2,1)S(1)}, bf16[72,768]{1,0:T(8,128)(2,1)S(1)}, u32[]{:S(2)}, u32[]{:S(2)}) collective-permute-start(bf16[72,768]{1,0:T(8,128)(2,1)S(1)} %get-tuple-element.112), channel_id=1, source_target_pairs={{0,32},{32,64},{64,96},{96,0},{1,33},{33,65},{65,97},{97,1},{2,34}... | collective-permute-start | bytes 331784 | tf_op jit(solution)/shard_map/ppermute | solution.py:310
  46.5 3.7 %collective-permute-start.13 = (bf16[72,768]{1,0:T(8,128)(2,1)S(1)}, bf16[72,768]{1,0:T(8,128)(2,1)S(1)}, u32[]{:S(2)}, u32[]{:S(2)}) collective-permute-start(bf16[72,768]{1,0:T(8,128)(2,1)S(1)} %get-tuple-element.113), channel_id=1, source_target_pairs={{0,64},{32,96},{64,0},{96,32},{1,65},{33,97},{65,1},{97,33},{2,66}... | collective-permute-start | bytes 331784 | tf_op jit(solution)/shard_map/ppermute | solution.py:310
  50.2 2.3 %collective-permute-start.14 = (bf16[72,768]{1,0:T(8,128)(2,1)S(1)}, bf16[72,768]{1,0:T(8,128)(2,1)S(1)}, u32[]{:S(2)}, u32[]{:S(2)}) collective-permute-start(bf16[72,768]{1,0:T(8,128)(2,1)S(1)} %get-tuple-element.114), channel_id=1, source_target_pairs={{0,96},{32,0},{64,32},{96,64},{1,97},{33,1},{65,33},{97,65},{2,98}... | collective-permute-start | bytes 331784 | tf_op jit(solution)/shard_map/ppermute | solution.py:310
  52.5 1.5 collective-permute-done.12.refs_1_
  54.0 4.0 %collective-permute-done.13.refs_2_ = bf16[72,768]{1,0:T(8,128)(2,1)S(1)} collective-permute-done((bf16[72,768]{1,0:T(8,128)(2,1)S(1)}, bf16[72,768]{1,0:T(8,128)(2,1)S(1)}, u32[]{:S(2)}, u32[]{:S(2)}) %collective-permute-start.13) | collective-permute-done | bytes 110624 | tf_op jit(solution)/shard_map/ppermute | solution.py:310
  58.0 1.3 collective-permute-done.14.refs_3_
  60.0 3.0 %collective-permute-start.18 = (bf16[144,768]{1,0:T(8,128)(2,1)S(1)}, bf16[144,768]{1,0:T(8,128)(2,1)S(1)}, u32[]{:S(2)}, u32[]{:S(2)}) collective-permute-start(bf16[144,768]{1,0:T(8,128)(2,1)S(1)} %get-tuple-element.122), channel_id=1, source_target_pairs={{0,2},{1,3},{2,0},{3,1},{4,6},{5,7},{6,4},{7,5},{8,10},{9,11},{10,... | collective-permute-start | bytes 663560 | tf_op jit(solution)/shard_map/ppermute | solution.py:310
  63.0 1.1 collective-permute-start.17
  65.0 2.1 %collective-permute-done.19 = bf16[144,768]{1,0:T(8,128)(2,1)S(1)} collective-permute-done((bf16[144,768]{1,0:T(8,128)(2,1)S(1)}, bf16[144,768]{1,0:T(8,128)(2,1)S(1)}, u32[]{:S(2)}, u32[]{:S(2)}) %collective-permute-start.19) | collective-permute-done | bytes 221216 | tf_op jit(solution)/shard_map/ppermute | solution.py:314
  67.2 2.7 %collective-permute-done.18 = bf16[144,768]{1,0:T(8,128)(2,1)S(1)} collective-permute-done((bf16[144,768]{1,0:T(8,128)(2,1)S(1)}, bf16[144,768]{1,0:T(8,128)(2,1)S(1)}, u32[]{:S(2)}, u32[]{:S(2)}) %collective-permute-start.18) | collective-permute-done | bytes 221216 | tf_op jit(solution)/shard_map/ppermute | solution.py:310
  69.8 2.7 %collective-permute-done.17 = bf16[144,768]{1,0:T(8,128)(2,1)S(1)} collective-permute-done((bf16[144,768]{1,0:T(8,128)(2,1)S(1)}, bf16[144,768]{1,0:T(8,128)(2,1)S(1)}, u32[]{:S(2)}, u32[]{:S(2)}) %collective-permute-start.17) | collective-permute-done | bytes 221216 | tf_op jit(solution)/shard_map/ppermute | solution.py:310
  73.4 3.1 %collective-permute-start.23 = (bf16[2,144,768]{2,1,0:T(8,128)(2,1)S(1)}, bf16[2,144,768]{2,1,0:T(8,128)(2,1)S(1)}, u32[]{:S(2)}, u32[]{:S(2)}) collective-permute-start(bf16[2,144,768]{2,1,0:T(8,128)(2,1)S(1)} %pad_maximum_fusion.1.refs_2_), channel_id=1, source_target_pairs={{0,2},{1,3},{2,0},{3,1},{4,6},{5,7},{6,4},{7,5},{8,10},{9,11},{10,... | collective-permute-start | bytes 1327112 | tf_op jit(solution)/shard_map/ppermute | solution.py:310
  76.5 1.1 collective-permute-start.22
  78.5 9.6 %collective-permute-done.23.refs_5_ = bf16[2,144,768]{2,1,0:T(8,128)(2,1)S(1)} collective-permute-done((bf16[2,144,768]{2,1,0:T(8,128)(2,1)S(1)}, bf16[2,144,768]{2,1,0:T(8,128)(2,1)S(1)}, u32[]{:S(2)}, u32[]{:S(2)}) %collective-permute-start.23) | collective-permute-done | bytes 442400 | tf_op jit(solution)/shard_map/ppermute | solution.py:310
  88.1 7.7 %collective-permute-done.22.refs_4_ = bf16[2,144,768]{2,1,0:T(8,128)(2,1)S(1)} collective-permute-done((bf16[2,144,768]{2,1,0:T(8,128)(2,1)S(1)}, bf16[2,144,768]{2,1,0:T(8,128)(2,1)S(1)}, u32[]{:S(2)}, u32[]{:S(2)}) %collective-permute-start.22) | collective-permute-done | bytes 442400 | tf_op jit(solution)/shard_map/ppermute | solution.py:310
  95.9 16.2 %experts.1 = (bf16[4,144,768]{2,1,0:T(8,128)(2,1)S(1)}, bf16[4,144,768]{2,1,0:T(8,128)(2,1)S(1)}, bf16[2,144,768]{2,1,0:T(8,128)(2,1)S(1)}, bf16[2,144,768]{2,1,...) custom-call(s32[4]{0:T(128)S(1)} %pad_add_fusion.where_ref, ...), custom_call_target="tpu_custom_call" | custom-call | tf_op jit(solution)/shard_map/experts/pallas_call | solution.py:31
  112.1 1.8 %collective-permute-start.28 = (bf16[4,144,768]{2,1,0:T(8,128)(2,1)S(1)}, bf16[4,144,768]{2,1,0:T(8,128)(2,1)S(1)}, u32[]{:S(2)}, u32[]{:S(2)}) collective-permute-start(bf16[4,144,768]{2,1,0:T(8,128)(2,1)S(1)} %get-tuple-element.139), channel_id=1, source_target_pairs={{0,8},{8,0},{1,9},{9,1},{2,10},{10,2},{3,11},{11,3},{4,12},{12,4},... | collective-permute-start | bytes 2654216 | tf_op jit(solution)/shard_map/ppermute | solution.py:318
  113.9 1.6 collective-permute-start.25
  115.5 1.7 collective-permute-start.26
  117.2 1.6 collective-permute-start.27
  118.8 7.9 %collective-permute-done.25.refs_3_ = bf16[2,144,768]{2,1,0:T(8,128)(2,1)S(1)} collective-permute-done((bf16[2,144,768]{2,1,0:T(8,128)(2,1)S(1)}, bf16[2,144,768]{2,1,0:T(8,128)(2,1)S(1)}, u32[]{:S(2)}, u32[]{:S(2)}) %collective-permute-start.25) | collective-permute-done | bytes 442400 | tf_op jit(solution)/shard_map/ppermute | solution.py:310
  126.7 1.9 %collective-permute-done.26.refs_4_ = bf16[2,144,768]{2,1,0:T(8,128)(2,1)S(1)} collective-permute-done((bf16[2,144,768]{2,1,0:T(8,128)(2,1)S(1)}, bf16[2,144,768]{2,1,0:T(8,128)(2,1)S(1)}, u32[]{:S(2)}, u32[]{:S(2)}) %collective-permute-start.26) | collective-permute-done | bytes 442400 | tf_op jit(solution)/shard_map/ppermute | solution.py:310
  128.6 8.7 %collective-permute-done.27.refs_5_ = bf16[2,144,768]{2,1,0:T(8,128)(2,1)S(1)} collective-permute-done((bf16[2,144,768]{2,1,0:T(8,128)(2,1)S(1)}, bf16[2,144,768]{2,1,0:T(8,128)(2,1)S(1)}, u32[]{:S(2)}, u32[]{:S(2)}) %collective-permute-start.27) | collective-permute-done | bytes 442400 | tf_op jit(solution)/shard_map/ppermute | solution.py:310
  138.2 1.1 collective-permute-start.29
  139.3 2.1 %collective-permute-start.30 = (bf16[144,768]{1,0:T(8,128)(2,1)S(1)}, bf16[144,768]{1,0:T(8,128)(2,1)S(1)}, u32[]{:S(2)}, u32[]{:S(2)}) collective-permute-start(bf16[144,768]{1,0:T(8,128)(2,1)S(1)} %get-tuple-element.147), channel_id=1, source_target_pairs={{0,3},{1,0},{2,1},{3,2},{4,7},{5,4},{6,5},{7,6},{8,11},{9,8},{10,9... | collective-permute-start | bytes 663560 | tf_op jit(solution)/shard_map/ppermute | solution.py:310
  141.5 2.4 %collective-permute-done.32 = bf16[144,768]{1,0:T(8,128)(2,1)S(1)} collective-permute-done((bf16[144,768]{1,0:T(8,128)(2,1)S(1)}, bf16[144,768]{1,0:T(8,128)(2,1)S(1)}, u32[]{:S(2)}, u32[]{:S(2)}) %collective-permute-start.32) | collective-permute-done | bytes 221216 | tf_op jit(solution)/shard_map/ppermute | solution.py:318
  144.0 2.8 %collective-permute-start.33 = (bf16[144,768]{1,0:T(8,128)(2,1)S(1)}, bf16[144,768]{1,0:T(8,128)(2,1)S(1)}, u32[]{:S(2)}, u32[]{:S(2)}) collective-permute-start(bf16[144,768]{1,0:T(8,128)(2,1)S(1)} %add_convert_fusion), channel_id=1, source_target_pairs={{0,24},{8,16},{16,8},{24,0},{1,25},{9,17},{17,9},{25,1},{2,26},{10... | collective-permute-start | bytes 663560 | tf_op jit(solution)/shard_map/ppermute | solution.py:314
  147.2 2.2 %collective-permute-done.30.refs_2_ = bf16[144,768]{1,0:T(8,128)(2,1)S(1)} collective-permute-done((bf16[144,768]{1,0:T(8,128)(2,1)S(1)}, bf16[144,768]{1,0:T(8,128)(2,1)S(1)}, u32[]{:S(2)}, u32[]{:S(2)}) %collective-permute-start.30) | collective-permute-done | bytes 221216 | tf_op jit(solution)/shard_map/ppermute | solution.py:310
  150.2 1.1 collective-permute-done.33.refs_4_
  151.4 3.6 %collective-permute-start.34 = (bf16[72,768]{1,0:T(8,128)(2,1)S(1)}, bf16[72,768]{1,0:T(8,128)(2,1)S(1)}, u32[]{:S(2)}, u32[]{:S(2)}) collective-permute-start(bf16[72,768]{1,0:T(8,128)(2,1)S(1)} %get-tuple-element.156), channel_id=1, source_target_pairs={{0,96},{32,0},{64,32},{96,64},{1,97},{33,1},{65,33},{97,65},{2,98}... | collective-permute-start | bytes 331784 | tf_op jit(solution)/shard_map/ppermute | solution.py:310
  155.0 1.7 collective-permute-start.35
  156.7 1.5 collective-permute-start.36
  158.8 6.7 %collective-permute-done.35.refs_2_ = bf16[72,768]{1,0:T(8,128)(2,1)S(1)} collective-permute-done((bf16[72,768]{1,0:T(8,128)(2,1)S(1)}, bf16[72,768]{1,0:T(8,128)(2,1)S(1)}, u32[]{:S(2)}, u32[]{:S(2)}) %collective-permute-start.35) | collective-permute-done | bytes 110624 | tf_op jit(solution)/shard_map/ppermute | solution.py:310
  165.5 3.4 %collective-permute-done.36.refs_3_ = bf16[72,768]{1,0:T(8,128)(2,1)S(1)} collective-permute-done((bf16[72,768]{1,0:T(8,128)(2,1)S(1)}, bf16[72,768]{1,0:T(8,128)(2,1)S(1)}, u32[]{:S(2)}, u32[]{:S(2)}) %collective-permute-start.36) | collective-permute-done | bytes 110624 | tf_op jit(solution)/shard_map/ppermute | solution.py:310
  168.9 2.2 %mix.1 = bf16[128,768]{1,0:T(8,128)(2,1)} custom-call(s32[4]{0:T(128)S(1)} %pad_add_fusion.where_ref, s32[2,128]{1,0:T(2,128)S(1)} %bitcast.20, f32[2,128]{1,0:T(2,128)S(1)} %bitcast.21, bf16[128,768]{1,0:T(8,128)(2,1)S(1)} %get-tuple-element.110.hid_ref, bf16[72,768]{1,0:T(8,128)(2,1)S(1)} %get-tuple-element.155.refs_0_, ...), custom_call_target="tpu_custom_call" | custom-call | tf_op jit(solution)/shard_map/mix/pallas_call | solution.py:31
  (61 shorter events, 12.0 us)
Async XLA Ops:
  0.0 16.5 %collective-permute-start.3 = (bf16[3072,512]{1,0:T(8,128)(2,1)}, bf16[3072,512]{1,0:T(8,128)(2,1)S(1)}, u32[]{:S(2)}, u32[]{:S(2)}) collective-permute-start(bf16[3072,512]{1,0:T(8,128)(2,1)} %refs_6_.1), channel_id=1, source_target_pairs={{0,4},{4,0},{1,5},{5,1},{2,6},{6,2},{3,7},{7,3},{8,12},{12,8},{9,1... | collective-permute-start | bytes 9437192 | tf_op jit(solution)/shard_map/ppermute | solution.py:322
  1.5 10.6 %collective-permute-start.2 = (bf16[2,128,128]{2,1,0:T(8,128)(2,1)}, bf16[2,128,128]{2,1,0:T(8,128)(2,1)S(1)}, u32[]{:S(2)}, u32[]{:S(2)}) collective-permute-start(bf16[2,128,128]{2,1,0:T(8,128)(2,1)} %get-tuple-element.159), channel_id=1, source_target_pairs={{0,64},{32,96},{64,0},{96,32},{1,65},{33,97},{65,1},{97,33},{2,66}... | collective-permute-start | bytes 196616 | tf_op jit(solution)/shard_map/ppermute | solution.py:310
  7.8 8.0 %collective-permute-start = (bf16[2,128,128]{2,1,0:T(8,128)(2,1)}, bf16[2,128,128]{2,1,0:T(8,128)(2,1)S(1)}, u32[]{:S(2)}, u32[]{:S(2)}) collective-permute-start(bf16[2,128,128]{2,1,0:T(8,128)(2,1)} %get-tuple-element.160), channel_id=1, source_target_pairs={{0,32},{32,64},{64,96},{96,0},{1,33},{33,65},{65,97},{97,1},{2,34}... | collective-permute-start | bytes 196616 | tf_op jit(solution)/shard_map/ppermute | solution.py:310
  9.3 6.5 %collective-permute-start.1 = (bf16[2,128,128]{2,1,0:T(8,128)(2,1)S(1)}, bf16[2,128,128]{2,1,0:T(8,128)(2,1)S(1)}, u32[]{:S(2)}, u32[]{:S(2)}) collective-permute-start(bf16[2,128,128]{2,1,0:T(8,128)(2,1)S(1)} %get-tuple-element.161), channel_id=1, source_target_pairs={{0,96},{32,0},{64,32},{96,64},{1,97},{33,1},{65,33},{97,65},{2,98}... | collective-permute-start | bytes 196616 | tf_op jit(solution)/shard_map/ppermute | solution.py:310
  16.5 42.8 %copy-start.7 = (bf16[3072,512]{1,0:T(8,128)(2,1)}, bf16[3072,512]{1,0:T(8,128)(2,1)S(1)}, u32[]{:S(2)}) copy-start(bf16[3072,512]{1,0:T(8,128)(2,1)S(1)} %collective-permute-done.3.refs_9_) | copy-start | bytes 9437188
  16.5 12.8 %collective-permute-start.7 = (bf16[3072,512]{1,0:T(8,128)(2,1)}, bf16[3072,512]{1,0:T(8,128)(2,1)S(1)}, u32[]{:S(2)}, u32[]{:S(2)}) collective-permute-start(bf16[3072,512]{1,0:T(8,128)(2,1)} %refs_7_.1), channel_id=1, source_target_pairs={{0,4},{4,0},{1,5},{5,1},{2,6},{6,2},{3,7},{7,3},{8,12},{12,8},{9,1... | collective-permute-start | bytes 9437192 | tf_op jit(solution)/shard_map/ppermute | solution.py:322
  16.6 6.8 %collective-permute-start.4 = (bf16[2,512,128]{2,1,0:T(8,128)(2,1)S(1)}, bf16[2,512,128]{2,1,0:T(8,128)(2,1)S(1)}, u32[]{:S(2)}, u32[]{:S(2)}) collective-permute-start(bf16[2,512,128]{2,1,0:T(8,128)(2,1)S(1)} %get-tuple-element.89.refs_0_), channel_id=1, source_target_pairs={{0,4},{4,0},{1,5},{5,1},{2,6},{6,2},{3,7},{7,3},{8,12},{12,8},{9,1... | collective-permute-start | bytes 786440 | tf_op jit(solution)/shard_map/ppermute | solution.py:322
  17.1 9.4 %collective-permute-start.6 = (bf16[2,512,128]{2,1,0:T(8,128)(2,1)S(1)}, bf16[2,512,128]{2,1,0:T(8,128)(2,1)S(1)}, u32[]{:S(2)}, u32[]{:S(2)}) collective-permute-start(bf16[2,512,128]{2,1,0:T(8,128)(2,1)S(1)} %get-tuple-element.94), channel_id=1, source_target_pairs={{0,24},{8,0},{16,8},{24,16},{1,25},{9,1},{17,9},{25,17},{2,26},{10... | collective-permute-start | bytes 786440 | tf_op jit(solution)/shard_map/ppermute | solution.py:310
  20.1 9.2 %collective-permute-start.5 = (bf16[2,512,128]{2,1,0:T(8,128)(2,1)S(1)}, bf16[2,512,128]{2,1,0:T(8,128)(2,1)S(1)}, u32[]{:S(2)}, u32[]{:S(2)}) collective-permute-start(bf16[2,512,128]{2,1,0:T(8,128)(2,1)S(1)} %get-tuple-element.93), channel_id=1, source_target_pairs={{0,8},{8,16},{16,24},{24,0},{1,9},{9,17},{17,25},{25,1},{2,10},{10... | collective-permute-start | bytes 786440 | tf_op jit(solution)/shard_map/ppermute | solution.py:310
  20.1 0.9 copy-start
  21.0 0.9 copy-start.1
  21.9 0.7 copy-start.3
  22.6 18.6 %copy-start.6 = (bf16[512,3072]{1,0:T(8,128)(2,1)S(1)}, bf16[512,3072]{1,0:T(8,128)(2,1)}, u32[]{:S(2)}) copy-start(bf16[512,3072]{1,0:T(8,128)(2,1)} %refs_8_.1) | copy-start | bytes 9437188
  29.3 43.9 %copy-start.8 = (bf16[3072,512]{1,0:T(8,128)(2,1)}, bf16[3072,512]{1,0:T(8,128)(2,1)S(1)}, u32[]{:S(2)}) copy-start(bf16[3072,512]{1,0:T(8,128)(2,1)S(1)} %collective-permute-done.7.refs_10_) | copy-start | bytes 9437188
  29.3 1.5 collective-permute-start.8
  29.3 1.9 %collective-permute-start.9 = (bf16[2,512,128]{2,1,0:T(8,128)(2,1)S(1)}, bf16[2,512,128]{2,1,0:T(8,128)(2,1)S(1)}, u32[]{:S(2)}, u32[]{:S(2)}) collective-permute-start(bf16[2,512,128]{2,1,0:T(8,128)(2,1)S(1)} %collective-permute-done.6.refs_1_), channel_id=1, source_target_pairs={{0,4},{4,0},{1,5},{5,1},{2,6},{6,2},{3,7},{7,3},{8,12},{12,8},{9,1... | collective-permute-start | bytes 786440 | tf_op jit(solution)/shard_map/ppermute | solution.py:322
  29.8 9.8 %collective-permute-start.10 = (bf16[2,512,128]{2,1,0:T(8,128)(2,1)S(1)}, bf16[2,512,128]{2,1,0:T(8,128)(2,1)S(1)}, u32[]{:S(2)}, u32[]{:S(2)}) collective-permute-start(bf16[2,512,128]{2,1,0:T(8,128)(2,1)S(1)} %get-tuple-element.105), channel_id=1, source_target_pairs={{0,16},{8,24},{16,0},{24,8},{1,17},{9,25},{17,1},{25,9},{2,18},{10... | collective-permute-start | bytes 786440 | tf_op jit(solution)/shard_map/ppermute | solution.py:310
  36.9 58.9 %copy-start.2 = (f32[3072]{0:T(1024)S(1)}, f32[3072]{0:T(1024)}, u32[]{:S(2)}) copy-start(f32[3072]{0:T(1024)} %param.18) | copy-start | bytes 36868
  39.6 1.5 collective-permute-start.11
  41.2 18.1 %collective-permute-start.15 = (bf16[512,3072]{1,0:T(8,128)(2,1)S(1)}, bf16[512,3072]{1,0:T(8,128)(2,1)S(1)}, u32[]{:S(2)}, u32[]{:S(2)}) collective-permute-start(bf16[512,3072]{1,0:T(8,128)(2,1)S(1)} %copy-done.6), channel_id=1, source_target_pairs={{0,4},{4,0},{1,5},{5,1},{2,6},{6,2},{3,7},{7,3},{8,12},{12,8},{9,1... | collective-permute-start | bytes 9437192 | tf_op jit(solution)/shard_map/ppermute | solution.py:322
  44.5 9.5 %collective-permute-start.12 = (bf16[72,768]{1,0:T(8,128)(2,1)S(1)}, bf16[72,768]{1,0:T(8,128)(2,1)S(1)}, u32[]{:S(2)}, u32[]{:S(2)}) collective-permute-start(bf16[72,768]{1,0:T(8,128)(2,1)S(1)} %get-tuple-element.112), channel_id=1, source_target_pairs={{0,32},{32,64},{64,96},{96,0},{1,33},{33,65},{65,97},{97,1},{2,34}... | collective-permute-start | bytes 331784 | tf_op jit(solution)/shard_map/ppermute | solution.py:310
  46.5 11.5 %collective-permute-start.13 = (bf16[72,768]{1,0:T(8,128)(2,1)S(1)}, bf16[72,768]{1,0:T(8,128)(2,1)S(1)}, u32[]{:S(2)}, u32[]{:S(2)}) collective-permute-start(bf16[72,768]{1,0:T(8,128)(2,1)S(1)} %get-tuple-element.113), channel_id=1, source_target_pairs={{0,64},{32,96},{64,0},{96,32},{1,65},{33,97},{65,1},{97,33},{2,66}... | collective-permute-start | bytes 331784 | tf_op jit(solution)/shard_map/ppermute | solution.py:310
  50.2 9.1 %collective-permute-start.14 = (bf16[72,768]{1,0:T(8,128)(2,1)S(1)}, bf16[72,768]{1,0:T(8,128)(2,1)S(1)}, u32[]{:S(2)}, u32[]{:S(2)}) collective-permute-start(bf16[72,768]{1,0:T(8,128)(2,1)S(1)} %get-tuple-element.114), channel_id=1, source_target_pairs={{0,96},{32,0},{64,32},{96,64},{1,97},{33,1},{65,33},{97,65},{2,98}... | collective-permute-start | bytes 331784 | tf_op jit(solution)/shard_map/ppermute | solution.py:310
  59.3 13.8 %copy-start.9 = (bf16[512,3072]{1,0:T(8,128)(2,1)}, bf16[512,3072]{1,0:T(8,128)(2,1)S(1)}, u32[]{:S(2)}) copy-start(bf16[512,3072]{1,0:T(8,128)(2,1)S(1)} %collective-permute-done.15.refs_11_) | copy-start | bytes 9437188
  59.3 7.8 %collective-permute-start.19 = (bf16[144,768]{1,0:T(8,128)(2,1)S(1)}, bf16[144,768]{1,0:T(8,128)(2,1)S(1)}, u32[]{:S(2)}, u32[]{:S(2)}) collective-permute-start(bf16[144,768]{1,0:T(8,128)(2,1)S(1)} %get-tuple-element.123), channel_id=1, source_target_pairs={{0,24},{8,16},{16,8},{24,0},{1,25},{9,17},{17,9},{25,1},{2,26},{10... | collective-permute-start | bytes 663560 | tf_op jit(solution)/shard_map/ppermute | solution.py:314
  60.0 9.9 %collective-permute-start.18 = (bf16[144,768]{1,0:T(8,128)(2,1)S(1)}, bf16[144,768]{1,0:T(8,128)(2,1)S(1)}, u32[]{:S(2)}, u32[]{:S(2)}) collective-permute-start(bf16[144,768]{1,0:T(8,128)(2,1)S(1)} %get-tuple-element.122), channel_id=1, source_target_pairs={{0,2},{1,3},{2,0},{3,1},{4,6},{5,7},{6,4},{7,5},{8,10},{9,11},{10,... | collective-permute-start | bytes 663560 | tf_op jit(solution)/shard_map/ppermute | solution.py:310
  63.0 9.6 %collective-permute-start.17 = (bf16[144,768]{1,0:T(8,128)(2,1)S(1)}, bf16[144,768]{1,0:T(8,128)(2,1)S(1)}, u32[]{:S(2)}, u32[]{:S(2)}) collective-permute-start(bf16[144,768]{1,0:T(8,128)(2,1)S(1)} %get-tuple-element.122), channel_id=1, source_target_pairs={{0,3},{1,0},{2,1},{3,2},{4,7},{5,4},{6,5},{7,6},{8,11},{9,8},{10,9... | collective-permute-start | bytes 663560 | tf_op jit(solution)/shard_map/ppermute | solution.py:310
  64.1 8.7 %collective-permute-start.16 = (bf16[144,768]{1,0:T(8,128)(2,1)S(1)}, bf16[144,768]{1,0:T(8,128)(2,1)S(1)}, u32[]{:S(2)}, u32[]{:S(2)}) collective-permute-start(bf16[144,768]{1,0:T(8,128)(2,1)S(1)} %get-tuple-element.122), channel_id=1, source_target_pairs={{0,1},{1,2},{2,3},{3,0},{4,5},{5,6},{6,7},{7,4},{8,9},{9,10},{10,1... | collective-permute-start | bytes 663560 | tf_op jit(solution)/shard_map/ppermute | solution.py:310
  67.2 5.9 %collective-permute-start.20 = (bf16[144,768]{1,0:T(8,128)(2,1)S(1)}, bf16[144,768]{1,0:T(8,128)(2,1)S(1)}, u32[]{:S(2)}, u32[]{:S(2)}) collective-permute-start(bf16[144,768]{1,0:T(8,128)(2,1)S(1)} %collective-permute-done.19), channel_id=1, source_target_pairs={{0,8},{8,0},{1,9},{9,1},{2,10},{10,2},{3,11},{11,3},{4,12},{12,4},... | collective-permute-start | bytes 663560 | tf_op jit(solution)/shard_map/ppermute | solution.py:318
  73.2 22.6 %collective-permute-start.24 = (bf16[4,144,768]{2,1,0:T(8,128)(2,1)S(1)}, bf16[4,144,768]{2,1,0:T(8,128)(2,1)S(1)}, u32[]{:S(2)}, u32[]{:S(2)}) collective-permute-start(bf16[4,144,768]{2,1,0:T(8,128)(2,1)S(1)} %pad_maximum_fusion.refs_0_), channel_id=1, source_target_pairs={{0,8},{8,0},{1,9},{9,1},{2,10},{10,2},{3,11},{11,3},{4,12},{12,4},... | collective-permute-start | bytes 2654216 | tf_op jit(solution)/shard_map/ppermute | solution.py:318
  73.4 14.7 %collective-permute-start.23 = (bf16[2,144,768]{2,1,0:T(8,128)(2,1)S(1)}, bf16[2,144,768]{2,1,0:T(8,128)(2,1)S(1)}, u32[]{:S(2)}, u32[]{:S(2)}) collective-permute-start(bf16[2,144,768]{2,1,0:T(8,128)(2,1)S(1)} %pad_maximum_fusion.1.refs_2_), channel_id=1, source_target_pairs={{0,2},{1,3},{2,0},{3,1},{4,6},{5,7},{6,4},{7,5},{8,10},{9,11},{10,... | collective-permute-start | bytes 1327112 | tf_op jit(solution)/shard_map/ppermute | solution.py:310
  76.5 19.4 %collective-permute-start.22 = (bf16[2,144,768]{2,1,0:T(8,128)(2,1)S(1)}, bf16[2,144,768]{2,1,0:T(8,128)(2,1)S(1)}, u32[]{:S(2)}, u32[]{:S(2)}) collective-permute-start(bf16[2,144,768]{2,1,0:T(8,128)(2,1)S(1)} %pad_maximum_fusion.1.refs_2_), channel_id=1, source_target_pairs={{0,3},{1,0},{2,1},{3,2},{4,7},{5,4},{6,5},{7,6},{8,11},{9,8},{10,9... | collective-permute-start | bytes 1327112 | tf_op jit(solution)/shard_map/ppermute | solution.py:310
  77.6 18.2 %collective-permute-start.21 = (bf16[2,144,768]{2,1,0:T(8,128)(2,1)S(1)}, bf16[2,144,768]{2,1,0:T(8,128)(2,1)S(1)}, u32[]{:S(2)}, u32[]{:S(2)}) collective-permute-start(bf16[2,144,768]{2,1,0:T(8,128)(2,1)S(1)} %pad_maximum_fusion.1.refs_2_), channel_id=1, source_target_pairs={{0,1},{1,2},{2,3},{3,0},{4,5},{5,6},{6,7},{7,4},{8,9},{9,10},{10,1... | collective-permute-start | bytes 1327112 | tf_op jit(solution)/shard_map/ppermute | solution.py:310
  112.1 56.8 %copy-start.4 = (s32[128,2]{0,1:T(2,128)S(1)}, s32[128,2]{0,1:T(2,128)}, u32[]{:S(2)}) copy-start(s32[128,2]{0,1:T(2,128)} %param.22) | copy-start | bytes 3076
  112.1 56.8 %copy-start.5 = (f32[128,2]{0,1:T(2,128)S(1)}, f32[128,2]{0,1:T(2,128)}, u32[]{:S(2)}) copy-start(f32[128,2]{0,1:T(2,128)} %param.23) | copy-start | bytes 3076
  112.1 25.2 %collective-permute-start.28 = (bf16[4,144,768]{2,1,0:T(8,128)(2,1)S(1)}, bf16[4,144,768]{2,1,0:T(8,128)(2,1)S(1)}, u32[]{:S(2)}, u32[]{:S(2)}) collective-permute-start(bf16[4,144,768]{2,1,0:T(8,128)(2,1)S(1)} %get-tuple-element.139), channel_id=1, source_target_pairs={{0,8},{8,0},{1,9},{9,1},{2,10},{10,2},{3,11},{11,3},{4,12},{12,4},... | collective-permute-start | bytes 2654216 | tf_op jit(solution)/shard_map/ppermute | solution.py:318
  113.9 12.8 %collective-permute-start.25 = (bf16[2,144,768]{2,1,0:T(8,128)(2,1)S(1)}, bf16[2,144,768]{2,1,0:T(8,128)(2,1)S(1)}, u32[]{:S(2)}, u32[]{:S(2)}) collective-permute-start(bf16[2,144,768]{2,1,0:T(8,128)(2,1)S(1)} %get-tuple-element.136), channel_id=1, source_target_pairs={{0,1},{1,2},{2,3},{3,0},{4,5},{5,6},{6,7},{7,4},{8,9},{9,10},{10,1... | collective-permute-start | bytes 1327112 | tf_op jit(solution)/shard_map/ppermute | solution.py:310
  115.5 13.1 %collective-permute-start.26 = (bf16[2,144,768]{2,1,0:T(8,128)(2,1)S(1)}, bf16[2,144,768]{2,1,0:T(8,128)(2,1)S(1)}, u32[]{:S(2)}, u32[]{:S(2)}) collective-permute-start(bf16[2,144,768]{2,1,0:T(8,128)(2,1)S(1)} %get-tuple-element.137), channel_id=1, source_target_pairs={{0,3},{1,0},{2,1},{3,2},{4,7},{5,4},{6,5},{7,6},{8,11},{9,8},{10,9... | collective-permute-start | bytes 1327112 | tf_op jit(solution)/shard_map/ppermute | solution.py:310
  117.2 20.1 %collective-permute-start.27 = (bf16[2,144,768]{2,1,0:T(8,128)(2,1)S(1)}, bf16[2,144,768]{2,1,0:T(8,128)(2,1)S(1)}, u32[]{:S(2)}, u32[]{:S(2)}) collective-permute-start(bf16[2,144,768]{2,1,0:T(8,128)(2,1)S(1)} %get-tuple-element.138), channel_id=1, source_target_pairs={{0,2},{1,3},{2,0},{3,1},{4,6},{5,7},{6,4},{7,5},{8,10},{9,11},{10,... | collective-permute-start | bytes 1327112 | tf_op jit(solution)/shard_map/ppermute | solution.py:310
  137.7 6.3 %collective-permute-start.32 = (bf16[144,768]{1,0:T(8,128)(2,1)S(1)}, bf16[144,768]{1,0:T(8,128)(2,1)S(1)}, u32[]{:S(2)}, u32[]{:S(2)}) collective-permute-start(bf16[144,768]{1,0:T(8,128)(2,1)S(1)} %get-tuple-element.150), channel_id=1, source_target_pairs={{0,8},{8,0},{1,9},{9,1},{2,10},{10,2},{3,11},{11,3},{4,12},{12,4},... | collective-permute-start | bytes 663560 | tf_op jit(solution)/shard_map/ppermute | solution.py:318
  138.2 9.0 %collective-permute-start.29 = (bf16[144,768]{1,0:T(8,128)(2,1)S(1)}, bf16[144,768]{1,0:T(8,128)(2,1)S(1)}, u32[]{:S(2)}, u32[]{:S(2)}) collective-permute-start(bf16[144,768]{1,0:T(8,128)(2,1)S(1)} %get-tuple-element.146), channel_id=1, source_target_pairs={{0,1},{1,2},{2,3},{3,0},{4,5},{5,6},{6,7},{7,4},{8,9},{9,10},{10,1... | collective-permute-start | bytes 663560 | tf_op jit(solution)/shard_map/ppermute | solution.py:310
  139.3 10.1 %collective-permute-start.30 = (bf16[144,768]{1,0:T(8,128)(2,1)S(1)}, bf16[144,768]{1,0:T(8,128)(2,1)S(1)}, u32[]{:S(2)}, u32[]{:S(2)}) collective-permute-start(bf16[144,768]{1,0:T(8,128)(2,1)S(1)} %get-tuple-element.147), channel_id=1, source_target_pairs={{0,3},{1,0},{2,1},{3,2},{4,7},{5,4},{6,5},{7,6},{8,11},{9,8},{10,9... | collective-permute-start | bytes 663560 | tf_op jit(solution)/shard_map/ppermute | solution.py:310
  141.4 8.8 %collective-permute-start.31 = (bf16[144,768]{1,0:T(8,128)(2,1)S(1)}, bf16[144,768]{1,0:T(8,128)(2,1)S(1)}, u32[]{:S(2)}, u32[]{:S(2)}) collective-permute-start(bf16[144,768]{1,0:T(8,128)(2,1)S(1)} %get-tuple-element.148), channel_id=1, source_target_pairs={{0,2},{1,3},{2,0},{3,1},{4,6},{5,7},{6,4},{7,5},{8,10},{9,11},{10,... | collective-permute-start | bytes 663560 | tf_op jit(solution)/shard_map/ppermute | solution.py:310
  144.0 7.2 %collective-permute-start.33 = (bf16[144,768]{1,0:T(8,128)(2,1)S(1)}, bf16[144,768]{1,0:T(8,128)(2,1)S(1)}, u32[]{:S(2)}, u32[]{:S(2)}) collective-permute-start(bf16[144,768]{1,0:T(8,128)(2,1)S(1)} %add_convert_fusion), channel_id=1, source_target_pairs={{0,24},{8,16},{16,8},{24,0},{1,25},{9,17},{17,9},{25,1},{2,26},{10... | collective-permute-start | bytes 663560 | tf_op jit(solution)/shard_map/ppermute | solution.py:314
  151.4 7.4 %collective-permute-start.34 = (bf16[72,768]{1,0:T(8,128)(2,1)S(1)}, bf16[72,768]{1,0:T(8,128)(2,1)S(1)}, u32[]{:S(2)}, u32[]{:S(2)}) collective-permute-start(bf16[72,768]{1,0:T(8,128)(2,1)S(1)} %get-tuple-element.156), channel_id=1, source_target_pairs={{0,96},{32,0},{64,32},{96,64},{1,97},{33,1},{65,33},{97,65},{2,98}... | collective-permute-start | bytes 331784 | tf_op jit(solution)/shard_map/ppermute | solution.py:310
  155.0 10.5 %collective-permute-start.35 = (bf16[72,768]{1,0:T(8,128)(2,1)S(1)}, bf16[72,768]{1,0:T(8,128)(2,1)S(1)}, u32[]{:S(2)}, u32[]{:S(2)}) collective-permute-start(bf16[72,768]{1,0:T(8,128)(2,1)S(1)} %get-tuple-element.157), channel_id=1, source_target_pairs={{0,64},{32,96},{64,0},{96,32},{1,65},{33,97},{65,1},{97,33},{2,66}... | collective-permute-start | bytes 331784 | tf_op jit(solution)/shard_map/ppermute | solution.py:310
  156.7 12.2 %collective-permute-start.36 = (bf16[72,768]{1,0:T(8,128)(2,1)S(1)}, bf16[72,768]{1,0:T(8,128)(2,1)S(1)}, u32[]{:S(2)}, u32[]{:S(2)}) collective-permute-start(bf16[72,768]{1,0:T(8,128)(2,1)S(1)} %get-tuple-element.158), channel_id=1, source_target_pairs={{0,32},{32,64},{64,96},{96,0},{1,33},{33,65},{65,97},{97,1},{2,34}... | collective-permute-start | bytes 331784 | tf_op jit(solution)/shard_map/ppermute | solution.py:310

commit v2 on v1

--- a/solution.py
+++ b/solution.py
@@ -17,6 +17,7 @@
 EPS = 1e-05
 NZ, NY, NX, NC = 4, 4, 4, 2
 SHIFTS = (1, 3, 2)
+KV_ORDER, Z_ORDER, X_ORDER = (0, 1, 2), (0, 1, 2), (2, 1, 0)
 MB = 1024 * 1024
 
 bf16 = jnp.bfloat16
@@ -171,7 +172,7 @@
 
 def merge_kernel(*refs):
     keep, away = refs[NZ:]
-    for d, ref in enumerate(refs[:NZ]):
+    for d, ref in zip((0,) + SHIFTS, refs[:NZ]):
         keep[d * CAP : (d + 1) * CAP, :] = ref[:CAP]
         away[d * CAP : (d + 1) * CAP, :] = ref[CAP:]
 
@@ -290,7 +291,7 @@
         weight.append(jnp.where(pick, gate, 0.0))
     held[...] = jnp.zeros_like(held)
     for g in range(EXPERTS):
-        part = part_refs[g // 2][(g % 2) * CAP : (g % 2 + 1) * CAP, :]
+        part = part_refs[(0, 3, 1, 2).index(g // 2)][(g % 2) * CAP : (g % 2 + 1) * CAP, :]
         held[g * PAD : g * PAD + CAP, :] = part.astype(f32)
     mixture = lax.dot_general(
         jnp.concatenate(weight, axis=0),
@@ -308,6 +309,16 @@
 def turn(v, axis, shift):
     n = 4
     return lax.ppermute(v, axis, [(i, (i + shift) % n) for i in range(n)])
+
+
+def turned(parts, axis, order):
+    got = {i: turn(parts[i], axis, SHIFTS[i]) for i in order}
+    return [got[i] for i in range(len(parts))]
+
+
+def together(parts, order):
+    got = dict(zip(order, lax.optimization_barrier([parts[i] for i in order])))
+    return [got[i] for i in range(len(parts))]
 
 
 def cross(v):
@@ -334,7 +345,7 @@
     shaped = lambda *dims: jax.ShapeDtypeStruct(dims, bf16)
 
     near, past = jnp.stack((keys, values)), jnp.stack((cache_keys, cache_values))
-    from_z = [turn(jnp.where(z + s < NZ, near, past), "zh", s) for s in SHIFTS]
+    from_z = turned([jnp.where(z + s < NZ, near, past) for s in SHIFTS], "zh", KV_ORDER)
     q_all, res, table = call(
         prep_kernel,
         [shaped(heads * rows, HEAD_DIM), shaped(rows, width), shaped(EXPERTS * PAD, rows)],
@@ -345,7 +356,7 @@
     packed = call(
         pack_kv_kernel,
         [shaped(2, NZ * rows, HEAD_DIM)] * 4,
-        [where, near, past, *from_z],
+        [where, near, past, *[from_z[i] for i in (1, 2, 0)]],
         "pack_kv",
         scalars=1,
     )
@@ -373,18 +384,16 @@
         [pltpu.VMEM((heads * rows, HEAD_DIM), f32)],
     )
 
-    arrived = [sent[0]] + [turn(sent[s], "zh", s) for s in (1, 2, 3)]
+    arrived = [sent[0]] + turned([sent[s] for s in SHIFTS], "zh", Z_ORDER)
     arrived, other = lax.optimization_barrier((arrived, other))
     rows_a = shaped(NZ * CAP, width)
     a, away = call(merge_kernel, [rows_a] * 2, arrived, "merge")
     b = cross(away)
     b_far = swap_y(b)
-    *a_turned, b_far = lax.optimization_barrier([turn(a, "x", s) for s in SHIFTS] + [b_far])
+    *a_turned, b_far = together(turned([a] * 3, "x", X_ORDER) + [b_far], (2, 1, 0, 3))
     a_own = jnp.stack([a] + a_turned)
     b_pair = jnp.stack((b, b_far))
-    *b_turned, a_far = lax.optimization_barrier(
-        [turn(b_pair, "x", s) for s in SHIFTS] + [swap_y(a_own)]
-    )
+    *b_turned, a_far = together(turned([b_pair] * 3, "x", X_ORDER) + [swap_y(a_own)], (2, 1, 0, 3))
     gain = norm_gain.reshape(NX, 1, width)
     a_own, a_far, b_all = experts(where, gain, a_own, a_far, [b_pair] + b_turned, own, other)
 
@@ -404,7 +413,8 @@
         [a_sums[0], *moved],
         "last_sum",
     )
-    back = [result[0]] + [turn(result[s], "zh", NZ - s) for s in (1, 2, 3)]
+    back = turned([result[NZ - s] for s in SHIFTS], "zh", Z_ORDER)
+    back = [result[0]] + back
     return call(
         mix_kernel,
         shaped(rows, width),

time: 173 us -> 167 us (0.965)
  waiting for transfers between devices: 80.5 us -> 73.6 us
    ppermute x24, waiting for transfers between devices: 71.6 us -> 65.2 us  [turn(): return lax.ppermute(v, axis, [(i, (i + shift) % n) for i in range(n)])]
    ppermute x24, starting transfers between devices: 46.6 us -> 49.7 us  [turn(): return lax.ppermute(v, axis, [(i, (i + shift) % n) for i in range(n)])]
  transfers between devices with their start and end apart: 37 -> 37, of which waited for: 28 -> 21; matrix products, arithmetic and copies ran while one was open for 1% -> 1% of each run, Pallas kernels for 8% -> 8%
where the time goes in v2:
time: 167 us; the launch traced here: 166 us
  waiting for transfers between devices  73.6 us (44%)
  starting transfers between devices  55.3 us (33%)
  Pallas kernels  32.4 us (19%)
  local copies, waits for them, and re-layouts  2.57 us (2%)
  other arithmetic  1.77 us (1%)
    ppermute x24, waiting for transfers between devices, turn(): return lax.ppermute(v, axis, [(i, (i + shift) % n) for i in range(n)])  65.2 us
    ppermute x24, starting transfers between devices, turn(): return lax.ppermute(v, axis, [(i, (i + shift) % n) for i in range(n)])  49.7 us
    pallas_call x10, Pallas kernels, call(): pl.pallas_call(body, out_shape=out_shape, in_specs=[SM] * scalars + [VM]...  32.4 us
    ppermute x2, waiting for transfers between devices, cross(): return lax.ppermute(v, ('yh', 'yl'), [(i, NY - 1 - i) for i in range(NY)])  4.26 us
  transfers between devices with their start and end apart: 37, of which 21 were waited for; matrix products, arithmetic and copies ran while one was open for 1% of the time, Pallas kernels for 8%

profile of v2, /device:TPU:32, one launch (start us, length us, event | category | flops | bytes accessed | tf_op | source)
XLA Modules:
  0.0 166.0 jit_solution(9990686381205584299)
XLA Ops:
  0.0 1.5 broadcast_select_fusion
  1.5 3.3 %collective-permute-start.2 = (bf16[2,128,128]{2,1,0:T(8,128)(2,1)}, bf16[2,128,128]{2,1,0:T(8,128)(2,1)S(1)}, u32[]{:S(2)}, u32[]{:S(2)}) collective-permute-start(bf16[2,128,128]{2,1,0:T(8,128)(2,1)} %get-tuple-element.159), channel_id=1, source_target_pairs={{0,32},{32,64},{64,96},{96,0},{1,33},{33,65},{65,97},{97,1},{2,34}... | collective-permute-start | bytes 196616 | tf_op jit(solution)/shard_map/ppermute | solution.py:311
  4.8 2.1 %collective-permute-start = (bf16[2,128,128]{2,1,0:T(8,128)(2,1)}, bf16[2,128,128]{2,1,0:T(8,128)(2,1)S(1)}, u32[]{:S(2)}, u32[]{:S(2)}) collective-permute-start(bf16[2,128,128]{2,1,0:T(8,128)(2,1)} %get-tuple-element.160), channel_id=1, source_target_pairs={{0,96},{32,0},{64,32},{96,64},{1,97},{33,1},{65,33},{97,65},{2,98}... | collective-permute-start | bytes 196616 | tf_op jit(solution)/shard_map/ppermute | solution.py:311
  6.9 5.0 %collective-permute-start.1 = (bf16[2,128,128]{2,1,0:T(8,128)(2,1)S(1)}, bf16[2,128,128]{2,1,0:T(8,128)(2,1)S(1)}, u32[]{:S(2)}, u32[]{:S(2)}) collective-permute-start(bf16[2,128,128]{2,1,0:T(8,128)(2,1)S(1)} %get-tuple-element.161), channel_id=1, source_target_pairs={{0,64},{32,96},{64,0},{96,32},{1,65},{33,97},{65,1},{97,33},{2,66}... | collective-permute-start | bytes 196616 | tf_op jit(solution)/shard_map/ppermute | solution.py:311
  12.0 6.0 %collective-permute-done.1.refs_1_ = bf16[2,128,128]{2,1,0:T(8,128)(2,1)S(1)} collective-permute-done((bf16[2,128,128]{2,1,0:T(8,128)(2,1)S(1)}, bf16[2,128,128]{2,1,0:T(8,128)(2,1)S(1)}, u32[]{:S(2)}, u32[]{:S(2)}) %collective-permute-start.1) | collective-permute-done | bytes 65568 | tf_op jit(solution)/shard_map/ppermute | solution.py:311
  19.3 3.0 %collective-permute-start.6 = (bf16[2,512,128]{2,1,0:T(8,128)(2,1)S(1)}, bf16[2,512,128]{2,1,0:T(8,128)(2,1)S(1)}, u32[]{:S(2)}, u32[]{:S(2)}) collective-permute-start(bf16[2,512,128]{2,1,0:T(8,128)(2,1)S(1)} %get-tuple-element.94), channel_id=1, source_target_pairs={{0,24},{8,0},{16,8},{24,16},{1,25},{9,1},{17,9},{25,17},{2,26},{10... | collective-permute-start | bytes 786440 | tf_op jit(solution)/shard_map/ppermute | solution.py:311
  22.3 0.9 copy-done
  25.6 3.1 %attend_own.1 = (f32[768,128]{1,0:T(8,128)S(1)}, f32[768,128]{1,0:T(8,128)S(1)}, f32[768,128]{1,0:T(8,128)S(1)}) custom-call(bf16[768,128]{1,0:T(8,128)(2,1)S(1)} %get-tuple-element.82.q_all, bf16[2,128,128]{2,1,0:T(8,128)(2,1)S(1)} %get-tuple-element.162.tract.tract_ref, bf16[2,128,128]{2,1,0:T(8,128)(2,1)S(1)} %get-tuple-element.163.cache.cache_ref, ...), custom_call_target="tpu_custom_call" | custom-call | tf_op jit(solution)/shard_map/attend_own/pallas_call | solution.py:32
  28.8 2.8 %collective-permute-done.5.refs_0_ = bf16[2,512,128]{2,1,0:T(8,128)(2,1)S(1)} collective-permute-done((bf16[2,512,128]{2,1,0:T(8,128)(2,1)S(1)}, bf16[2,512,128]{2,1,0:T(8,128)(2,1)S(1)}, u32[]{:S(2)}, u32[]{:S(2)}) %collective-permute-start.5) | collective-permute-done | bytes 262176 | tf_op jit(solution)/shard_map/ppermute | solution.py:311
  32.1 1.0 collective-permute-done.8.refs_2_
  33.5 5.7 %attend_more.1 = (f32[768,128]{1,0:T(8,128)S(1)}, f32[768,128]{1,0:T(8,128)S(1)}, f32[768,128]{1,0:T(8,128)S(1)}) custom-call(bf16[768,128]{1,0:T(8,128)(2,1)S(1)} %get-tuple-element.82.q_all, f32[768,128]{1,0:T(8,128)S(1)} %get-tuple-element.97.m_ref, f32[768,128]{1,0:T(8,128)S(1)} %get-tuple-element.98.l_ref, f32[768,128]{1,0:T(8,128)S(1)} %get-tuple-element.99.acc_ref, ...), custom_call_target="tpu_custom_call" | custom-call | tf_op jit(solution)/shard_map/attend_more/pallas_call | solution.py:32
  39.1 2.7 %collective-permute-done.10.refs_0_ = bf16[2,512,128]{2,1,0:T(8,128)(2,1)S(1)} collective-permute-done((bf16[2,512,128]{2,1,0:T(8,128)(2,1)S(1)}, bf16[2,512,128]{2,1,0:T(8,128)(2,1)S(1)}, u32[]{:S(2)}, u32[]{:S(2)}) %collective-permute-start.10) | collective-permute-done | bytes 262176 | tf_op jit(solution)/shard_map/ppermute | solution.py:311
  41.9 1.5 collective-permute-done.11.refs_1_
  43.6 3.1 %attend.1 = (bf16[128,768]{1,0:T(8,128)(2,1)S(1)}, bf16[72,768]{1,0:T(8,128)(2,1)S(1)}, bf16[72,768]{1,0:T(8,128)(2,1)S(1)}, bf16[72,768]{1,0:T(8,128)(2,1)S(1)}, bf16[72,768]{1,0:T(8,128)(2,1)S(1)}) custom-call(bf16[768,128]{1,0:T(8,128)(2,1)S(1)} %get-tuple-element.82.q_all, bf16[128,768]{1,0:T(8,128)(2,1)S(1)} %get-tuple-element.83.res_ref, ...), custom_call_target="tpu_custom_call" | custom-call | tf_op jit(solution)/shard_map/attend/pallas_call | solution.py:32
  47.0 4.1 %collective-permute-start.13 = (bf16[72,768]{1,0:T(8,128)(2,1)S(1)}, bf16[72,768]{1,0:T(8,128)(2,1)S(1)}, u32[]{:S(2)}, u32[]{:S(2)}) collective-permute-start(bf16[72,768]{1,0:T(8,128)(2,1)S(1)} %get-tuple-element.113), channel_id=1, source_target_pairs={{0,96},{32,0},{64,32},{96,64},{1,97},{33,1},{65,33},{97,65},{2,98}... | collective-permute-start | bytes 331784 | tf_op jit(solution)/shard_map/ppermute | solution.py:311
  51.1 3.2 %collective-permute-start.14 = (bf16[72,768]{1,0:T(8,128)(2,1)S(1)}, bf16[72,768]{1,0:T(8,128)(2,1)S(1)}, u32[]{:S(2)}, u32[]{:S(2)}) collective-permute-start(bf16[72,768]{1,0:T(8,128)(2,1)S(1)} %get-tuple-element.114), channel_id=1, source_target_pairs={{0,64},{32,96},{64,0},{96,32},{1,65},{33,97},{65,1},{97,33},{2,66}... | collective-permute-start | bytes 331784 | tf_op jit(solution)/shard_map/ppermute | solution.py:311
  54.7 3.1 %collective-permute-done.13.refs_2_ = bf16[72,768]{1,0:T(8,128)(2,1)S(1)} collective-permute-done((bf16[72,768]{1,0:T(8,128)(2,1)S(1)}, bf16[72,768]{1,0:T(8,128)(2,1)S(1)}, u32[]{:S(2)}, u32[]{:S(2)}) %collective-permute-start.13) | collective-permute-done | bytes 110624 | tf_op jit(solution)/shard_map/ppermute | solution.py:311
  57.7 4.6 %collective-permute-done.14.refs_3_ = bf16[72,768]{1,0:T(8,128)(2,1)S(1)} collective-permute-done((bf16[72,768]{1,0:T(8,128)(2,1)S(1)}, bf16[72,768]{1,0:T(8,128)(2,1)S(1)}, u32[]{:S(2)}, u32[]{:S(2)}) %collective-permute-start.14) | collective-permute-done | bytes 110624 | tf_op jit(solution)/shard_map/ppermute | solution.py:311
  63.0 1.5 collective-permute-start.18
  64.5 1.8 %collective-permute-start.17 = (bf16[144,768]{1,0:T(8,128)(2,1)S(1)}, bf16[144,768]{1,0:T(8,128)(2,1)S(1)}, u32[]{:S(2)}, u32[]{:S(2)}) collective-permute-start(bf16[144,768]{1,0:T(8,128)(2,1)S(1)} %get-tuple-element.122), channel_id=1, source_target_pairs={{0,3},{1,0},{2,1},{3,2},{4,7},{5,4},{6,5},{7,6},{8,11},{9,8},{10,9... | collective-permute-start | bytes 663560 | tf_op jit(solution)/shard_map/ppermute | solution.py:311
  66.3 1.8 %collective-permute-start.16 = (bf16[144,768]{1,0:T(8,128)(2,1)S(1)}, bf16[144,768]{1,0:T(8,128)(2,1)S(1)}, u32[]{:S(2)}, u32[]{:S(2)}) collective-permute-start(bf16[144,768]{1,0:T(8,128)(2,1)S(1)} %get-tuple-element.122), channel_id=1, source_target_pairs={{0,2},{1,3},{2,0},{3,1},{4,6},{5,7},{6,4},{7,5},{8,10},{9,11},{10,... | collective-permute-start | bytes 663560 | tf_op jit(solution)/shard_map/ppermute | solution.py:311
  68.1 2.0 %collective-permute-done.19 = bf16[144,768]{1,0:T(8,128)(2,1)S(1)} collective-permute-done((bf16[144,768]{1,0:T(8,128)(2,1)S(1)}, bf16[144,768]{1,0:T(8,128)(2,1)S(1)}, u32[]{:S(2)}, u32[]{:S(2)}) %collective-permute-start.19) | collective-permute-done | bytes 221216 | tf_op jit(solution)/shard_map/ppermute | solution.py:325
  70.1 1.5 collective-permute-done.18
  71.6 2.8 %collective-permute-done.17 = bf16[144,768]{1,0:T(8,128)(2,1)S(1)} collective-permute-done((bf16[144,768]{1,0:T(8,128)(2,1)S(1)}, bf16[144,768]{1,0:T(8,128)(2,1)S(1)}, u32[]{:S(2)}, u32[]{:S(2)}) %collective-permute-start.17) | collective-permute-done | bytes 221216 | tf_op jit(solution)/shard_map/ppermute | solution.py:311
  74.4 1.7 %collective-permute-done.16 = bf16[144,768]{1,0:T(8,128)(2,1)S(1)} collective-permute-done((bf16[144,768]{1,0:T(8,128)(2,1)S(1)}, bf16[144,768]{1,0:T(8,128)(2,1)S(1)}, u32[]{:S(2)}, u32[]{:S(2)}) %collective-permute-start.16) | collective-permute-done | bytes 221216 | tf_op jit(solution)/shard_map/ppermute | solution.py:311
  76.4 1.6 collective-permute-start.23
  78.0 1.7 %collective-permute-start.22 = (bf16[2,144,768]{2,1,0:T(8,128)(2,1)S(1)}, bf16[2,144,768]{2,1,0:T(8,128)(2,1)S(1)}, u32[]{:S(2)}, u32[]{:S(2)}) collective-permute-start(bf16[2,144,768]{2,1,0:T(8,128)(2,1)S(1)} %pad_maximum_fusion.1.refs_2_), channel_id=1, source_target_pairs={{0,3},{1,0},{2,1},{3,2},{4,7},{5,4},{6,5},{7,6},{8,11},{9,8},{10,9... | collective-permute-start | bytes 1327112 | tf_op jit(solution)/shard_map/ppermute | solution.py:311
  79.7 1.7 %collective-permute-start.21 = (bf16[2,144,768]{2,1,0:T(8,128)(2,1)S(1)}, bf16[2,144,768]{2,1,0:T(8,128)(2,1)S(1)}, u32[]{:S(2)}, u32[]{:S(2)}) collective-permute-start(bf16[2,144,768]{2,1,0:T(8,128)(2,1)S(1)} %pad_maximum_fusion.1.refs_2_), channel_id=1, source_target_pairs={{0,2},{1,3},{2,0},{3,1},{4,6},{5,7},{6,4},{7,5},{8,10},{9,11},{10,... | collective-permute-start | bytes 1327112 | tf_op jit(solution)/shard_map/ppermute | solution.py:311
  81.4 9.6 %collective-permute-done.23.refs_3_ = bf16[2,144,768]{2,1,0:T(8,128)(2,1)S(1)} collective-permute-done((bf16[2,144,768]{2,1,0:T(8,128)(2,1)S(1)}, bf16[2,144,768]{2,1,0:T(8,128)(2,1)S(1)}, u32[]{:S(2)}, u32[]{:S(2)}) %collective-permute-start.23) | collective-permute-done | bytes 442400 | tf_op jit(solution)/shard_map/ppermute | solution.py:311
  91.0 5.4 %collective-permute-done.22.refs_4_ = bf16[2,144,768]{2,1,0:T(8,128)(2,1)S(1)} collective-permute-done((bf16[2,144,768]{2,1,0:T(8,128)(2,1)S(1)}, bf16[2,144,768]{2,1,0:T(8,128)(2,1)S(1)}, u32[]{:S(2)}, u32[]{:S(2)}) %collective-permute-start.22) | collective-permute-done | bytes 442400 | tf_op jit(solution)/shard_map/ppermute | solution.py:311
  96.4 1.0 collective-permute-done.21.refs_5_
  97.5 16.2 %experts.1 = (bf16[4,144,768]{2,1,0:T(8,128)(2,1)S(1)}, bf16[4,144,768]{2,1,0:T(8,128)(2,1)S(1)}, bf16[2,144,768]{2,1,0:T(8,128)(2,1)S(1)}, bf16[2,144,768]{2,1,...) custom-call(s32[4]{0:T(128)S(1)} %pad_add_fusion.where_ref, ...), custom_call_target="tpu_custom_call" | custom-call | tf_op jit(solution)/shard_map/experts/pallas_call | solution.py:32
  113.7 1.8 %collective-permute-start.28 = (bf16[4,144,768]{2,1,0:T(8,128)(2,1)S(1)}, bf16[4,144,768]{2,1,0:T(8,128)(2,1)S(1)}, u32[]{:S(2)}, u32[]{:S(2)}) collective-permute-start(bf16[4,144,768]{2,1,0:T(8,128)(2,1)S(1)} %get-tuple-element.139), channel_id=1, source_target_pairs={{0,8},{8,0},{1,9},{9,1},{2,10},{10,2},{3,11},{11,3},{4,12},{12,4},... | collective-permute-start | bytes 2654216 | tf_op jit(solution)/shard_map/ppermute | solution.py:329
  115.5 1.1 collective-permute-start.25
  116.7 2.1 %collective-permute-start.26 = (bf16[2,144,768]{2,1,0:T(8,128)(2,1)S(1)}, bf16[2,144,768]{2,1,0:T(8,128)(2,1)S(1)}, u32[]{:S(2)}, u32[]{:S(2)}) collective-permute-start(bf16[2,144,768]{2,1,0:T(8,128)(2,1)S(1)} %get-tuple-element.137), channel_id=1, source_target_pairs={{0,3},{1,0},{2,1},{3,2},{4,7},{5,4},{6,5},{7,6},{8,11},{9,8},{10,9... | collective-permute-start | bytes 1327112 | tf_op jit(solution)/shard_map/ppermute | solution.py:311
  119.6 15.3 %collective-permute-done.25.refs_3_ = bf16[2,144,768]{2,1,0:T(8,128)(2,1)S(1)} collective-permute-done((bf16[2,144,768]{2,1,0:T(8,128)(2,1)S(1)}, bf16[2,144,768]{2,1,0:T(8,128)(2,1)S(1)}, u32[]{:S(2)}, u32[]{:S(2)}) %collective-permute-start.25) | collective-permute-done | bytes 442400 | tf_op jit(solution)/shard_map/ppermute | solution.py:311
  135.5 0.9 collective-permute-start.29
  136.4 2.4 %collective-permute-start.30 = (bf16[144,768]{1,0:T(8,128)(2,1)S(1)}, bf16[144,768]{1,0:T(8,128)(2,1)S(1)}, u32[]{:S(2)}, u32[]{:S(2)}) collective-permute-start(bf16[144,768]{1,0:T(8,128)(2,1)S(1)} %get-tuple-element.147), channel_id=1, source_target_pairs={{0,3},{1,0},{2,1},{3,2},{4,7},{5,4},{6,5},{7,6},{8,11},{9,8},{10,9... | collective-permute-start | bytes 663560 | tf_op jit(solution)/shard_map/ppermute | solution.py:311
  138.8 1.4 collective-permute-start.31
  140.2 1.2 collective-permute-done.32
  141.4 1.8 %collective-permute-start.33 = (bf16[144,768]{1,0:T(8,128)(2,1)S(1)}, bf16[144,768]{1,0:T(8,128)(2,1)S(1)}, u32[]{:S(2)}, u32[]{:S(2)}) collective-permute-start(bf16[144,768]{1,0:T(8,128)(2,1)S(1)} %add_convert_fusion), channel_id=1, source_target_pairs={{0,24},{8,16},{16,8},{24,0},{1,25},{9,17},{17,9},{25,1},{2,26},{10... | collective-permute-start | bytes 663560 | tf_op jit(solution)/shard_map/ppermute | solution.py:325
  143.2 3.2 %collective-permute-done.31.refs_3_ = bf16[144,768]{1,0:T(8,128)(2,1)S(1)} collective-permute-done((bf16[144,768]{1,0:T(8,128)(2,1)S(1)}, bf16[144,768]{1,0:T(8,128)(2,1)S(1)}, u32[]{:S(2)}, u32[]{:S(2)}) %collective-permute-start.31) | collective-permute-done | bytes 221216 | tf_op jit(solution)/shard_map/ppermute | solution.py:311
  146.4 2.2 %collective-permute-done.33.refs_4_ = bf16[144,768]{1,0:T(8,128)(2,1)S(1)} collective-permute-done((bf16[144,768]{1,0:T(8,128)(2,1)S(1)}, bf16[144,768]{1,0:T(8,128)(2,1)S(1)}, u32[]{:S(2)}, u32[]{:S(2)}) %collective-permute-start.33) | collective-permute-done | bytes 221216 | tf_op jit(solution)/shard_map/ppermute | solution.py:325
  148.8 1.1 collective-permute-start.34
  149.9 3.1 %collective-permute-start.35 = (bf16[72,768]{1,0:T(8,128)(2,1)S(1)}, bf16[72,768]{1,0:T(8,128)(2,1)S(1)}, u32[]{:S(2)}, u32[]{:S(2)}) collective-permute-start(bf16[72,768]{1,0:T(8,128)(2,1)S(1)} %get-tuple-element.157), channel_id=1, source_target_pairs={{0,96},{32,0},{64,32},{96,64},{1,97},{33,1},{65,33},{97,65},{2,98}... | collective-permute-start | bytes 331784 | tf_op jit(solution)/shard_map/ppermute | solution.py:311
  153.0 5.6 %collective-permute-start.36 = (bf16[72,768]{1,0:T(8,128)(2,1)S(1)}, bf16[72,768]{1,0:T(8,128)(2,1)S(1)}, u32[]{:S(2)}, u32[]{:S(2)}) collective-permute-start(bf16[72,768]{1,0:T(8,128)(2,1)S(1)} %get-tuple-element.158), channel_id=1, source_target_pairs={{0,64},{32,96},{64,0},{96,32},{1,65},{33,97},{65,1},{97,33},{2,66}... | collective-permute-start | bytes 331784 | tf_op jit(solution)/shard_map/ppermute | solution.py:311
  158.6 5.1 %collective-permute-done.36.refs_3_ = bf16[72,768]{1,0:T(8,128)(2,1)S(1)} collective-permute-done((bf16[72,768]{1,0:T(8,128)(2,1)S(1)}, bf16[72,768]{1,0:T(8,128)(2,1)S(1)}, u32[]{:S(2)}, u32[]{:S(2)}) %collective-permute-start.36) | collective-permute-done | bytes 110624 | tf_op jit(solution)/shard_map/ppermute | solution.py:311
  163.7 2.2 %mix.1 = bf16[128,768]{1,0:T(8,128)(2,1)} custom-call(s32[4]{0:T(128)S(1)} %pad_add_fusion.where_ref, s32[2,128]{1,0:T(2,128)S(1)} %bitcast.20, f32[2,128]{1,0:T(2,128)S(1)} %bitcast.21, bf16[128,768]{1,0:T(8,128)(2,1)S(1)} %get-tuple-element.110.hid_ref, bf16[72,768]{1,0:T(8,128)(2,1)S(1)} %get-tuple-element.155.refs_0_, ...), custom_call_target="tpu_custom_call" | custom-call | tf_op jit(solution)/shard_map/mix/pallas_call | solution.py:32
  (61 shorter events, 7.9 us)
Async XLA Ops:
  0.0 18.7 %collective-permute-start.3 = (bf16[3072,512]{1,0:T(8,128)(2,1)}, bf16[3072,512]{1,0:T(8,128)(2,1)S(1)}, u32[]{:S(2)}, u32[]{:S(2)}) collective-permute-start(bf16[3072,512]{1,0:T(8,128)(2,1)} %refs_6_.1), channel_id=1, source_target_pairs={{0,4},{4,0},{1,5},{5,1},{2,6},{6,2},{3,7},{7,3},{8,12},{12,8},{9,1... | collective-permute-start | bytes 9437192 | tf_op jit(solution)/shard_map/ppermute | solution.py:333
  1.5 10.5 %collective-permute-start.2 = (bf16[2,128,128]{2,1,0:T(8,128)(2,1)}, bf16[2,128,128]{2,1,0:T(8,128)(2,1)S(1)}, u32[]{:S(2)}, u32[]{:S(2)}) collective-permute-start(bf16[2,128,128]{2,1,0:T(8,128)(2,1)} %get-tuple-element.159), channel_id=1, source_target_pairs={{0,32},{32,64},{64,96},{96,0},{1,33},{33,65},{65,97},{97,1},{2,34}... | collective-permute-start | bytes 196616 | tf_op jit(solution)/shard_map/ppermute | solution.py:311
  4.8 7.2 %collective-permute-start = (bf16[2,128,128]{2,1,0:T(8,128)(2,1)}, bf16[2,128,128]{2,1,0:T(8,128)(2,1)S(1)}, u32[]{:S(2)}, u32[]{:S(2)}) collective-permute-start(bf16[2,128,128]{2,1,0:T(8,128)(2,1)} %get-tuple-element.160), channel_id=1, source_target_pairs={{0,96},{32,0},{64,32},{96,64},{1,97},{33,1},{65,33},{97,65},{2,98}... | collective-permute-start | bytes 196616 | tf_op jit(solution)/shard_map/ppermute | solution.py:311
  6.9 11.1 %collective-permute-start.1 = (bf16[2,128,128]{2,1,0:T(8,128)(2,1)S(1)}, bf16[2,128,128]{2,1,0:T(8,128)(2,1)S(1)}, u32[]{:S(2)}, u32[]{:S(2)}) collective-permute-start(bf16[2,128,128]{2,1,0:T(8,128)(2,1)S(1)} %get-tuple-element.161), channel_id=1, source_target_pairs={{0,64},{32,96},{64,0},{96,32},{1,65},{33,97},{65,1},{97,33},{2,66}... | collective-permute-start | bytes 196616 | tf_op jit(solution)/shard_map/ppermute | solution.py:311
  18.7 43.7 %copy-start.7 = (bf16[3072,512]{1,0:T(8,128)(2,1)}, bf16[3072,512]{1,0:T(8,128)(2,1)S(1)}, u32[]{:S(2)}) copy-start(bf16[3072,512]{1,0:T(8,128)(2,1)S(1)} %collective-permute-done.3.refs_9_) | copy-start | bytes 9437188
  18.7 12.9 %collective-permute-start.7 = (bf16[3072,512]{1,0:T(8,128)(2,1)}, bf16[3072,512]{1,0:T(8,128)(2,1)S(1)}, u32[]{:S(2)}, u32[]{:S(2)}) collective-permute-start(bf16[3072,512]{1,0:T(8,128)(2,1)} %refs_7_.1), channel_id=1, source_target_pairs={{0,4},{4,0},{1,5},{5,1},{2,6},{6,2},{3,7},{7,3},{8,12},{12,8},{9,1... | collective-permute-start | bytes 9437192 | tf_op jit(solution)/shard_map/ppermute | solution.py:333
  18.8 6.8 %collective-permute-start.4 = (bf16[2,512,128]{2,1,0:T(8,128)(2,1)S(1)}, bf16[2,512,128]{2,1,0:T(8,128)(2,1)S(1)}, u32[]{:S(2)}, u32[]{:S(2)}) collective-permute-start(bf16[2,512,128]{2,1,0:T(8,128)(2,1)S(1)} %get-tuple-element.89.refs_0_), channel_id=1, source_target_pairs={{0,4},{4,0},{1,5},{5,1},{2,6},{6,2},{3,7},{7,3},{8,12},{12,8},{9,1... | collective-permute-start | bytes 786440 | tf_op jit(solution)/shard_map/ppermute | solution.py:333
  19.3 9.4 %collective-permute-start.6 = (bf16[2,512,128]{2,1,0:T(8,128)(2,1)S(1)}, bf16[2,512,128]{2,1,0:T(8,128)(2,1)S(1)}, u32[]{:S(2)}, u32[]{:S(2)}) collective-permute-start(bf16[2,512,128]{2,1,0:T(8,128)(2,1)S(1)} %get-tuple-element.94), channel_id=1, source_target_pairs={{0,24},{8,0},{16,8},{24,16},{1,25},{9,1},{17,9},{25,17},{2,26},{10... | collective-permute-start | bytes 786440 | tf_op jit(solution)/shard_map/ppermute | solution.py:311
  22.3 9.2 %collective-permute-start.5 = (bf16[2,512,128]{2,1,0:T(8,128)(2,1)S(1)}, bf16[2,512,128]{2,1,0:T(8,128)(2,1)S(1)}, u32[]{:S(2)}, u32[]{:S(2)}) collective-permute-start(bf16[2,512,128]{2,1,0:T(8,128)(2,1)S(1)} %get-tuple-element.93), channel_id=1, source_target_pairs={{0,8},{8,16},{16,24},{24,0},{1,9},{9,17},{17,25},{25,1},{2,10},{10... | collective-permute-start | bytes 786440 | tf_op jit(solution)/shard_map/ppermute | solution.py:311
  22.3 0.9 copy-start
  23.2 0.9 copy-start.1
  24.2 0.7 copy-start.3
  24.9 18.6 %copy-start.6 = (bf16[512,3072]{1,0:T(8,128)(2,1)S(1)}, bf16[512,3072]{1,0:T(8,128)(2,1)}, u32[]{:S(2)}) copy-start(bf16[512,3072]{1,0:T(8,128)(2,1)} %refs_8_.1) | copy-start | bytes 9437188
  31.6 44.7 %copy-start.8 = (bf16[3072,512]{1,0:T(8,128)(2,1)}, bf16[3072,512]{1,0:T(8,128)(2,1)S(1)}, u32[]{:S(2)}) copy-start(bf16[3072,512]{1,0:T(8,128)(2,1)S(1)} %collective-permute-done.7.refs_10_) | copy-start | bytes 9437188
  31.6 1.5 collective-permute-start.8
  31.6 1.9 %collective-permute-start.9 = (bf16[2,512,128]{2,1,0:T(8,128)(2,1)S(1)}, bf16[2,512,128]{2,1,0:T(8,128)(2,1)S(1)}, u32[]{:S(2)}, u32[]{:S(2)}) collective-permute-start(bf16[2,512,128]{2,1,0:T(8,128)(2,1)S(1)} %collective-permute-done.6.refs_1_), channel_id=1, source_target_pairs={{0,4},{4,0},{1,5},{5,1},{2,6},{6,2},{3,7},{7,3},{8,12},{12,8},{9,1... | collective-permute-start | bytes 786440 | tf_op jit(solution)/shard_map/ppermute | solution.py:333
  32.1 9.8 %collective-permute-start.10 = (bf16[2,512,128]{2,1,0:T(8,128)(2,1)S(1)}, bf16[2,512,128]{2,1,0:T(8,128)(2,1)S(1)}, u32[]{:S(2)}, u32[]{:S(2)}) collective-permute-start(bf16[2,512,128]{2,1,0:T(8,128)(2,1)S(1)} %get-tuple-element.105), channel_id=1, source_target_pairs={{0,16},{8,24},{16,0},{24,8},{1,17},{9,25},{17,1},{25,9},{2,18},{10... | collective-permute-start | bytes 786440 | tf_op jit(solution)/shard_map/ppermute | solution.py:311
  39.1 58.3 %copy-start.2 = (f32[3072]{0:T(1024)S(1)}, f32[3072]{0:T(1024)}, u32[]{:S(2)}) copy-start(f32[3072]{0:T(1024)} %param.18) | copy-start | bytes 36868
  41.9 1.5 collective-permute-start.11
  43.4 18.9 %collective-permute-start.15 = (bf16[512,3072]{1,0:T(8,128)(2,1)S(1)}, bf16[512,3072]{1,0:T(8,128)(2,1)S(1)}, u32[]{:S(2)}, u32[]{:S(2)}) collective-permute-start(bf16[512,3072]{1,0:T(8,128)(2,1)S(1)} %copy-done.6), channel_id=1, source_target_pairs={{0,4},{4,0},{1,5},{5,1},{2,6},{6,2},{3,7},{7,3},{8,12},{12,8},{9,1... | collective-permute-start | bytes 9437192 | tf_op jit(solution)/shard_map/ppermute | solution.py:333
  46.7 7.9 %collective-permute-start.12 = (bf16[72,768]{1,0:T(8,128)(2,1)S(1)}, bf16[72,768]{1,0:T(8,128)(2,1)S(1)}, u32[]{:S(2)}, u32[]{:S(2)}) collective-permute-start(bf16[72,768]{1,0:T(8,128)(2,1)S(1)} %get-tuple-element.112), channel_id=1, source_target_pairs={{0,32},{32,64},{64,96},{96,0},{1,33},{33,65},{65,97},{97,1},{2,34}... | collective-permute-start | bytes 331784 | tf_op jit(solution)/shard_map/ppermute | solution.py:311
  47.0 10.7 %collective-permute-start.13 = (bf16[72,768]{1,0:T(8,128)(2,1)S(1)}, bf16[72,768]{1,0:T(8,128)(2,1)S(1)}, u32[]{:S(2)}, u32[]{:S(2)}) collective-permute-start(bf16[72,768]{1,0:T(8,128)(2,1)S(1)} %get-tuple-element.113), channel_id=1, source_target_pairs={{0,96},{32,0},{64,32},{96,64},{1,97},{33,1},{65,33},{97,65},{2,98}... | collective-permute-start | bytes 331784 | tf_op jit(solution)/shard_map/ppermute | solution.py:311
  51.1 11.2 %collective-permute-start.14 = (bf16[72,768]{1,0:T(8,128)(2,1)S(1)}, bf16[72,768]{1,0:T(8,128)(2,1)S(1)}, u32[]{:S(2)}, u32[]{:S(2)}) collective-permute-start(bf16[72,768]{1,0:T(8,128)(2,1)S(1)} %get-tuple-element.114), channel_id=1, source_target_pairs={{0,64},{32,96},{64,0},{96,32},{1,65},{33,97},{65,1},{97,33},{2,66}... | collective-permute-start | bytes 331784 | tf_op jit(solution)/shard_map/ppermute | solution.py:311
  62.3 13.8 %copy-start.9 = (bf16[512,3072]{1,0:T(8,128)(2,1)}, bf16[512,3072]{1,0:T(8,128)(2,1)S(1)}, u32[]{:S(2)}) copy-start(bf16[512,3072]{1,0:T(8,128)(2,1)S(1)} %collective-permute-done.15.refs_11_) | copy-start | bytes 9437188
  62.4 7.7 %collective-permute-start.19 = (bf16[144,768]{1,0:T(8,128)(2,1)S(1)}, bf16[144,768]{1,0:T(8,128)(2,1)S(1)}, u32[]{:S(2)}, u32[]{:S(2)}) collective-permute-start(bf16[144,768]{1,0:T(8,128)(2,1)S(1)} %get-tuple-element.123), channel_id=1, source_target_pairs={{0,24},{8,16},{16,8},{24,0},{1,25},{9,17},{17,9},{25,1},{2,26},{10... | collective-permute-start | bytes 663560 | tf_op jit(solution)/shard_map/ppermute | solution.py:325
  63.0 8.6 %collective-permute-start.18 = (bf16[144,768]{1,0:T(8,128)(2,1)S(1)}, bf16[144,768]{1,0:T(8,128)(2,1)S(1)}, u32[]{:S(2)}, u32[]{:S(2)}) collective-permute-start(bf16[144,768]{1,0:T(8,128)(2,1)S(1)} %get-tuple-element.122), channel_id=1, source_target_pairs={{0,1},{1,2},{2,3},{3,0},{4,5},{5,6},{6,7},{7,4},{8,9},{9,10},{10,1... | collective-permute-start | bytes 663560 | tf_op jit(solution)/shard_map/ppermute | solution.py:311
  64.5 9.9 %collective-permute-start.17 = (bf16[144,768]{1,0:T(8,128)(2,1)S(1)}, bf16[144,768]{1,0:T(8,128)(2,1)S(1)}, u32[]{:S(2)}, u32[]{:S(2)}) collective-permute-start(bf16[144,768]{1,0:T(8,128)(2,1)S(1)} %get-tuple-element.122), channel_id=1, source_target_pairs={{0,3},{1,0},{2,1},{3,2},{4,7},{5,4},{6,5},{7,6},{8,11},{9,8},{10,9... | collective-permute-start | bytes 663560 | tf_op jit(solution)/shard_map/ppermute | solution.py:311
  66.3 9.8 %collective-permute-start.16 = (bf16[144,768]{1,0:T(8,128)(2,1)S(1)}, bf16[144,768]{1,0:T(8,128)(2,1)S(1)}, u32[]{:S(2)}, u32[]{:S(2)}) collective-permute-start(bf16[144,768]{1,0:T(8,128)(2,1)S(1)} %get-tuple-element.122), channel_id=1, source_target_pairs={{0,2},{1,3},{2,0},{3,1},{4,6},{5,7},{6,4},{7,5},{8,10},{9,11},{10,... | collective-permute-start | bytes 663560 | tf_op jit(solution)/shard_map/ppermute | solution.py:311
  70.1 6.0 %collective-permute-start.20 = (bf16[144,768]{1,0:T(8,128)(2,1)S(1)}, bf16[144,768]{1,0:T(8,128)(2,1)S(1)}, u32[]{:S(2)}, u32[]{:S(2)}) collective-permute-start(bf16[144,768]{1,0:T(8,128)(2,1)S(1)} %collective-permute-done.19), channel_id=1, source_target_pairs={{0,8},{8,0},{1,9},{9,1},{2,10},{10,2},{3,11},{11,3},{4,12},{12,4},... | collective-permute-start | bytes 663560 | tf_op jit(solution)/shard_map/ppermute | solution.py:329
  76.2 21.2 %collective-permute-start.24 = (bf16[4,144,768]{2,1,0:T(8,128)(2,1)S(1)}, bf16[4,144,768]{2,1,0:T(8,128)(2,1)S(1)}, u32[]{:S(2)}, u32[]{:S(2)}) collective-permute-start(bf16[4,144,768]{2,1,0:T(8,128)(2,1)S(1)} %pad_maximum_fusion.refs_0_), channel_id=1, source_target_pairs={{0,8},{8,0},{1,9},{9,1},{2,10},{10,2},{3,11},{11,3},{4,12},{12,4},... | collective-permute-start | bytes 2654216 | tf_op jit(solution)/shard_map/ppermute | solution.py:329
  76.4 14.6 %collective-permute-start.23 = (bf16[2,144,768]{2,1,0:T(8,128)(2,1)S(1)}, bf16[2,144,768]{2,1,0:T(8,128)(2,1)S(1)}, u32[]{:S(2)}, u32[]{:S(2)}) collective-permute-start(bf16[2,144,768]{2,1,0:T(8,128)(2,1)S(1)} %pad_maximum_fusion.1.refs_2_), channel_id=1, source_target_pairs={{0,1},{1,2},{2,3},{3,0},{4,5},{5,6},{6,7},{7,4},{8,9},{9,10},{10,1... | collective-permute-start | bytes 1327112 | tf_op jit(solution)/shard_map/ppermute | solution.py:311
  78.0 18.4 %collective-permute-start.22 = (bf16[2,144,768]{2,1,0:T(8,128)(2,1)S(1)}, bf16[2,144,768]{2,1,0:T(8,128)(2,1)S(1)}, u32[]{:S(2)}, u32[]{:S(2)}) collective-permute-start(bf16[2,144,768]{2,1,0:T(8,128)(2,1)S(1)} %pad_maximum_fusion.1.refs_2_), channel_id=1, source_target_pairs={{0,3},{1,0},{2,1},{3,2},{4,7},{5,4},{6,5},{7,6},{8,11},{9,8},{10,9... | collective-permute-start | bytes 1327112 | tf_op jit(solution)/shard_map/ppermute | solution.py:311
  79.7 17.7 %collective-permute-start.21 = (bf16[2,144,768]{2,1,0:T(8,128)(2,1)S(1)}, bf16[2,144,768]{2,1,0:T(8,128)(2,1)S(1)}, u32[]{:S(2)}, u32[]{:S(2)}) collective-permute-start(bf16[2,144,768]{2,1,0:T(8,128)(2,1)S(1)} %pad_maximum_fusion.1.refs_2_), channel_id=1, source_target_pairs={{0,2},{1,3},{2,0},{3,1},{4,6},{5,7},{6,4},{7,5},{8,10},{9,11},{10,... | collective-permute-start | bytes 1327112 | tf_op jit(solution)/shard_map/ppermute | solution.py:311
  113.7 50.1 %copy-start.4 = (s32[128,2]{0,1:T(2,128)S(1)}, s32[128,2]{0,1:T(2,128)}, u32[]{:S(2)}) copy-start(s32[128,2]{0,1:T(2,128)} %param.22) | copy-start | bytes 3076
  113.7 50.0 %copy-start.5 = (f32[128,2]{0,1:T(2,128)S(1)}, f32[128,2]{0,1:T(2,128)}, u32[]{:S(2)}) copy-start(f32[128,2]{0,1:T(2,128)} %param.23) | copy-start | bytes 3076
  113.7 21.2 %collective-permute-start.28 = (bf16[4,144,768]{2,1,0:T(8,128)(2,1)S(1)}, bf16[4,144,768]{2,1,0:T(8,128)(2,1)S(1)}, u32[]{:S(2)}, u32[]{:S(2)}) collective-permute-start(bf16[4,144,768]{2,1,0:T(8,128)(2,1)S(1)} %get-tuple-element.139), channel_id=1, source_target_pairs={{0,8},{8,0},{1,9},{9,1},{2,10},{10,2},{3,11},{11,3},{4,12},{12,4},... | collective-permute-start | bytes 2654216 | tf_op jit(solution)/shard_map/ppermute | solution.py:329
  115.5 19.4 %collective-permute-start.25 = (bf16[2,144,768]{2,1,0:T(8,128)(2,1)S(1)}, bf16[2,144,768]{2,1,0:T(8,128)(2,1)S(1)}, u32[]{:S(2)}, u32[]{:S(2)}) collective-permute-start(bf16[2,144,768]{2,1,0:T(8,128)(2,1)S(1)} %get-tuple-element.136), channel_id=1, source_target_pairs={{0,1},{1,2},{2,3},{3,0},{4,5},{5,6},{6,7},{7,4},{8,9},{9,10},{10,1... | collective-permute-start | bytes 1327112 | tf_op jit(solution)/shard_map/ppermute | solution.py:311
  116.7 18.3 %collective-permute-start.26 = (bf16[2,144,768]{2,1,0:T(8,128)(2,1)S(1)}, bf16[2,144,768]{2,1,0:T(8,128)(2,1)S(1)}, u32[]{:S(2)}, u32[]{:S(2)}) collective-permute-start(bf16[2,144,768]{2,1,0:T(8,128)(2,1)S(1)} %get-tuple-element.137), channel_id=1, source_target_pairs={{0,3},{1,0},{2,1},{3,2},{4,7},{5,4},{6,5},{7,6},{8,11},{9,8},{10,9... | collective-permute-start | bytes 1327112 | tf_op jit(solution)/shard_map/ppermute | solution.py:311
  118.8 16.2 %collective-permute-start.27 = (bf16[2,144,768]{2,1,0:T(8,128)(2,1)S(1)}, bf16[2,144,768]{2,1,0:T(8,128)(2,1)S(1)}, u32[]{:S(2)}, u32[]{:S(2)}) collective-permute-start(bf16[2,144,768]{2,1,0:T(8,128)(2,1)S(1)} %get-tuple-element.138), channel_id=1, source_target_pairs={{0,2},{1,3},{2,0},{3,1},{4,6},{5,7},{6,4},{7,5},{8,10},{9,11},{10,... | collective-permute-start | bytes 1327112 | tf_op jit(solution)/shard_map/ppermute | solution.py:311
  135.4 6.0 %collective-permute-start.32 = (bf16[144,768]{1,0:T(8,128)(2,1)S(1)}, bf16[144,768]{1,0:T(8,128)(2,1)S(1)}, u32[]{:S(2)}, u32[]{:S(2)}) collective-permute-start(bf16[144,768]{1,0:T(8,128)(2,1)S(1)} %get-tuple-element.150), channel_id=1, source_target_pairs={{0,8},{8,0},{1,9},{9,1},{2,10},{10,2},{3,11},{11,3},{4,12},{12,4},... | collective-permute-start | bytes 663560 | tf_op jit(solution)/shard_map/ppermute | solution.py:329
  135.5 7.8 %collective-permute-start.29 = (bf16[144,768]{1,0:T(8,128)(2,1)S(1)}, bf16[144,768]{1,0:T(8,128)(2,1)S(1)}, u32[]{:S(2)}, u32[]{:S(2)}) collective-permute-start(bf16[144,768]{1,0:T(8,128)(2,1)S(1)} %get-tuple-element.146), channel_id=1, source_target_pairs={{0,1},{1,2},{2,3},{3,0},{4,5},{5,6},{6,7},{7,4},{8,9},{9,10},{10,1... | collective-permute-start | bytes 663560 | tf_op jit(solution)/shard_map/ppermute | solution.py:311
  136.4 6.8 %collective-permute-start.30 = (bf16[144,768]{1,0:T(8,128)(2,1)S(1)}, bf16[144,768]{1,0:T(8,128)(2,1)S(1)}, u32[]{:S(2)}, u32[]{:S(2)}) collective-permute-start(bf16[144,768]{1,0:T(8,128)(2,1)S(1)} %get-tuple-element.147), channel_id=1, source_target_pairs={{0,3},{1,0},{2,1},{3,2},{4,7},{5,4},{6,5},{7,6},{8,11},{9,8},{10,9... | collective-permute-start | bytes 663560 | tf_op jit(solution)/shard_map/ppermute | solution.py:311
  138.8 7.6 %collective-permute-start.31 = (bf16[144,768]{1,0:T(8,128)(2,1)S(1)}, bf16[144,768]{1,0:T(8,128)(2,1)S(1)}, u32[]{:S(2)}, u32[]{:S(2)}) collective-permute-start(bf16[144,768]{1,0:T(8,128)(2,1)S(1)} %get-tuple-element.148), channel_id=1, source_target_pairs={{0,2},{1,3},{2,0},{3,1},{4,6},{5,7},{6,4},{7,5},{8,10},{9,11},{10,... | collective-permute-start | bytes 663560 | tf_op jit(solution)/shard_map/ppermute | solution.py:311
  141.4 7.2 %collective-permute-start.33 = (bf16[144,768]{1,0:T(8,128)(2,1)S(1)}, bf16[144,768]{1,0:T(8,128)(2,1)S(1)}, u32[]{:S(2)}, u32[]{:S(2)}) collective-permute-start(bf16[144,768]{1,0:T(8,128)(2,1)S(1)} %add_convert_fusion), channel_id=1, source_target_pairs={{0,24},{8,16},{16,8},{24,0},{1,25},{9,17},{17,9},{25,1},{2,26},{10... | collective-permute-start | bytes 663560 | tf_op jit(solution)/shard_map/ppermute | solution.py:325
  148.8 9.8 %collective-permute-start.34 = (bf16[72,768]{1,0:T(8,128)(2,1)S(1)}, bf16[72,768]{1,0:T(8,128)(2,1)S(1)}, u32[]{:S(2)}, u32[]{:S(2)}) collective-permute-start(bf16[72,768]{1,0:T(8,128)(2,1)S(1)} %get-tuple-element.156), channel_id=1, source_target_pairs={{0,32},{32,64},{64,96},{96,0},{1,33},{33,65},{65,97},{97,1},{2,34}... | collective-permute-start | bytes 331784 | tf_op jit(solution)/shard_map/ppermute | solution.py:311
  149.9 8.7 %collective-permute-start.35 = (bf16[72,768]{1,0:T(8,128)(2,1)S(1)}, bf16[72,768]{1,0:T(8,128)(2,1)S(1)}, u32[]{:S(2)}, u32[]{:S(2)}) collective-permute-start(bf16[72,768]{1,0:T(8,128)(2,1)S(1)} %get-tuple-element.157), channel_id=1, source_target_pairs={{0,96},{32,0},{64,32},{96,64},{1,97},{33,1},{65,33},{97,65},{2,98}... | collective-permute-start | bytes 331784 | tf_op jit(solution)/shard_map/ppermute | solution.py:311
  153.0 10.7 %collective-permute-start.36 = (bf16[72,768]{1,0:T(8,128)(2,1)S(1)}, bf16[72,768]{1,0:T(8,128)(2,1)S(1)}, u32[]{:S(2)}, u32[]{:S(2)}) collective-permute-start(bf16[72,768]{1,0:T(8,128)(2,1)S(1)} %get-tuple-element.158), channel_id=1, source_target_pairs={{0,64},{32,96},{64,0},{96,32},{1,65},{33,97},{65,1},{97,33},{2,66}... | collective-permute-start | bytes 331784 | tf_op jit(solution)/shard_map/ppermute | solution.py:311

commit v3 on v2

--- a/solution.py
+++ b/solution.py
@@ -19,6 +19,7 @@
 SHIFTS = (1, 3, 2)
 KV_ORDER, Z_ORDER, X_ORDER = (0, 1, 2), (0, 1, 2), (2, 1, 0)
 MB = 1024 * 1024
+LIMIT = 47
 
 bf16 = jnp.bfloat16
 f32 = jnp.float32
@@ -61,13 +62,19 @@
     return [rank[g : g + 1, :] == row for g in range(EXPERTS)]
 
 
-def prep_kernel(where_ref, ids_ref, q_ref, res_ref, q_all, res_out, table):
+def prep_kernel(where_ref, ids_ref, gates_ref, q_ref, res_ref, q_all, res_out, table, weight):
     rows = q_ref.shape[0]
     for h in range(q_ref.shape[1] // HEAD_DIM):
         q_all[h * rows : (h + 1) * rows, :] = q_ref[:, h * HEAD_DIM : (h + 1) * HEAD_DIM]
     res_out[...] = res_ref[...]
-    picks = pick_table(where_ref[0], lax.div(where_ref[1], 2), ids_ref)
+    z, yh = where_ref[0], lax.div(where_ref[1], 2)
+    picks = pick_table(z, yh, ids_ref)
     table[...] = jnp.concatenate([t.astype(f32) for t in picks], axis=0).astype(bf16)
+    for g, pick in enumerate(picks):
+        e = group_expert(z, yh, g)
+        gate = jnp.where(ids_ref[0:1, :] == e, gates_ref[0:1, :], 0.0)
+        gate = gate + jnp.where(ids_ref[1:2, :] == e, gates_ref[1:2, :], 0.0)
+        weight[g * PAD : (g + 1) * PAD, :] = jnp.where(pick, gate, 0.0)
 
 
 def pack_kv_kernel(where_ref, tract, cache, *refs):
@@ -177,14 +184,16 @@
         away[d * CAP : (d + 1) * CAP, :] = ref[CAP:]
 
 
-def expert_kernel(where_ref, gain_ref, *refs):
-    a_own, a_far, b_all = refs[0], refs[1], refs[2 : 2 + NX]
-    weights = refs[2 + NX : 8 + NX]
-    a_own_out, a_far_out = refs[8 + NX : 10 + NX]
-    b_out = refs[10 + NX : 10 + 2 * NX]
-    normed, act, gate_v, up_v, down_v, sems = refs[10 + 2 * NX :]
-    rows, width = a_own.shape[1:]
+def expert_kernel(stacks, pairs, where_ref, gain_ref, *refs):
+    refs = list(refs)
+    take = lambda n: [refs.pop(0) for _ in range(n)]
+    stack_in, pair_in = take(stacks), take(NX * pairs)
+    weights = take(6)
+    stack_out, pair_out = take(stacks), take(NX * pairs)
+    normed, act, gate_v, up_v, down_v, sems = refs
     total, ff = weights[0].shape
+    width = total // NX
+    rows = normed.shape[0] // (stacks + 2 * pairs)
     gate_loads, up_loads, down_loads = [
         [pltpu.make_async_copy(weights[3 * h + j], place(h), sems.at[h, j]) for h in range(2)]
         for j, place in enumerate(
@@ -199,23 +208,33 @@
         c.start()
     x = where_ref[3]
     order = (0,) + SHIFTS
-    parts = [
-        lambda i: a_own[i],
-        lambda i: a_far[i],
-        lambda i: b_all[i][0],
-        lambda i: b_all[i][1],
-    ]
-    for r, part in enumerate(parts):
+
+    def place(r, shift, v, inverse):
+        src = lax.rem(x - shift + NX, NX)
+        cols = pl.ds(pl.multiple_of(src * width, width), width)
+        v = v.astype(f32) * inverse * gain_ref[src]
+        normed[r * rows : (r + 1) * rows, cols] = v.astype(bf16)
+
+    def square(v, sq):
+        v = v.astype(f32)
+        return sq + jnp.sum(v * v, axis=1, keepdims=True)
+
+    for r, ref in enumerate(stack_in):
+        sq = lax.fori_loop(0, NX, lambda i, sq: square(ref[i], sq), jnp.zeros((rows, 1), f32))
+        inverse = lax.rsqrt(sq * (1.0 / total) + EPS)
+
+        def put(i, carry):
+            place(r, i ^ (i >> 1), ref[i], inverse)
+            return carry
+
+        lax.fori_loop(0, NX, put, 0)
+    for r in range(2 * pairs):
         sq = jnp.zeros((rows, 1), f32)
-        for i in range(NX):
-            v = part(i).astype(f32)
-            sq = sq + jnp.sum(v * v, axis=1, keepdims=True)
+        for ref in pair_in:
+            sq = square(ref[r], sq)
         inverse = lax.rsqrt(sq * (1.0 / total) + EPS)
-        for i, shift in enumerate(order):
-            src = lax.rem(x - shift + NX, NX)
-            cols = pl.ds(pl.multiple_of(src * width, width), width)
-            v = part(i).astype(f32) * inverse * gain_ref[src]
-            normed[r * rows : (r + 1) * rows, cols] = v.astype(bf16)
+        for shift, ref in zip(order, pair_in):
+            place(stacks + r, shift, ref[r], inverse)
 
     def hidden_units(half, carry):
         for j, v in enumerate((gate_v, up_v)):
@@ -232,29 +251,34 @@
     for i, shift in enumerate(order):
         cols = pl.ds(pl.multiple_of(lax.rem(x + shift, NX) * width, width), width)
         out = jnp.dot(act[...], down_v[:, cols], preferred_element_type=f32).astype(bf16)
-        a_own_out[i] = out[0:rows]
-        a_far_out[i] = out[rows : 2 * rows]
-        b_out[i][0] = out[2 * rows : 3 * rows]
-        b_out[i][1] = out[3 * rows :]
-
-
-def experts(where, gain, a_own, a_far, b_all, own, other):
-    rows, width = a_own.shape[1:]
+        for r, ref in enumerate(stack_out):
+            ref[i] = out[r * rows : (r + 1) * rows]
+        for r in range(2 * pairs):
+            at = (stacks + r) * rows
+            pair_out[i][r] = out[at : at + rows]
+
+
+def experts(where, gain, stacks, pairs, own, other, name):
+    rows, width = stacks[0].shape[1:]
     total, ff = own[0].shape
-    out = call(
-        expert_kernel,
-        [jax.ShapeDtypeStruct((NX, rows, width), bf16)] * 2
-        + [jax.ShapeDtypeStruct((2, rows, width), bf16)] * NX,
-        [where, gain, a_own, a_far, *b_all, *own, *other],
-        "experts",
-        [pltpu.VMEM((4 * rows, total), bf16), pltpu.VMEM((4 * rows, 2 * ff), bf16)]
+    groups = 1 if pairs else 0
+    n = rows * (len(stacks) + 2 * groups)
+
+    def body(*refs):
+        expert_kernel(len(stacks), groups, *refs)
+
+    return call(
+        body,
+        [jax.ShapeDtypeStruct(v.shape, bf16) for v in (*stacks, *pairs)],
+        [where, gain, *stacks, *pairs, *own, *other],
+        name,
+        [pltpu.VMEM((n, total), bf16), pltpu.VMEM((n, 2 * ff), bf16)]
         + [pltpu.VMEM((2, total, ff), bf16)] * 2
         + [pltpu.VMEM((2 * ff, total), bf16), pltpu.SemaphoreType.DMA((2, 3))],
-        limit=47,
+        limit=LIMIT,
         scalars=1,
         hbm=6,
     )
-    return out[0], out[1], out[2:]
 
 
 def first_sum_kernel(*refs):
@@ -280,21 +304,14 @@
         out[CAP:] = back[d * CAP : (d + 1) * CAP, :]
 
 
-def mix_kernel(where_ref, ids_ref, gates_ref, hid_ref, *refs):
+def mix_kernel(weight_ref, hid_ref, *refs):
     part_refs, out_ref, held = refs[:NZ], refs[NZ], refs[NZ + 1]
-    z, yh = where_ref[0], lax.div(where_ref[1], 2)
-    weight = []
-    for g, pick in enumerate(pick_table(z, yh, ids_ref)):
-        e = group_expert(z, yh, g)
-        gate = jnp.where(ids_ref[0:1, :] == e, gates_ref[0:1, :], 0.0)
-        gate = gate + jnp.where(ids_ref[1:2, :] == e, gates_ref[1:2, :], 0.0)
-        weight.append(jnp.where(pick, gate, 0.0))
     held[...] = jnp.zeros_like(held)
     for g in range(EXPERTS):
         part = part_refs[(0, 3, 1, 2).index(g // 2)][(g % 2) * CAP : (g % 2 + 1) * CAP, :]
         held[g * PAD : g * PAD + CAP, :] = part.astype(f32)
     mixture = lax.dot_general(
-        jnp.concatenate(weight, axis=0),
+        weight_ref[...],
         held[...],
         (((0,), (0,)), ((), ())),
         precision=lax.Precision.HIGHEST,
@@ -346,10 +363,16 @@
 
     near, past = jnp.stack((keys, values)), jnp.stack((cache_keys, cache_values))
     from_z = turned([jnp.where(z + s < NZ, near, past) for s in SHIFTS], "zh", KV_ORDER)
-    q_all, res, table = call(
+    slots = EXPERTS * PAD
+    q_all, res, table, weight = call(
         prep_kernel,
-        [shaped(heads * rows, HEAD_DIM), shaped(rows, width), shaped(EXPERTS * PAD, rows)],
-        [where, ids, queries, residual],
+        [
+            shaped(heads * rows, HEAD_DIM),
+            shaped(rows, width),
+            shaped(slots, rows),
+            jax.ShapeDtypeStruct((slots, rows), f32),
+        ],
+        [where, ids, gates, queries, residual],
         "prep",
         scalars=1,
     )
@@ -395,7 +418,8 @@
     b_pair = jnp.stack((b, b_far))
     *b_turned, a_far = together(turned([b_pair] * 3, "x", X_ORDER) + [swap_y(a_own)], (2, 1, 0, 3))
     gain = norm_gain.reshape(NX, 1, width)
-    a_own, a_far, b_all = experts(where, gain, a_own, a_far, [b_pair] + b_turned, own, other)
+    a_own = experts(where, gain, [a_own], [], own, other, "experts_own")[0]
+    a_far, *b_all = experts(where, gain, [a_far], [b_pair] + b_turned, own, other, "experts")
 
     *b_turned, a_far = lax.optimization_barrier(
         [turn(v, "x", s) for v, s in zip(b_all[1:], SHIFTS)] + [swap_y(a_far)]
@@ -418,10 +442,9 @@
     return call(
         mix_kernel,
         shaped(rows, width),
-        [where, ids, gates, hidden, *back],
+        [weight, hidden, *back],
         "mix",
         [pltpu.VMEM((EXPERTS * PAD, width), f32)],
-        scalars=1,
     )
 
 

time: 167 us -> 162 us (0.970)
  waiting for transfers between devices: 73.6 us -> 64.5 us
  Pallas kernels: 32.4 us -> 35.5 us
  starting transfers between devices: 55.3 us -> 57 us
    ppermute x24, waiting for transfers between devices: 65.2 us -> 57.4 us  [turn(): return lax.ppermute(v, axis, [(i, (i + shift) % n) for i in range(n)])]
    pallas_call x10 -> x11, Pallas kernels: 32.4 us -> 35.5 us  [call(): pl.pallas_call(body, out_shape=out_shape, in_specs=[SM] * scalars + [VM]...]
  transfers between devices with their start and end apart: 37 -> 37, of which waited for: 21 -> 22; matrix products, arithmetic and copies ran while one was open for 1% -> 1% of each run, Pallas kernels for 8% -> 13%
where the time goes in v3:
time: 162 us
  waiting for transfers between devices  64.5 us (40%)
  starting transfers between devices  57 us (35%)
  Pallas kernels  35.5 us (22%)
  local copies, waits for them, and re-layouts  3.24 us (2%)
  other arithmetic  1.77 us (1%)
    ppermute x24, waiting for transfers between devices, turn(): return lax.ppermute(v, axis, [(i, (i + shift) % n) for i in range(n)])  57.4 us
    ppermute x24, starting transfers between devices, turn(): return lax.ppermute(v, axis, [(i, (i + shift) % n) for i in range(n)])  50.3 us
    pallas_call x11, Pallas kernels, call(): pl.pallas_call(body, out_shape=out_shape, in_specs=[SM] * scalars + [VM]...  35.5 us
    ppermute x2, waiting for transfers between devices, cross(): return lax.ppermute(v, ('yh', 'yl'), [(i, NY - 1 - i) for i in range(NY)])  3.32 us
  transfers between devices with their start and end apart: 37, of which 22 were waited for; matrix products, arithmetic and copies ran while one was open for 1% of the time, Pallas kernels for 13%

profile of v3, /device:TPU:32, one launch (start us, length us, event | category | flops | bytes accessed | tf_op | source)
XLA Modules:
  0.0 162.3 jit_solution(2448382982965867810)
XLA Ops:
  0.0 1.5 broadcast_select_fusion
  1.5 3.3 %collective-permute-start.2 = (bf16[2,128,128]{2,1,0:T(8,128)(2,1)}, bf16[2,128,128]{2,1,0:T(8,128)(2,1)S(1)}, u32[]{:S(2)}, u32[]{:S(2)}) collective-permute-start(bf16[2,128,128]{2,1,0:T(8,128)(2,1)} %get-tuple-element.159), channel_id=1, source_target_pairs={{0,32},{32,64},{64,96},{96,0},{1,33},{33,65},{65,97},{97,1},{2,34}... | collective-permute-start | bytes 196616 | tf_op jit(solution)/shard_map/ppermute | solution.py:328
  4.8 2.1 %collective-permute-start = (bf16[2,128,128]{2,1,0:T(8,128)(2,1)}, bf16[2,128,128]{2,1,0:T(8,128)(2,1)S(1)}, u32[]{:S(2)}, u32[]{:S(2)}) collective-permute-start(bf16[2,128,128]{2,1,0:T(8,128)(2,1)} %get-tuple-element.160), channel_id=1, source_target_pairs={{0,96},{32,0},{64,32},{96,64},{1,97},{33,1},{65,33},{97,65},{2,98}... | collective-permute-start | bytes 196616 | tf_op jit(solution)/shard_map/ppermute | solution.py:328
  6.9 5.0 %collective-permute-start.1 = (bf16[2,128,128]{2,1,0:T(8,128)(2,1)S(1)}, bf16[2,128,128]{2,1,0:T(8,128)(2,1)S(1)}, u32[]{:S(2)}, u32[]{:S(2)}) collective-permute-start(bf16[2,128,128]{2,1,0:T(8,128)(2,1)S(1)} %get-tuple-element.161), channel_id=1, source_target_pairs={{0,64},{32,96},{64,0},{96,32},{1,65},{33,97},{65,1},{97,33},{2,66}... | collective-permute-start | bytes 196616 | tf_op jit(solution)/shard_map/ppermute | solution.py:328
  12.0 6.0 %collective-permute-done.1.refs_1_ = bf16[2,128,128]{2,1,0:T(8,128)(2,1)S(1)} collective-permute-done((bf16[2,128,128]{2,1,0:T(8,128)(2,1)S(1)}, bf16[2,128,128]{2,1,0:T(8,128)(2,1)S(1)}, u32[]{:S(2)}, u32[]{:S(2)}) %collective-permute-start.1) | collective-permute-done | bytes 65568 | tf_op jit(solution)/shard_map/ppermute | solution.py:328
  19.3 3.0 %collective-permute-start.6 = (bf16[2,512,128]{2,1,0:T(8,128)(2,1)S(1)}, bf16[2,512,128]{2,1,0:T(8,128)(2,1)S(1)}, u32[]{:S(2)}, u32[]{:S(2)}) collective-permute-start(bf16[2,512,128]{2,1,0:T(8,128)(2,1)S(1)} %get-tuple-element.95), channel_id=1, source_target_pairs={{0,24},{8,0},{16,8},{24,16},{1,25},{9,1},{17,9},{25,17},{2,26},{10... | collective-permute-start | bytes 786440 | tf_op jit(solution)/shard_map/ppermute | solution.py:328
  26.3 3.1 %attend_own.1 = (f32[768,128]{1,0:T(8,128)S(1)}, f32[768,128]{1,0:T(8,128)S(1)}, f32[768,128]{1,0:T(8,128)S(1)}) custom-call(bf16[768,128]{1,0:T(8,128)(2,1)S(1)} %get-tuple-element.83.q_all, bf16[2,128,128]{2,1,0:T(8,128)(2,1)S(1)} %get-tuple-element.162.tract.tract_ref, bf16[2,128,128]{2,1,0:T(8,128)(2,1)S(1)} %get-tuple-element.163.cache.cache_ref, ...), custom_call_target="tpu_custom_call" | custom-call | tf_op jit(solution)/shard_map/attend_own/pallas_call | solution.py:33
  29.4 2.1 %collective-permute-done.5.refs_0_ = bf16[2,512,128]{2,1,0:T(8,128)(2,1)S(1)} collective-permute-done((bf16[2,512,128]{2,1,0:T(8,128)(2,1)S(1)}, bf16[2,512,128]{2,1,0:T(8,128)(2,1)S(1)}, u32[]{:S(2)}, u32[]{:S(2)}) %collective-permute-start.5) | collective-permute-done | bytes 262176 | tf_op jit(solution)/shard_map/ppermute | solution.py:328
  33.5 5.7 %attend_more.1 = (f32[768,128]{1,0:T(8,128)S(1)}, f32[768,128]{1,0:T(8,128)S(1)}, f32[768,128]{1,0:T(8,128)S(1)}) custom-call(bf16[768,128]{1,0:T(8,128)(2,1)S(1)} %get-tuple-element.83.q_all, f32[768,128]{1,0:T(8,128)S(1)} %get-tuple-element.98.m_ref, f32[768,128]{1,0:T(8,128)S(1)} %get-tuple-element.99.l_ref, f32[768,128]{1,0:T(8,128)S(1)} %get-tuple-element.100.acc_ref, ...), custom_call_target="tpu_custom_call" | custom-call | tf_op jit(solution)/shard_map/attend_more/pallas_call | solution.py:33
  39.2 2.7 %collective-permute-done.10.refs_0_ = bf16[2,512,128]{2,1,0:T(8,128)(2,1)S(1)} collective-permute-done((bf16[2,512,128]{2,1,0:T(8,128)(2,1)S(1)}, bf16[2,512,128]{2,1,0:T(8,128)(2,1)S(1)}, u32[]{:S(2)}, u32[]{:S(2)}) %collective-permute-start.10) | collective-permute-done | bytes 262176 | tf_op jit(solution)/shard_map/ppermute | solution.py:328
  41.9 1.5 collective-permute-done.11.refs_1_
  43.6 3.1 %attend.1 = (bf16[128,768]{1,0:T(8,128)(2,1)S(1)}, bf16[72,768]{1,0:T(8,128)(2,1)S(1)}, bf16[72,768]{1,0:T(8,128)(2,1)S(1)}, bf16[72,768]{1,0:T(8,128)(2,1)S(1)}, bf16[72,768]{1,0:T(8,128)(2,1)S(1)}) custom-call(bf16[768,128]{1,0:T(8,128)(2,1)S(1)} %get-tuple-element.83.q_all, bf16[128,768]{1,0:T(8,128)(2,1)S(1)} %get-tuple-element.84.res_ref, ...), custom_call_target="tpu_custom_call" | custom-call | tf_op jit(solution)/shard_map/attend/pallas_call | solution.py:33
  47.0 4.1 %collective-permute-start.13 = (bf16[72,768]{1,0:T(8,128)(2,1)S(1)}, bf16[72,768]{1,0:T(8,128)(2,1)S(1)}, u32[]{:S(2)}, u32[]{:S(2)}) collective-permute-start(bf16[72,768]{1,0:T(8,128)(2,1)S(1)} %get-tuple-element.114), channel_id=1, source_target_pairs={{0,96},{32,0},{64,32},{96,64},{1,97},{33,1},{65,33},{97,65},{2,98}... | collective-permute-start | bytes 331784 | tf_op jit(solution)/shard_map/ppermute | solution.py:328
  51.1 3.2 %collective-permute-start.14 = (bf16[72,768]{1,0:T(8,128)(2,1)S(1)}, bf16[72,768]{1,0:T(8,128)(2,1)S(1)}, u32[]{:S(2)}, u32[]{:S(2)}) collective-permute-start(bf16[72,768]{1,0:T(8,128)(2,1)S(1)} %get-tuple-element.115), channel_id=1, source_target_pairs={{0,64},{32,96},{64,0},{96,32},{1,65},{33,97},{65,1},{97,33},{2,66}... | collective-permute-start | bytes 331784 | tf_op jit(solution)/shard_map/ppermute | solution.py:328
  54.7 3.1 %collective-permute-done.13.refs_2_ = bf16[72,768]{1,0:T(8,128)(2,1)S(1)} collective-permute-done((bf16[72,768]{1,0:T(8,128)(2,1)S(1)}, bf16[72,768]{1,0:T(8,128)(2,1)S(1)}, u32[]{:S(2)}, u32[]{:S(2)}) %collective-permute-start.13) | collective-permute-done | bytes 110624 | tf_op jit(solution)/shard_map/ppermute | solution.py:328
  57.7 4.6 %collective-permute-done.14.refs_3_ = bf16[72,768]{1,0:T(8,128)(2,1)S(1)} collective-permute-done((bf16[72,768]{1,0:T(8,128)(2,1)S(1)}, bf16[72,768]{1,0:T(8,128)(2,1)S(1)}, u32[]{:S(2)}, u32[]{:S(2)}) %collective-permute-start.14) | collective-permute-done | bytes 110624 | tf_op jit(solution)/shard_map/ppermute | solution.py:328
  62.4 1.3 collective-permute-start.19
  63.7 1.5 collective-permute-start.18
  65.2 1.7 %collective-permute-start.17 = (bf16[144,768]{1,0:T(8,128)(2,1)S(1)}, bf16[144,768]{1,0:T(8,128)(2,1)S(1)}, u32[]{:S(2)}, u32[]{:S(2)}) collective-permute-start(bf16[144,768]{1,0:T(8,128)(2,1)S(1)} %get-tuple-element.123), channel_id=1, source_target_pairs={{0,3},{1,0},{2,1},{3,2},{4,7},{5,4},{6,5},{7,6},{8,11},{9,8},{10,9... | collective-permute-start | bytes 663560 | tf_op jit(solution)/shard_map/ppermute | solution.py:328
  67.0 1.8 %collective-permute-start.16 = (bf16[144,768]{1,0:T(8,128)(2,1)S(1)}, bf16[144,768]{1,0:T(8,128)(2,1)S(1)}, u32[]{:S(2)}, u32[]{:S(2)}) collective-permute-start(bf16[144,768]{1,0:T(8,128)(2,1)S(1)} %get-tuple-element.123), channel_id=1, source_target_pairs={{0,2},{1,3},{2,0},{3,1},{4,6},{5,7},{6,4},{7,5},{8,10},{9,11},{10,... | collective-permute-start | bytes 663560 | tf_op jit(solution)/shard_map/ppermute | solution.py:328
  68.8 1.3 collective-permute-done.19
  70.1 2.3 %collective-permute-done.18 = bf16[144,768]{1,0:T(8,128)(2,1)S(1)} collective-permute-done((bf16[144,768]{1,0:T(8,128)(2,1)S(1)}, bf16[144,768]{1,0:T(8,128)(2,1)S(1)}, u32[]{:S(2)}, u32[]{:S(2)}) %collective-permute-start.18) | collective-permute-done | bytes 221216 | tf_op jit(solution)/shard_map/ppermute | solution.py:328
  72.4 2.7 %collective-permute-done.17 = bf16[144,768]{1,0:T(8,128)(2,1)S(1)} collective-permute-done((bf16[144,768]{1,0:T(8,128)(2,1)S(1)}, bf16[144,768]{1,0:T(8,128)(2,1)S(1)}, u32[]{:S(2)}, u32[]{:S(2)}) %collective-permute-start.17) | collective-permute-done | bytes 221216 | tf_op jit(solution)/shard_map/ppermute | solution.py:328
  75.1 1.6 %collective-permute-done.16 = bf16[144,768]{1,0:T(8,128)(2,1)S(1)} collective-permute-done((bf16[144,768]{1,0:T(8,128)(2,1)S(1)}, bf16[144,768]{1,0:T(8,128)(2,1)S(1)}, u32[]{:S(2)}, u32[]{:S(2)}) %collective-permute-start.16) | collective-permute-done | bytes 221216 | tf_op jit(solution)/shard_map/ppermute | solution.py:328
  77.0 1.2 collective-permute-start.23
  78.2 2.1 %collective-permute-start.22 = (bf16[2,144,768]{2,1,0:T(8,128)(2,1)S(1)}, bf16[2,144,768]{2,1,0:T(8,128)(2,1)S(1)}, u32[]{:S(2)}, u32[]{:S(2)}) collective-permute-start(bf16[2,144,768]{2,1,0:T(8,128)(2,1)S(1)} %pad_maximum_fusion.1.refs_3_), channel_id=1, source_target_pairs={{0,3},{1,0},{2,1},{3,2},{4,7},{5,4},{6,5},{7,6},{8,11},{9,8},{10,9... | collective-permute-start | bytes 1327112 | tf_op jit(solution)/shard_map/ppermute | solution.py:328
  80.3 1.1 collective-permute-start.21
  81.4 16.3 %collective-permute-done.23.refs_4_ = bf16[2,144,768]{2,1,0:T(8,128)(2,1)S(1)} collective-permute-done((bf16[2,144,768]{2,1,0:T(8,128)(2,1)S(1)}, bf16[2,144,768]{2,1,0:T(8,128)(2,1)S(1)}, u32[]{:S(2)}, u32[]{:S(2)}) %collective-permute-start.23) | collective-permute-done | bytes 442400 | tf_op jit(solution)/shard_map/ppermute | solution.py:328
  97.8 12.5 %experts.1 = (bf16[4,144,768]{2,1,0:T(8,128)(2,1)S(1)}, bf16[2,144,768]{2,1,0:T(8,128)(2,1)S(1)}, bf16[2,144,768]{2,1,0:T(8,128)(2,1)S(1)}, bf16[2,144,768]{2,1,0:T(8,128)(2,1)S(1)}, bf16[2,144,768]{2,1,0:T(8,128)(2,1)S(1)}) custom-call(s32[4]{0:T(128)S(1)} %pad_add_fusion.where_ref.refs_0_, f32[4,1,768]{2,1,0:T(1,128)S(1)} %bitcast.18, ...), custom_call_target="tpu_custom_call" | custom-call | tf_op jit(solution)/shard_map/experts/pallas_call | solution.py:33
  110.3 1.8 %collective-permute-start.28 = (bf16[4,144,768]{2,1,0:T(8,128)(2,1)S(1)}, bf16[4,144,768]{2,1,0:T(8,128)(2,1)S(1)}, u32[]{:S(2)}, u32[]{:S(2)}) collective-permute-start(bf16[4,144,768]{2,1,0:T(8,128)(2,1)S(1)} %get-tuple-element.139), channel_id=1, source_target_pairs={{0,8},{8,0},{1,9},{9,1},{2,10},{10,2},{3,11},{11,3},{4,12},{12,4},... | collective-permute-start | bytes 2654216 | tf_op jit(solution)/shard_map/ppermute | solution.py:346
  112.9 2.4 %collective-permute-start.26 = (bf16[2,144,768]{2,1,0:T(8,128)(2,1)S(1)}, bf16[2,144,768]{2,1,0:T(8,128)(2,1)S(1)}, u32[]{:S(2)}, u32[]{:S(2)}) collective-permute-start(bf16[2,144,768]{2,1,0:T(8,128)(2,1)S(1)} %get-tuple-element.137), channel_id=1, source_target_pairs={{0,3},{1,0},{2,1},{3,2},{4,7},{5,4},{6,5},{7,6},{8,11},{9,8},{10,9... | collective-permute-start | bytes 1327112 | tf_op jit(solution)/shard_map/ppermute | solution.py:328
  115.3 1.2 collective-permute-start.27
  116.5 7.5 %experts_own.1.refs_0_ = bf16[4,144,768]{2,1,0:T(8,128)(2,1)S(1)} custom-call(s32[4]{0:T(128)S(1)} %pad_add_fusion.where_ref.refs_0_, f32[4,1,768]{2,1,0:T(1,128)S(1)} %bitcast.19, bf16[4,144,768]{2,1,0:T(8,128)(2,1)S(1)} %pad_maximum_fusion.refs_2_, bf16[3072,512]{1,0:T(8,128)(2,1)S(1)} %copy-done, bf16[3072,512]{1,0:T(8,128)(2,1)} %refs_8_.1, ...), custom_call_target="tpu_custom_call" | custom-call | tf_op jit(solution)/shard_map/experts_own/pallas_call | solution.py:33
  124.0 1.7 %collective-permute-done.25.refs_3_ = bf16[2,144,768]{2,1,0:T(8,128)(2,1)S(1)} collective-permute-done((bf16[2,144,768]{2,1,0:T(8,128)(2,1)S(1)}, bf16[2,144,768]{2,1,0:T(8,128)(2,1)S(1)}, u32[]{:S(2)}, u32[]{:S(2)}) %collective-permute-start.25) | collective-permute-done | bytes 442400 | tf_op jit(solution)/shard_map/ppermute | solution.py:328
  125.7 3.2 %collective-permute-done.26.refs_4_ = bf16[2,144,768]{2,1,0:T(8,128)(2,1)S(1)} collective-permute-done((bf16[2,144,768]{2,1,0:T(8,128)(2,1)S(1)}, bf16[2,144,768]{2,1,0:T(8,128)(2,1)S(1)}, u32[]{:S(2)}, u32[]{:S(2)}) %collective-permute-start.26) | collective-permute-done | bytes 442400 | tf_op jit(solution)/shard_map/ppermute | solution.py:328
  128.9 2.2 %collective-permute-done.27.refs_5_ = bf16[2,144,768]{2,1,0:T(8,128)(2,1)S(1)} collective-permute-done((bf16[2,144,768]{2,1,0:T(8,128)(2,1)S(1)}, bf16[2,144,768]{2,1,0:T(8,128)(2,1)S(1)}, u32[]{:S(2)}, u32[]{:S(2)}) %collective-permute-start.27) | collective-permute-done | bytes 442400 | tf_op jit(solution)/shard_map/ppermute | solution.py:328
  132.7 2.7 %collective-permute-start.30 = (bf16[144,768]{1,0:T(8,128)(2,1)S(1)}, bf16[144,768]{1,0:T(8,128)(2,1)S(1)}, u32[]{:S(2)}, u32[]{:S(2)}) collective-permute-start(bf16[144,768]{1,0:T(8,128)(2,1)S(1)} %get-tuple-element.147), channel_id=1, source_target_pairs={{0,3},{1,0},{2,1},{3,2},{4,7},{5,4},{6,5},{7,6},{8,11},{9,8},{10,9... | collective-permute-start | bytes 663560 | tf_op jit(solution)/shard_map/ppermute | solution.py:328
  135.4 1.1 collective-permute-start.31
  136.5 1.0 collective-permute-done.32
  137.6 1.8 %collective-permute-start.33 = (bf16[144,768]{1,0:T(8,128)(2,1)S(1)}, bf16[144,768]{1,0:T(8,128)(2,1)S(1)}, u32[]{:S(2)}, u32[]{:S(2)}) collective-permute-start(bf16[144,768]{1,0:T(8,128)(2,1)S(1)} %add_convert_fusion), channel_id=1, source_target_pairs={{0,24},{8,16},{16,8},{24,0},{1,25},{9,17},{17,9},{25,1},{2,26},{10... | collective-permute-start | bytes 663560 | tf_op jit(solution)/shard_map/ppermute | solution.py:342
  139.5 1.8 %collective-permute-done.30.refs_2_ = bf16[144,768]{1,0:T(8,128)(2,1)S(1)} collective-permute-done((bf16[144,768]{1,0:T(8,128)(2,1)S(1)}, bf16[144,768]{1,0:T(8,128)(2,1)S(1)}, u32[]{:S(2)}, u32[]{:S(2)}) %collective-permute-start.30) | collective-permute-done | bytes 221216 | tf_op jit(solution)/shard_map/ppermute | solution.py:328
  141.2 1.6 collective-permute-done.31.refs_3_
  142.8 2.0 %collective-permute-done.33.refs_4_ = bf16[144,768]{1,0:T(8,128)(2,1)S(1)} collective-permute-done((bf16[144,768]{1,0:T(8,128)(2,1)S(1)}, bf16[144,768]{1,0:T(8,128)(2,1)S(1)}, u32[]{:S(2)}, u32[]{:S(2)}) %collective-permute-start.33) | collective-permute-done | bytes 221216 | tf_op jit(solution)/shard_map/ppermute | solution.py:342
  145.0 1.7 %collective-permute-start.34 = (bf16[72,768]{1,0:T(8,128)(2,1)S(1)}, bf16[72,768]{1,0:T(8,128)(2,1)S(1)}, u32[]{:S(2)}, u32[]{:S(2)}) collective-permute-start(bf16[72,768]{1,0:T(8,128)(2,1)S(1)} %get-tuple-element.156), channel_id=1, source_target_pairs={{0,32},{32,64},{64,96},{96,0},{1,33},{33,65},{65,97},{97,1},{2,34}... | collective-permute-start | bytes 331784 | tf_op jit(solution)/shard_map/ppermute | solution.py:328
  146.6 2.6 %collective-permute-start.35 = (bf16[72,768]{1,0:T(8,128)(2,1)S(1)}, bf16[72,768]{1,0:T(8,128)(2,1)S(1)}, u32[]{:S(2)}, u32[]{:S(2)}) collective-permute-start(bf16[72,768]{1,0:T(8,128)(2,1)S(1)} %get-tuple-element.157), channel_id=1, source_target_pairs={{0,96},{32,0},{64,32},{96,64},{1,97},{33,1},{65,33},{97,65},{2,98}... | collective-permute-start | bytes 331784 | tf_op jit(solution)/shard_map/ppermute | solution.py:328
  149.2 6.4 %collective-permute-start.36 = (bf16[72,768]{1,0:T(8,128)(2,1)S(1)}, bf16[72,768]{1,0:T(8,128)(2,1)S(1)}, u32[]{:S(2)}, u32[]{:S(2)}) collective-permute-start(bf16[72,768]{1,0:T(8,128)(2,1)S(1)} %get-tuple-element.158), channel_id=1, source_target_pairs={{0,64},{32,96},{64,0},{96,32},{1,65},{33,97},{65,1},{97,33},{2,66}... | collective-permute-start | bytes 331784 | tf_op jit(solution)/shard_map/ppermute | solution.py:328
  155.6 5.1 %collective-permute-done.36.refs_3_ = bf16[72,768]{1,0:T(8,128)(2,1)S(1)} collective-permute-done((bf16[72,768]{1,0:T(8,128)(2,1)S(1)}, bf16[72,768]{1,0:T(8,128)(2,1)S(1)}, u32[]{:S(2)}, u32[]{:S(2)}) %collective-permute-start.36) | collective-permute-done | bytes 110624 | tf_op jit(solution)/shard_map/ppermute | solution.py:328
  160.7 1.6 mix.1
  (62 shorter events, 11.0 us)
Async XLA Ops:
  0.0 18.7 %collective-permute-start.3 = (bf16[3072,512]{1,0:T(8,128)(2,1)}, bf16[3072,512]{1,0:T(8,128)(2,1)S(1)}, u32[]{:S(2)}, u32[]{:S(2)}) collective-permute-start(bf16[3072,512]{1,0:T(8,128)(2,1)} %refs_7_.1), channel_id=1, source_target_pairs={{0,4},{4,0},{1,5},{5,1},{2,6},{6,2},{3,7},{7,3},{8,12},{12,8},{9,1... | collective-permute-start | bytes 9437192 | tf_op jit(solution)/shard_map/ppermute | solution.py:350
  1.5 10.5 %collective-permute-start.2 = (bf16[2,128,128]{2,1,0:T(8,128)(2,1)}, bf16[2,128,128]{2,1,0:T(8,128)(2,1)S(1)}, u32[]{:S(2)}, u32[]{:S(2)}) collective-permute-start(bf16[2,128,128]{2,1,0:T(8,128)(2,1)} %get-tuple-element.159), channel_id=1, source_target_pairs={{0,32},{32,64},{64,96},{96,0},{1,33},{33,65},{65,97},{97,1},{2,34}... | collective-permute-start | bytes 196616 | tf_op jit(solution)/shard_map/ppermute | solution.py:328
  4.8 7.2 %collective-permute-start = (bf16[2,128,128]{2,1,0:T(8,128)(2,1)}, bf16[2,128,128]{2,1,0:T(8,128)(2,1)S(1)}, u32[]{:S(2)}, u32[]{:S(2)}) collective-permute-start(bf16[2,128,128]{2,1,0:T(8,128)(2,1)} %get-tuple-element.160), channel_id=1, source_target_pairs={{0,96},{32,0},{64,32},{96,64},{1,97},{33,1},{65,33},{97,65},{2,98}... | collective-permute-start | bytes 196616 | tf_op jit(solution)/shard_map/ppermute | solution.py:328
  6.9 11.1 %collective-permute-start.1 = (bf16[2,128,128]{2,1,0:T(8,128)(2,1)S(1)}, bf16[2,128,128]{2,1,0:T(8,128)(2,1)S(1)}, u32[]{:S(2)}, u32[]{:S(2)}) collective-permute-start(bf16[2,128,128]{2,1,0:T(8,128)(2,1)S(1)} %get-tuple-element.161), channel_id=1, source_target_pairs={{0,64},{32,96},{64,0},{96,32},{1,65},{33,97},{65,1},{97,33},{2,66}... | collective-permute-start | bytes 196616 | tf_op jit(solution)/shard_map/ppermute | solution.py:328
  18.7 3.6 %copy-start.7 = (bf16[3072,512]{1,0:T(8,128)(2,1)}, bf16[3072,512]{1,0:T(8,128)(2,1)S(1)}, u32[]{:S(2)}) copy-start(bf16[3072,512]{1,0:T(8,128)(2,1)S(1)} %collective-permute-done.3.refs_6_.refs_10_) | copy-start | bytes 9437188
  18.7 12.9 %collective-permute-start.7 = (bf16[3072,512]{1,0:T(8,128)(2,1)}, bf16[3072,512]{1,0:T(8,128)(2,1)S(1)}, u32[]{:S(2)}, u32[]{:S(2)}) collective-permute-start(bf16[3072,512]{1,0:T(8,128)(2,1)} %refs_8_.1), channel_id=1, source_target_pairs={{0,4},{4,0},{1,5},{5,1},{2,6},{6,2},{3,7},{7,3},{8,12},{12,8},{9,1... | collective-permute-start | bytes 9437192 | tf_op jit(solution)/shard_map/ppermute | solution.py:350
  18.8 7.5 %collective-permute-start.4 = (bf16[2,512,128]{2,1,0:T(8,128)(2,1)S(1)}, bf16[2,512,128]{2,1,0:T(8,128)(2,1)S(1)}, u32[]{:S(2)}, u32[]{:S(2)}) collective-permute-start(bf16[2,512,128]{2,1,0:T(8,128)(2,1)S(1)} %get-tuple-element.90.refs_0_), channel_id=1, source_target_pairs={{0,4},{4,0},{1,5},{5,1},{2,6},{6,2},{3,7},{7,3},{8,12},{12,8},{9,1... | collective-permute-start | bytes 786440 | tf_op jit(solution)/shard_map/ppermute | solution.py:350
  19.3 10.1 %collective-permute-start.6 = (bf16[2,512,128]{2,1,0:T(8,128)(2,1)S(1)}, bf16[2,512,128]{2,1,0:T(8,128)(2,1)S(1)}, u32[]{:S(2)}, u32[]{:S(2)}) collective-permute-start(bf16[2,512,128]{2,1,0:T(8,128)(2,1)S(1)} %get-tuple-element.95), channel_id=1, source_target_pairs={{0,24},{8,0},{16,8},{24,16},{1,25},{9,1},{17,9},{25,17},{2,26},{10... | collective-permute-start | bytes 786440 | tf_op jit(solution)/shard_map/ppermute | solution.py:328
  22.3 9.2 %collective-permute-start.5 = (bf16[2,512,128]{2,1,0:T(8,128)(2,1)S(1)}, bf16[2,512,128]{2,1,0:T(8,128)(2,1)S(1)}, u32[]{:S(2)}, u32[]{:S(2)}) collective-permute-start(bf16[2,512,128]{2,1,0:T(8,128)(2,1)S(1)} %get-tuple-element.94), channel_id=1, source_target_pairs={{0,8},{8,16},{16,24},{24,0},{1,9},{9,17},{17,25},{25,1},{2,10},{10... | collective-permute-start | bytes 786440 | tf_op jit(solution)/shard_map/ppermute | solution.py:328
  22.3 0.9 copy-start.1
  23.3 0.9 copy-start.2
  24.2 0.7 copy-start.4
  24.9 0.7 copy-start.5
  25.5 17.9 %copy-start.6 = (bf16[512,3072]{1,0:T(8,128)(2,1)S(1)}, bf16[512,3072]{1,0:T(8,128)(2,1)}, u32[]{:S(2)}) copy-start(bf16[512,3072]{1,0:T(8,128)(2,1)} %refs_9_.1) | copy-start | bytes 9437188
  31.6 1.9 %copy-start.8 = (bf16[3072,512]{1,0:T(8,128)(2,1)}, bf16[3072,512]{1,0:T(8,128)(2,1)S(1)}, u32[]{:S(2)}) copy-start(bf16[3072,512]{1,0:T(8,128)(2,1)S(1)} %collective-permute-done.7.refs_7_.refs_11_) | copy-start | bytes 9437188
  31.6 1.5 collective-permute-start.8
  31.6 1.9 %collective-permute-start.9 = (bf16[2,512,128]{2,1,0:T(8,128)(2,1)S(1)}, bf16[2,512,128]{2,1,0:T(8,128)(2,1)S(1)}, u32[]{:S(2)}, u32[]{:S(2)}) collective-permute-start(bf16[2,512,128]{2,1,0:T(8,128)(2,1)S(1)} %collective-permute-done.6.refs_1_), channel_id=1, source_target_pairs={{0,4},{4,0},{1,5},{5,1},{2,6},{6,2},{3,7},{7,3},{8,12},{12,8},{9,1... | collective-permute-start | bytes 786440 | tf_op jit(solution)/shard_map/ppermute | solution.py:350
  32.1 9.8 %collective-permute-start.10 = (bf16[2,512,128]{2,1,0:T(8,128)(2,1)S(1)}, bf16[2,512,128]{2,1,0:T(8,128)(2,1)S(1)}, u32[]{:S(2)}, u32[]{:S(2)}) collective-permute-start(bf16[2,512,128]{2,1,0:T(8,128)(2,1)S(1)} %get-tuple-element.106), channel_id=1, source_target_pairs={{0,16},{8,24},{16,0},{24,8},{1,17},{9,25},{17,1},{25,9},{2,18},{10... | collective-permute-start | bytes 786440 | tf_op jit(solution)/shard_map/ppermute | solution.py:328
  39.1 58.6 %copy-start.3 = (f32[3072]{0:T(1024)S(1)}, f32[3072]{0:T(1024)}, u32[]{:S(2)}) copy-start(f32[3072]{0:T(1024)} %param.18) | copy-start | bytes 36868
  41.9 1.5 collective-permute-start.11
  43.4 18.9 %collective-permute-start.15 = (bf16[512,3072]{1,0:T(8,128)(2,1)S(1)}, bf16[512,3072]{1,0:T(8,128)(2,1)S(1)}, u32[]{:S(2)}, u32[]{:S(2)}) collective-permute-start(bf16[512,3072]{1,0:T(8,128)(2,1)S(1)} %copy-done.6), channel_id=1, source_target_pairs={{0,4},{4,0},{1,5},{5,1},{2,6},{6,2},{3,7},{7,3},{8,12},{12,8},{9,1... | collective-permute-start | bytes 9437192 | tf_op jit(solution)/shard_map/ppermute | solution.py:350
  46.7 7.9 %collective-permute-start.12 = (bf16[72,768]{1,0:T(8,128)(2,1)S(1)}, bf16[72,768]{1,0:T(8,128)(2,1)S(1)}, u32[]{:S(2)}, u32[]{:S(2)}) collective-permute-start(bf16[72,768]{1,0:T(8,128)(2,1)S(1)} %get-tuple-element.113), channel_id=1, source_target_pairs={{0,32},{32,64},{64,96},{96,0},{1,33},{33,65},{65,97},{97,1},{2,34}... | collective-permute-start | bytes 331784 | tf_op jit(solution)/shard_map/ppermute | solution.py:328
  47.0 10.7 %collective-permute-start.13 = (bf16[72,768]{1,0:T(8,128)(2,1)S(1)}, bf16[72,768]{1,0:T(8,128)(2,1)S(1)}, u32[]{:S(2)}, u32[]{:S(2)}) collective-permute-start(bf16[72,768]{1,0:T(8,128)(2,1)S(1)} %get-tuple-element.114), channel_id=1, source_target_pairs={{0,96},{32,0},{64,32},{96,64},{1,97},{33,1},{65,33},{97,65},{2,98}... | collective-permute-start | bytes 331784 | tf_op jit(solution)/shard_map/ppermute | solution.py:328
  51.1 11.2 %collective-permute-start.14 = (bf16[72,768]{1,0:T(8,128)(2,1)S(1)}, bf16[72,768]{1,0:T(8,128)(2,1)S(1)}, u32[]{:S(2)}, u32[]{:S(2)}) collective-permute-start(bf16[72,768]{1,0:T(8,128)(2,1)S(1)} %get-tuple-element.115), channel_id=1, source_target_pairs={{0,64},{32,96},{64,0},{96,32},{1,65},{33,97},{65,1},{97,33},{2,66}... | collective-permute-start | bytes 331784 | tf_op jit(solution)/shard_map/ppermute | solution.py:328
  62.3 35.4 %copy-start.9 = (bf16[512,3072]{1,0:T(8,128)(2,1)}, bf16[512,3072]{1,0:T(8,128)(2,1)S(1)}, u32[]{:S(2)}) copy-start(bf16[512,3072]{1,0:T(8,128)(2,1)S(1)} %collective-permute-done.15.refs_8_.refs_12_) | copy-start | bytes 9437188
  62.4 7.7 %collective-permute-start.19 = (bf16[144,768]{1,0:T(8,128)(2,1)S(1)}, bf16[144,768]{1,0:T(8,128)(2,1)S(1)}, u32[]{:S(2)}, u32[]{:S(2)}) collective-permute-start(bf16[144,768]{1,0:T(8,128)(2,1)S(1)} %get-tuple-element.124), channel_id=1, source_target_pairs={{0,24},{8,16},{16,8},{24,0},{1,25},{9,17},{17,9},{25,1},{2,26},{10... | collective-permute-start | bytes 663560 | tf_op jit(solution)/shard_map/ppermute | solution.py:342
  63.7 8.7 %collective-permute-start.18 = (bf16[144,768]{1,0:T(8,128)(2,1)S(1)}, bf16[144,768]{1,0:T(8,128)(2,1)S(1)}, u32[]{:S(2)}, u32[]{:S(2)}) collective-permute-start(bf16[144,768]{1,0:T(8,128)(2,1)S(1)} %get-tuple-element.123), channel_id=1, source_target_pairs={{0,1},{1,2},{2,3},{3,0},{4,5},{5,6},{6,7},{7,4},{8,9},{9,10},{10,1... | collective-permute-start | bytes 663560 | tf_op jit(solution)/shard_map/ppermute | solution.py:328
  65.2 9.9 %collective-permute-start.17 = (bf16[144,768]{1,0:T(8,128)(2,1)S(1)}, bf16[144,768]{1,0:T(8,128)(2,1)S(1)}, u32[]{:S(2)}, u32[]{:S(2)}) collective-permute-start(bf16[144,768]{1,0:T(8,128)(2,1)S(1)} %get-tuple-element.123), channel_id=1, source_target_pairs={{0,3},{1,0},{2,1},{3,2},{4,7},{5,4},{6,5},{7,6},{8,11},{9,8},{10,9... | collective-permute-start | bytes 663560 | tf_op jit(solution)/shard_map/ppermute | solution.py:328
  67.0 9.8 %collective-permute-start.16 = (bf16[144,768]{1,0:T(8,128)(2,1)S(1)}, bf16[144,768]{1,0:T(8,128)(2,1)S(1)}, u32[]{:S(2)}, u32[]{:S(2)}) collective-permute-start(bf16[144,768]{1,0:T(8,128)(2,1)S(1)} %get-tuple-element.123), channel_id=1, source_target_pairs={{0,2},{1,3},{2,0},{3,1},{4,6},{5,7},{6,4},{7,5},{8,10},{9,11},{10,... | collective-permute-start | bytes 663560 | tf_op jit(solution)/shard_map/ppermute | solution.py:328
  70.1 6.7 %collective-permute-start.20 = (bf16[144,768]{1,0:T(8,128)(2,1)S(1)}, bf16[144,768]{1,0:T(8,128)(2,1)S(1)}, u32[]{:S(2)}, u32[]{:S(2)}) collective-permute-start(bf16[144,768]{1,0:T(8,128)(2,1)S(1)} %collective-permute-done.19), channel_id=1, source_target_pairs={{0,8},{8,0},{1,9},{9,1},{2,10},{10,2},{3,11},{11,3},{4,12},{12,4},... | collective-permute-start | bytes 663560 | tf_op jit(solution)/shard_map/ppermute | solution.py:346
  76.9 20.9 %collective-permute-start.24 = (bf16[4,144,768]{2,1,0:T(8,128)(2,1)S(1)}, bf16[4,144,768]{2,1,0:T(8,128)(2,1)S(1)}, u32[]{:S(2)}, u32[]{:S(2)}) collective-permute-start(bf16[4,144,768]{2,1,0:T(8,128)(2,1)S(1)} %pad_maximum_fusion.refs_2_), channel_id=1, source_target_pairs={{0,8},{8,0},{1,9},{9,1},{2,10},{10,2},{3,11},{11,3},{4,12},{12,4},... | collective-permute-start | bytes 2654216 | tf_op jit(solution)/shard_map/ppermute | solution.py:346
  77.0 20.7 %collective-permute-start.23 = (bf16[2,144,768]{2,1,0:T(8,128)(2,1)S(1)}, bf16[2,144,768]{2,1,0:T(8,128)(2,1)S(1)}, u32[]{:S(2)}, u32[]{:S(2)}) collective-permute-start(bf16[2,144,768]{2,1,0:T(8,128)(2,1)S(1)} %pad_maximum_fusion.1.refs_3_), channel_id=1, source_target_pairs={{0,1},{1,2},{2,3},{3,0},{4,5},{5,6},{6,7},{7,4},{8,9},{9,10},{10,1... | collective-permute-start | bytes 1327112 | tf_op jit(solution)/shard_map/ppermute | solution.py:328
  78.2 19.5 %collective-permute-start.22 = (bf16[2,144,768]{2,1,0:T(8,128)(2,1)S(1)}, bf16[2,144,768]{2,1,0:T(8,128)(2,1)S(1)}, u32[]{:S(2)}, u32[]{:S(2)}) collective-permute-start(bf16[2,144,768]{2,1,0:T(8,128)(2,1)S(1)} %pad_maximum_fusion.1.refs_3_), channel_id=1, source_target_pairs={{0,3},{1,0},{2,1},{3,2},{4,7},{5,4},{6,5},{7,6},{8,11},{9,8},{10,9... | collective-permute-start | bytes 1327112 | tf_op jit(solution)/shard_map/ppermute | solution.py:328
  80.3 17.4 %collective-permute-start.21 = (bf16[2,144,768]{2,1,0:T(8,128)(2,1)S(1)}, bf16[2,144,768]{2,1,0:T(8,128)(2,1)S(1)}, u32[]{:S(2)}, u32[]{:S(2)}) collective-permute-start(bf16[2,144,768]{2,1,0:T(8,128)(2,1)S(1)} %pad_maximum_fusion.1.refs_3_), channel_id=1, source_target_pairs={{0,2},{1,3},{2,0},{3,1},{4,6},{5,7},{6,4},{7,5},{8,10},{9,11},{10,... | collective-permute-start | bytes 1327112 | tf_op jit(solution)/shard_map/ppermute | solution.py:328
  97.7 18.7 %copy-start = (bf16[3072,512]{1,0:T(8,128)(2,1)S(1)}, bf16[3072,512]{1,0:T(8,128)(2,1)}, u32[]{:S(2)}) copy-start(bf16[3072,512]{1,0:T(8,128)(2,1)} %refs_7_.1) | copy-start | bytes 9437188
  110.3 20.8 %collective-permute-start.28 = (bf16[4,144,768]{2,1,0:T(8,128)(2,1)S(1)}, bf16[4,144,768]{2,1,0:T(8,128)(2,1)S(1)}, u32[]{:S(2)}, u32[]{:S(2)}) collective-permute-start(bf16[4,144,768]{2,1,0:T(8,128)(2,1)S(1)} %get-tuple-element.139), channel_id=1, source_target_pairs={{0,8},{8,0},{1,9},{9,1},{2,10},{10,2},{3,11},{11,3},{4,12},{12,4},... | collective-permute-start | bytes 2654216 | tf_op jit(solution)/shard_map/ppermute | solution.py:346
  112.1 13.6 %collective-permute-start.25 = (bf16[2,144,768]{2,1,0:T(8,128)(2,1)S(1)}, bf16[2,144,768]{2,1,0:T(8,128)(2,1)S(1)}, u32[]{:S(2)}, u32[]{:S(2)}) collective-permute-start(bf16[2,144,768]{2,1,0:T(8,128)(2,1)S(1)} %get-tuple-element.136), channel_id=1, source_target_pairs={{0,1},{1,2},{2,3},{3,0},{4,5},{5,6},{6,7},{7,4},{8,9},{9,10},{10,1... | collective-permute-start | bytes 1327112 | tf_op jit(solution)/shard_map/ppermute | solution.py:328
  112.9 15.9 %collective-permute-start.26 = (bf16[2,144,768]{2,1,0:T(8,128)(2,1)S(1)}, bf16[2,144,768]{2,1,0:T(8,128)(2,1)S(1)}, u32[]{:S(2)}, u32[]{:S(2)}) collective-permute-start(bf16[2,144,768]{2,1,0:T(8,128)(2,1)S(1)} %get-tuple-element.137), channel_id=1, source_target_pairs={{0,3},{1,0},{2,1},{3,2},{4,7},{5,4},{6,5},{7,6},{8,11},{9,8},{10,9... | collective-permute-start | bytes 1327112 | tf_op jit(solution)/shard_map/ppermute | solution.py:328
  115.3 15.8 %collective-permute-start.27 = (bf16[2,144,768]{2,1,0:T(8,128)(2,1)S(1)}, bf16[2,144,768]{2,1,0:T(8,128)(2,1)S(1)}, u32[]{:S(2)}, u32[]{:S(2)}) collective-permute-start(bf16[2,144,768]{2,1,0:T(8,128)(2,1)S(1)} %get-tuple-element.138), channel_id=1, source_target_pairs={{0,2},{1,3},{2,0},{3,1},{4,6},{5,7},{6,4},{7,5},{8,10},{9,11},{10,... | collective-permute-start | bytes 1327112 | tf_op jit(solution)/shard_map/ppermute | solution.py:328
  131.5 6.0 %collective-permute-start.32 = (bf16[144,768]{1,0:T(8,128)(2,1)S(1)}, bf16[144,768]{1,0:T(8,128)(2,1)S(1)}, u32[]{:S(2)}, u32[]{:S(2)}) collective-permute-start(bf16[144,768]{1,0:T(8,128)(2,1)S(1)} %get-tuple-element.150), channel_id=1, source_target_pairs={{0,8},{8,0},{1,9},{9,1},{2,10},{10,2},{3,11},{11,3},{4,12},{12,4},... | collective-permute-start | bytes 663560 | tf_op jit(solution)/shard_map/ppermute | solution.py:346
  131.9 7.6 %collective-permute-start.29 = (bf16[144,768]{1,0:T(8,128)(2,1)S(1)}, bf16[144,768]{1,0:T(8,128)(2,1)S(1)}, u32[]{:S(2)}, u32[]{:S(2)}) collective-permute-start(bf16[144,768]{1,0:T(8,128)(2,1)S(1)} %get-tuple-element.146), channel_id=1, source_target_pairs={{0,1},{1,2},{2,3},{3,0},{4,5},{5,6},{6,7},{7,4},{8,9},{9,10},{10,1... | collective-permute-start | bytes 663560 | tf_op jit(solution)/shard_map/ppermute | solution.py:328
  132.7 8.5 %collective-permute-start.30 = (bf16[144,768]{1,0:T(8,128)(2,1)S(1)}, bf16[144,768]{1,0:T(8,128)(2,1)S(1)}, u32[]{:S(2)}, u32[]{:S(2)}) collective-permute-start(bf16[144,768]{1,0:T(8,128)(2,1)S(1)} %get-tuple-element.147), channel_id=1, source_target_pairs={{0,3},{1,0},{2,1},{3,2},{4,7},{5,4},{6,5},{7,6},{8,11},{9,8},{10,9... | collective-permute-start | bytes 663560 | tf_op jit(solution)/shard_map/ppermute | solution.py:328
  135.4 7.4 %collective-permute-start.31 = (bf16[144,768]{1,0:T(8,128)(2,1)S(1)}, bf16[144,768]{1,0:T(8,128)(2,1)S(1)}, u32[]{:S(2)}, u32[]{:S(2)}) collective-permute-start(bf16[144,768]{1,0:T(8,128)(2,1)S(1)} %get-tuple-element.148), channel_id=1, source_target_pairs={{0,2},{1,3},{2,0},{3,1},{4,6},{5,7},{6,4},{7,5},{8,10},{9,11},{10,... | collective-permute-start | bytes 663560 | tf_op jit(solution)/shard_map/ppermute | solution.py:328
  137.6 7.2 %collective-permute-start.33 = (bf16[144,768]{1,0:T(8,128)(2,1)S(1)}, bf16[144,768]{1,0:T(8,128)(2,1)S(1)}, u32[]{:S(2)}, u32[]{:S(2)}) collective-permute-start(bf16[144,768]{1,0:T(8,128)(2,1)S(1)} %add_convert_fusion), channel_id=1, source_target_pairs={{0,24},{8,16},{16,8},{24,0},{1,25},{9,17},{17,9},{25,1},{2,26},{10... | collective-permute-start | bytes 663560 | tf_op jit(solution)/shard_map/ppermute | solution.py:342
  145.0 10.6 %collective-permute-start.34 = (bf16[72,768]{1,0:T(8,128)(2,1)S(1)}, bf16[72,768]{1,0:T(8,128)(2,1)S(1)}, u32[]{:S(2)}, u32[]{:S(2)}) collective-permute-start(bf16[72,768]{1,0:T(8,128)(2,1)S(1)} %get-tuple-element.156), channel_id=1, source_target_pairs={{0,32},{32,64},{64,96},{96,0},{1,33},{33,65},{65,97},{97,1},{2,34}... | collective-permute-start | bytes 331784 | tf_op jit(solution)/shard_map/ppermute | solution.py:328
  146.6 9.0 %collective-permute-start.35 = (bf16[72,768]{1,0:T(8,128)(2,1)S(1)}, bf16[72,768]{1,0:T(8,128)(2,1)S(1)}, u32[]{:S(2)}, u32[]{:S(2)}) collective-permute-start(bf16[72,768]{1,0:T(8,128)(2,1)S(1)} %get-tuple-element.157), channel_id=1, source_target_pairs={{0,96},{32,0},{64,32},{96,64},{1,97},{33,1},{65,33},{97,65},{2,98}... | collective-permute-start | bytes 331784 | tf_op jit(solution)/shard_map/ppermute | solution.py:328
  149.2 11.5 %collective-permute-start.36 = (bf16[72,768]{1,0:T(8,128)(2,1)S(1)}, bf16[72,768]{1,0:T(8,128)(2,1)S(1)}, u32[]{:S(2)}, u32[]{:S(2)}) collective-permute-start(bf16[72,768]{1,0:T(8,128)(2,1)S(1)} %get-tuple-element.158), channel_id=1, source_target_pairs={{0,64},{32,96},{64,0},{96,32},{1,65},{33,97},{65,1},{97,33},{2,66}... | collective-permute-start | bytes 331784 | tf_op jit(solution)/shard_map/ppermute | solution.py:328

commit v4 on v3

--- a/solution.py
+++ b/solution.py
@@ -19,7 +19,7 @@
 SHIFTS = (1, 3, 2)
 KV_ORDER, Z_ORDER, X_ORDER = (0, 1, 2), (0, 1, 2), (2, 1, 0)
 MB = 1024 * 1024
-LIMIT = 47
+LIMIT = 20
 
 bf16 = jnp.bfloat16
 f32 = jnp.float32
@@ -187,25 +187,12 @@
 def expert_kernel(stacks, pairs, where_ref, gain_ref, *refs):
     refs = list(refs)
     take = lambda n: [refs.pop(0) for _ in range(n)]
-    stack_in, pair_in = take(stacks), take(NX * pairs)
-    weights = take(6)
+    stack_in, pair_in, weights = take(stacks), take(NX * pairs), take(6)
     stack_out, pair_out = take(stacks), take(NX * pairs)
-    normed, act, gate_v, up_v, down_v, sems = refs
+    normed, act = refs
     total, ff = weights[0].shape
     width = total // NX
     rows = normed.shape[0] // (stacks + 2 * pairs)
-    gate_loads, up_loads, down_loads = [
-        [pltpu.make_async_copy(weights[3 * h + j], place(h), sems.at[h, j]) for h in range(2)]
-        for j, place in enumerate(
-            (
-                lambda h: gate_v.at[h],
-                lambda h: up_v.at[h],
-                lambda h: down_v.at[pl.ds(h * ff, ff)],
-            )
-        )
-    ]
-    for c in (gate_loads[0], up_loads[0], gate_loads[1], up_loads[1], *down_loads):
-        c.start()
     x = where_ref[3]
     order = (0,) + SHIFTS
 
@@ -236,31 +223,41 @@
         for shift, ref in zip(order, pair_in):
             place(stacks + r, shift, ref[r], inverse)
 
-    def hidden_units(half, carry):
-        for j, v in enumerate((gate_v, up_v)):
-            pltpu.make_async_copy(v.at[half], v.at[half], sems.at[half, j]).wait()
-        gate = jnp.dot(normed[...], gate_v[half], preferred_element_type=f32)
-        up = jnp.dot(normed[...], up_v[half], preferred_element_type=f32)
-        low = (gate / (1.0 + jnp.exp(-gate)) * up).astype(bf16)
-        act[:, pl.ds(pl.multiple_of(half * ff, ff), ff)] = low
-        return carry
-
-    lax.fori_loop(0, 2, hidden_units, 0)
-    for c in down_loads:
-        c.wait()
+    tile = 256
+    for half in range(2):
+        w_gate, w_up, _ = weights[3 * half : 3 * half + 3]
+
+        def units(j, carry):
+            cols = pl.ds(pl.multiple_of(j * tile, tile), tile)
+            gate = jnp.dot(normed[...], w_gate[:, cols], preferred_element_type=f32)
+            up = jnp.dot(normed[...], w_up[:, cols], preferred_element_type=f32)
+            at = pl.ds(pl.multiple_of(half * ff + j * tile, tile), tile)
+            act[:, at] = (gate / (1.0 + jnp.exp(-gate)) * up).astype(bf16)
+            return carry
+
+        lax.fori_loop(0, ff // tile, units, 0)
     for i, shift in enumerate(order):
-        cols = pl.ds(pl.multiple_of(lax.rem(x + shift, NX) * width, width), width)
-        out = jnp.dot(act[...], down_v[:, cols], preferred_element_type=f32).astype(bf16)
-        for r, ref in enumerate(stack_out):
-            ref[i] = out[r * rows : (r + 1) * rows]
-        for r in range(2 * pairs):
-            at = (stacks + r) * rows
-            pair_out[i][r] = out[at : at + rows]
-
-
-def experts(where, gain, stacks, pairs, own, other, name):
+        start = lax.rem(x + shift, NX) * width
+
+        def down(j, carry):
+            cols = pl.ds(pl.multiple_of(start + j * tile, tile), tile)
+            out = jnp.dot(act[:, :ff], weights[2][:, cols], preferred_element_type=f32)
+            out += jnp.dot(act[:, ff:], weights[5][:, cols], preferred_element_type=f32)
+            out = out.astype(bf16)
+            at = pl.ds(pl.multiple_of(j * tile, tile), tile)
+            for r, ref in enumerate(stack_out):
+                ref[i, :, at] = out[r * rows : (r + 1) * rows]
+            for r in range(2 * pairs):
+                first = (stacks + r) * rows
+                pair_out[i][r, :, at] = out[first : first + rows]
+            return carry
+
+        lax.fori_loop(0, width // tile, down, 0)
+
+
+def experts(where, gain, stacks, pairs, weights, name):
     rows, width = stacks[0].shape[1:]
-    total, ff = own[0].shape
+    total, ff = weights[0].shape
     groups = 1 if pairs else 0
     n = rows * (len(stacks) + 2 * groups)
 
@@ -270,14 +267,11 @@
     return call(
         body,
         [jax.ShapeDtypeStruct(v.shape, bf16) for v in (*stacks, *pairs)],
-        [where, gain, *stacks, *pairs, *own, *other],
+        [where, gain, *stacks, *pairs, *weights],
         name,
-        [pltpu.VMEM((n, total), bf16), pltpu.VMEM((n, 2 * ff), bf16)]
-        + [pltpu.VMEM((2, total, ff), bf16)] * 2
-        + [pltpu.VMEM((2 * ff, total), bf16), pltpu.SemaphoreType.DMA((2, 3))],
+        [pltpu.VMEM((n, total), bf16), pltpu.VMEM((n, 2 * ff), bf16)],
         limit=LIMIT,
         scalars=1,
-        hbm=6,
     )
 
 
@@ -418,8 +412,9 @@
     b_pair = jnp.stack((b, b_far))
     *b_turned, a_far = together(turned([b_pair] * 3, "x", X_ORDER) + [swap_y(a_own)], (2, 1, 0, 3))
     gain = norm_gain.reshape(NX, 1, width)
-    a_own = experts(where, gain, [a_own], [], own, other, "experts_own")[0]
-    a_far, *b_all = experts(where, gain, [a_far], [b_pair] + b_turned, own, other, "experts")
+    weights = (*own, *other)
+    a_own = experts(where, gain, [a_own], [], weights, "experts_own")[0]
+    a_far, *b_all = experts(where, gain, [a_far], [b_pair] + b_turned, weights, "experts")
 
     *b_turned, a_far = lax.optimization_barrier(
         [turn(v, "x", s) for v, s in zip(b_all[1:], SHIFTS)] + [swap_y(a_far)]

time: 162 us -> 165 us (1.019)
  Pallas kernels: 35.5 us -> 38.6 us
  waiting for transfers between devices: 64.5 us -> 62.8 us
    pallas_call x11, Pallas kernels: 35.5 us -> 38.6 us  [call(): pl.pallas_call(body, out_shape=out_shape, in_specs=[SM] * scalars + [VM]...]
  transfers between devices with their start and end apart: 37 -> 37, of which waited for: 22 -> 21; matrix products, arithmetic and copies ran while one was open for 1% -> 1% of each run, Pallas kernels for 13% -> 13%
where the time goes in v4:
time: 165 us
  waiting for transfers between devices  62.8 us (38%)
  starting transfers between devices  58.1 us (35%)
  Pallas kernels  38.6 us (23%)
  local copies, waits for them, and re-layouts  3.23 us (2%)
  other arithmetic  1.92 us (1%)
    ppermute x24, waiting for transfers between devices, turn(): return lax.ppermute(v, axis, [(i, (i + shift) % n) for i in range(n)])  56.3 us
    ppermute x24, starting transfers between devices, turn(): return lax.ppermute(v, axis, [(i, (i + shift) % n) for i in range(n)])  51.3 us
    pallas_call x11, Pallas kernels, call(): pl.pallas_call(body, out_shape=out_shape, in_specs=[SM] * scalars + [VM]...  38.6 us
    ppermute x2, starting transfers between devices, cross(): return lax.ppermute(v, ('yh', 'yl'), [(i, NY - 1 - i) for i in range(NY)])  3.39 us
  transfers between devices with their start and end apart: 37, of which 21 were waited for; matrix products, arithmetic and copies ran while one was open for 1% of the time, Pallas kernels for 13%

profile of v4, /device:TPU:32, one launch (start us, length us, event | category | flops | bytes accessed | tf_op | source)
XLA Modules:
  0.0 164.8 jit_solution(10652795939173290877)
XLA Ops:
  0.0 1.6 broadcast_select_fusion
  1.6 3.3 %collective-permute-start.2 = (bf16[2,128,128]{2,1,0:T(8,128)(2,1)}, bf16[2,128,128]{2,1,0:T(8,128)(2,1)S(1)}, u32[]{:S(2)}, u32[]{:S(2)}) collective-permute-start(bf16[2,128,128]{2,1,0:T(8,128)(2,1)} %get-tuple-element.159), channel_id=1, source_target_pairs={{0,32},{32,64},{64,96},{96,0},{1,33},{33,65},{65,97},{97,1},{2,34}... | collective-permute-start | bytes 196616 | tf_op jit(solution)/shard_map/ppermute | solution.py:322
  4.9 2.1 %collective-permute-start = (bf16[2,128,128]{2,1,0:T(8,128)(2,1)}, bf16[2,128,128]{2,1,0:T(8,128)(2,1)S(1)}, u32[]{:S(2)}, u32[]{:S(2)}) collective-permute-start(bf16[2,128,128]{2,1,0:T(8,128)(2,1)} %get-tuple-element.160), channel_id=1, source_target_pairs={{0,96},{32,0},{64,32},{96,64},{1,97},{33,1},{65,33},{97,65},{2,98}... | collective-permute-start | bytes 196616 | tf_op jit(solution)/shard_map/ppermute | solution.py:322
  7.0 5.0 %collective-permute-start.1 = (bf16[2,128,128]{2,1,0:T(8,128)(2,1)S(1)}, bf16[2,128,128]{2,1,0:T(8,128)(2,1)S(1)}, u32[]{:S(2)}, u32[]{:S(2)}) collective-permute-start(bf16[2,128,128]{2,1,0:T(8,128)(2,1)S(1)} %get-tuple-element.161), channel_id=1, source_target_pairs={{0,64},{32,96},{64,0},{96,32},{1,65},{33,97},{65,1},{97,33},{2,66}... | collective-permute-start | bytes 196616 | tf_op jit(solution)/shard_map/ppermute | solution.py:322
  12.2 6.1 %collective-permute-done.1.refs_1_ = bf16[2,128,128]{2,1,0:T(8,128)(2,1)S(1)} collective-permute-done((bf16[2,128,128]{2,1,0:T(8,128)(2,1)S(1)}, bf16[2,128,128]{2,1,0:T(8,128)(2,1)S(1)}, u32[]{:S(2)}, u32[]{:S(2)}) %collective-permute-start.1) | collective-permute-done | bytes 65568 | tf_op jit(solution)/shard_map/ppermute | solution.py:322
  19.6 3.0 %collective-permute-start.6 = (bf16[2,512,128]{2,1,0:T(8,128)(2,1)S(1)}, bf16[2,512,128]{2,1,0:T(8,128)(2,1)S(1)}, u32[]{:S(2)}, u32[]{:S(2)}) collective-permute-start(bf16[2,512,128]{2,1,0:T(8,128)(2,1)S(1)} %get-tuple-element.95), channel_id=1, source_target_pairs={{0,24},{8,0},{16,8},{24,16},{1,25},{9,1},{17,9},{25,17},{2,26},{10... | collective-permute-start | bytes 786440 | tf_op jit(solution)/shard_map/ppermute | solution.py:322
  22.6 0.9 copy-done.3
  23.5 0.9 copy-done.4
  26.6 3.1 %attend_own.1 = (f32[768,128]{1,0:T(8,128)S(1)}, f32[768,128]{1,0:T(8,128)S(1)}, f32[768,128]{1,0:T(8,128)S(1)}) custom-call(bf16[768,128]{1,0:T(8,128)(2,1)S(1)} %get-tuple-element.83.q_all, bf16[2,128,128]{2,1,0:T(8,128)(2,1)S(1)} %get-tuple-element.162.tract.tract_ref, bf16[2,128,128]{2,1,0:T(8,128)(2,1)S(1)} %get-tuple-element.163.cache.cache_ref, ...), custom_call_target="tpu_custom_call" | custom-call | tf_op jit(solution)/shard_map/attend_own/pallas_call | solution.py:33
  29.7 2.1 %collective-permute-done.5.refs_0_ = bf16[2,512,128]{2,1,0:T(8,128)(2,1)S(1)} collective-permute-done((bf16[2,512,128]{2,1,0:T(8,128)(2,1)S(1)}, bf16[2,512,128]{2,1,0:T(8,128)(2,1)S(1)}, u32[]{:S(2)}, u32[]{:S(2)}) %collective-permute-start.5) | collective-permute-done | bytes 262176 | tf_op jit(solution)/shard_map/ppermute | solution.py:322
  33.7 5.7 %attend_more.1 = (f32[768,128]{1,0:T(8,128)S(1)}, f32[768,128]{1,0:T(8,128)S(1)}, f32[768,128]{1,0:T(8,128)S(1)}) custom-call(bf16[768,128]{1,0:T(8,128)(2,1)S(1)} %get-tuple-element.83.q_all, f32[768,128]{1,0:T(8,128)S(1)} %get-tuple-element.98.m_ref, f32[768,128]{1,0:T(8,128)S(1)} %get-tuple-element.99.l_ref, f32[768,128]{1,0:T(8,128)S(1)} %get-tuple-element.100.acc_ref, ...), custom_call_target="tpu_custom_call" | custom-call | tf_op jit(solution)/shard_map/attend_more/pallas_call | solution.py:33
  39.4 2.6 %collective-permute-done.10.refs_0_ = bf16[2,512,128]{2,1,0:T(8,128)(2,1)S(1)} collective-permute-done((bf16[2,512,128]{2,1,0:T(8,128)(2,1)S(1)}, bf16[2,512,128]{2,1,0:T(8,128)(2,1)S(1)}, u32[]{:S(2)}, u32[]{:S(2)}) %collective-permute-start.10) | collective-permute-done | bytes 262176 | tf_op jit(solution)/shard_map/ppermute | solution.py:322
  42.1 1.5 collective-permute-done.11.refs_1_
  43.7 3.1 %attend.1 = (bf16[128,768]{1,0:T(8,128)(2,1)S(1)}, bf16[72,768]{1,0:T(8,128)(2,1)S(1)}, bf16[72,768]{1,0:T(8,128)(2,1)S(1)}, bf16[72,768]{1,0:T(8,128)(2,1)S(1)}, bf16[72,768]{1,0:T(8,128)(2,1)S(1)}) custom-call(bf16[768,128]{1,0:T(8,128)(2,1)S(1)} %get-tuple-element.83.q_all, bf16[128,768]{1,0:T(8,128)(2,1)S(1)} %get-tuple-element.84.res_ref, ...), custom_call_target="tpu_custom_call" | custom-call | tf_op jit(solution)/shard_map/attend/pallas_call | solution.py:33
  47.2 4.1 %collective-permute-start.13 = (bf16[72,768]{1,0:T(8,128)(2,1)S(1)}, bf16[72,768]{1,0:T(8,128)(2,1)S(1)}, u32[]{:S(2)}, u32[]{:S(2)}) collective-permute-start(bf16[72,768]{1,0:T(8,128)(2,1)S(1)} %get-tuple-element.114), channel_id=1, source_target_pairs={{0,96},{32,0},{64,32},{96,64},{1,97},{33,1},{65,33},{97,65},{2,98}... | collective-permute-start | bytes 331784 | tf_op jit(solution)/shard_map/ppermute | solution.py:322
  51.3 3.2 %collective-permute-start.14 = (bf16[72,768]{1,0:T(8,128)(2,1)S(1)}, bf16[72,768]{1,0:T(8,128)(2,1)S(1)}, u32[]{:S(2)}, u32[]{:S(2)}) collective-permute-start(bf16[72,768]{1,0:T(8,128)(2,1)S(1)} %get-tuple-element.115), channel_id=1, source_target_pairs={{0,64},{32,96},{64,0},{96,32},{1,65},{33,97},{65,1},{97,33},{2,66}... | collective-permute-start | bytes 331784 | tf_op jit(solution)/shard_map/ppermute | solution.py:322
  54.8 3.1 %collective-permute-done.13.refs_2_ = bf16[72,768]{1,0:T(8,128)(2,1)S(1)} collective-permute-done((bf16[72,768]{1,0:T(8,128)(2,1)S(1)}, bf16[72,768]{1,0:T(8,128)(2,1)S(1)}, u32[]{:S(2)}, u32[]{:S(2)}) %collective-permute-start.13) | collective-permute-done | bytes 110624 | tf_op jit(solution)/shard_map/ppermute | solution.py:322
  57.9 4.5 %collective-permute-done.14.refs_3_ = bf16[72,768]{1,0:T(8,128)(2,1)S(1)} collective-permute-done((bf16[72,768]{1,0:T(8,128)(2,1)S(1)}, bf16[72,768]{1,0:T(8,128)(2,1)S(1)}, u32[]{:S(2)}, u32[]{:S(2)}) %collective-permute-start.14) | collective-permute-done | bytes 110624 | tf_op jit(solution)/shard_map/ppermute | solution.py:322
  62.5 1.4 collective-permute-start.19
  63.9 1.5 collective-permute-start.18
  65.3 1.7 %collective-permute-start.17 = (bf16[144,768]{1,0:T(8,128)(2,1)S(1)}, bf16[144,768]{1,0:T(8,128)(2,1)S(1)}, u32[]{:S(2)}, u32[]{:S(2)}) collective-permute-start(bf16[144,768]{1,0:T(8,128)(2,1)S(1)} %get-tuple-element.123), channel_id=1, source_target_pairs={{0,3},{1,0},{2,1},{3,2},{4,7},{5,4},{6,5},{7,6},{8,11},{9,8},{10,9... | collective-permute-start | bytes 663560 | tf_op jit(solution)/shard_map/ppermute | solution.py:322
  67.1 1.8 %collective-permute-start.16 = (bf16[144,768]{1,0:T(8,128)(2,1)S(1)}, bf16[144,768]{1,0:T(8,128)(2,1)S(1)}, u32[]{:S(2)}, u32[]{:S(2)}) collective-permute-start(bf16[144,768]{1,0:T(8,128)(2,1)S(1)} %get-tuple-element.123), channel_id=1, source_target_pairs={{0,2},{1,3},{2,0},{3,1},{4,6},{5,7},{6,4},{7,5},{8,10},{9,11},{10,... | collective-permute-start | bytes 663560 | tf_op jit(solution)/shard_map/ppermute | solution.py:322
  68.9 1.2 collective-permute-done.19
  70.1 2.4 %collective-permute-done.18 = bf16[144,768]{1,0:T(8,128)(2,1)S(1)} collective-permute-done((bf16[144,768]{1,0:T(8,128)(2,1)S(1)}, bf16[144,768]{1,0:T(8,128)(2,1)S(1)}, u32[]{:S(2)}, u32[]{:S(2)}) %collective-permute-start.18) | collective-permute-done | bytes 221216 | tf_op jit(solution)/shard_map/ppermute | solution.py:322
  72.5 2.7 %collective-permute-done.17 = bf16[144,768]{1,0:T(8,128)(2,1)S(1)} collective-permute-done((bf16[144,768]{1,0:T(8,128)(2,1)S(1)}, bf16[144,768]{1,0:T(8,128)(2,1)S(1)}, u32[]{:S(2)}, u32[]{:S(2)}) %collective-permute-start.17) | collective-permute-done | bytes 221216 | tf_op jit(solution)/shard_map/ppermute | solution.py:322
  75.1 1.7 %collective-permute-done.16 = bf16[144,768]{1,0:T(8,128)(2,1)S(1)} collective-permute-done((bf16[144,768]{1,0:T(8,128)(2,1)S(1)}, bf16[144,768]{1,0:T(8,128)(2,1)S(1)}, u32[]{:S(2)}, u32[]{:S(2)}) %collective-permute-start.16) | collective-permute-done | bytes 221216 | tf_op jit(solution)/shard_map/ppermute | solution.py:322
  77.1 1.2 collective-permute-start.23
  78.3 2.1 %collective-permute-start.22 = (bf16[2,144,768]{2,1,0:T(8,128)(2,1)S(1)}, bf16[2,144,768]{2,1,0:T(8,128)(2,1)S(1)}, u32[]{:S(2)}, u32[]{:S(2)}) collective-permute-start(bf16[2,144,768]{2,1,0:T(8,128)(2,1)S(1)} %pad_maximum_fusion.1.refs_3_), channel_id=1, source_target_pairs={{0,3},{1,0},{2,1},{3,2},{4,7},{5,4},{6,5},{7,6},{8,11},{9,8},{10,9... | collective-permute-start | bytes 1327112 | tf_op jit(solution)/shard_map/ppermute | solution.py:322
  80.4 1.0 collective-permute-start.21
  81.4 16.3 %collective-permute-done.23.refs_4_ = bf16[2,144,768]{2,1,0:T(8,128)(2,1)S(1)} collective-permute-done((bf16[2,144,768]{2,1,0:T(8,128)(2,1)S(1)}, bf16[2,144,768]{2,1,0:T(8,128)(2,1)S(1)}, u32[]{:S(2)}, u32[]{:S(2)}) %collective-permute-start.23) | collective-permute-done | bytes 442400 | tf_op jit(solution)/shard_map/ppermute | solution.py:322
  97.7 14.6 %experts.1 = (bf16[4,144,768]{2,1,0:T(8,128)(2,1)S(1)}, bf16[2,144,768]{2,1,0:T(8,128)(2,1)S(1)}, bf16[2,144,768]{2,1,0:T(8,128)(2,1)S(1)}, bf16[2,144,768]{2,1,0:T(8,128)(2,1)S(1)}, bf16[2,144,768]{2,1,0:T(8,128)(2,1)S(1)}) custom-call(s32[4]{0:T(128)S(1)} %pad_add_fusion.where_ref.refs_0_, f32[4,1,768]{2,1,0:T(1,128)S(1)} %bitcast.18, ...), custom_call_target="tpu_custom_call" | custom-call | tf_op jit(solution)/shard_map/experts/pallas_call | solution.py:33
  112.4 1.8 %collective-permute-start.28 = (bf16[4,144,768]{2,1,0:T(8,128)(2,1)S(1)}, bf16[4,144,768]{2,1,0:T(8,128)(2,1)S(1)}, u32[]{:S(2)}, u32[]{:S(2)}) collective-permute-start(bf16[4,144,768]{2,1,0:T(8,128)(2,1)S(1)} %get-tuple-element.139), channel_id=1, source_target_pairs={{0,8},{8,0},{1,9},{9,1},{2,10},{10,2},{3,11},{11,3},{4,12},{12,4},... | collective-permute-start | bytes 2654216 | tf_op jit(solution)/shard_map/ppermute | solution.py:340
  115.0 2.4 %collective-permute-start.26 = (bf16[2,144,768]{2,1,0:T(8,128)(2,1)S(1)}, bf16[2,144,768]{2,1,0:T(8,128)(2,1)S(1)}, u32[]{:S(2)}, u32[]{:S(2)}) collective-permute-start(bf16[2,144,768]{2,1,0:T(8,128)(2,1)S(1)} %get-tuple-element.137), channel_id=1, source_target_pairs={{0,3},{1,0},{2,1},{3,2},{4,7},{5,4},{6,5},{7,6},{8,11},{9,8},{10,9... | collective-permute-start | bytes 1327112 | tf_op jit(solution)/shard_map/ppermute | solution.py:322
  117.4 1.2 collective-permute-start.27
  118.6 8.4 %experts_own.1.refs_0_ = bf16[4,144,768]{2,1,0:T(8,128)(2,1)S(1)} custom-call(s32[4]{0:T(128)S(1)} %pad_add_fusion.where_ref.refs_0_, f32[4,1,768]{2,1,0:T(1,128)S(1)} %bitcast.19, bf16[4,144,768]{2,1,0:T(8,128)(2,1)S(1)} %pad_maximum_fusion.refs_2_, bf16[3072,512]{1,0:T(8,128)(2,1)S(1)} %copy-done, bf16[3072,512]{1,0:T(8,128)(2,1)S(1)} %copy-done.1, ...), custom_call_target="tpu_custom_call" | custom-call | tf_op jit(solution)/shard_map/experts_own/pallas_call | solution.py:33
  127.6 2.3 %collective-permute-done.26.refs_4_ = bf16[2,144,768]{2,1,0:T(8,128)(2,1)S(1)} collective-permute-done((bf16[2,144,768]{2,1,0:T(8,128)(2,1)S(1)}, bf16[2,144,768]{2,1,0:T(8,128)(2,1)S(1)}, u32[]{:S(2)}, u32[]{:S(2)}) %collective-permute-start.26) | collective-permute-done | bytes 442400 | tf_op jit(solution)/shard_map/ppermute | solution.py:322
  129.9 3.1 %collective-permute-done.27.refs_5_ = bf16[2,144,768]{2,1,0:T(8,128)(2,1)S(1)} collective-permute-done((bf16[2,144,768]{2,1,0:T(8,128)(2,1)S(1)}, bf16[2,144,768]{2,1,0:T(8,128)(2,1)S(1)}, u32[]{:S(2)}, u32[]{:S(2)}) %collective-permute-start.27) | collective-permute-done | bytes 442400 | tf_op jit(solution)/shard_map/ppermute | solution.py:322
  133.6 1.2 collective-permute-start.29
  134.8 2.4 %collective-permute-start.30 = (bf16[144,768]{1,0:T(8,128)(2,1)S(1)}, bf16[144,768]{1,0:T(8,128)(2,1)S(1)}, u32[]{:S(2)}, u32[]{:S(2)}) collective-permute-start(bf16[144,768]{1,0:T(8,128)(2,1)S(1)} %get-tuple-element.147), channel_id=1, source_target_pairs={{0,3},{1,0},{2,1},{3,2},{4,7},{5,4},{6,5},{7,6},{8,11},{9,8},{10,9... | collective-permute-start | bytes 663560 | tf_op jit(solution)/shard_map/ppermute | solution.py:322
  137.2 1.4 collective-permute-start.31
  139.5 2.0 %collective-permute-start.33 = (bf16[144,768]{1,0:T(8,128)(2,1)S(1)}, bf16[144,768]{1,0:T(8,128)(2,1)S(1)}, u32[]{:S(2)}, u32[]{:S(2)}) collective-permute-start(bf16[144,768]{1,0:T(8,128)(2,1)S(1)} %add_convert_fusion), channel_id=1, source_target_pairs={{0,24},{8,16},{16,8},{24,0},{1,25},{9,17},{17,9},{25,1},{2,26},{10... | collective-permute-start | bytes 663560 | tf_op jit(solution)/shard_map/ppermute | solution.py:336
  141.5 3.4 %collective-permute-done.31.refs_3_ = bf16[144,768]{1,0:T(8,128)(2,1)S(1)} collective-permute-done((bf16[144,768]{1,0:T(8,128)(2,1)S(1)}, bf16[144,768]{1,0:T(8,128)(2,1)S(1)}, u32[]{:S(2)}, u32[]{:S(2)}) %collective-permute-start.31) | collective-permute-done | bytes 221216 | tf_op jit(solution)/shard_map/ppermute | solution.py:322
  144.9 1.8 %collective-permute-done.33.refs_4_ = bf16[144,768]{1,0:T(8,128)(2,1)S(1)} collective-permute-done((bf16[144,768]{1,0:T(8,128)(2,1)S(1)}, bf16[144,768]{1,0:T(8,128)(2,1)S(1)}, u32[]{:S(2)}, u32[]{:S(2)}) %collective-permute-start.33) | collective-permute-done | bytes 221216 | tf_op jit(solution)/shard_map/ppermute | solution.py:336
  146.9 2.3 %collective-permute-start.34 = (bf16[72,768]{1,0:T(8,128)(2,1)S(1)}, bf16[72,768]{1,0:T(8,128)(2,1)S(1)}, u32[]{:S(2)}, u32[]{:S(2)}) collective-permute-start(bf16[72,768]{1,0:T(8,128)(2,1)S(1)} %get-tuple-element.156), channel_id=1, source_target_pairs={{0,32},{32,64},{64,96},{96,0},{1,33},{33,65},{65,97},{97,1},{2,34}... | collective-permute-start | bytes 331784 | tf_op jit(solution)/shard_map/ppermute | solution.py:322
  149.1 2.0 %collective-permute-start.35 = (bf16[72,768]{1,0:T(8,128)(2,1)S(1)}, bf16[72,768]{1,0:T(8,128)(2,1)S(1)}, u32[]{:S(2)}, u32[]{:S(2)}) collective-permute-start(bf16[72,768]{1,0:T(8,128)(2,1)S(1)} %get-tuple-element.157), channel_id=1, source_target_pairs={{0,96},{32,0},{64,32},{96,64},{1,97},{33,1},{65,33},{97,65},{2,98}... | collective-permute-start | bytes 331784 | tf_op jit(solution)/shard_map/ppermute | solution.py:322
  151.1 7.1 %collective-permute-start.36 = (bf16[72,768]{1,0:T(8,128)(2,1)S(1)}, bf16[72,768]{1,0:T(8,128)(2,1)S(1)}, u32[]{:S(2)}, u32[]{:S(2)}) collective-permute-start(bf16[72,768]{1,0:T(8,128)(2,1)S(1)} %get-tuple-element.158), channel_id=1, source_target_pairs={{0,64},{32,96},{64,0},{96,32},{1,65},{33,97},{65,1},{97,33},{2,66}... | collective-permute-start | bytes 331784 | tf_op jit(solution)/shard_map/ppermute | solution.py:322
  158.2 5.1 %collective-permute-done.36.refs_3_ = bf16[72,768]{1,0:T(8,128)(2,1)S(1)} collective-permute-done((bf16[72,768]{1,0:T(8,128)(2,1)S(1)}, bf16[72,768]{1,0:T(8,128)(2,1)S(1)}, u32[]{:S(2)}, u32[]{:S(2)}) %collective-permute-start.36) | collective-permute-done | bytes 110624 | tf_op jit(solution)/shard_map/ppermute | solution.py:322
  163.3 1.6 mix.1
  (58 shorter events, 9.5 us)
Async XLA Ops:
  0.0 43.6 %copy-start.2 = (bf16[512,3072]{1,0:T(8,128)(2,1)S(1)}, bf16[512,3072]{1,0:T(8,128)(2,1)}, u32[]{:S(2)}) copy-start(bf16[512,3072]{1,0:T(8,128)(2,1)} %refs_9_.1) | copy-start | bytes 9437188
  0.0 19.0 %collective-permute-start.3 = (bf16[3072,512]{1,0:T(8,128)(2,1)}, bf16[3072,512]{1,0:T(8,128)(2,1)}, u32[]{:S(2)}, u32[]{:S(2)}) collective-permute-start(bf16[3072,512]{1,0:T(8,128)(2,1)} %refs_7_.1), channel_id=1, source_target_pairs={{0,4},{4,0},{1,5},{5,1},{2,6},{6,2},{3,7},{7,3},{8,12},{12,8},{9,1... | collective-permute-start | bytes 9437192 | tf_op jit(solution)/shard_map/ppermute | solution.py:344
  1.6 10.5 %collective-permute-start.2 = (bf16[2,128,128]{2,1,0:T(8,128)(2,1)}, bf16[2,128,128]{2,1,0:T(8,128)(2,1)S(1)}, u32[]{:S(2)}, u32[]{:S(2)}) collective-permute-start(bf16[2,128,128]{2,1,0:T(8,128)(2,1)} %get-tuple-element.159), channel_id=1, source_target_pairs={{0,32},{32,64},{64,96},{96,0},{1,33},{33,65},{65,97},{97,1},{2,34}... | collective-permute-start | bytes 196616 | tf_op jit(solution)/shard_map/ppermute | solution.py:322
  4.9 7.2 %collective-permute-start = (bf16[2,128,128]{2,1,0:T(8,128)(2,1)}, bf16[2,128,128]{2,1,0:T(8,128)(2,1)S(1)}, u32[]{:S(2)}, u32[]{:S(2)}) collective-permute-start(bf16[2,128,128]{2,1,0:T(8,128)(2,1)} %get-tuple-element.160), channel_id=1, source_target_pairs={{0,96},{32,0},{64,32},{96,64},{1,97},{33,1},{65,33},{97,65},{2,98}... | collective-permute-start | bytes 196616 | tf_op jit(solution)/shard_map/ppermute | solution.py:322
  7.0 11.2 %collective-permute-start.1 = (bf16[2,128,128]{2,1,0:T(8,128)(2,1)S(1)}, bf16[2,128,128]{2,1,0:T(8,128)(2,1)S(1)}, u32[]{:S(2)}, u32[]{:S(2)}) collective-permute-start(bf16[2,128,128]{2,1,0:T(8,128)(2,1)S(1)} %get-tuple-element.161), channel_id=1, source_target_pairs={{0,64},{32,96},{64,0},{96,32},{1,65},{33,97},{65,1},{97,33},{2,66}... | collective-permute-start | bytes 196616 | tf_op jit(solution)/shard_map/ppermute | solution.py:322
  19.0 12.9 %collective-permute-start.7 = (bf16[3072,512]{1,0:T(8,128)(2,1)}, bf16[3072,512]{1,0:T(8,128)(2,1)S(1)}, u32[]{:S(2)}, u32[]{:S(2)}) collective-permute-start(bf16[3072,512]{1,0:T(8,128)(2,1)} %refs_8_.1), channel_id=1, source_target_pairs={{0,4},{4,0},{1,5},{5,1},{2,6},{6,2},{3,7},{7,3},{8,12},{12,8},{9,1... | collective-permute-start | bytes 9437192 | tf_op jit(solution)/shard_map/ppermute | solution.py:344
  19.1 7.5 %collective-permute-start.4 = (bf16[2,512,128]{2,1,0:T(8,128)(2,1)S(1)}, bf16[2,512,128]{2,1,0:T(8,128)(2,1)S(1)}, u32[]{:S(2)}, u32[]{:S(2)}) collective-permute-start(bf16[2,512,128]{2,1,0:T(8,128)(2,1)S(1)} %get-tuple-element.90.refs_0_), channel_id=1, source_target_pairs={{0,4},{4,0},{1,5},{5,1},{2,6},{6,2},{3,7},{7,3},{8,12},{12,8},{9,1... | collective-permute-start | bytes 786440 | tf_op jit(solution)/shard_map/ppermute | solution.py:344
  19.6 10.1 %collective-permute-start.6 = (bf16[2,512,128]{2,1,0:T(8,128)(2,1)S(1)}, bf16[2,512,128]{2,1,0:T(8,128)(2,1)S(1)}, u32[]{:S(2)}, u32[]{:S(2)}) collective-permute-start(bf16[2,512,128]{2,1,0:T(8,128)(2,1)S(1)} %get-tuple-element.95), channel_id=1, source_target_pairs={{0,24},{8,0},{16,8},{24,16},{1,25},{9,1},{17,9},{25,17},{2,26},{10... | collective-permute-start | bytes 786440 | tf_op jit(solution)/shard_map/ppermute | solution.py:322
  22.6 9.2 %collective-permute-start.5 = (bf16[2,512,128]{2,1,0:T(8,128)(2,1)S(1)}, bf16[2,512,128]{2,1,0:T(8,128)(2,1)S(1)}, u32[]{:S(2)}, u32[]{:S(2)}) collective-permute-start(bf16[2,512,128]{2,1,0:T(8,128)(2,1)S(1)} %get-tuple-element.94), channel_id=1, source_target_pairs={{0,8},{8,16},{16,24},{24,0},{1,9},{9,17},{17,25},{25,1},{2,10},{10... | collective-permute-start | bytes 786440 | tf_op jit(solution)/shard_map/ppermute | solution.py:322
  22.6 0.9 copy-start.3
  23.5 0.9 copy-start.4
  24.4 0.7 copy-start.6
  25.1 0.7 copy-start.7
  31.8 1.5 collective-permute-start.8
  31.8 1.9 %collective-permute-start.9 = (bf16[2,512,128]{2,1,0:T(8,128)(2,1)S(1)}, bf16[2,512,128]{2,1,0:T(8,128)(2,1)S(1)}, u32[]{:S(2)}, u32[]{:S(2)}) collective-permute-start(bf16[2,512,128]{2,1,0:T(8,128)(2,1)S(1)} %collective-permute-done.6.refs_1_), channel_id=1, source_target_pairs={{0,4},{4,0},{1,5},{5,1},{2,6},{6,2},{3,7},{7,3},{8,12},{12,8},{9,1... | collective-permute-start | bytes 786440 | tf_op jit(solution)/shard_map/ppermute | solution.py:344
  32.3 9.7 %collective-permute-start.10 = (bf16[2,512,128]{2,1,0:T(8,128)(2,1)S(1)}, bf16[2,512,128]{2,1,0:T(8,128)(2,1)S(1)}, u32[]{:S(2)}, u32[]{:S(2)}) collective-permute-start(bf16[2,512,128]{2,1,0:T(8,128)(2,1)S(1)} %get-tuple-element.106), channel_id=1, source_target_pairs={{0,16},{8,24},{16,0},{24,8},{1,17},{9,25},{17,1},{25,9},{2,18},{10... | collective-permute-start | bytes 786440 | tf_op jit(solution)/shard_map/ppermute | solution.py:322
  33.7 64.0 %copy-start.1 = (bf16[3072,512]{1,0:T(8,128)(2,1)S(1)}, bf16[3072,512]{1,0:T(8,128)(2,1)}, u32[]{:S(2)}) copy-start(bf16[3072,512]{1,0:T(8,128)(2,1)} %refs_8_.1) | copy-start | bytes 9437188
  39.4 58.3 %copy-start = (bf16[3072,512]{1,0:T(8,128)(2,1)S(1)}, bf16[3072,512]{1,0:T(8,128)(2,1)}, u32[]{:S(2)}) copy-start(bf16[3072,512]{1,0:T(8,128)(2,1)} %refs_7_.1) | copy-start | bytes 9437188
  39.4 58.3 %copy-start.5 = (f32[3072]{0:T(1024)S(1)}, f32[3072]{0:T(1024)}, u32[]{:S(2)}) copy-start(f32[3072]{0:T(1024)} %param.18) | copy-start | bytes 36868
  42.1 1.5 collective-permute-start.11
  43.6 18.8 %collective-permute-start.15 = (bf16[512,3072]{1,0:T(8,128)(2,1)S(1)}, bf16[512,3072]{1,0:T(8,128)(2,1)S(1)}, u32[]{:S(2)}, u32[]{:S(2)}) collective-permute-start(bf16[512,3072]{1,0:T(8,128)(2,1)S(1)} %copy-done.2), channel_id=1, source_target_pairs={{0,4},{4,0},{1,5},{5,1},{2,6},{6,2},{3,7},{7,3},{8,12},{12,8},{9,1... | collective-permute-start | bytes 9437192 | tf_op jit(solution)/shard_map/ppermute | solution.py:344
  46.9 7.9 %collective-permute-start.12 = (bf16[72,768]{1,0:T(8,128)(2,1)S(1)}, bf16[72,768]{1,0:T(8,128)(2,1)S(1)}, u32[]{:S(2)}, u32[]{:S(2)}) collective-permute-start(bf16[72,768]{1,0:T(8,128)(2,1)S(1)} %get-tuple-element.113), channel_id=1, source_target_pairs={{0,32},{32,64},{64,96},{96,0},{1,33},{33,65},{65,97},{97,1},{2,34}... | collective-permute-start | bytes 331784 | tf_op jit(solution)/shard_map/ppermute | solution.py:322
  47.2 10.7 %collective-permute-start.13 = (bf16[72,768]{1,0:T(8,128)(2,1)S(1)}, bf16[72,768]{1,0:T(8,128)(2,1)S(1)}, u32[]{:S(2)}, u32[]{:S(2)}) collective-permute-start(bf16[72,768]{1,0:T(8,128)(2,1)S(1)} %get-tuple-element.114), channel_id=1, source_target_pairs={{0,96},{32,0},{64,32},{96,64},{1,97},{33,1},{65,33},{97,65},{2,98}... | collective-permute-start | bytes 331784 | tf_op jit(solution)/shard_map/ppermute | solution.py:322
  51.3 11.1 %collective-permute-start.14 = (bf16[72,768]{1,0:T(8,128)(2,1)S(1)}, bf16[72,768]{1,0:T(8,128)(2,1)S(1)}, u32[]{:S(2)}, u32[]{:S(2)}) collective-permute-start(bf16[72,768]{1,0:T(8,128)(2,1)S(1)} %get-tuple-element.115), channel_id=1, source_target_pairs={{0,64},{32,96},{64,0},{96,32},{1,65},{33,97},{65,1},{97,33},{2,66}... | collective-permute-start | bytes 331784 | tf_op jit(solution)/shard_map/ppermute | solution.py:322
  62.5 7.6 %collective-permute-start.19 = (bf16[144,768]{1,0:T(8,128)(2,1)S(1)}, bf16[144,768]{1,0:T(8,128)(2,1)S(1)}, u32[]{:S(2)}, u32[]{:S(2)}) collective-permute-start(bf16[144,768]{1,0:T(8,128)(2,1)S(1)} %get-tuple-element.124), channel_id=1, source_target_pairs={{0,24},{8,16},{16,8},{24,0},{1,25},{9,17},{17,9},{25,1},{2,26},{10... | collective-permute-start | bytes 663560 | tf_op jit(solution)/shard_map/ppermute | solution.py:336
  63.9 8.6 %collective-permute-start.18 = (bf16[144,768]{1,0:T(8,128)(2,1)S(1)}, bf16[144,768]{1,0:T(8,128)(2,1)S(1)}, u32[]{:S(2)}, u32[]{:S(2)}) collective-permute-start(bf16[144,768]{1,0:T(8,128)(2,1)S(1)} %get-tuple-element.123), channel_id=1, source_target_pairs={{0,1},{1,2},{2,3},{3,0},{4,5},{5,6},{6,7},{7,4},{8,9},{9,10},{10,1... | collective-permute-start | bytes 663560 | tf_op jit(solution)/shard_map/ppermute | solution.py:322
  65.3 9.8 %collective-permute-start.17 = (bf16[144,768]{1,0:T(8,128)(2,1)S(1)}, bf16[144,768]{1,0:T(8,128)(2,1)S(1)}, u32[]{:S(2)}, u32[]{:S(2)}) collective-permute-start(bf16[144,768]{1,0:T(8,128)(2,1)S(1)} %get-tuple-element.123), channel_id=1, source_target_pairs={{0,3},{1,0},{2,1},{3,2},{4,7},{5,4},{6,5},{7,6},{8,11},{9,8},{10,9... | collective-permute-start | bytes 663560 | tf_op jit(solution)/shard_map/ppermute | solution.py:322
  67.1 9.7 %collective-permute-start.16 = (bf16[144,768]{1,0:T(8,128)(2,1)S(1)}, bf16[144,768]{1,0:T(8,128)(2,1)S(1)}, u32[]{:S(2)}, u32[]{:S(2)}) collective-permute-start(bf16[144,768]{1,0:T(8,128)(2,1)S(1)} %get-tuple-element.123), channel_id=1, source_target_pairs={{0,2},{1,3},{2,0},{3,1},{4,6},{5,7},{6,4},{7,5},{8,10},{9,11},{10,... | collective-permute-start | bytes 663560 | tf_op jit(solution)/shard_map/ppermute | solution.py:322
  70.1 6.7 %collective-permute-start.20 = (bf16[144,768]{1,0:T(8,128)(2,1)S(1)}, bf16[144,768]{1,0:T(8,128)(2,1)S(1)}, u32[]{:S(2)}, u32[]{:S(2)}) collective-permute-start(bf16[144,768]{1,0:T(8,128)(2,1)S(1)} %collective-permute-done.19), channel_id=1, source_target_pairs={{0,8},{8,0},{1,9},{9,1},{2,10},{10,2},{3,11},{11,3},{4,12},{12,4},... | collective-permute-start | bytes 663560 | tf_op jit(solution)/shard_map/ppermute | solution.py:340
  76.9 20.8 %collective-permute-start.24 = (bf16[4,144,768]{2,1,0:T(8,128)(2,1)S(1)}, bf16[4,144,768]{2,1,0:T(8,128)(2,1)S(1)}, u32[]{:S(2)}, u32[]{:S(2)}) collective-permute-start(bf16[4,144,768]{2,1,0:T(8,128)(2,1)S(1)} %pad_maximum_fusion.refs_2_), channel_id=1, source_target_pairs={{0,8},{8,0},{1,9},{9,1},{2,10},{10,2},{3,11},{11,3},{4,12},{12,4},... | collective-permute-start | bytes 2654216 | tf_op jit(solution)/shard_map/ppermute | solution.py:340
  77.1 20.6 %collective-permute-start.23 = (bf16[2,144,768]{2,1,0:T(8,128)(2,1)S(1)}, bf16[2,144,768]{2,1,0:T(8,128)(2,1)S(1)}, u32[]{:S(2)}, u32[]{:S(2)}) collective-permute-start(bf16[2,144,768]{2,1,0:T(8,128)(2,1)S(1)} %pad_maximum_fusion.1.refs_3_), channel_id=1, source_target_pairs={{0,1},{1,2},{2,3},{3,0},{4,5},{5,6},{6,7},{7,4},{8,9},{9,10},{10,1... | collective-permute-start | bytes 1327112 | tf_op jit(solution)/shard_map/ppermute | solution.py:322
  78.3 19.4 %collective-permute-start.22 = (bf16[2,144,768]{2,1,0:T(8,128)(2,1)S(1)}, bf16[2,144,768]{2,1,0:T(8,128)(2,1)S(1)}, u32[]{:S(2)}, u32[]{:S(2)}) collective-permute-start(bf16[2,144,768]{2,1,0:T(8,128)(2,1)S(1)} %pad_maximum_fusion.1.refs_3_), channel_id=1, source_target_pairs={{0,3},{1,0},{2,1},{3,2},{4,7},{5,4},{6,5},{7,6},{8,11},{9,8},{10,9... | collective-permute-start | bytes 1327112 | tf_op jit(solution)/shard_map/ppermute | solution.py:322
  80.4 17.3 %collective-permute-start.21 = (bf16[2,144,768]{2,1,0:T(8,128)(2,1)S(1)}, bf16[2,144,768]{2,1,0:T(8,128)(2,1)S(1)}, u32[]{:S(2)}, u32[]{:S(2)}) collective-permute-start(bf16[2,144,768]{2,1,0:T(8,128)(2,1)S(1)} %pad_maximum_fusion.1.refs_3_), channel_id=1, source_target_pairs={{0,2},{1,3},{2,0},{3,1},{4,6},{5,7},{6,4},{7,5},{8,10},{9,11},{10,... | collective-permute-start | bytes 1327112 | tf_op jit(solution)/shard_map/ppermute | solution.py:322
  112.4 20.6 %collective-permute-start.28 = (bf16[4,144,768]{2,1,0:T(8,128)(2,1)S(1)}, bf16[4,144,768]{2,1,0:T(8,128)(2,1)S(1)}, u32[]{:S(2)}, u32[]{:S(2)}) collective-permute-start(bf16[4,144,768]{2,1,0:T(8,128)(2,1)S(1)} %get-tuple-element.139), channel_id=1, source_target_pairs={{0,8},{8,0},{1,9},{9,1},{2,10},{10,2},{3,11},{11,3},{4,12},{12,4},... | collective-permute-start | bytes 2654216 | tf_op jit(solution)/shard_map/ppermute | solution.py:340
  114.2 13.4 %collective-permute-start.25 = (bf16[2,144,768]{2,1,0:T(8,128)(2,1)S(1)}, bf16[2,144,768]{2,1,0:T(8,128)(2,1)S(1)}, u32[]{:S(2)}, u32[]{:S(2)}) collective-permute-start(bf16[2,144,768]{2,1,0:T(8,128)(2,1)S(1)} %get-tuple-element.136), channel_id=1, source_target_pairs={{0,1},{1,2},{2,3},{3,0},{4,5},{5,6},{6,7},{7,4},{8,9},{9,10},{10,1... | collective-permute-start | bytes 1327112 | tf_op jit(solution)/shard_map/ppermute | solution.py:322
  115.0 14.9 %collective-permute-start.26 = (bf16[2,144,768]{2,1,0:T(8,128)(2,1)S(1)}, bf16[2,144,768]{2,1,0:T(8,128)(2,1)S(1)}, u32[]{:S(2)}, u32[]{:S(2)}) collective-permute-start(bf16[2,144,768]{2,1,0:T(8,128)(2,1)S(1)} %get-tuple-element.137), channel_id=1, source_target_pairs={{0,3},{1,0},{2,1},{3,2},{4,7},{5,4},{6,5},{7,6},{8,11},{9,8},{10,9... | collective-permute-start | bytes 1327112 | tf_op jit(solution)/shard_map/ppermute | solution.py:322
  117.4 15.6 %collective-permute-start.27 = (bf16[2,144,768]{2,1,0:T(8,128)(2,1)S(1)}, bf16[2,144,768]{2,1,0:T(8,128)(2,1)S(1)}, u32[]{:S(2)}, u32[]{:S(2)}) collective-permute-start(bf16[2,144,768]{2,1,0:T(8,128)(2,1)S(1)} %get-tuple-element.138), channel_id=1, source_target_pairs={{0,2},{1,3},{2,0},{3,1},{4,6},{5,7},{6,4},{7,5},{8,10},{9,11},{10,... | collective-permute-start | bytes 1327112 | tf_op jit(solution)/shard_map/ppermute | solution.py:322
  133.4 6.0 %collective-permute-start.32 = (bf16[144,768]{1,0:T(8,128)(2,1)S(1)}, bf16[144,768]{1,0:T(8,128)(2,1)S(1)}, u32[]{:S(2)}, u32[]{:S(2)}) collective-permute-start(bf16[144,768]{1,0:T(8,128)(2,1)S(1)} %get-tuple-element.150), channel_id=1, source_target_pairs={{0,8},{8,0},{1,9},{9,1},{2,10},{10,2},{3,11},{11,3},{4,12},{12,4},... | collective-permute-start | bytes 663560 | tf_op jit(solution)/shard_map/ppermute | solution.py:340
  133.6 7.8 %collective-permute-start.29 = (bf16[144,768]{1,0:T(8,128)(2,1)S(1)}, bf16[144,768]{1,0:T(8,128)(2,1)S(1)}, u32[]{:S(2)}, u32[]{:S(2)}) collective-permute-start(bf16[144,768]{1,0:T(8,128)(2,1)S(1)} %get-tuple-element.146), channel_id=1, source_target_pairs={{0,1},{1,2},{2,3},{3,0},{4,5},{5,6},{6,7},{7,4},{8,9},{9,10},{10,1... | collective-permute-start | bytes 663560 | tf_op jit(solution)/shard_map/ppermute | solution.py:322
  134.8 6.6 %collective-permute-start.30 = (bf16[144,768]{1,0:T(8,128)(2,1)S(1)}, bf16[144,768]{1,0:T(8,128)(2,1)S(1)}, u32[]{:S(2)}, u32[]{:S(2)}) collective-permute-start(bf16[144,768]{1,0:T(8,128)(2,1)S(1)} %get-tuple-element.147), channel_id=1, source_target_pairs={{0,3},{1,0},{2,1},{3,2},{4,7},{5,4},{6,5},{7,6},{8,11},{9,8},{10,9... | collective-permute-start | bytes 663560 | tf_op jit(solution)/shard_map/ppermute | solution.py:322
  137.2 7.7 %collective-permute-start.31 = (bf16[144,768]{1,0:T(8,128)(2,1)S(1)}, bf16[144,768]{1,0:T(8,128)(2,1)S(1)}, u32[]{:S(2)}, u32[]{:S(2)}) collective-permute-start(bf16[144,768]{1,0:T(8,128)(2,1)S(1)} %get-tuple-element.148), channel_id=1, source_target_pairs={{0,2},{1,3},{2,0},{3,1},{4,6},{5,7},{6,4},{7,5},{8,10},{9,11},{10,... | collective-permute-start | bytes 663560 | tf_op jit(solution)/shard_map/ppermute | solution.py:322
  139.5 7.2 %collective-permute-start.33 = (bf16[144,768]{1,0:T(8,128)(2,1)S(1)}, bf16[144,768]{1,0:T(8,128)(2,1)S(1)}, u32[]{:S(2)}, u32[]{:S(2)}) collective-permute-start(bf16[144,768]{1,0:T(8,128)(2,1)S(1)} %add_convert_fusion), channel_id=1, source_target_pairs={{0,24},{8,16},{16,8},{24,0},{1,25},{9,17},{17,9},{25,1},{2,26},{10... | collective-permute-start | bytes 663560 | tf_op jit(solution)/shard_map/ppermute | solution.py:336
  146.9 11.3 %collective-permute-start.34 = (bf16[72,768]{1,0:T(8,128)(2,1)S(1)}, bf16[72,768]{1,0:T(8,128)(2,1)S(1)}, u32[]{:S(2)}, u32[]{:S(2)}) collective-permute-start(bf16[72,768]{1,0:T(8,128)(2,1)S(1)} %get-tuple-element.156), channel_id=1, source_target_pairs={{0,32},{32,64},{64,96},{96,0},{1,33},{33,65},{65,97},{97,1},{2,34}... | collective-permute-start | bytes 331784 | tf_op jit(solution)/shard_map/ppermute | solution.py:322
  149.1 9.1 %collective-permute-start.35 = (bf16[72,768]{1,0:T(8,128)(2,1)S(1)}, bf16[72,768]{1,0:T(8,128)(2,1)S(1)}, u32[]{:S(2)}, u32[]{:S(2)}) collective-permute-start(bf16[72,768]{1,0:T(8,128)(2,1)S(1)} %get-tuple-element.157), channel_id=1, source_target_pairs={{0,96},{32,0},{64,32},{96,64},{1,97},{33,1},{65,33},{97,65},{2,98}... | collective-permute-start | bytes 331784 | tf_op jit(solution)/shard_map/ppermute | solution.py:322
  151.1 12.2 %collective-permute-start.36 = (bf16[72,768]{1,0:T(8,128)(2,1)S(1)}, bf16[72,768]{1,0:T(8,128)(2,1)S(1)}, u32[]{:S(2)}, u32[]{:S(2)}) collective-permute-start(bf16[72,768]{1,0:T(8,128)(2,1)S(1)} %get-tuple-element.158), channel_id=1, source_target_pairs={{0,64},{32,96},{64,0},{96,32},{1,65},{33,97},{65,1},{97,33},{2,66}... | collective-permute-start | bytes 331784 | tf_op jit(solution)/shard_map/ppermute | solution.py:322

commit v5 on v3

--- a/solution.py
+++ b/solution.py
@@ -19,7 +19,7 @@
 SHIFTS = (1, 3, 2)
 KV_ORDER, Z_ORDER, X_ORDER = (0, 1, 2), (0, 1, 2), (2, 1, 0)
 MB = 1024 * 1024
-LIMIT = 47
+LIMIT = 13
 
 bf16 = jnp.bfloat16
 f32 = jnp.float32
@@ -184,28 +184,32 @@
         away[d * CAP : (d + 1) * CAP, :] = ref[CAP:]
 
 
-def expert_kernel(stacks, pairs, where_ref, gain_ref, *refs):
+def expert_kernel(stacks, pairs, loading, where_ref, gain_ref, *refs):
     refs = list(refs)
     take = lambda n: [refs.pop(0) for _ in range(n)]
     stack_in, pair_in = take(stacks), take(NX * pairs)
-    weights = take(6)
+    weights = take(6 if loading else 3)
     stack_out, pair_out = take(stacks), take(NX * pairs)
-    normed, act, gate_v, up_v, down_v, sems = refs
-    total, ff = weights[0].shape
+    gate_v, up_v, down_v = take(3) if loading else weights
+    normed, act = take(2)
+    _, total, ff = gate_v.shape
     width = total // NX
     rows = normed.shape[0] // (stacks + 2 * pairs)
-    gate_loads, up_loads, down_loads = [
-        [pltpu.make_async_copy(weights[3 * h + j], place(h), sems.at[h, j]) for h in range(2)]
-        for j, place in enumerate(
-            (
-                lambda h: gate_v.at[h],
-                lambda h: up_v.at[h],
-                lambda h: down_v.at[pl.ds(h * ff, ff)],
+    down_loads = []
+    if loading:
+        sems = refs[0]
+        gate_loads, up_loads, down_loads = [
+            [pltpu.make_async_copy(weights[3 * h + j], place(h), sems.at[h, j]) for h in range(2)]
+            for j, place in enumerate(
+                (
+                    lambda h: gate_v.at[h],
+                    lambda h: up_v.at[h],
+                    lambda h: down_v.at[pl.ds(h * ff, ff)],
+                )
             )
-        )
-    ]
-    for c in (gate_loads[0], up_loads[0], gate_loads[1], up_loads[1], *down_loads):
-        c.start()
+        ]
+        for c in (gate_loads[0], up_loads[0], gate_loads[1], up_loads[1], *down_loads):
+            c.start()
     x = where_ref[3]
     order = (0,) + SHIFTS
 
@@ -237,7 +241,7 @@
             place(stacks + r, shift, ref[r], inverse)
 
     def hidden_units(half, carry):
-        for j, v in enumerate((gate_v, up_v)):
+        for j, v in enumerate((gate_v, up_v) if loading else ()):
             pltpu.make_async_copy(v.at[half], v.at[half], sems.at[half, j]).wait()
         gate = jnp.dot(normed[...], gate_v[half], preferred_element_type=f32)
         up = jnp.dot(normed[...], up_v[half], preferred_element_type=f32)
@@ -258,26 +262,30 @@
             pair_out[i][r] = out[at : at + rows]
 
 
-def experts(where, gain, stacks, pairs, own, other, name):
+def experts(where, gain, stacks, pairs, weights, name):
     rows, width = stacks[0].shape[1:]
-    total, ff = own[0].shape
+    loading = len(weights) == 6
+    total = width * NX
+    ff = weights[0].shape[-1]
     groups = 1 if pairs else 0
     n = rows * (len(stacks) + 2 * groups)
 
     def body(*refs):
-        expert_kernel(len(stacks), groups, *refs)
-
+        expert_kernel(len(stacks), groups, loading, *refs)
+
+    shapes = [v.shape for v in (*stacks, *pairs)]
+    if loading:
+        shapes += [(2, total, ff), (2, total, ff), (2 * ff, total)]
     return call(
         body,
-        [jax.ShapeDtypeStruct(v.shape, bf16) for v in (*stacks, *pairs)],
-        [where, gain, *stacks, *pairs, *own, *other],
+        [jax.ShapeDtypeStruct(v, bf16) for v in shapes],
+        [where, gain, *stacks, *pairs, *weights],
         name,
         [pltpu.VMEM((n, total), bf16), pltpu.VMEM((n, 2 * ff), bf16)]
-        + [pltpu.VMEM((2, total, ff), bf16)] * 2
-        + [pltpu.VMEM((2 * ff, total), bf16), pltpu.SemaphoreType.DMA((2, 3))],
+        + [pltpu.SemaphoreType.DMA((2, 3))] * loading,
         limit=LIMIT,
         scalars=1,
-        hbm=6,
+        hbm=6 * loading,
     )
 
 
@@ -379,7 +387,7 @@
     packed = call(
         pack_kv_kernel,
         [shaped(2, NZ * rows, HEAD_DIM)] * 4,
-        [where, near, past, *[from_z[i] for i in (1, 2, 0)]],
+        [where, near, past, *[from_z[i] for i in (0, 1, 2)]],
         "pack_kv",
         scalars=1,
     )
@@ -413,13 +421,13 @@
     a, away = call(merge_kernel, [rows_a] * 2, arrived, "merge")
     b = cross(away)
     b_far = swap_y(b)
-    *a_turned, b_far = together(turned([a] * 3, "x", X_ORDER) + [b_far], (2, 1, 0, 3))
+    *a_turned, b_far = together(turned([a] * 3, "x", X_ORDER) + [b_far], (0, 1, 2, 3))
     a_own = jnp.stack([a] + a_turned)
     b_pair = jnp.stack((b, b_far))
-    *b_turned, a_far = together(turned([b_pair] * 3, "x", X_ORDER) + [swap_y(a_own)], (2, 1, 0, 3))
+    *b_turned, a_far = together(turned([b_pair] * 3, "x", X_ORDER) + [swap_y(a_own)], (0, 1, 2, 3))
     gain = norm_gain.reshape(NX, 1, width)
-    a_own = experts(where, gain, [a_own], [], own, other, "experts_own")[0]
-    a_far, *b_all = experts(where, gain, [a_far], [b_pair] + b_turned, own, other, "experts")
+    a_own, *weights = experts(where, gain, [a_own], [], [*own, *other], "experts_own")
+    a_far, *b_all = experts(where, gain, [a_far], [b_pair] + b_turned, weights, "experts")
 
     *b_turned, a_far = lax.optimization_barrier(
         [turn(v, "x", s) for v, s in zip(b_all[1:], SHIFTS)] + [swap_y(a_far)]

time: 162 us -> 160 us (0.988)
  Pallas kernels: 35.5 us -> 32.1 us
  starting transfers between devices: 57 us -> 59.6 us
  waiting for transfers between devices: 64.5 us -> 62.7 us
    pallas_call x11, Pallas kernels: 35.5 us -> 32.1 us  [call(): pl.pallas_call(body, out_shape=out_shape, in_specs=[SM] * scalars + [VM]...]
    ppermute x24, starting transfers between devices: 50.3 us -> 52.6 us  [turn(): return lax.ppermute(v, axis, [(i, (i + shift) % n) for i in range(n)])]
  transfers between devices with their start and end apart: 37 -> 37, of which waited for: 22 -> 20; matrix products, arithmetic and copies ran while one was open for 1% -> 1% of each run, Pallas kernels for 13% -> 12%
where the time goes in v5:
time: 160 us
  waiting for transfers between devices  62.7 us (39%)
  starting transfers between devices  59.6 us (37%)
  Pallas kernels  32.1 us (20%)
  local copies, waits for them, and re-layouts  3.23 us (2%)
  other arithmetic  1.91 us (1%)
    ppermute x24, waiting for transfers between devices, turn(): return lax.ppermute(v, axis, [(i, (i + shift) % n) for i in range(n)])  58.3 us
    ppermute x24, starting transfers between devices, turn(): return lax.ppermute(v, axis, [(i, (i + shift) % n) for i in range(n)])  52.6 us
    pallas_call x11, Pallas kernels, call(): pl.pallas_call(body, out_shape=out_shape, in_specs=[SM] * scalars + [VM]...  32.1 us
    ppermute x2, starting transfers between devices, cross(): return lax.ppermute(v, ('yh', 'yl'), [(i, NY - 1 - i) for i in range(NY)])  3.55 us
    unnamed x16, local copies, waits for them, and re-layouts  3.23 us
  transfers between devices with their start and end apart: 37, of which 20 were waited for; matrix products, arithmetic and copies ran while one was open for 1% of the time, Pallas kernels for 12%

profile of v5, /device:TPU:32, one launch (start us, length us, event | category | flops | bytes accessed | tf_op | source)
XLA Modules:
  0.0 159.8 jit_solution(7369276082079510440)
XLA Ops:
  0.0 1.6 %broadcast_select_fusion = (bf16[2,128,128]{2,1,0:T(8,128)(2,1)S(1)}, bf16[2,128,128]{2,1,0:T(8,128)(2,1)}, bf16[2,128,128]{2,1,0:T(8,128)(2,1)}, bf16[2,128,128]{2,1,0:T(8,128)(2,1)S(1)}, bf16[2,128,128]{2,1,0:T(8,128)(2,1)S(1)}) fusion(pred[]{:T(512)S(6)} %lt.11, bf16[1,128,128]{2,1,0:T(8,128)(2,1)} %bitcast.27, bf16[1,128,128]{2,1,0:T(8,128)(2,1)} %bitcast.28, ...), kind=kLoop, calls=%fused_computation.5 | loop fusion | flops 163840 | bytes 458755 | tf_op jit(solution)/shard_map/jit(_where)/select_n | solution.py:373
  1.6 3.3 %collective-permute-start = (bf16[2,128,128]{2,1,0:T(8,128)(2,1)}, bf16[2,128,128]{2,1,0:T(8,128)(2,1)S(1)}, u32[]{:S(2)}, u32[]{:S(2)}) collective-permute-start(bf16[2,128,128]{2,1,0:T(8,128)(2,1)} %get-tuple-element.168), channel_id=1, source_target_pairs={{0,32},{32,64},{64,96},{96,0},{1,33},{33,65},{65,97},{97,1},{2,34}... | collective-permute-start | bytes 196616 | tf_op jit(solution)/shard_map/ppermute | solution.py:336
  4.9 2.1 %collective-permute-start.1 = (bf16[2,128,128]{2,1,0:T(8,128)(2,1)}, bf16[2,128,128]{2,1,0:T(8,128)(2,1)S(1)}, u32[]{:S(2)}, u32[]{:S(2)}) collective-permute-start(bf16[2,128,128]{2,1,0:T(8,128)(2,1)} %get-tuple-element.169), channel_id=1, source_target_pairs={{0,96},{32,0},{64,32},{96,64},{1,97},{33,1},{65,33},{97,65},{2,98}... | collective-permute-start | bytes 196616 | tf_op jit(solution)/shard_map/ppermute | solution.py:336
  7.0 5.0 %collective-permute-start.2 = (bf16[2,128,128]{2,1,0:T(8,128)(2,1)S(1)}, bf16[2,128,128]{2,1,0:T(8,128)(2,1)S(1)}, u32[]{:S(2)}, u32[]{:S(2)}) collective-permute-start(bf16[2,128,128]{2,1,0:T(8,128)(2,1)S(1)} %get-tuple-element.167), channel_id=1, source_target_pairs={{0,64},{32,96},{64,0},{96,32},{1,65},{33,97},{65,1},{97,33},{2,66}... | collective-permute-start | bytes 196616 | tf_op jit(solution)/shard_map/ppermute | solution.py:336
  12.1 6.1 %collective-permute-done.2.refs_2_ = bf16[2,128,128]{2,1,0:T(8,128)(2,1)S(1)} collective-permute-done((bf16[2,128,128]{2,1,0:T(8,128)(2,1)S(1)}, bf16[2,128,128]{2,1,0:T(8,128)(2,1)S(1)}, u32[]{:S(2)}, u32[]{:S(2)}) %collective-permute-start.2) | collective-permute-done | bytes 65568 | tf_op jit(solution)/shard_map/ppermute | solution.py:336
  19.5 1.6 collective-permute-start.5
  21.1 1.7 %collective-permute-start.6 = (bf16[2,512,128]{2,1,0:T(8,128)(2,1)S(1)}, bf16[2,512,128]{2,1,0:T(8,128)(2,1)S(1)}, u32[]{:S(2)}, u32[]{:S(2)}) collective-permute-start(bf16[2,512,128]{2,1,0:T(8,128)(2,1)S(1)} %get-tuple-element.99), channel_id=1, source_target_pairs={{0,24},{8,0},{16,8},{24,16},{1,25},{9,1},{17,9},{25,17},{2,26},{10... | collective-permute-start | bytes 786440 | tf_op jit(solution)/shard_map/ppermute | solution.py:336
  22.8 0.9 copy-done.3
  23.7 0.9 copy-done.4
  26.8 3.1 %attend_own.1 = (f32[768,128]{1,0:T(8,128)S(1)}, f32[768,128]{1,0:T(8,128)S(1)}, f32[768,128]{1,0:T(8,128)S(1)}) custom-call(bf16[768,128]{1,0:T(8,128)(2,1)S(1)} %get-tuple-element.87.q_all, bf16[2,128,128]{2,1,0:T(8,128)(2,1)S(1)} %get-tuple-element.170.tract.tract_ref, bf16[2,128,128]{2,1,0:T(8,128)(2,1)S(1)} %get-tuple-element.171.cache.cache_ref, ...), custom_call_target="tpu_custom_call" | custom-call | tf_op jit(solution)/shard_map/attend_own/pallas_call | solution.py:33
  30.5 2.1 %collective-permute-start.10 = (bf16[2,512,128]{2,1,0:T(8,128)(2,1)S(1)}, bf16[2,512,128]{2,1,0:T(8,128)(2,1)S(1)}, u32[]{:S(2)}, u32[]{:S(2)}) collective-permute-start(bf16[2,512,128]{2,1,0:T(8,128)(2,1)S(1)} %get-tuple-element.110), channel_id=1, source_target_pairs={{0,16},{8,24},{16,0},{24,8},{1,17},{9,25},{17,1},{25,9},{2,18},{10... | collective-permute-start | bytes 786440 | tf_op jit(solution)/shard_map/ppermute | solution.py:336
  32.6 5.7 %attend_more.1 = (f32[768,128]{1,0:T(8,128)S(1)}, f32[768,128]{1,0:T(8,128)S(1)}, f32[768,128]{1,0:T(8,128)S(1)}) custom-call(bf16[768,128]{1,0:T(8,128)(2,1)S(1)} %get-tuple-element.87.q_all, f32[768,128]{1,0:T(8,128)S(1)} %get-tuple-element.102.m_ref, f32[768,128]{1,0:T(8,128)S(1)} %get-tuple-element.103.l_ref, f32[768,128]{1,0:T(8,128)S(1)} %get-tuple-element.104.acc_ref, ...), custom_call_target="tpu_custom_call" | custom-call | tf_op jit(solution)/shard_map/attend_more/pallas_call | solution.py:33
  38.3 2.0 %collective-permute-done.10.refs_0_ = bf16[2,512,128]{2,1,0:T(8,128)(2,1)S(1)} collective-permute-done((bf16[2,512,128]{2,1,0:T(8,128)(2,1)S(1)}, bf16[2,512,128]{2,1,0:T(8,128)(2,1)S(1)}, u32[]{:S(2)}, u32[]{:S(2)}) %collective-permute-start.10) | collective-permute-done | bytes 262176 | tf_op jit(solution)/shard_map/ppermute | solution.py:336
  40.3 1.5 collective-permute-done.11.refs_1_
  42.0 3.1 %attend.1 = (bf16[128,768]{1,0:T(8,128)(2,1)S(1)}, bf16[72,768]{1,0:T(8,128)(2,1)S(1)}, bf16[72,768]{1,0:T(8,128)(2,1)S(1)}, bf16[72,768]{1,0:T(8,128)(2,1)S(1)}, bf16[72,768]{1,0:T(8,128)(2,1)S(1)}) custom-call(bf16[768,128]{1,0:T(8,128)(2,1)S(1)} %get-tuple-element.87.q_all, bf16[128,768]{1,0:T(8,128)(2,1)S(1)} %get-tuple-element.88.res_ref, ...), custom_call_target="tpu_custom_call" | custom-call | tf_op jit(solution)/shard_map/attend/pallas_call | solution.py:33
  45.4 4.1 %collective-permute-start.13 = (bf16[72,768]{1,0:T(8,128)(2,1)S(1)}, bf16[72,768]{1,0:T(8,128)(2,1)S(1)}, u32[]{:S(2)}, u32[]{:S(2)}) collective-permute-start(bf16[72,768]{1,0:T(8,128)(2,1)S(1)} %get-tuple-element.118), channel_id=1, source_target_pairs={{0,96},{32,0},{64,32},{96,64},{1,97},{33,1},{65,33},{97,65},{2,98}... | collective-permute-start | bytes 331784 | tf_op jit(solution)/shard_map/ppermute | solution.py:336
  49.6 3.2 %collective-permute-start.14 = (bf16[72,768]{1,0:T(8,128)(2,1)S(1)}, bf16[72,768]{1,0:T(8,128)(2,1)S(1)}, u32[]{:S(2)}, u32[]{:S(2)}) collective-permute-start(bf16[72,768]{1,0:T(8,128)(2,1)S(1)} %get-tuple-element.119), channel_id=1, source_target_pairs={{0,64},{32,96},{64,0},{96,32},{1,65},{33,97},{65,1},{97,33},{2,66}... | collective-permute-start | bytes 331784 | tf_op jit(solution)/shard_map/ppermute | solution.py:336
  53.1 3.1 %collective-permute-done.13.refs_2_ = bf16[72,768]{1,0:T(8,128)(2,1)S(1)} collective-permute-done((bf16[72,768]{1,0:T(8,128)(2,1)S(1)}, bf16[72,768]{1,0:T(8,128)(2,1)S(1)}, u32[]{:S(2)}, u32[]{:S(2)}) %collective-permute-start.13) | collective-permute-done | bytes 110624 | tf_op jit(solution)/shard_map/ppermute | solution.py:336
  56.2 4.5 %collective-permute-done.14.refs_3_ = bf16[72,768]{1,0:T(8,128)(2,1)S(1)} collective-permute-done((bf16[72,768]{1,0:T(8,128)(2,1)S(1)}, bf16[72,768]{1,0:T(8,128)(2,1)S(1)}, u32[]{:S(2)}, u32[]{:S(2)}) %collective-permute-start.14) | collective-permute-done | bytes 110624 | tf_op jit(solution)/shard_map/ppermute | solution.py:336
  60.7 2.1 %collective-permute-start.19 = (bf16[144,768]{1,0:T(8,128)(2,1)S(1)}, bf16[144,768]{1,0:T(8,128)(2,1)S(1)}, u32[]{:S(2)}, u32[]{:S(2)}) collective-permute-start(bf16[144,768]{1,0:T(8,128)(2,1)S(1)} %get-tuple-element.128), channel_id=1, source_target_pairs={{0,24},{8,16},{16,8},{24,0},{1,25},{9,17},{17,9},{25,1},{2,26},{10... | collective-permute-start | bytes 663560 | tf_op jit(solution)/shard_map/ppermute | solution.py:350
  62.8 1.5 collective-permute-start.16
  64.3 1.7 %collective-permute-start.17 = (bf16[144,768]{1,0:T(8,128)(2,1)S(1)}, bf16[144,768]{1,0:T(8,128)(2,1)S(1)}, u32[]{:S(2)}, u32[]{:S(2)}) collective-permute-start(bf16[144,768]{1,0:T(8,128)(2,1)S(1)} %get-tuple-element.127), channel_id=1, source_target_pairs={{0,3},{1,0},{2,1},{3,2},{4,7},{5,4},{6,5},{7,6},{8,11},{9,8},{10,9... | collective-permute-start | bytes 663560 | tf_op jit(solution)/shard_map/ppermute | solution.py:336
  66.0 1.8 %collective-permute-start.18 = (bf16[144,768]{1,0:T(8,128)(2,1)S(1)}, bf16[144,768]{1,0:T(8,128)(2,1)S(1)}, u32[]{:S(2)}, u32[]{:S(2)}) collective-permute-start(bf16[144,768]{1,0:T(8,128)(2,1)S(1)} %get-tuple-element.127), channel_id=1, source_target_pairs={{0,2},{1,3},{2,0},{3,1},{4,6},{5,7},{6,4},{7,5},{8,10},{9,11},{10,... | collective-permute-start | bytes 663560 | tf_op jit(solution)/shard_map/ppermute | solution.py:336
  68.3 3.0 %collective-permute-done.16 = bf16[144,768]{1,0:T(8,128)(2,1)S(1)} collective-permute-done((bf16[144,768]{1,0:T(8,128)(2,1)S(1)}, bf16[144,768]{1,0:T(8,128)(2,1)S(1)}, u32[]{:S(2)}, u32[]{:S(2)}) %collective-permute-start.16) | collective-permute-done | bytes 221216 | tf_op jit(solution)/shard_map/ppermute | solution.py:336
  71.3 2.7 %collective-permute-done.17 = bf16[144,768]{1,0:T(8,128)(2,1)S(1)} collective-permute-done((bf16[144,768]{1,0:T(8,128)(2,1)S(1)}, bf16[144,768]{1,0:T(8,128)(2,1)S(1)}, u32[]{:S(2)}, u32[]{:S(2)}) %collective-permute-start.17) | collective-permute-done | bytes 221216 | tf_op jit(solution)/shard_map/ppermute | solution.py:336
  74.1 1.7 %collective-permute-done.18 = bf16[144,768]{1,0:T(8,128)(2,1)S(1)} collective-permute-done((bf16[144,768]{1,0:T(8,128)(2,1)S(1)}, bf16[144,768]{1,0:T(8,128)(2,1)S(1)}, u32[]{:S(2)}, u32[]{:S(2)}) %collective-permute-start.18) | collective-permute-done | bytes 221216 | tf_op jit(solution)/shard_map/ppermute | solution.py:336
  76.1 1.2 collective-permute-start.21
  77.3 2.1 %collective-permute-start.22 = (bf16[2,144,768]{2,1,0:T(8,128)(2,1)S(1)}, bf16[2,144,768]{2,1,0:T(8,128)(2,1)S(1)}, u32[]{:S(2)}, u32[]{:S(2)}) collective-permute-start(bf16[2,144,768]{2,1,0:T(8,128)(2,1)S(1)} %pad_maximum_fusion.1.refs_3_), channel_id=1, source_target_pairs={{0,3},{1,0},{2,1},{3,2},{4,7},{5,4},{6,5},{7,6},{8,11},{9,8},{10,9... | collective-permute-start | bytes 1327112 | tf_op jit(solution)/shard_map/ppermute | solution.py:336
  79.7 5.7 %experts_own.1 = (bf16[4,144,768]{2,1,0:T(8,128)(2,1)S(1)}, bf16[2,3072,512]{2,1,0:T(8,128)(2,1)S(1)}, bf16[2,3072,512]{2,1,0:T(8,128)(2,1)S(1)}, bf16[1024,3072]{1,0:T(8,128)(2,1)S(1)}) custom-call(s32[4]{0:T(128)S(1)} %pad_add_fusion.where_ref.refs_0_, f32[4,1,768]{2,1,0:T(1,128)S(1)} %bitcast.18, bf16[4,144,768]{2,1,0:T(8,128)(2,1)S(1)} %pad_maximum_fusion.refs_2_, ...), custom_call_target="tpu_custom_call" | custom-call | tf_op jit(solution)/shard_map/experts_own/pallas_call | solution.py:33
  85.4 11.3 %collective-permute-done.21.refs_4_ = bf16[2,144,768]{2,1,0:T(8,128)(2,1)S(1)} collective-permute-done((bf16[2,144,768]{2,1,0:T(8,128)(2,1)S(1)}, bf16[2,144,768]{2,1,0:T(8,128)(2,1)S(1)}, u32[]{:S(2)}, u32[]{:S(2)}) %collective-permute-start.21) | collective-permute-done | bytes 442400 | tf_op jit(solution)/shard_map/ppermute | solution.py:336
  96.7 10.9 %experts.1 = (bf16[4,144,768]{2,1,0:T(8,128)(2,1)S(1)}, bf16[2,144,768]{2,1,0:T(8,128)(2,1)S(1)}, bf16[2,144,768]{2,1,0:T(8,128)(2,1)S(1)}, bf16[2,144,768]{2,1,0:T(8,128)(2,1)S(1)}, bf16[2,144,768]{2,1,0:T(8,128)(2,1)S(1)}) custom-call(s32[4]{0:T(128)S(1)} %pad_add_fusion.where_ref.refs_0_, f32[4,1,768]{2,1,0:T(1,128)S(1)} %bitcast.19, ...), custom_call_target="tpu_custom_call" | custom-call | tf_op jit(solution)/shard_map/experts/pallas_call | solution.py:33
  107.6 1.8 %collective-permute-start.28 = (bf16[4,144,768]{2,1,0:T(8,128)(2,1)S(1)}, bf16[4,144,768]{2,1,0:T(8,128)(2,1)S(1)}, u32[]{:S(2)}, u32[]{:S(2)}) collective-permute-start(bf16[4,144,768]{2,1,0:T(8,128)(2,1)S(1)} %get-tuple-element.147), channel_id=1, source_target_pairs={{0,8},{8,0},{1,9},{9,1},{2,10},{10,2},{3,11},{11,3},{4,12},{12,4},... | collective-permute-start | bytes 2654216 | tf_op jit(solution)/shard_map/ppermute | solution.py:354
  110.2 2.4 %collective-permute-start.26 = (bf16[2,144,768]{2,1,0:T(8,128)(2,1)S(1)}, bf16[2,144,768]{2,1,0:T(8,128)(2,1)S(1)}, u32[]{:S(2)}, u32[]{:S(2)}) collective-permute-start(bf16[2,144,768]{2,1,0:T(8,128)(2,1)S(1)} %get-tuple-element.145), channel_id=1, source_target_pairs={{0,3},{1,0},{2,1},{3,2},{4,7},{5,4},{6,5},{7,6},{8,11},{9,8},{10,9... | collective-permute-start | bytes 1327112 | tf_op jit(solution)/shard_map/ppermute | solution.py:336
  112.6 1.2 collective-permute-start.27
  113.8 9.0 %collective-permute-done.25.refs_3_ = bf16[2,144,768]{2,1,0:T(8,128)(2,1)S(1)} collective-permute-done((bf16[2,144,768]{2,1,0:T(8,128)(2,1)S(1)}, bf16[2,144,768]{2,1,0:T(8,128)(2,1)S(1)}, u32[]{:S(2)}, u32[]{:S(2)}) %collective-permute-start.25) | collective-permute-done | bytes 442400 | tf_op jit(solution)/shard_map/ppermute | solution.py:336
  122.8 2.0 %collective-permute-done.26.refs_4_ = bf16[2,144,768]{2,1,0:T(8,128)(2,1)S(1)} collective-permute-done((bf16[2,144,768]{2,1,0:T(8,128)(2,1)S(1)}, bf16[2,144,768]{2,1,0:T(8,128)(2,1)S(1)}, u32[]{:S(2)}, u32[]{:S(2)}) %collective-permute-start.26) | collective-permute-done | bytes 442400 | tf_op jit(solution)/shard_map/ppermute | solution.py:336
  124.8 3.3 %collective-permute-done.27.refs_5_ = bf16[2,144,768]{2,1,0:T(8,128)(2,1)S(1)} collective-permute-done((bf16[2,144,768]{2,1,0:T(8,128)(2,1)S(1)}, bf16[2,144,768]{2,1,0:T(8,128)(2,1)S(1)}, u32[]{:S(2)}, u32[]{:S(2)}) %collective-permute-start.27) | collective-permute-done | bytes 442400 | tf_op jit(solution)/shard_map/ppermute | solution.py:336
  128.8 1.3 collective-permute-start.29
  130.0 2.6 %collective-permute-start.30 = (bf16[144,768]{1,0:T(8,128)(2,1)S(1)}, bf16[144,768]{1,0:T(8,128)(2,1)S(1)}, u32[]{:S(2)}, u32[]{:S(2)}) collective-permute-start(bf16[144,768]{1,0:T(8,128)(2,1)S(1)} %get-tuple-element.155), channel_id=1, source_target_pairs={{0,3},{1,0},{2,1},{3,2},{4,7},{5,4},{6,5},{7,6},{8,11},{9,8},{10,9... | collective-permute-start | bytes 663560 | tf_op jit(solution)/shard_map/ppermute | solution.py:336
  132.6 1.2 collective-permute-start.31
  134.6 1.5 collective-permute-start.33
  136.3 3.8 %collective-permute-done.31.refs_3_ = bf16[144,768]{1,0:T(8,128)(2,1)S(1)} collective-permute-done((bf16[144,768]{1,0:T(8,128)(2,1)S(1)}, bf16[144,768]{1,0:T(8,128)(2,1)S(1)}, u32[]{:S(2)}, u32[]{:S(2)}) %collective-permute-start.31) | collective-permute-done | bytes 221216 | tf_op jit(solution)/shard_map/ppermute | solution.py:336
  140.1 1.7 %collective-permute-done.33.refs_4_ = bf16[144,768]{1,0:T(8,128)(2,1)S(1)} collective-permute-done((bf16[144,768]{1,0:T(8,128)(2,1)S(1)}, bf16[144,768]{1,0:T(8,128)(2,1)S(1)}, u32[]{:S(2)}, u32[]{:S(2)}) %collective-permute-start.33) | collective-permute-done | bytes 221216 | tf_op jit(solution)/shard_map/ppermute | solution.py:350
  142.0 2.4 %collective-permute-start.34 = (bf16[72,768]{1,0:T(8,128)(2,1)S(1)}, bf16[72,768]{1,0:T(8,128)(2,1)S(1)}, u32[]{:S(2)}, u32[]{:S(2)}) collective-permute-start(bf16[72,768]{1,0:T(8,128)(2,1)S(1)} %get-tuple-element.164), channel_id=1, source_target_pairs={{0,32},{32,64},{64,96},{96,0},{1,33},{33,65},{65,97},{97,1},{2,34}... | collective-permute-start | bytes 331784 | tf_op jit(solution)/shard_map/ppermute | solution.py:336
  144.4 1.8 %collective-permute-start.35 = (bf16[72,768]{1,0:T(8,128)(2,1)S(1)}, bf16[72,768]{1,0:T(8,128)(2,1)S(1)}, u32[]{:S(2)}, u32[]{:S(2)}) collective-permute-start(bf16[72,768]{1,0:T(8,128)(2,1)S(1)} %get-tuple-element.165), channel_id=1, source_target_pairs={{0,96},{32,0},{64,32},{96,64},{1,97},{33,1},{65,33},{97,65},{2,98}... | collective-permute-start | bytes 331784 | tf_op jit(solution)/shard_map/ppermute | solution.py:336
  146.2 6.9 %collective-permute-start.36 = (bf16[72,768]{1,0:T(8,128)(2,1)S(1)}, bf16[72,768]{1,0:T(8,128)(2,1)S(1)}, u32[]{:S(2)}, u32[]{:S(2)}) collective-permute-start(bf16[72,768]{1,0:T(8,128)(2,1)S(1)} %get-tuple-element.166), channel_id=1, source_target_pairs={{0,64},{32,96},{64,0},{96,32},{1,65},{33,97},{65,1},{97,33},{2,66}... | collective-permute-start | bytes 331784 | tf_op jit(solution)/shard_map/ppermute | solution.py:336
  153.2 5.0 %collective-permute-done.36.refs_3_ = bf16[72,768]{1,0:T(8,128)(2,1)S(1)} collective-permute-done((bf16[72,768]{1,0:T(8,128)(2,1)S(1)}, bf16[72,768]{1,0:T(8,128)(2,1)S(1)}, u32[]{:S(2)}, u32[]{:S(2)}) %collective-permute-start.36) | collective-permute-done | bytes 110624 | tf_op jit(solution)/shard_map/ppermute | solution.py:336
  158.2 1.6 mix.1
  (58 shorter events, 8.6 us)
Async XLA Ops:
  0.0 41.9 %copy-start.2 = (bf16[512,3072]{1,0:T(8,128)(2,1)S(1)}, bf16[512,3072]{1,0:T(8,128)(2,1)}, u32[]{:S(2)}) copy-start(bf16[512,3072]{1,0:T(8,128)(2,1)} %refs_5_.1) | copy-start | bytes 9437188
  0.0 18.9 %collective-permute-start.3 = (bf16[3072,512]{1,0:T(8,128)(2,1)}, bf16[3072,512]{1,0:T(8,128)(2,1)}, u32[]{:S(2)}, u32[]{:S(2)}) collective-permute-start(bf16[3072,512]{1,0:T(8,128)(2,1)} %refs_3_.1), channel_id=1, source_target_pairs={{0,4},{4,0},{1,5},{5,1},{2,6},{6,2},{3,7},{7,3},{8,12},{12,8},{9,1... | collective-permute-start | bytes 9437192 | tf_op jit(solution)/shard_map/ppermute | solution.py:358
  1.6 10.5 %collective-permute-start = (bf16[2,128,128]{2,1,0:T(8,128)(2,1)}, bf16[2,128,128]{2,1,0:T(8,128)(2,1)S(1)}, u32[]{:S(2)}, u32[]{:S(2)}) collective-permute-start(bf16[2,128,128]{2,1,0:T(8,128)(2,1)} %get-tuple-element.168), channel_id=1, source_target_pairs={{0,32},{32,64},{64,96},{96,0},{1,33},{33,65},{65,97},{97,1},{2,34}... | collective-permute-start | bytes 196616 | tf_op jit(solution)/shard_map/ppermute | solution.py:336
  4.9 7.2 %collective-permute-start.1 = (bf16[2,128,128]{2,1,0:T(8,128)(2,1)}, bf16[2,128,128]{2,1,0:T(8,128)(2,1)S(1)}, u32[]{:S(2)}, u32[]{:S(2)}) collective-permute-start(bf16[2,128,128]{2,1,0:T(8,128)(2,1)} %get-tuple-element.169), channel_id=1, source_target_pairs={{0,96},{32,0},{64,32},{96,64},{1,97},{33,1},{65,33},{97,65},{2,98}... | collective-permute-start | bytes 196616 | tf_op jit(solution)/shard_map/ppermute | solution.py:336
  7.0 11.2 %collective-permute-start.2 = (bf16[2,128,128]{2,1,0:T(8,128)(2,1)S(1)}, bf16[2,128,128]{2,1,0:T(8,128)(2,1)S(1)}, u32[]{:S(2)}, u32[]{:S(2)}) collective-permute-start(bf16[2,128,128]{2,1,0:T(8,128)(2,1)S(1)} %get-tuple-element.167), channel_id=1, source_target_pairs={{0,64},{32,96},{64,0},{96,32},{1,65},{33,97},{65,1},{97,33},{2,66}... | collective-permute-start | bytes 196616 | tf_op jit(solution)/shard_map/ppermute | solution.py:336
  19.0 11.0 %collective-permute-start.7 = (bf16[3072,512]{1,0:T(8,128)(2,1)}, bf16[3072,512]{1,0:T(8,128)(2,1)S(1)}, u32[]{:S(2)}, u32[]{:S(2)}) collective-permute-start(bf16[3072,512]{1,0:T(8,128)(2,1)} %refs_4_.1), channel_id=1, source_target_pairs={{0,4},{4,0},{1,5},{5,1},{2,6},{6,2},{3,7},{7,3},{8,12},{12,8},{9,1... | collective-permute-start | bytes 9437192 | tf_op jit(solution)/shard_map/ppermute | solution.py:358
  19.1 7.7 %collective-permute-start.4 = (bf16[2,512,128]{2,1,0:T(8,128)(2,1)S(1)}, bf16[2,512,128]{2,1,0:T(8,128)(2,1)S(1)}, u32[]{:S(2)}, u32[]{:S(2)}) collective-permute-start(bf16[2,512,128]{2,1,0:T(8,128)(2,1)S(1)} %get-tuple-element.94.refs_0_), channel_id=1, source_target_pairs={{0,4},{4,0},{1,5},{5,1},{2,6},{6,2},{3,7},{7,3},{8,12},{12,8},{9,1... | collective-permute-start | bytes 786440 | tf_op jit(solution)/shard_map/ppermute | solution.py:358
  19.5 10.3 %collective-permute-start.5 = (bf16[2,512,128]{2,1,0:T(8,128)(2,1)S(1)}, bf16[2,512,128]{2,1,0:T(8,128)(2,1)S(1)}, u32[]{:S(2)}, u32[]{:S(2)}) collective-permute-start(bf16[2,512,128]{2,1,0:T(8,128)(2,1)S(1)} %get-tuple-element.98), channel_id=1, source_target_pairs={{0,8},{8,16},{16,24},{24,0},{1,9},{9,17},{17,25},{25,1},{2,10},{10... | collective-permute-start | bytes 786440 | tf_op jit(solution)/shard_map/ppermute | solution.py:336
  21.1 8.8 %collective-permute-start.6 = (bf16[2,512,128]{2,1,0:T(8,128)(2,1)S(1)}, bf16[2,512,128]{2,1,0:T(8,128)(2,1)S(1)}, u32[]{:S(2)}, u32[]{:S(2)}) collective-permute-start(bf16[2,512,128]{2,1,0:T(8,128)(2,1)S(1)} %get-tuple-element.99), channel_id=1, source_target_pairs={{0,24},{8,0},{16,8},{24,16},{1,25},{9,1},{17,9},{25,17},{2,26},{10... | collective-permute-start | bytes 786440 | tf_op jit(solution)/shard_map/ppermute | solution.py:336
  22.8 0.9 copy-start.3
  23.7 0.9 copy-start.4
  24.6 0.7 copy-start.6
  25.3 0.7 copy-start.7
  29.9 2.7 %collective-permute-start.8 = (bf16[2,512,128]{2,1,0:T(8,128)(2,1)S(1)}, bf16[2,512,128]{2,1,0:T(8,128)(2,1)S(1)}, u32[]{:S(2)}, u32[]{:S(2)}) collective-permute-start(bf16[2,512,128]{2,1,0:T(8,128)(2,1)S(1)} %collective-permute-done.5.refs_0_), channel_id=1, source_target_pairs={{0,4},{4,0},{1,5},{5,1},{2,6},{6,2},{3,7},{7,3},{8,12},{12,8},{9,1... | collective-permute-start | bytes 786440 | tf_op jit(solution)/shard_map/ppermute | solution.py:358
  30.0 2.6 %collective-permute-start.9 = (bf16[2,512,128]{2,1,0:T(8,128)(2,1)S(1)}, bf16[2,512,128]{2,1,0:T(8,128)(2,1)S(1)}, u32[]{:S(2)}, u32[]{:S(2)}) collective-permute-start(bf16[2,512,128]{2,1,0:T(8,128)(2,1)S(1)} %collective-permute-done.6.refs_1_), channel_id=1, source_target_pairs={{0,4},{4,0},{1,5},{5,1},{2,6},{6,2},{3,7},{7,3},{8,12},{12,8},{9,1... | collective-permute-start | bytes 786440 | tf_op jit(solution)/shard_map/ppermute | solution.py:358
  30.5 9.8 %collective-permute-start.10 = (bf16[2,512,128]{2,1,0:T(8,128)(2,1)S(1)}, bf16[2,512,128]{2,1,0:T(8,128)(2,1)S(1)}, u32[]{:S(2)}, u32[]{:S(2)}) collective-permute-start(bf16[2,512,128]{2,1,0:T(8,128)(2,1)S(1)} %get-tuple-element.110), channel_id=1, source_target_pairs={{0,16},{8,24},{16,0},{24,8},{1,17},{9,25},{17,1},{25,9},{2,18},{10... | collective-permute-start | bytes 786440 | tf_op jit(solution)/shard_map/ppermute | solution.py:336
  32.6 47.1 %copy-start.1 = (bf16[3072,512]{1,0:T(8,128)(2,1)S(1)}, bf16[3072,512]{1,0:T(8,128)(2,1)}, u32[]{:S(2)}) copy-start(bf16[3072,512]{1,0:T(8,128)(2,1)} %refs_4_.1) | copy-start | bytes 9437188
  38.3 41.4 %copy-start = (bf16[3072,512]{1,0:T(8,128)(2,1)S(1)}, bf16[3072,512]{1,0:T(8,128)(2,1)}, u32[]{:S(2)}) copy-start(bf16[3072,512]{1,0:T(8,128)(2,1)} %refs_3_.1) | copy-start | bytes 9437188
  38.3 41.4 %copy-start.5 = (f32[3072]{0:T(1024)S(1)}, f32[3072]{0:T(1024)}, u32[]{:S(2)}) copy-start(f32[3072]{0:T(1024)} %param.18) | copy-start | bytes 36868
  40.3 1.5 collective-permute-start.11
  41.9 18.8 %collective-permute-start.15 = (bf16[512,3072]{1,0:T(8,128)(2,1)S(1)}, bf16[512,3072]{1,0:T(8,128)(2,1)S(1)}, u32[]{:S(2)}, u32[]{:S(2)}) collective-permute-start(bf16[512,3072]{1,0:T(8,128)(2,1)S(1)} %copy-done.2), channel_id=1, source_target_pairs={{0,4},{4,0},{1,5},{5,1},{2,6},{6,2},{3,7},{7,3},{8,12},{12,8},{9,1... | collective-permute-start | bytes 9437192 | tf_op jit(solution)/shard_map/ppermute | solution.py:358
  45.2 7.9 %collective-permute-start.12 = (bf16[72,768]{1,0:T(8,128)(2,1)S(1)}, bf16[72,768]{1,0:T(8,128)(2,1)S(1)}, u32[]{:S(2)}, u32[]{:S(2)}) collective-permute-start(bf16[72,768]{1,0:T(8,128)(2,1)S(1)} %get-tuple-element.117), channel_id=1, source_target_pairs={{0,32},{32,64},{64,96},{96,0},{1,33},{33,65},{65,97},{97,1},{2,34}... | collective-permute-start | bytes 331784 | tf_op jit(solution)/shard_map/ppermute | solution.py:336
  45.4 10.7 %collective-permute-start.13 = (bf16[72,768]{1,0:T(8,128)(2,1)S(1)}, bf16[72,768]{1,0:T(8,128)(2,1)S(1)}, u32[]{:S(2)}, u32[]{:S(2)}) collective-permute-start(bf16[72,768]{1,0:T(8,128)(2,1)S(1)} %get-tuple-element.118), channel_id=1, source_target_pairs={{0,96},{32,0},{64,32},{96,64},{1,97},{33,1},{65,33},{97,65},{2,98}... | collective-permute-start | bytes 331784 | tf_op jit(solution)/shard_map/ppermute | solution.py:336
  49.6 11.1 %collective-permute-start.14 = (bf16[72,768]{1,0:T(8,128)(2,1)S(1)}, bf16[72,768]{1,0:T(8,128)(2,1)S(1)}, u32[]{:S(2)}, u32[]{:S(2)}) collective-permute-start(bf16[72,768]{1,0:T(8,128)(2,1)S(1)} %get-tuple-element.119), channel_id=1, source_target_pairs={{0,64},{32,96},{64,0},{96,32},{1,65},{33,97},{65,1},{97,33},{2,66}... | collective-permute-start | bytes 331784 | tf_op jit(solution)/shard_map/ppermute | solution.py:336
  60.7 7.6 %collective-permute-start.19 = (bf16[144,768]{1,0:T(8,128)(2,1)S(1)}, bf16[144,768]{1,0:T(8,128)(2,1)S(1)}, u32[]{:S(2)}, u32[]{:S(2)}) collective-permute-start(bf16[144,768]{1,0:T(8,128)(2,1)S(1)} %get-tuple-element.128), channel_id=1, source_target_pairs={{0,24},{8,16},{16,8},{24,0},{1,25},{9,17},{17,9},{25,1},{2,26},{10... | collective-permute-start | bytes 663560 | tf_op jit(solution)/shard_map/ppermute | solution.py:350
  62.8 8.5 %collective-permute-start.16 = (bf16[144,768]{1,0:T(8,128)(2,1)S(1)}, bf16[144,768]{1,0:T(8,128)(2,1)S(1)}, u32[]{:S(2)}, u32[]{:S(2)}) collective-permute-start(bf16[144,768]{1,0:T(8,128)(2,1)S(1)} %get-tuple-element.127), channel_id=1, source_target_pairs={{0,1},{1,2},{2,3},{3,0},{4,5},{5,6},{6,7},{7,4},{8,9},{9,10},{10,1... | collective-permute-start | bytes 663560 | tf_op jit(solution)/shard_map/ppermute | solution.py:336
  64.3 9.8 %collective-permute-start.17 = (bf16[144,768]{1,0:T(8,128)(2,1)S(1)}, bf16[144,768]{1,0:T(8,128)(2,1)S(1)}, u32[]{:S(2)}, u32[]{:S(2)}) collective-permute-start(bf16[144,768]{1,0:T(8,128)(2,1)S(1)} %get-tuple-element.127), channel_id=1, source_target_pairs={{0,3},{1,0},{2,1},{3,2},{4,7},{5,4},{6,5},{7,6},{8,11},{9,8},{10,9... | collective-permute-start | bytes 663560 | tf_op jit(solution)/shard_map/ppermute | solution.py:336
  66.0 9.7 %collective-permute-start.18 = (bf16[144,768]{1,0:T(8,128)(2,1)S(1)}, bf16[144,768]{1,0:T(8,128)(2,1)S(1)}, u32[]{:S(2)}, u32[]{:S(2)}) collective-permute-start(bf16[144,768]{1,0:T(8,128)(2,1)S(1)} %get-tuple-element.127), channel_id=1, source_target_pairs={{0,2},{1,3},{2,0},{3,1},{4,6},{5,7},{6,4},{7,5},{8,10},{9,11},{10,... | collective-permute-start | bytes 663560 | tf_op jit(solution)/shard_map/ppermute | solution.py:336
  68.3 7.5 %collective-permute-start.20 = (bf16[144,768]{1,0:T(8,128)(2,1)S(1)}, bf16[144,768]{1,0:T(8,128)(2,1)S(1)}, u32[]{:S(2)}, u32[]{:S(2)}) collective-permute-start(bf16[144,768]{1,0:T(8,128)(2,1)S(1)} %collective-permute-done.19), channel_id=1, source_target_pairs={{0,8},{8,0},{1,9},{9,1},{2,10},{10,2},{3,11},{11,3},{4,12},{12,4},... | collective-permute-start | bytes 663560 | tf_op jit(solution)/shard_map/ppermute | solution.py:354
  75.9 20.8 %collective-permute-start.24 = (bf16[4,144,768]{2,1,0:T(8,128)(2,1)S(1)}, bf16[4,144,768]{2,1,0:T(8,128)(2,1)S(1)}, u32[]{:S(2)}, u32[]{:S(2)}) collective-permute-start(bf16[4,144,768]{2,1,0:T(8,128)(2,1)S(1)} %pad_maximum_fusion.refs_2_), channel_id=1, source_target_pairs={{0,8},{8,0},{1,9},{9,1},{2,10},{10,2},{3,11},{11,3},{4,12},{12,4},... | collective-permute-start | bytes 2654216 | tf_op jit(solution)/shard_map/ppermute | solution.py:354
  76.1 20.6 %collective-permute-start.21 = (bf16[2,144,768]{2,1,0:T(8,128)(2,1)S(1)}, bf16[2,144,768]{2,1,0:T(8,128)(2,1)S(1)}, u32[]{:S(2)}, u32[]{:S(2)}) collective-permute-start(bf16[2,144,768]{2,1,0:T(8,128)(2,1)S(1)} %pad_maximum_fusion.1.refs_3_), channel_id=1, source_target_pairs={{0,1},{1,2},{2,3},{3,0},{4,5},{5,6},{6,7},{7,4},{8,9},{9,10},{10,1... | collective-permute-start | bytes 1327112 | tf_op jit(solution)/shard_map/ppermute | solution.py:336
  77.3 19.4 %collective-permute-start.22 = (bf16[2,144,768]{2,1,0:T(8,128)(2,1)S(1)}, bf16[2,144,768]{2,1,0:T(8,128)(2,1)S(1)}, u32[]{:S(2)}, u32[]{:S(2)}) collective-permute-start(bf16[2,144,768]{2,1,0:T(8,128)(2,1)S(1)} %pad_maximum_fusion.1.refs_3_), channel_id=1, source_target_pairs={{0,3},{1,0},{2,1},{3,2},{4,7},{5,4},{6,5},{7,6},{8,11},{9,8},{10,9... | collective-permute-start | bytes 1327112 | tf_op jit(solution)/shard_map/ppermute | solution.py:336
  79.4 17.3 %collective-permute-start.23 = (bf16[2,144,768]{2,1,0:T(8,128)(2,1)S(1)}, bf16[2,144,768]{2,1,0:T(8,128)(2,1)S(1)}, u32[]{:S(2)}, u32[]{:S(2)}) collective-permute-start(bf16[2,144,768]{2,1,0:T(8,128)(2,1)S(1)} %pad_maximum_fusion.1.refs_3_), channel_id=1, source_target_pairs={{0,2},{1,3},{2,0},{3,1},{4,6},{5,7},{6,4},{7,5},{8,10},{9,11},{10,... | collective-permute-start | bytes 1327112 | tf_op jit(solution)/shard_map/ppermute | solution.py:336
  107.6 20.5 %collective-permute-start.28 = (bf16[4,144,768]{2,1,0:T(8,128)(2,1)S(1)}, bf16[4,144,768]{2,1,0:T(8,128)(2,1)S(1)}, u32[]{:S(2)}, u32[]{:S(2)}) collective-permute-start(bf16[4,144,768]{2,1,0:T(8,128)(2,1)S(1)} %get-tuple-element.147), channel_id=1, source_target_pairs={{0,8},{8,0},{1,9},{9,1},{2,10},{10,2},{3,11},{11,3},{4,12},{12,4},... | collective-permute-start | bytes 2654216 | tf_op jit(solution)/shard_map/ppermute | solution.py:354
  109.4 13.4 %collective-permute-start.25 = (bf16[2,144,768]{2,1,0:T(8,128)(2,1)S(1)}, bf16[2,144,768]{2,1,0:T(8,128)(2,1)S(1)}, u32[]{:S(2)}, u32[]{:S(2)}) collective-permute-start(bf16[2,144,768]{2,1,0:T(8,128)(2,1)S(1)} %get-tuple-element.144), channel_id=1, source_target_pairs={{0,1},{1,2},{2,3},{3,0},{4,5},{5,6},{6,7},{7,4},{8,9},{9,10},{10,1... | collective-permute-start | bytes 1327112 | tf_op jit(solution)/shard_map/ppermute | solution.py:336
  110.2 14.6 %collective-permute-start.26 = (bf16[2,144,768]{2,1,0:T(8,128)(2,1)S(1)}, bf16[2,144,768]{2,1,0:T(8,128)(2,1)S(1)}, u32[]{:S(2)}, u32[]{:S(2)}) collective-permute-start(bf16[2,144,768]{2,1,0:T(8,128)(2,1)S(1)} %get-tuple-element.145), channel_id=1, source_target_pairs={{0,3},{1,0},{2,1},{3,2},{4,7},{5,4},{6,5},{7,6},{8,11},{9,8},{10,9... | collective-permute-start | bytes 1327112 | tf_op jit(solution)/shard_map/ppermute | solution.py:336
  112.6 15.5 %collective-permute-start.27 = (bf16[2,144,768]{2,1,0:T(8,128)(2,1)S(1)}, bf16[2,144,768]{2,1,0:T(8,128)(2,1)S(1)}, u32[]{:S(2)}, u32[]{:S(2)}) collective-permute-start(bf16[2,144,768]{2,1,0:T(8,128)(2,1)S(1)} %get-tuple-element.146), channel_id=1, source_target_pairs={{0,2},{1,3},{2,0},{3,1},{4,6},{5,7},{6,4},{7,5},{8,10},{9,11},{10,... | collective-permute-start | bytes 1327112 | tf_op jit(solution)/shard_map/ppermute | solution.py:336
  128.5 6.0 %collective-permute-start.32 = (bf16[144,768]{1,0:T(8,128)(2,1)S(1)}, bf16[144,768]{1,0:T(8,128)(2,1)S(1)}, u32[]{:S(2)}, u32[]{:S(2)}) collective-permute-start(bf16[144,768]{1,0:T(8,128)(2,1)S(1)} %get-tuple-element.158), channel_id=1, source_target_pairs={{0,8},{8,0},{1,9},{9,1},{2,10},{10,2},{3,11},{11,3},{4,12},{12,4},... | collective-permute-start | bytes 663560 | tf_op jit(solution)/shard_map/ppermute | solution.py:354
  128.8 7.5 %collective-permute-start.29 = (bf16[144,768]{1,0:T(8,128)(2,1)S(1)}, bf16[144,768]{1,0:T(8,128)(2,1)S(1)}, u32[]{:S(2)}, u32[]{:S(2)}) collective-permute-start(bf16[144,768]{1,0:T(8,128)(2,1)S(1)} %get-tuple-element.154), channel_id=1, source_target_pairs={{0,1},{1,2},{2,3},{3,0},{4,5},{5,6},{6,7},{7,4},{8,9},{9,10},{10,1... | collective-permute-start | bytes 663560 | tf_op jit(solution)/shard_map/ppermute | solution.py:336
  130.0 6.3 %collective-permute-start.30 = (bf16[144,768]{1,0:T(8,128)(2,1)S(1)}, bf16[144,768]{1,0:T(8,128)(2,1)S(1)}, u32[]{:S(2)}, u32[]{:S(2)}) collective-permute-start(bf16[144,768]{1,0:T(8,128)(2,1)S(1)} %get-tuple-element.155), channel_id=1, source_target_pairs={{0,3},{1,0},{2,1},{3,2},{4,7},{5,4},{6,5},{7,6},{8,11},{9,8},{10,9... | collective-permute-start | bytes 663560 | tf_op jit(solution)/shard_map/ppermute | solution.py:336
  132.6 7.5 %collective-permute-start.31 = (bf16[144,768]{1,0:T(8,128)(2,1)S(1)}, bf16[144,768]{1,0:T(8,128)(2,1)S(1)}, u32[]{:S(2)}, u32[]{:S(2)}) collective-permute-start(bf16[144,768]{1,0:T(8,128)(2,1)S(1)} %get-tuple-element.156), channel_id=1, source_target_pairs={{0,2},{1,3},{2,0},{3,1},{4,6},{5,7},{6,4},{7,5},{8,10},{9,11},{10,... | collective-permute-start | bytes 663560 | tf_op jit(solution)/shard_map/ppermute | solution.py:336
  134.6 7.2 %collective-permute-start.33 = (bf16[144,768]{1,0:T(8,128)(2,1)S(1)}, bf16[144,768]{1,0:T(8,128)(2,1)S(1)}, u32[]{:S(2)}, u32[]{:S(2)}) collective-permute-start(bf16[144,768]{1,0:T(8,128)(2,1)S(1)} %add_convert_fusion), channel_id=1, source_target_pairs={{0,24},{8,16},{16,8},{24,0},{1,25},{9,17},{17,9},{25,1},{2,26},{10... | collective-permute-start | bytes 663560 | tf_op jit(solution)/shard_map/ppermute | solution.py:350
  142.0 11.2 %collective-permute-start.34 = (bf16[72,768]{1,0:T(8,128)(2,1)S(1)}, bf16[72,768]{1,0:T(8,128)(2,1)S(1)}, u32[]{:S(2)}, u32[]{:S(2)}) collective-permute-start(bf16[72,768]{1,0:T(8,128)(2,1)S(1)} %get-tuple-element.164), channel_id=1, source_target_pairs={{0,32},{32,64},{64,96},{96,0},{1,33},{33,65},{65,97},{97,1},{2,34}... | collective-permute-start | bytes 331784 | tf_op jit(solution)/shard_map/ppermute | solution.py:336
  144.4 8.8 %collective-permute-start.35 = (bf16[72,768]{1,0:T(8,128)(2,1)S(1)}, bf16[72,768]{1,0:T(8,128)(2,1)S(1)}, u32[]{:S(2)}, u32[]{:S(2)}) collective-permute-start(bf16[72,768]{1,0:T(8,128)(2,1)S(1)} %get-tuple-element.165), channel_id=1, source_target_pairs={{0,96},{32,0},{64,32},{96,64},{1,97},{33,1},{65,33},{97,65},{2,98}... | collective-permute-start | bytes 331784 | tf_op jit(solution)/shard_map/ppermute | solution.py:336
  146.2 12.0 %collective-permute-start.36 = (bf16[72,768]{1,0:T(8,128)(2,1)S(1)}, bf16[72,768]{1,0:T(8,128)(2,1)S(1)}, u32[]{:S(2)}, u32[]{:S(2)}) collective-permute-start(bf16[72,768]{1,0:T(8,128)(2,1)S(1)} %get-tuple-element.166), channel_id=1, source_target_pairs={{0,64},{32,96},{64,0},{96,32},{1,65},{33,97},{65,1},{97,33},{2,66}... | collective-permute-start | bytes 331784 | tf_op jit(solution)/shard_map/ppermute | solution.py:336

commit v6 on v5

--- a/solution.py
+++ b/solution.py
@@ -302,14 +302,15 @@
 
 
 def last_sum_kernel(*refs):
-    parts, back, outs = refs[:NX], refs[NX], refs[NX + 1 :]
+    parts, (back, far), outs = refs[:NX], refs[NX : NX + 2], refs[NX + 2 :]
     total = parts[0][...].astype(f32)
     for ref in parts[1:]:
         total = total + ref[...].astype(f32)
     total = total.astype(bf16)
+    crossed = (back[...].astype(f32) + far[...].astype(f32)).astype(bf16)
     for d, out in enumerate(outs):
         out[:CAP] = total[d * CAP : (d + 1) * CAP]
-        out[CAP:] = back[d * CAP : (d + 1) * CAP, :]
+        out[CAP:] = crossed[d * CAP : (d + 1) * CAP]
 
 
 def mix_kernel(weight_ref, hid_ref, *refs):
@@ -372,6 +373,10 @@
     near, past = jnp.stack((keys, values)), jnp.stack((cache_keys, cache_values))
     from_z = turned([jnp.where(z + s < NZ, near, past) for s in SHIFTS], "zh", KV_ORDER)
     slots = EXPERTS * PAD
+    (keys, values), (cache_keys, cache_values) = lax.optimization_barrier(
+        ((keys, values), (cache_keys, cache_values))
+    )
+    near, past = jnp.stack((keys, values)), jnp.stack((cache_keys, cache_values))
     q_all, res, table, weight = call(
         prep_kernel,
         [
@@ -435,9 +440,9 @@
     *a_sums, b_own, b_far = call(
         first_sum_kernel, [rows_a] * (NX + 2), [a_own, a_far, b_all[0], *b_turned], "first_sum"
     )
-    b_sum = (b_own.astype(f32) + swap_y(b_far).astype(f32)).astype(bf16)
     moved = lax.optimization_barrier(
-        [turn(v, "x", s) for v, s in zip(a_sums[1:], SHIFTS)] + [cross(b_sum)]
+        [turn(v, "x", s) for v, s in zip(a_sums[1:], SHIFTS)]
+        + [cross(b_own), turn(b_far, ("yh", "yl"), 2)]
     )
     result = call(
         last_sum_kernel,

time: 160 us -> 161 us (level)
  waiting for transfers between devices: 62.7 us -> 66.5 us
  starting transfers between devices: 59.6 us -> 56 us
    ppermute x24 -> x25, waiting for transfers between devices: 58.3 us -> 61.6 us  [turn(): return lax.ppermute(v, axis, [(i, (i + shift) % n) for i in range(n)])]
    ppermute x24 -> x25, starting transfers between devices: 52.6 us -> 49.3 us  [turn(): return lax.ppermute(v, axis, [(i, (i + shift) % n) for i in range(n)])]
  transfers between devices with their start and end apart: 37 -> 37, of which waited for: 20 -> 19; matrix products, arithmetic and copies ran while one was open for 1% -> 1% of each run, Pallas kernels for 12% -> 12%
where the time goes in v6:
time: 161 us; the launch traced here: 160 us
  waiting for transfers between devices  66.5 us (41%)
  starting transfers between devices  56 us (35%)
  Pallas kernels  32.1 us (20%)
  local copies, waits for them, and re-layouts  3.23 us (2%)
  other arithmetic  2.03 us (1%)
    ppermute x25, waiting for transfers between devices, turn(): return lax.ppermute(v, axis, [(i, (i + shift) % n) for i in range(n)])  61.6 us
    ppermute x25, starting transfers between devices, turn(): return lax.ppermute(v, axis, [(i, (i + shift) % n) for i in range(n)])  49.3 us
    pallas_call x11, Pallas kernels, call(): pl.pallas_call(body, out_shape=out_shape, in_specs=[SM] * scalars + [VM]...  32.1 us
    ppermute x2, starting transfers between devices, cross(): return lax.ppermute(v, ('yh', 'yl'), [(i, NY - 1 - i) for i in range(NY)])  3.51 us
    ppermute x2, waiting for transfers between devices, cross(): return lax.ppermute(v, ('yh', 'yl'), [(i, NY - 1 - i) for i in range(NY)])  3.37 us
    unnamed x16, local copies, waits for them, and re-layouts  3.23 us
  transfers between devices with their start and end apart: 37, of which 19 were waited for; matrix products, arithmetic and copies ran while one was open for 1% of the time, Pallas kernels for 12%

profile of v6, /device:TPU:32, one launch (start us, length us, event | category | flops | bytes accessed | tf_op | source)
XLA Modules:
  0.0 160.2 jit_solution(7872813254024209114)
XLA Ops:
  0.0 1.0 broadcast_select_fusion
  1.0 3.3 %collective-permute-start = (bf16[2,128,128]{2,1,0:T(8,128)(2,1)S(1)}, bf16[2,128,128]{2,1,0:T(8,128)(2,1)S(1)}, u32[]{:S(2)}, u32[]{:S(2)}) collective-permute-start(bf16[2,128,128]{2,1,0:T(8,128)(2,1)S(1)} %get-tuple-element.179), channel_id=1, source_target_pairs={{0,32},{32,64},{64,96},{96,0},{1,33},{33,65},{65,97},{97,1},{2,34}... | collective-permute-start | bytes 196616 | tf_op jit(solution)/shard_map/ppermute | solution.py:337
  4.3 2.2 %collective-permute-start.1 = (bf16[2,128,128]{2,1,0:T(8,128)(2,1)S(1)}, bf16[2,128,128]{2,1,0:T(8,128)(2,1)S(1)}, u32[]{:S(2)}, u32[]{:S(2)}) collective-permute-start(bf16[2,128,128]{2,1,0:T(8,128)(2,1)S(1)} %get-tuple-element.178), channel_id=1, source_target_pairs={{0,96},{32,0},{64,32},{96,64},{1,97},{33,1},{65,33},{97,65},{2,98}... | collective-permute-start | bytes 196616 | tf_op jit(solution)/shard_map/ppermute | solution.py:337
  6.6 4.9 %collective-permute-start.2 = (bf16[2,128,128]{2,1,0:T(8,128)(2,1)S(1)}, bf16[2,128,128]{2,1,0:T(8,128)(2,1)S(1)}, u32[]{:S(2)}, u32[]{:S(2)}) collective-permute-start(bf16[2,128,128]{2,1,0:T(8,128)(2,1)S(1)} %get-tuple-element.177), channel_id=1, source_target_pairs={{0,64},{32,96},{64,0},{96,32},{1,65},{33,97},{65,1},{97,33},{2,66}... | collective-permute-start | bytes 196616 | tf_op jit(solution)/shard_map/ppermute | solution.py:337
  12.4 5.1 %collective-permute-done.2.refs_2_ = bf16[2,128,128]{2,1,0:T(8,128)(2,1)S(1)} collective-permute-done((bf16[2,128,128]{2,1,0:T(8,128)(2,1)S(1)}, bf16[2,128,128]{2,1,0:T(8,128)(2,1)S(1)}, u32[]{:S(2)}, u32[]{:S(2)}) %collective-permute-start.2) | collective-permute-done | bytes 65568 | tf_op jit(solution)/shard_map/ppermute | solution.py:337
  18.8 1.6 collective-permute-start.5
  20.3 1.7 %collective-permute-start.6 = (bf16[2,512,128]{2,1,0:T(8,128)(2,1)S(1)}, bf16[2,512,128]{2,1,0:T(8,128)(2,1)S(1)}, u32[]{:S(2)}, u32[]{:S(2)}) collective-permute-start(bf16[2,512,128]{2,1,0:T(8,128)(2,1)S(1)} %get-tuple-element.108), channel_id=1, source_target_pairs={{0,24},{8,0},{16,8},{24,16},{1,25},{9,1},{17,9},{25,17},{2,26},{10... | collective-permute-start | bytes 786440 | tf_op jit(solution)/shard_map/ppermute | solution.py:337
  22.0 0.9 copy-done.3
  26.0 3.1 %attend_own.1 = (f32[768,128]{1,0:T(8,128)S(1)}, f32[768,128]{1,0:T(8,128)S(1)}, f32[768,128]{1,0:T(8,128)S(1)}) custom-call(bf16[768,128]{1,0:T(8,128)(2,1)S(1)} %get-tuple-element.92.q_all, bf16[2,128,128]{2,1,0:T(8,128)(2,1)S(1)} %get-tuple-element.180.tract.tract_ref, bf16[2,128,128]{2,1,0:T(8,128)(2,1)S(1)} %get-tuple-element.181.cache.cache_ref, ...), custom_call_target="tpu_custom_call" | custom-call | tf_op jit(solution)/shard_map/attend_own/pallas_call | solution.py:33
  29.7 2.0 %collective-permute-start.10 = (bf16[2,512,128]{2,1,0:T(8,128)(2,1)S(1)}, bf16[2,512,128]{2,1,0:T(8,128)(2,1)S(1)}, u32[]{:S(2)}, u32[]{:S(2)}) collective-permute-start(bf16[2,512,128]{2,1,0:T(8,128)(2,1)S(1)} %get-tuple-element.119), channel_id=1, source_target_pairs={{0,16},{8,24},{16,0},{24,8},{1,17},{9,25},{17,1},{25,9},{2,18},{10... | collective-permute-start | bytes 786440 | tf_op jit(solution)/shard_map/ppermute | solution.py:337
  31.8 5.7 %attend_more.1 = (f32[768,128]{1,0:T(8,128)S(1)}, f32[768,128]{1,0:T(8,128)S(1)}, f32[768,128]{1,0:T(8,128)S(1)}) custom-call(bf16[768,128]{1,0:T(8,128)(2,1)S(1)} %get-tuple-element.92.q_all, f32[768,128]{1,0:T(8,128)S(1)} %get-tuple-element.111.m_ref, f32[768,128]{1,0:T(8,128)S(1)} %get-tuple-element.112.l_ref, f32[768,128]{1,0:T(8,128)S(1)} %get-tuple-element.113.acc_ref, ...), custom_call_target="tpu_custom_call" | custom-call | tf_op jit(solution)/shard_map/attend_more/pallas_call | solution.py:33
  37.5 2.1 %collective-permute-done.10.refs_0_ = bf16[2,512,128]{2,1,0:T(8,128)(2,1)S(1)} collective-permute-done((bf16[2,512,128]{2,1,0:T(8,128)(2,1)S(1)}, bf16[2,512,128]{2,1,0:T(8,128)(2,1)S(1)}, u32[]{:S(2)}, u32[]{:S(2)}) %collective-permute-start.10) | collective-permute-done | bytes 262176 | tf_op jit(solution)/shard_map/ppermute | solution.py:337
  39.6 1.5 collective-permute-done.11.refs_1_
  41.2 3.1 %attend.1 = (bf16[128,768]{1,0:T(8,128)(2,1)S(1)}, bf16[72,768]{1,0:T(8,128)(2,1)S(1)}, bf16[72,768]{1,0:T(8,128)(2,1)S(1)}, bf16[72,768]{1,0:T(8,128)(2,1)S(1)}, bf16[72,768]{1,0:T(8,128)(2,1)S(1)}) custom-call(bf16[768,128]{1,0:T(8,128)(2,1)S(1)} %get-tuple-element.92.q_all, bf16[128,768]{1,0:T(8,128)(2,1)S(1)} %get-tuple-element.93.res_ref, ...), custom_call_target="tpu_custom_call" | custom-call | tf_op jit(solution)/shard_map/attend/pallas_call | solution.py:33
  44.7 4.1 %collective-permute-start.13 = (bf16[72,768]{1,0:T(8,128)(2,1)S(1)}, bf16[72,768]{1,0:T(8,128)(2,1)S(1)}, u32[]{:S(2)}, u32[]{:S(2)}) collective-permute-start(bf16[72,768]{1,0:T(8,128)(2,1)S(1)} %get-tuple-element.127), channel_id=1, source_target_pairs={{0,96},{32,0},{64,32},{96,64},{1,97},{33,1},{65,33},{97,65},{2,98}... | collective-permute-start | bytes 331784 | tf_op jit(solution)/shard_map/ppermute | solution.py:337
  48.8 3.2 %collective-permute-start.14 = (bf16[72,768]{1,0:T(8,128)(2,1)S(1)}, bf16[72,768]{1,0:T(8,128)(2,1)S(1)}, u32[]{:S(2)}, u32[]{:S(2)}) collective-permute-start(bf16[72,768]{1,0:T(8,128)(2,1)S(1)} %get-tuple-element.128), channel_id=1, source_target_pairs={{0,64},{32,96},{64,0},{96,32},{1,65},{33,97},{65,1},{97,33},{2,66}... | collective-permute-start | bytes 331784 | tf_op jit(solution)/shard_map/ppermute | solution.py:337
  52.6 3.1 %collective-permute-done.13.refs_2_ = bf16[72,768]{1,0:T(8,128)(2,1)S(1)} collective-permute-done((bf16[72,768]{1,0:T(8,128)(2,1)S(1)}, bf16[72,768]{1,0:T(8,128)(2,1)S(1)}, u32[]{:S(2)}, u32[]{:S(2)}) %collective-permute-start.13) | collective-permute-done | bytes 110624 | tf_op jit(solution)/shard_map/ppermute | solution.py:337
  55.8 4.7 %collective-permute-done.14.refs_3_ = bf16[72,768]{1,0:T(8,128)(2,1)S(1)} collective-permute-done((bf16[72,768]{1,0:T(8,128)(2,1)S(1)}, bf16[72,768]{1,0:T(8,128)(2,1)S(1)}, u32[]{:S(2)}, u32[]{:S(2)}) %collective-permute-start.14) | collective-permute-done | bytes 110624 | tf_op jit(solution)/shard_map/ppermute | solution.py:337
  60.6 2.1 %collective-permute-start.19 = (bf16[144,768]{1,0:T(8,128)(2,1)S(1)}, bf16[144,768]{1,0:T(8,128)(2,1)S(1)}, u32[]{:S(2)}, u32[]{:S(2)}) collective-permute-start(bf16[144,768]{1,0:T(8,128)(2,1)S(1)} %get-tuple-element.137), channel_id=1, source_target_pairs={{0,24},{8,16},{16,8},{24,0},{1,25},{9,17},{17,9},{25,1},{2,26},{10... | collective-permute-start | bytes 663560 | tf_op jit(solution)/shard_map/ppermute | solution.py:351
  62.6 1.5 collective-permute-start.16
  64.1 1.8 %collective-permute-start.17 = (bf16[144,768]{1,0:T(8,128)(2,1)S(1)}, bf16[144,768]{1,0:T(8,128)(2,1)S(1)}, u32[]{:S(2)}, u32[]{:S(2)}) collective-permute-start(bf16[144,768]{1,0:T(8,128)(2,1)S(1)} %get-tuple-element.136), channel_id=1, source_target_pairs={{0,3},{1,0},{2,1},{3,2},{4,7},{5,4},{6,5},{7,6},{8,11},{9,8},{10,9... | collective-permute-start | bytes 663560 | tf_op jit(solution)/shard_map/ppermute | solution.py:337
  65.9 1.8 %collective-permute-start.18 = (bf16[144,768]{1,0:T(8,128)(2,1)S(1)}, bf16[144,768]{1,0:T(8,128)(2,1)S(1)}, u32[]{:S(2)}, u32[]{:S(2)}) collective-permute-start(bf16[144,768]{1,0:T(8,128)(2,1)S(1)} %get-tuple-element.136), channel_id=1, source_target_pairs={{0,2},{1,3},{2,0},{3,1},{4,6},{5,7},{6,4},{7,5},{8,10},{9,11},{10,... | collective-permute-start | bytes 663560 | tf_op jit(solution)/shard_map/ppermute | solution.py:337
  67.7 1.1 collective-permute-done.19
  68.8 2.4 %collective-permute-done.16 = bf16[144,768]{1,0:T(8,128)(2,1)S(1)} collective-permute-done((bf16[144,768]{1,0:T(8,128)(2,1)S(1)}, bf16[144,768]{1,0:T(8,128)(2,1)S(1)}, u32[]{:S(2)}, u32[]{:S(2)}) %collective-permute-start.16) | collective-permute-done | bytes 221216 | tf_op jit(solution)/shard_map/ppermute | solution.py:337
  71.2 3.3 %collective-permute-done.17 = bf16[144,768]{1,0:T(8,128)(2,1)S(1)} collective-permute-done((bf16[144,768]{1,0:T(8,128)(2,1)S(1)}, bf16[144,768]{1,0:T(8,128)(2,1)S(1)}, u32[]{:S(2)}, u32[]{:S(2)}) %collective-permute-start.17) | collective-permute-done | bytes 221216 | tf_op jit(solution)/shard_map/ppermute | solution.py:337
  74.6 1.7 %collective-permute-done.18 = bf16[144,768]{1,0:T(8,128)(2,1)S(1)} collective-permute-done((bf16[144,768]{1,0:T(8,128)(2,1)S(1)}, bf16[144,768]{1,0:T(8,128)(2,1)S(1)}, u32[]{:S(2)}, u32[]{:S(2)}) %collective-permute-start.18) | collective-permute-done | bytes 221216 | tf_op jit(solution)/shard_map/ppermute | solution.py:337
  76.5 1.2 collective-permute-start.21
  77.7 2.1 %collective-permute-start.22 = (bf16[2,144,768]{2,1,0:T(8,128)(2,1)S(1)}, bf16[2,144,768]{2,1,0:T(8,128)(2,1)S(1)}, u32[]{:S(2)}, u32[]{:S(2)}) collective-permute-start(bf16[2,144,768]{2,1,0:T(8,128)(2,1)S(1)} %pad_maximum_fusion.1.refs_3_), channel_id=1, source_target_pairs={{0,3},{1,0},{2,1},{3,2},{4,7},{5,4},{6,5},{7,6},{8,11},{9,8},{10,9... | collective-permute-start | bytes 1327112 | tf_op jit(solution)/shard_map/ppermute | solution.py:337
  80.5 5.7 %experts_own.1 = (bf16[4,144,768]{2,1,0:T(8,128)(2,1)S(1)}, bf16[2,3072,512]{2,1,0:T(8,128)(2,1)S(1)}, bf16[2,3072,512]{2,1,0:T(8,128)(2,1)S(1)}, bf16[1024,3072]{1,0:T(8,128)(2,1)S(1)}) custom-call(s32[4]{0:T(128)S(1)} %pad_add_fusion.where_ref.refs_0_, f32[4,1,768]{2,1,0:T(1,128)S(1)} %bitcast.22, bf16[4,144,768]{2,1,0:T(8,128)(2,1)S(1)} %pad_maximum_fusion.refs_2_, ...), custom_call_target="tpu_custom_call" | custom-call | tf_op jit(solution)/shard_map/experts_own/pallas_call | solution.py:33
  86.2 11.6 %collective-permute-done.21.refs_4_ = bf16[2,144,768]{2,1,0:T(8,128)(2,1)S(1)} collective-permute-done((bf16[2,144,768]{2,1,0:T(8,128)(2,1)S(1)}, bf16[2,144,768]{2,1,0:T(8,128)(2,1)S(1)}, u32[]{:S(2)}, u32[]{:S(2)}) %collective-permute-start.21) | collective-permute-done | bytes 442400 | tf_op jit(solution)/shard_map/ppermute | solution.py:337
  97.8 10.9 %experts.1 = (bf16[4,144,768]{2,1,0:T(8,128)(2,1)S(1)}, bf16[2,144,768]{2,1,0:T(8,128)(2,1)S(1)}, bf16[2,144,768]{2,1,0:T(8,128)(2,1)S(1)}, bf16[2,144,768]{2,1,0:T(8,128)(2,1)S(1)}, bf16[2,144,768]{2,1,0:T(8,128)(2,1)S(1)}) custom-call(s32[4]{0:T(128)S(1)} %pad_add_fusion.where_ref.refs_0_, f32[4,1,768]{2,1,0:T(1,128)S(1)} %bitcast.23, ...), custom_call_target="tpu_custom_call" | custom-call | tf_op jit(solution)/shard_map/experts/pallas_call | solution.py:33
  108.7 1.8 %collective-permute-start.28 = (bf16[4,144,768]{2,1,0:T(8,128)(2,1)S(1)}, bf16[4,144,768]{2,1,0:T(8,128)(2,1)S(1)}, u32[]{:S(2)}, u32[]{:S(2)}) collective-permute-start(bf16[4,144,768]{2,1,0:T(8,128)(2,1)S(1)} %get-tuple-element.156), channel_id=1, source_target_pairs={{0,8},{8,0},{1,9},{9,1},{2,10},{10,2},{3,11},{11,3},{4,12},{12,4},... | collective-permute-start | bytes 2654216 | tf_op jit(solution)/shard_map/ppermute | solution.py:355
  111.3 2.4 %collective-permute-start.26 = (bf16[2,144,768]{2,1,0:T(8,128)(2,1)S(1)}, bf16[2,144,768]{2,1,0:T(8,128)(2,1)S(1)}, u32[]{:S(2)}, u32[]{:S(2)}) collective-permute-start(bf16[2,144,768]{2,1,0:T(8,128)(2,1)S(1)} %get-tuple-element.154), channel_id=1, source_target_pairs={{0,3},{1,0},{2,1},{3,2},{4,7},{5,4},{6,5},{7,6},{8,11},{9,8},{10,9... | collective-permute-start | bytes 1327112 | tf_op jit(solution)/shard_map/ppermute | solution.py:337
  113.7 1.2 collective-permute-start.27
  114.9 9.8 %collective-permute-done.25.refs_3_ = bf16[2,144,768]{2,1,0:T(8,128)(2,1)S(1)} collective-permute-done((bf16[2,144,768]{2,1,0:T(8,128)(2,1)S(1)}, bf16[2,144,768]{2,1,0:T(8,128)(2,1)S(1)}, u32[]{:S(2)}, u32[]{:S(2)}) %collective-permute-start.25) | collective-permute-done | bytes 442400 | tf_op jit(solution)/shard_map/ppermute | solution.py:337
  124.8 3.4 %collective-permute-done.26.refs_4_ = bf16[2,144,768]{2,1,0:T(8,128)(2,1)S(1)} collective-permute-done((bf16[2,144,768]{2,1,0:T(8,128)(2,1)S(1)}, bf16[2,144,768]{2,1,0:T(8,128)(2,1)S(1)}, u32[]{:S(2)}, u32[]{:S(2)}) %collective-permute-start.26) | collective-permute-done | bytes 442400 | tf_op jit(solution)/shard_map/ppermute | solution.py:337
  128.2 3.0 %collective-permute-done.27.refs_5_ = bf16[2,144,768]{2,1,0:T(8,128)(2,1)S(1)} collective-permute-done((bf16[2,144,768]{2,1,0:T(8,128)(2,1)S(1)}, bf16[2,144,768]{2,1,0:T(8,128)(2,1)S(1)}, u32[]{:S(2)}, u32[]{:S(2)}) %collective-permute-start.27) | collective-permute-done | bytes 442400 | tf_op jit(solution)/shard_map/ppermute | solution.py:337
  131.6 1.3 collective-permute-start.29
  132.9 2.0 %collective-permute-start.30 = (bf16[144,768]{1,0:T(8,128)(2,1)S(1)}, bf16[144,768]{1,0:T(8,128)(2,1)S(1)}, u32[]{:S(2)}, u32[]{:S(2)}) collective-permute-start(bf16[144,768]{1,0:T(8,128)(2,1)S(1)} %get-tuple-element.164), channel_id=1, source_target_pairs={{0,3},{1,0},{2,1},{3,2},{4,7},{5,4},{6,5},{7,6},{8,11},{9,8},{10,9... | collective-permute-start | bytes 663560 | tf_op jit(solution)/shard_map/ppermute | solution.py:337
  135.0 1.4 collective-permute-start.32
  137.3 1.5 collective-permute-done.29.refs_1_
  138.8 1.9 %collective-permute-done.30.refs_2_ = bf16[144,768]{1,0:T(8,128)(2,1)S(1)} collective-permute-done((bf16[144,768]{1,0:T(8,128)(2,1)S(1)}, bf16[144,768]{1,0:T(8,128)(2,1)S(1)}, u32[]{:S(2)}, u32[]{:S(2)}) %collective-permute-start.30) | collective-permute-done | bytes 221216 | tf_op jit(solution)/shard_map/ppermute | solution.py:337
  140.7 1.6 collective-permute-done.31.refs_3_
  142.3 2.2 %collective-permute-done.32.refs_4_ = bf16[144,768]{1,0:T(8,128)(2,1)S(1)} collective-permute-done((bf16[144,768]{1,0:T(8,128)(2,1)S(1)}, bf16[144,768]{1,0:T(8,128)(2,1)S(1)}, u32[]{:S(2)}, u32[]{:S(2)}) %collective-permute-start.32) | collective-permute-done | bytes 221216 | tf_op jit(solution)/shard_map/ppermute | solution.py:351
  144.8 4.1 %collective-permute-start.35 = (bf16[72,768]{1,0:T(8,128)(2,1)S(1)}, bf16[72,768]{1,0:T(8,128)(2,1)S(1)}, u32[]{:S(2)}, u32[]{:S(2)}) collective-permute-start(bf16[72,768]{1,0:T(8,128)(2,1)S(1)} %get-tuple-element.175), channel_id=1, source_target_pairs={{0,96},{32,0},{64,32},{96,64},{1,97},{33,1},{65,33},{97,65},{2,98}... | collective-permute-start | bytes 331784 | tf_op jit(solution)/shard_map/ppermute | solution.py:337
  149.0 3.9 %collective-permute-start.36 = (bf16[72,768]{1,0:T(8,128)(2,1)S(1)}, bf16[72,768]{1,0:T(8,128)(2,1)S(1)}, u32[]{:S(2)}, u32[]{:S(2)}) collective-permute-start(bf16[72,768]{1,0:T(8,128)(2,1)S(1)} %get-tuple-element.176), channel_id=1, source_target_pairs={{0,64},{32,96},{64,0},{96,32},{1,65},{33,97},{65,1},{97,33},{2,66}... | collective-permute-start | bytes 331784 | tf_op jit(solution)/shard_map/ppermute | solution.py:337
  152.9 5.7 %collective-permute-done.36.refs_3_ = bf16[72,768]{1,0:T(8,128)(2,1)S(1)} collective-permute-done((bf16[72,768]{1,0:T(8,128)(2,1)S(1)}, bf16[72,768]{1,0:T(8,128)(2,1)S(1)}, u32[]{:S(2)}, u32[]{:S(2)}) %collective-permute-start.36) | collective-permute-done | bytes 110624 | tf_op jit(solution)/shard_map/ppermute | solution.py:337
  158.6 1.6 mix.1
  (58 shorter events, 10.4 us)
Async XLA Ops:
  0.0 41.1 %copy-start.2 = (bf16[512,3072]{1,0:T(8,128)(2,1)S(1)}, bf16[512,3072]{1,0:T(8,128)(2,1)}, u32[]{:S(2)}) copy-start(bf16[512,3072]{1,0:T(8,128)(2,1)} %refs_5_.1) | copy-start | bytes 9437188
  0.0 18.2 %collective-permute-start.3 = (bf16[3072,512]{1,0:T(8,128)(2,1)}, bf16[3072,512]{1,0:T(8,128)(2,1)}, u32[]{:S(2)}, u32[]{:S(2)}) collective-permute-start(bf16[3072,512]{1,0:T(8,128)(2,1)} %refs_3_.1), channel_id=1, source_target_pairs={{0,4},{4,0},{1,5},{5,1},{2,6},{6,2},{3,7},{7,3},{8,12},{12,8},{9,1... | collective-permute-start | bytes 9437192 | tf_op jit(solution)/shard_map/ppermute | solution.py:359
  1.0 11.4 %collective-permute-start = (bf16[2,128,128]{2,1,0:T(8,128)(2,1)S(1)}, bf16[2,128,128]{2,1,0:T(8,128)(2,1)S(1)}, u32[]{:S(2)}, u32[]{:S(2)}) collective-permute-start(bf16[2,128,128]{2,1,0:T(8,128)(2,1)S(1)} %get-tuple-element.179), channel_id=1, source_target_pairs={{0,32},{32,64},{64,96},{96,0},{1,33},{33,65},{65,97},{97,1},{2,34}... | collective-permute-start | bytes 196616 | tf_op jit(solution)/shard_map/ppermute | solution.py:337
  4.3 8.1 %collective-permute-start.1 = (bf16[2,128,128]{2,1,0:T(8,128)(2,1)S(1)}, bf16[2,128,128]{2,1,0:T(8,128)(2,1)S(1)}, u32[]{:S(2)}, u32[]{:S(2)}) collective-permute-start(bf16[2,128,128]{2,1,0:T(8,128)(2,1)S(1)} %get-tuple-element.178), channel_id=1, source_target_pairs={{0,96},{32,0},{64,32},{96,64},{1,97},{33,1},{65,33},{97,65},{2,98}... | collective-permute-start | bytes 196616 | tf_op jit(solution)/shard_map/ppermute | solution.py:337
  6.6 10.9 %collective-permute-start.2 = (bf16[2,128,128]{2,1,0:T(8,128)(2,1)S(1)}, bf16[2,128,128]{2,1,0:T(8,128)(2,1)S(1)}, u32[]{:S(2)}, u32[]{:S(2)}) collective-permute-start(bf16[2,128,128]{2,1,0:T(8,128)(2,1)S(1)} %get-tuple-element.177), channel_id=1, source_target_pairs={{0,64},{32,96},{64,0},{96,32},{1,65},{33,97},{65,1},{97,33},{2,66}... | collective-permute-start | bytes 196616 | tf_op jit(solution)/shard_map/ppermute | solution.py:337
  18.2 11.0 %collective-permute-start.7 = (bf16[3072,512]{1,0:T(8,128)(2,1)}, bf16[3072,512]{1,0:T(8,128)(2,1)S(1)}, u32[]{:S(2)}, u32[]{:S(2)}) collective-permute-start(bf16[3072,512]{1,0:T(8,128)(2,1)} %refs_4_.1), channel_id=1, source_target_pairs={{0,4},{4,0},{1,5},{5,1},{2,6},{6,2},{3,7},{7,3},{8,12},{12,8},{9,1... | collective-permute-start | bytes 9437192 | tf_op jit(solution)/shard_map/ppermute | solution.py:359
  18.3 7.7 %collective-permute-start.4 = (bf16[2,512,128]{2,1,0:T(8,128)(2,1)S(1)}, bf16[2,512,128]{2,1,0:T(8,128)(2,1)S(1)}, u32[]{:S(2)}, u32[]{:S(2)}) collective-permute-start(bf16[2,512,128]{2,1,0:T(8,128)(2,1)S(1)} %get-tuple-element.103.refs_0_), channel_id=1, source_target_pairs={{0,4},{4,0},{1,5},{5,1},{2,6},{6,2},{3,7},{7,3},{8,12},{12,8},{9,1... | collective-permute-start | bytes 786440 | tf_op jit(solution)/shard_map/ppermute | solution.py:359
  18.8 10.4 %collective-permute-start.5 = (bf16[2,512,128]{2,1,0:T(8,128)(2,1)S(1)}, bf16[2,512,128]{2,1,0:T(8,128)(2,1)S(1)}, u32[]{:S(2)}, u32[]{:S(2)}) collective-permute-start(bf16[2,512,128]{2,1,0:T(8,128)(2,1)S(1)} %get-tuple-element.107), channel_id=1, source_target_pairs={{0,8},{8,16},{16,24},{24,0},{1,9},{9,17},{17,25},{25,1},{2,10},{10... | collective-permute-start | bytes 786440 | tf_op jit(solution)/shard_map/ppermute | solution.py:337
  20.3 8.8 %collective-permute-start.6 = (bf16[2,512,128]{2,1,0:T(8,128)(2,1)S(1)}, bf16[2,512,128]{2,1,0:T(8,128)(2,1)S(1)}, u32[]{:S(2)}, u32[]{:S(2)}) collective-permute-start(bf16[2,512,128]{2,1,0:T(8,128)(2,1)S(1)} %get-tuple-element.108), channel_id=1, source_target_pairs={{0,24},{8,0},{16,8},{24,16},{1,25},{9,1},{17,9},{25,17},{2,26},{10... | collective-permute-start | bytes 786440 | tf_op jit(solution)/shard_map/ppermute | solution.py:337
  22.0 0.9 copy-start.3
  22.9 0.9 copy-start.4
  23.9 0.7 copy-start.6
  24.5 0.7 copy-start.7
  29.2 2.6 %collective-permute-start.8 = (bf16[2,512,128]{2,1,0:T(8,128)(2,1)S(1)}, bf16[2,512,128]{2,1,0:T(8,128)(2,1)S(1)}, u32[]{:S(2)}, u32[]{:S(2)}) collective-permute-start(bf16[2,512,128]{2,1,0:T(8,128)(2,1)S(1)} %collective-permute-done.5.refs_0_), channel_id=1, source_target_pairs={{0,4},{4,0},{1,5},{5,1},{2,6},{6,2},{3,7},{7,3},{8,12},{12,8},{9,1... | collective-permute-start | bytes 786440 | tf_op jit(solution)/shard_map/ppermute | solution.py:359
  29.3 2.6 %collective-permute-start.9 = (bf16[2,512,128]{2,1,0:T(8,128)(2,1)S(1)}, bf16[2,512,128]{2,1,0:T(8,128)(2,1)S(1)}, u32[]{:S(2)}, u32[]{:S(2)}) collective-permute-start(bf16[2,512,128]{2,1,0:T(8,128)(2,1)S(1)} %collective-permute-done.6.refs_1_), channel_id=1, source_target_pairs={{0,4},{4,0},{1,5},{5,1},{2,6},{6,2},{3,7},{7,3},{8,12},{12,8},{9,1... | collective-permute-start | bytes 786440 | tf_op jit(solution)/shard_map/ppermute | solution.py:359
  29.7 9.8 %collective-permute-start.10 = (bf16[2,512,128]{2,1,0:T(8,128)(2,1)S(1)}, bf16[2,512,128]{2,1,0:T(8,128)(2,1)S(1)}, u32[]{:S(2)}, u32[]{:S(2)}) collective-permute-start(bf16[2,512,128]{2,1,0:T(8,128)(2,1)S(1)} %get-tuple-element.119), channel_id=1, source_target_pairs={{0,16},{8,24},{16,0},{24,8},{1,17},{9,25},{17,1},{25,9},{2,18},{10... | collective-permute-start | bytes 786440 | tf_op jit(solution)/shard_map/ppermute | solution.py:337
  31.8 48.7 %copy-start.1 = (bf16[3072,512]{1,0:T(8,128)(2,1)S(1)}, bf16[3072,512]{1,0:T(8,128)(2,1)}, u32[]{:S(2)}) copy-start(bf16[3072,512]{1,0:T(8,128)(2,1)} %refs_4_.1) | copy-start | bytes 9437188
  37.5 43.1 %copy-start = (bf16[3072,512]{1,0:T(8,128)(2,1)S(1)}, bf16[3072,512]{1,0:T(8,128)(2,1)}, u32[]{:S(2)}) copy-start(bf16[3072,512]{1,0:T(8,128)(2,1)} %refs_3_.1) | copy-start | bytes 9437188
  37.5 43.1 %copy-start.5 = (f32[3072]{0:T(1024)S(1)}, f32[3072]{0:T(1024)}, u32[]{:S(2)}) copy-start(f32[3072]{0:T(1024)} %param.18) | copy-start | bytes 36868
  39.6 1.5 collective-permute-start.11
  41.1 19.4 %collective-permute-start.15 = (bf16[512,3072]{1,0:T(8,128)(2,1)S(1)}, bf16[512,3072]{1,0:T(8,128)(2,1)S(1)}, u32[]{:S(2)}, u32[]{:S(2)}) collective-permute-start(bf16[512,3072]{1,0:T(8,128)(2,1)S(1)} %copy-done.2), channel_id=1, source_target_pairs={{0,4},{4,0},{1,5},{5,1},{2,6},{6,2},{3,7},{7,3},{8,12},{12,8},{9,1... | collective-permute-start | bytes 9437192 | tf_op jit(solution)/shard_map/ppermute | solution.py:359
  44.4 8.2 %collective-permute-start.12 = (bf16[72,768]{1,0:T(8,128)(2,1)S(1)}, bf16[72,768]{1,0:T(8,128)(2,1)S(1)}, u32[]{:S(2)}, u32[]{:S(2)}) collective-permute-start(bf16[72,768]{1,0:T(8,128)(2,1)S(1)} %get-tuple-element.126), channel_id=1, source_target_pairs={{0,32},{32,64},{64,96},{96,0},{1,33},{33,65},{65,97},{97,1},{2,34}... | collective-permute-start | bytes 331784 | tf_op jit(solution)/shard_map/ppermute | solution.py:337
  44.7 11.1 %collective-permute-start.13 = (bf16[72,768]{1,0:T(8,128)(2,1)S(1)}, bf16[72,768]{1,0:T(8,128)(2,1)S(1)}, u32[]{:S(2)}, u32[]{:S(2)}) collective-permute-start(bf16[72,768]{1,0:T(8,128)(2,1)S(1)} %get-tuple-element.127), channel_id=1, source_target_pairs={{0,96},{32,0},{64,32},{96,64},{1,97},{33,1},{65,33},{97,65},{2,98}... | collective-permute-start | bytes 331784 | tf_op jit(solution)/shard_map/ppermute | solution.py:337
  48.8 11.7 %collective-permute-start.14 = (bf16[72,768]{1,0:T(8,128)(2,1)S(1)}, bf16[72,768]{1,0:T(8,128)(2,1)S(1)}, u32[]{:S(2)}, u32[]{:S(2)}) collective-permute-start(bf16[72,768]{1,0:T(8,128)(2,1)S(1)} %get-tuple-element.128), channel_id=1, source_target_pairs={{0,64},{32,96},{64,0},{96,32},{1,65},{33,97},{65,1},{97,33},{2,66}... | collective-permute-start | bytes 331784 | tf_op jit(solution)/shard_map/ppermute | solution.py:337
  60.6 8.3 %collective-permute-start.19 = (bf16[144,768]{1,0:T(8,128)(2,1)S(1)}, bf16[144,768]{1,0:T(8,128)(2,1)S(1)}, u32[]{:S(2)}, u32[]{:S(2)}) collective-permute-start(bf16[144,768]{1,0:T(8,128)(2,1)S(1)} %get-tuple-element.137), channel_id=1, source_target_pairs={{0,24},{8,16},{16,8},{24,0},{1,25},{9,17},{17,9},{25,1},{2,26},{10... | collective-permute-start | bytes 663560 | tf_op jit(solution)/shard_map/ppermute | solution.py:351
  62.6 8.6 %collective-permute-start.16 = (bf16[144,768]{1,0:T(8,128)(2,1)S(1)}, bf16[144,768]{1,0:T(8,128)(2,1)S(1)}, u32[]{:S(2)}, u32[]{:S(2)}) collective-permute-start(bf16[144,768]{1,0:T(8,128)(2,1)S(1)} %get-tuple-element.136), channel_id=1, source_target_pairs={{0,1},{1,2},{2,3},{3,0},{4,5},{5,6},{6,7},{7,4},{8,9},{9,10},{10,1... | collective-permute-start | bytes 663560 | tf_op jit(solution)/shard_map/ppermute | solution.py:337
  64.1 10.5 %collective-permute-start.17 = (bf16[144,768]{1,0:T(8,128)(2,1)S(1)}, bf16[144,768]{1,0:T(8,128)(2,1)S(1)}, u32[]{:S(2)}, u32[]{:S(2)}) collective-permute-start(bf16[144,768]{1,0:T(8,128)(2,1)S(1)} %get-tuple-element.136), channel_id=1, source_target_pairs={{0,3},{1,0},{2,1},{3,2},{4,7},{5,4},{6,5},{7,6},{8,11},{9,8},{10,9... | collective-permute-start | bytes 663560 | tf_op jit(solution)/shard_map/ppermute | solution.py:337
  65.9 10.4 %collective-permute-start.18 = (bf16[144,768]{1,0:T(8,128)(2,1)S(1)}, bf16[144,768]{1,0:T(8,128)(2,1)S(1)}, u32[]{:S(2)}, u32[]{:S(2)}) collective-permute-start(bf16[144,768]{1,0:T(8,128)(2,1)S(1)} %get-tuple-element.136), channel_id=1, source_target_pairs={{0,2},{1,3},{2,0},{3,1},{4,6},{5,7},{6,4},{7,5},{8,10},{9,11},{10,... | collective-permute-start | bytes 663560 | tf_op jit(solution)/shard_map/ppermute | solution.py:337
  68.8 7.5 %collective-permute-start.20 = (bf16[144,768]{1,0:T(8,128)(2,1)S(1)}, bf16[144,768]{1,0:T(8,128)(2,1)S(1)}, u32[]{:S(2)}, u32[]{:S(2)}) collective-permute-start(bf16[144,768]{1,0:T(8,128)(2,1)S(1)} %collective-permute-done.19), channel_id=1, source_target_pairs={{0,8},{8,0},{1,9},{9,1},{2,10},{10,2},{3,11},{11,3},{4,12},{12,4},... | collective-permute-start | bytes 663560 | tf_op jit(solution)/shard_map/ppermute | solution.py:355
  76.4 21.4 %collective-permute-start.24 = (bf16[4,144,768]{2,1,0:T(8,128)(2,1)S(1)}, bf16[4,144,768]{2,1,0:T(8,128)(2,1)S(1)}, u32[]{:S(2)}, u32[]{:S(2)}) collective-permute-start(bf16[4,144,768]{2,1,0:T(8,128)(2,1)S(1)} %pad_maximum_fusion.refs_2_), channel_id=1, source_target_pairs={{0,8},{8,0},{1,9},{9,1},{2,10},{10,2},{3,11},{11,3},{4,12},{12,4},... | collective-permute-start | bytes 2654216 | tf_op jit(solution)/shard_map/ppermute | solution.py:355
  76.5 21.3 %collective-permute-start.21 = (bf16[2,144,768]{2,1,0:T(8,128)(2,1)S(1)}, bf16[2,144,768]{2,1,0:T(8,128)(2,1)S(1)}, u32[]{:S(2)}, u32[]{:S(2)}) collective-permute-start(bf16[2,144,768]{2,1,0:T(8,128)(2,1)S(1)} %pad_maximum_fusion.1.refs_3_), channel_id=1, source_target_pairs={{0,1},{1,2},{2,3},{3,0},{4,5},{5,6},{6,7},{7,4},{8,9},{9,10},{10,1... | collective-permute-start | bytes 1327112 | tf_op jit(solution)/shard_map/ppermute | solution.py:337
  77.7 20.1 %collective-permute-start.22 = (bf16[2,144,768]{2,1,0:T(8,128)(2,1)S(1)}, bf16[2,144,768]{2,1,0:T(8,128)(2,1)S(1)}, u32[]{:S(2)}, u32[]{:S(2)}) collective-permute-start(bf16[2,144,768]{2,1,0:T(8,128)(2,1)S(1)} %pad_maximum_fusion.1.refs_3_), channel_id=1, source_target_pairs={{0,3},{1,0},{2,1},{3,2},{4,7},{5,4},{6,5},{7,6},{8,11},{9,8},{10,9... | collective-permute-start | bytes 1327112 | tf_op jit(solution)/shard_map/ppermute | solution.py:337
  79.8 18.0 %collective-permute-start.23 = (bf16[2,144,768]{2,1,0:T(8,128)(2,1)S(1)}, bf16[2,144,768]{2,1,0:T(8,128)(2,1)S(1)}, u32[]{:S(2)}, u32[]{:S(2)}) collective-permute-start(bf16[2,144,768]{2,1,0:T(8,128)(2,1)S(1)} %pad_maximum_fusion.1.refs_3_), channel_id=1, source_target_pairs={{0,2},{1,3},{2,0},{3,1},{4,6},{5,7},{6,4},{7,5},{8,10},{9,11},{10,... | collective-permute-start | bytes 1327112 | tf_op jit(solution)/shard_map/ppermute | solution.py:337
  108.7 22.5 %collective-permute-start.28 = (bf16[4,144,768]{2,1,0:T(8,128)(2,1)S(1)}, bf16[4,144,768]{2,1,0:T(8,128)(2,1)S(1)}, u32[]{:S(2)}, u32[]{:S(2)}) collective-permute-start(bf16[4,144,768]{2,1,0:T(8,128)(2,1)S(1)} %get-tuple-element.156), channel_id=1, source_target_pairs={{0,8},{8,0},{1,9},{9,1},{2,10},{10,2},{3,11},{11,3},{4,12},{12,4},... | collective-permute-start | bytes 2654216 | tf_op jit(solution)/shard_map/ppermute | solution.py:355
  110.5 14.3 %collective-permute-start.25 = (bf16[2,144,768]{2,1,0:T(8,128)(2,1)S(1)}, bf16[2,144,768]{2,1,0:T(8,128)(2,1)S(1)}, u32[]{:S(2)}, u32[]{:S(2)}) collective-permute-start(bf16[2,144,768]{2,1,0:T(8,128)(2,1)S(1)} %get-tuple-element.153), channel_id=1, source_target_pairs={{0,1},{1,2},{2,3},{3,0},{4,5},{5,6},{6,7},{7,4},{8,9},{9,10},{10,1... | collective-permute-start | bytes 1327112 | tf_op jit(solution)/shard_map/ppermute | solution.py:337
  111.3 16.8 %collective-permute-start.26 = (bf16[2,144,768]{2,1,0:T(8,128)(2,1)S(1)}, bf16[2,144,768]{2,1,0:T(8,128)(2,1)S(1)}, u32[]{:S(2)}, u32[]{:S(2)}) collective-permute-start(bf16[2,144,768]{2,1,0:T(8,128)(2,1)S(1)} %get-tuple-element.154), channel_id=1, source_target_pairs={{0,3},{1,0},{2,1},{3,2},{4,7},{5,4},{6,5},{7,6},{8,11},{9,8},{10,9... | collective-permute-start | bytes 1327112 | tf_op jit(solution)/shard_map/ppermute | solution.py:337
  113.7 17.4 %collective-permute-start.27 = (bf16[2,144,768]{2,1,0:T(8,128)(2,1)S(1)}, bf16[2,144,768]{2,1,0:T(8,128)(2,1)S(1)}, u32[]{:S(2)}, u32[]{:S(2)}) collective-permute-start(bf16[2,144,768]{2,1,0:T(8,128)(2,1)S(1)} %get-tuple-element.155), channel_id=1, source_target_pairs={{0,2},{1,3},{2,0},{3,1},{4,6},{5,7},{6,4},{7,5},{8,10},{9,11},{10,... | collective-permute-start | bytes 1327112 | tf_op jit(solution)/shard_map/ppermute | solution.py:337
  131.6 7.2 %collective-permute-start.29 = (bf16[144,768]{1,0:T(8,128)(2,1)S(1)}, bf16[144,768]{1,0:T(8,128)(2,1)S(1)}, u32[]{:S(2)}, u32[]{:S(2)}) collective-permute-start(bf16[144,768]{1,0:T(8,128)(2,1)S(1)} %get-tuple-element.163), channel_id=1, source_target_pairs={{0,1},{1,2},{2,3},{3,0},{4,5},{5,6},{6,7},{7,4},{8,9},{9,10},{10,1... | collective-permute-start | bytes 663560 | tf_op jit(solution)/shard_map/ppermute | solution.py:337
  132.9 7.9 %collective-permute-start.30 = (bf16[144,768]{1,0:T(8,128)(2,1)S(1)}, bf16[144,768]{1,0:T(8,128)(2,1)S(1)}, u32[]{:S(2)}, u32[]{:S(2)}) collective-permute-start(bf16[144,768]{1,0:T(8,128)(2,1)S(1)} %get-tuple-element.164), channel_id=1, source_target_pairs={{0,3},{1,0},{2,1},{3,2},{4,7},{5,4},{6,5},{7,6},{8,11},{9,8},{10,9... | collective-permute-start | bytes 663560 | tf_op jit(solution)/shard_map/ppermute | solution.py:337
  134.9 7.4 %collective-permute-start.31 = (bf16[144,768]{1,0:T(8,128)(2,1)S(1)}, bf16[144,768]{1,0:T(8,128)(2,1)S(1)}, u32[]{:S(2)}, u32[]{:S(2)}) collective-permute-start(bf16[144,768]{1,0:T(8,128)(2,1)S(1)} %get-tuple-element.165), channel_id=1, source_target_pairs={{0,2},{1,3},{2,0},{3,1},{4,6},{5,7},{6,4},{7,5},{8,10},{9,11},{10,... | collective-permute-start | bytes 663560 | tf_op jit(solution)/shard_map/ppermute | solution.py:337
  135.0 9.5 %collective-permute-start.32 = (bf16[144,768]{1,0:T(8,128)(2,1)S(1)}, bf16[144,768]{1,0:T(8,128)(2,1)S(1)}, u32[]{:S(2)}, u32[]{:S(2)}) collective-permute-start(bf16[144,768]{1,0:T(8,128)(2,1)S(1)} %get-tuple-element.166), channel_id=1, source_target_pairs={{0,24},{8,16},{16,8},{24,0},{1,25},{9,17},{17,9},{25,1},{2,26},{10... | collective-permute-start | bytes 663560 | tf_op jit(solution)/shard_map/ppermute | solution.py:351
  136.5 8.1 %collective-permute-start.33 = (bf16[144,768]{1,0:T(8,128)(2,1)S(1)}, bf16[144,768]{1,0:T(8,128)(2,1)S(1)}, u32[]{:S(2)}, u32[]{:S(2)}) collective-permute-start(bf16[144,768]{1,0:T(8,128)(2,1)S(1)} %get-tuple-element.167), channel_id=1, source_target_pairs={{0,16},{8,24},{16,0},{24,8},{1,17},{9,25},{17,1},{25,9},{2,18},{10... | collective-permute-start | bytes 663560 | tf_op jit(solution)/shard_map/ppermute | solution.py:337
  144.8 8.2 %collective-permute-start.34 = (bf16[72,768]{1,0:T(8,128)(2,1)S(1)}, bf16[72,768]{1,0:T(8,128)(2,1)S(1)}, u32[]{:S(2)}, u32[]{:S(2)}) collective-permute-start(bf16[72,768]{1,0:T(8,128)(2,1)S(1)} %get-tuple-element.174), channel_id=1, source_target_pairs={{0,32},{32,64},{64,96},{96,0},{1,33},{33,65},{65,97},{97,1},{2,34}... | collective-permute-start | bytes 331784 | tf_op jit(solution)/shard_map/ppermute | solution.py:337
  144.8 8.1 %collective-permute-start.35 = (bf16[72,768]{1,0:T(8,128)(2,1)S(1)}, bf16[72,768]{1,0:T(8,128)(2,1)S(1)}, u32[]{:S(2)}, u32[]{:S(2)}) collective-permute-start(bf16[72,768]{1,0:T(8,128)(2,1)S(1)} %get-tuple-element.175), channel_id=1, source_target_pairs={{0,96},{32,0},{64,32},{96,64},{1,97},{33,1},{65,33},{97,65},{2,98}... | collective-permute-start | bytes 331784 | tf_op jit(solution)/shard_map/ppermute | solution.py:337
  149.0 9.6 %collective-permute-start.36 = (bf16[72,768]{1,0:T(8,128)(2,1)S(1)}, bf16[72,768]{1,0:T(8,128)(2,1)S(1)}, u32[]{:S(2)}, u32[]{:S(2)}) collective-permute-start(bf16[72,768]{1,0:T(8,128)(2,1)S(1)} %get-tuple-element.176), channel_id=1, source_target_pairs={{0,64},{32,96},{64,0},{96,32},{1,65},{33,97},{65,1},{97,33},{2,66}... | collective-permute-start | bytes 331784 | tf_op jit(solution)/shard_map/ppermute | solution.py:337

commit v7 on v5

--- a/solution.py
+++ b/solution.py
@@ -372,6 +372,10 @@
     near, past = jnp.stack((keys, values)), jnp.stack((cache_keys, cache_values))
     from_z = turned([jnp.where(z + s < NZ, near, past) for s in SHIFTS], "zh", KV_ORDER)
     slots = EXPERTS * PAD
+    (keys, values), (cache_keys, cache_values) = lax.optimization_barrier(
+        ((keys, values), (cache_keys, cache_values))
+    )
+    near, past = jnp.stack((keys, values)), jnp.stack((cache_keys, cache_values))
     q_all, res, table, weight = call(
         prep_kernel,
         [

time: 160 us -> 160 us (level)
  starting transfers between devices: 59.6 us -> 55.5 us
  waiting for transfers between devices: 62.7 us -> 66.8 us
    ppermute x24, starting transfers between devices: 52.6 us -> 48.8 us  [turn(): return lax.ppermute(v, axis, [(i, (i + shift) % n) for i in range(n)])]
  transfers between devices with their start and end apart: 37 -> 37, of which waited for: 20 -> 19; matrix products, arithmetic and copies ran while one was open for 1% -> 1% of each run, Pallas kernels for 12% -> 12%
where the time goes in v7:
time: 160 us
  waiting for transfers between devices  66.8 us (42%)
  starting transfers between devices  55.5 us (35%)
  Pallas kernels  32.1 us (20%)
  local copies, waits for them, and re-layouts  3.23 us (2%)
  other arithmetic  2.08 us (1%)
    ppermute x24, waiting for transfers between devices, turn(): return lax.ppermute(v, axis, [(i, (i + shift) % n) for i in range(n)])  59.5 us
    ppermute x24, starting transfers between devices, turn(): return lax.ppermute(v, axis, [(i, (i + shift) % n) for i in range(n)])  48.8 us
    pallas_call x11, Pallas kernels, call(): pl.pallas_call(body, out_shape=out_shape, in_specs=[SM] * scalars + [VM]...  32.1 us
    ppermute x2, waiting for transfers between devices, cross(): return lax.ppermute(v, ('yh', 'yl'), [(i, NY - 1 - i) for i in range(NY)])  3.59 us
    ppermute x2, starting transfers between devices, cross(): return lax.ppermute(v, ('yh', 'yl'), [(i, NY - 1 - i) for i in range(NY)])  3.35 us
    unnamed x16, local copies, waits for them, and re-layouts  3.23 us
  transfers between devices with their start and end apart: 37, of which 19 were waited for; matrix products, arithmetic and copies ran while one was open for 1% of the time, Pallas kernels for 12%

profile of v7, /device:TPU:32, one launch (start us, length us, event | category | flops | bytes accessed | tf_op | source)
XLA Modules:
  0.0 159.9 jit_solution(4691852287255386490)
XLA Ops:
  0.0 1.0 broadcast_select_fusion
  1.0 3.3 %collective-permute-start = (bf16[2,128,128]{2,1,0:T(8,128)(2,1)S(1)}, bf16[2,128,128]{2,1,0:T(8,128)(2,1)S(1)}, u32[]{:S(2)}, u32[]{:S(2)}) collective-permute-start(bf16[2,128,128]{2,1,0:T(8,128)(2,1)S(1)} %get-tuple-element.177), channel_id=1, source_target_pairs={{0,32},{32,64},{64,96},{96,0},{1,33},{33,65},{65,97},{97,1},{2,34}... | collective-permute-start | bytes 196616 | tf_op jit(solution)/shard_map/ppermute | solution.py:336
  4.3 2.2 %collective-permute-start.1 = (bf16[2,128,128]{2,1,0:T(8,128)(2,1)S(1)}, bf16[2,128,128]{2,1,0:T(8,128)(2,1)S(1)}, u32[]{:S(2)}, u32[]{:S(2)}) collective-permute-start(bf16[2,128,128]{2,1,0:T(8,128)(2,1)S(1)} %get-tuple-element.176), channel_id=1, source_target_pairs={{0,96},{32,0},{64,32},{96,64},{1,97},{33,1},{65,33},{97,65},{2,98}... | collective-permute-start | bytes 196616 | tf_op jit(solution)/shard_map/ppermute | solution.py:336
  6.6 4.9 %collective-permute-start.2 = (bf16[2,128,128]{2,1,0:T(8,128)(2,1)S(1)}, bf16[2,128,128]{2,1,0:T(8,128)(2,1)S(1)}, u32[]{:S(2)}, u32[]{:S(2)}) collective-permute-start(bf16[2,128,128]{2,1,0:T(8,128)(2,1)S(1)} %get-tuple-element.175), channel_id=1, source_target_pairs={{0,64},{32,96},{64,0},{96,32},{1,65},{33,97},{65,1},{97,33},{2,66}... | collective-permute-start | bytes 196616 | tf_op jit(solution)/shard_map/ppermute | solution.py:336
  12.4 5.1 %collective-permute-done.2.refs_2_ = bf16[2,128,128]{2,1,0:T(8,128)(2,1)S(1)} collective-permute-done((bf16[2,128,128]{2,1,0:T(8,128)(2,1)S(1)}, bf16[2,128,128]{2,1,0:T(8,128)(2,1)S(1)}, u32[]{:S(2)}, u32[]{:S(2)}) %collective-permute-start.2) | collective-permute-done | bytes 65568 | tf_op jit(solution)/shard_map/ppermute | solution.py:336
  18.8 1.6 collective-permute-start.5
  20.3 1.7 %collective-permute-start.6 = (bf16[2,512,128]{2,1,0:T(8,128)(2,1)S(1)}, bf16[2,512,128]{2,1,0:T(8,128)(2,1)S(1)}, u32[]{:S(2)}, u32[]{:S(2)}) collective-permute-start(bf16[2,512,128]{2,1,0:T(8,128)(2,1)S(1)} %get-tuple-element.107), channel_id=1, source_target_pairs={{0,24},{8,0},{16,8},{24,16},{1,25},{9,1},{17,9},{25,17},{2,26},{10... | collective-permute-start | bytes 786440 | tf_op jit(solution)/shard_map/ppermute | solution.py:336
  22.0 0.9 copy-done.3
  26.0 3.1 %attend_own.1 = (f32[768,128]{1,0:T(8,128)S(1)}, f32[768,128]{1,0:T(8,128)S(1)}, f32[768,128]{1,0:T(8,128)S(1)}) custom-call(bf16[768,128]{1,0:T(8,128)(2,1)S(1)} %get-tuple-element.91.q_all, bf16[2,128,128]{2,1,0:T(8,128)(2,1)S(1)} %get-tuple-element.178.tract.tract_ref, bf16[2,128,128]{2,1,0:T(8,128)(2,1)S(1)} %get-tuple-element.179.cache.cache_ref, ...), custom_call_target="tpu_custom_call" | custom-call | tf_op jit(solution)/shard_map/attend_own/pallas_call | solution.py:33
  29.7 2.0 %collective-permute-start.10 = (bf16[2,512,128]{2,1,0:T(8,128)(2,1)S(1)}, bf16[2,512,128]{2,1,0:T(8,128)(2,1)S(1)}, u32[]{:S(2)}, u32[]{:S(2)}) collective-permute-start(bf16[2,512,128]{2,1,0:T(8,128)(2,1)S(1)} %get-tuple-element.118), channel_id=1, source_target_pairs={{0,16},{8,24},{16,0},{24,8},{1,17},{9,25},{17,1},{25,9},{2,18},{10... | collective-permute-start | bytes 786440 | tf_op jit(solution)/shard_map/ppermute | solution.py:336
  31.8 5.7 %attend_more.1 = (f32[768,128]{1,0:T(8,128)S(1)}, f32[768,128]{1,0:T(8,128)S(1)}, f32[768,128]{1,0:T(8,128)S(1)}) custom-call(bf16[768,128]{1,0:T(8,128)(2,1)S(1)} %get-tuple-element.91.q_all, f32[768,128]{1,0:T(8,128)S(1)} %get-tuple-element.110.m_ref, f32[768,128]{1,0:T(8,128)S(1)} %get-tuple-element.111.l_ref, f32[768,128]{1,0:T(8,128)S(1)} %get-tuple-element.112.acc_ref, ...), custom_call_target="tpu_custom_call" | custom-call | tf_op jit(solution)/shard_map/attend_more/pallas_call | solution.py:33
  37.5 2.1 %collective-permute-done.10.refs_0_ = bf16[2,512,128]{2,1,0:T(8,128)(2,1)S(1)} collective-permute-done((bf16[2,512,128]{2,1,0:T(8,128)(2,1)S(1)}, bf16[2,512,128]{2,1,0:T(8,128)(2,1)S(1)}, u32[]{:S(2)}, u32[]{:S(2)}) %collective-permute-start.10) | collective-permute-done | bytes 262176 | tf_op jit(solution)/shard_map/ppermute | solution.py:336
  39.6 1.5 collective-permute-done.11.refs_1_
  41.2 3.1 %attend.1 = (bf16[128,768]{1,0:T(8,128)(2,1)S(1)}, bf16[72,768]{1,0:T(8,128)(2,1)S(1)}, bf16[72,768]{1,0:T(8,128)(2,1)S(1)}, bf16[72,768]{1,0:T(8,128)(2,1)S(1)}, bf16[72,768]{1,0:T(8,128)(2,1)S(1)}) custom-call(bf16[768,128]{1,0:T(8,128)(2,1)S(1)} %get-tuple-element.91.q_all, bf16[128,768]{1,0:T(8,128)(2,1)S(1)} %get-tuple-element.92.res_ref, ...), custom_call_target="tpu_custom_call" | custom-call | tf_op jit(solution)/shard_map/attend/pallas_call | solution.py:33
  44.7 4.1 %collective-permute-start.13 = (bf16[72,768]{1,0:T(8,128)(2,1)S(1)}, bf16[72,768]{1,0:T(8,128)(2,1)S(1)}, u32[]{:S(2)}, u32[]{:S(2)}) collective-permute-start(bf16[72,768]{1,0:T(8,128)(2,1)S(1)} %get-tuple-element.126), channel_id=1, source_target_pairs={{0,96},{32,0},{64,32},{96,64},{1,97},{33,1},{65,33},{97,65},{2,98}... | collective-permute-start | bytes 331784 | tf_op jit(solution)/shard_map/ppermute | solution.py:336
  48.8 3.2 %collective-permute-start.14 = (bf16[72,768]{1,0:T(8,128)(2,1)S(1)}, bf16[72,768]{1,0:T(8,128)(2,1)S(1)}, u32[]{:S(2)}, u32[]{:S(2)}) collective-permute-start(bf16[72,768]{1,0:T(8,128)(2,1)S(1)} %get-tuple-element.127), channel_id=1, source_target_pairs={{0,64},{32,96},{64,0},{96,32},{1,65},{33,97},{65,1},{97,33},{2,66}... | collective-permute-start | bytes 331784 | tf_op jit(solution)/shard_map/ppermute | solution.py:336
  52.6 3.1 %collective-permute-done.13.refs_2_ = bf16[72,768]{1,0:T(8,128)(2,1)S(1)} collective-permute-done((bf16[72,768]{1,0:T(8,128)(2,1)S(1)}, bf16[72,768]{1,0:T(8,128)(2,1)S(1)}, u32[]{:S(2)}, u32[]{:S(2)}) %collective-permute-start.13) | collective-permute-done | bytes 110624 | tf_op jit(solution)/shard_map/ppermute | solution.py:336
  55.8 4.7 %collective-permute-done.14.refs_3_ = bf16[72,768]{1,0:T(8,128)(2,1)S(1)} collective-permute-done((bf16[72,768]{1,0:T(8,128)(2,1)S(1)}, bf16[72,768]{1,0:T(8,128)(2,1)S(1)}, u32[]{:S(2)}, u32[]{:S(2)}) %collective-permute-start.14) | collective-permute-done | bytes 110624 | tf_op jit(solution)/shard_map/ppermute | solution.py:336
  60.6 2.1 %collective-permute-start.19 = (bf16[144,768]{1,0:T(8,128)(2,1)S(1)}, bf16[144,768]{1,0:T(8,128)(2,1)S(1)}, u32[]{:S(2)}, u32[]{:S(2)}) collective-permute-start(bf16[144,768]{1,0:T(8,128)(2,1)S(1)} %get-tuple-element.136), channel_id=1, source_target_pairs={{0,24},{8,16},{16,8},{24,0},{1,25},{9,17},{17,9},{25,1},{2,26},{10... | collective-permute-start | bytes 663560 | tf_op jit(solution)/shard_map/ppermute | solution.py:350
  62.6 1.5 collective-permute-start.16
  64.1 1.8 %collective-permute-start.17 = (bf16[144,768]{1,0:T(8,128)(2,1)S(1)}, bf16[144,768]{1,0:T(8,128)(2,1)S(1)}, u32[]{:S(2)}, u32[]{:S(2)}) collective-permute-start(bf16[144,768]{1,0:T(8,128)(2,1)S(1)} %get-tuple-element.135), channel_id=1, source_target_pairs={{0,3},{1,0},{2,1},{3,2},{4,7},{5,4},{6,5},{7,6},{8,11},{9,8},{10,9... | collective-permute-start | bytes 663560 | tf_op jit(solution)/shard_map/ppermute | solution.py:336
  65.9 1.8 %collective-permute-start.18 = (bf16[144,768]{1,0:T(8,128)(2,1)S(1)}, bf16[144,768]{1,0:T(8,128)(2,1)S(1)}, u32[]{:S(2)}, u32[]{:S(2)}) collective-permute-start(bf16[144,768]{1,0:T(8,128)(2,1)S(1)} %get-tuple-element.135), channel_id=1, source_target_pairs={{0,2},{1,3},{2,0},{3,1},{4,6},{5,7},{6,4},{7,5},{8,10},{9,11},{10,... | collective-permute-start | bytes 663560 | tf_op jit(solution)/shard_map/ppermute | solution.py:336
  67.7 1.1 collective-permute-done.19
  68.8 2.4 %collective-permute-done.16 = bf16[144,768]{1,0:T(8,128)(2,1)S(1)} collective-permute-done((bf16[144,768]{1,0:T(8,128)(2,1)S(1)}, bf16[144,768]{1,0:T(8,128)(2,1)S(1)}, u32[]{:S(2)}, u32[]{:S(2)}) %collective-permute-start.16) | collective-permute-done | bytes 221216 | tf_op jit(solution)/shard_map/ppermute | solution.py:336
  71.2 3.3 %collective-permute-done.17 = bf16[144,768]{1,0:T(8,128)(2,1)S(1)} collective-permute-done((bf16[144,768]{1,0:T(8,128)(2,1)S(1)}, bf16[144,768]{1,0:T(8,128)(2,1)S(1)}, u32[]{:S(2)}, u32[]{:S(2)}) %collective-permute-start.17) | collective-permute-done | bytes 221216 | tf_op jit(solution)/shard_map/ppermute | solution.py:336
  74.6 1.7 %collective-permute-done.18 = bf16[144,768]{1,0:T(8,128)(2,1)S(1)} collective-permute-done((bf16[144,768]{1,0:T(8,128)(2,1)S(1)}, bf16[144,768]{1,0:T(8,128)(2,1)S(1)}, u32[]{:S(2)}, u32[]{:S(2)}) %collective-permute-start.18) | collective-permute-done | bytes 221216 | tf_op jit(solution)/shard_map/ppermute | solution.py:336
  76.5 1.2 collective-permute-start.21
  77.7 2.1 %collective-permute-start.22 = (bf16[2,144,768]{2,1,0:T(8,128)(2,1)S(1)}, bf16[2,144,768]{2,1,0:T(8,128)(2,1)S(1)}, u32[]{:S(2)}, u32[]{:S(2)}) collective-permute-start(bf16[2,144,768]{2,1,0:T(8,128)(2,1)S(1)} %pad_maximum_fusion.1.refs_3_), channel_id=1, source_target_pairs={{0,3},{1,0},{2,1},{3,2},{4,7},{5,4},{6,5},{7,6},{8,11},{9,8},{10,9... | collective-permute-start | bytes 1327112 | tf_op jit(solution)/shard_map/ppermute | solution.py:336
  80.5 5.7 %experts_own.1 = (bf16[4,144,768]{2,1,0:T(8,128)(2,1)S(1)}, bf16[2,3072,512]{2,1,0:T(8,128)(2,1)S(1)}, bf16[2,3072,512]{2,1,0:T(8,128)(2,1)S(1)}, bf16[1024,3072]{1,0:T(8,128)(2,1)S(1)}) custom-call(s32[4]{0:T(128)S(1)} %pad_add_fusion.where_ref.refs_0_, f32[4,1,768]{2,1,0:T(1,128)S(1)} %bitcast.22, bf16[4,144,768]{2,1,0:T(8,128)(2,1)S(1)} %pad_maximum_fusion.refs_2_, ...), custom_call_target="tpu_custom_call" | custom-call | tf_op jit(solution)/shard_map/experts_own/pallas_call | solution.py:33
  86.2 11.6 %collective-permute-done.21.refs_4_ = bf16[2,144,768]{2,1,0:T(8,128)(2,1)S(1)} collective-permute-done((bf16[2,144,768]{2,1,0:T(8,128)(2,1)S(1)}, bf16[2,144,768]{2,1,0:T(8,128)(2,1)S(1)}, u32[]{:S(2)}, u32[]{:S(2)}) %collective-permute-start.21) | collective-permute-done | bytes 442400 | tf_op jit(solution)/shard_map/ppermute | solution.py:336
  97.8 10.9 %experts.1 = (bf16[4,144,768]{2,1,0:T(8,128)(2,1)S(1)}, bf16[2,144,768]{2,1,0:T(8,128)(2,1)S(1)}, bf16[2,144,768]{2,1,0:T(8,128)(2,1)S(1)}, bf16[2,144,768]{2,1,0:T(8,128)(2,1)S(1)}, bf16[2,144,768]{2,1,0:T(8,128)(2,1)S(1)}) custom-call(s32[4]{0:T(128)S(1)} %pad_add_fusion.where_ref.refs_0_, f32[4,1,768]{2,1,0:T(1,128)S(1)} %bitcast.23, ...), custom_call_target="tpu_custom_call" | custom-call | tf_op jit(solution)/shard_map/experts/pallas_call | solution.py:33
  108.7 1.8 %collective-permute-start.28 = (bf16[4,144,768]{2,1,0:T(8,128)(2,1)S(1)}, bf16[4,144,768]{2,1,0:T(8,128)(2,1)S(1)}, u32[]{:S(2)}, u32[]{:S(2)}) collective-permute-start(bf16[4,144,768]{2,1,0:T(8,128)(2,1)S(1)} %get-tuple-element.155), channel_id=1, source_target_pairs={{0,8},{8,0},{1,9},{9,1},{2,10},{10,2},{3,11},{11,3},{4,12},{12,4},... | collective-permute-start | bytes 2654216 | tf_op jit(solution)/shard_map/ppermute | solution.py:354
  111.3 2.4 %collective-permute-start.26 = (bf16[2,144,768]{2,1,0:T(8,128)(2,1)S(1)}, bf16[2,144,768]{2,1,0:T(8,128)(2,1)S(1)}, u32[]{:S(2)}, u32[]{:S(2)}) collective-permute-start(bf16[2,144,768]{2,1,0:T(8,128)(2,1)S(1)} %get-tuple-element.153), channel_id=1, source_target_pairs={{0,3},{1,0},{2,1},{3,2},{4,7},{5,4},{6,5},{7,6},{8,11},{9,8},{10,9... | collective-permute-start | bytes 1327112 | tf_op jit(solution)/shard_map/ppermute | solution.py:336
  113.7 1.2 collective-permute-start.27
  114.9 9.8 %collective-permute-done.25.refs_3_ = bf16[2,144,768]{2,1,0:T(8,128)(2,1)S(1)} collective-permute-done((bf16[2,144,768]{2,1,0:T(8,128)(2,1)S(1)}, bf16[2,144,768]{2,1,0:T(8,128)(2,1)S(1)}, u32[]{:S(2)}, u32[]{:S(2)}) %collective-permute-start.25) | collective-permute-done | bytes 442400 | tf_op jit(solution)/shard_map/ppermute | solution.py:336
  124.8 3.7 %collective-permute-done.26.refs_4_ = bf16[2,144,768]{2,1,0:T(8,128)(2,1)S(1)} collective-permute-done((bf16[2,144,768]{2,1,0:T(8,128)(2,1)S(1)}, bf16[2,144,768]{2,1,0:T(8,128)(2,1)S(1)}, u32[]{:S(2)}, u32[]{:S(2)}) %collective-permute-start.26) | collective-permute-done | bytes 442400 | tf_op jit(solution)/shard_map/ppermute | solution.py:336
  128.4 2.1 %collective-permute-done.27.refs_5_ = bf16[2,144,768]{2,1,0:T(8,128)(2,1)S(1)} collective-permute-done((bf16[2,144,768]{2,1,0:T(8,128)(2,1)S(1)}, bf16[2,144,768]{2,1,0:T(8,128)(2,1)S(1)}, u32[]{:S(2)}, u32[]{:S(2)}) %collective-permute-start.27) | collective-permute-done | bytes 442400 | tf_op jit(solution)/shard_map/ppermute | solution.py:336
  131.1 1.3 collective-permute-start.29
  132.4 2.0 %collective-permute-start.30 = (bf16[144,768]{1,0:T(8,128)(2,1)S(1)}, bf16[144,768]{1,0:T(8,128)(2,1)S(1)}, u32[]{:S(2)}, u32[]{:S(2)}) collective-permute-start(bf16[144,768]{1,0:T(8,128)(2,1)S(1)} %get-tuple-element.163), channel_id=1, source_target_pairs={{0,3},{1,0},{2,1},{3,2},{4,7},{5,4},{6,5},{7,6},{8,11},{9,8},{10,9... | collective-permute-start | bytes 663560 | tf_op jit(solution)/shard_map/ppermute | solution.py:336
  134.8 2.2 %collective-permute-done.32 = bf16[144,768]{1,0:T(8,128)(2,1)S(1)} collective-permute-done((bf16[144,768]{1,0:T(8,128)(2,1)S(1)}, bf16[144,768]{1,0:T(8,128)(2,1)S(1)}, u32[]{:S(2)}, u32[]{:S(2)}) %collective-permute-start.32) | collective-permute-done | bytes 221216 | tf_op jit(solution)/shard_map/ppermute | solution.py:354
  137.0 1.3 collective-permute-start.33
  138.3 1.9 %collective-permute-done.30.refs_2_ = bf16[144,768]{1,0:T(8,128)(2,1)S(1)} collective-permute-done((bf16[144,768]{1,0:T(8,128)(2,1)S(1)}, bf16[144,768]{1,0:T(8,128)(2,1)S(1)}, u32[]{:S(2)}, u32[]{:S(2)}) %collective-permute-start.30) | collective-permute-done | bytes 221216 | tf_op jit(solution)/shard_map/ppermute | solution.py:336
  140.2 1.6 collective-permute-done.31.refs_3_
  141.8 2.5 %collective-permute-done.33.refs_4_ = bf16[144,768]{1,0:T(8,128)(2,1)S(1)} collective-permute-done((bf16[144,768]{1,0:T(8,128)(2,1)S(1)}, bf16[144,768]{1,0:T(8,128)(2,1)S(1)}, u32[]{:S(2)}, u32[]{:S(2)}) %collective-permute-start.33) | collective-permute-done | bytes 221216 | tf_op jit(solution)/shard_map/ppermute | solution.py:350
  144.5 4.1 %collective-permute-start.35 = (bf16[72,768]{1,0:T(8,128)(2,1)S(1)}, bf16[72,768]{1,0:T(8,128)(2,1)S(1)}, u32[]{:S(2)}, u32[]{:S(2)}) collective-permute-start(bf16[72,768]{1,0:T(8,128)(2,1)S(1)} %get-tuple-element.173), channel_id=1, source_target_pairs={{0,96},{32,0},{64,32},{96,64},{1,97},{33,1},{65,33},{97,65},{2,98}... | collective-permute-start | bytes 331784 | tf_op jit(solution)/shard_map/ppermute | solution.py:336
  148.6 4.0 %collective-permute-start.36 = (bf16[72,768]{1,0:T(8,128)(2,1)S(1)}, bf16[72,768]{1,0:T(8,128)(2,1)S(1)}, u32[]{:S(2)}, u32[]{:S(2)}) collective-permute-start(bf16[72,768]{1,0:T(8,128)(2,1)S(1)} %get-tuple-element.174), channel_id=1, source_target_pairs={{0,64},{32,96},{64,0},{96,32},{1,65},{33,97},{65,1},{97,33},{2,66}... | collective-permute-start | bytes 331784 | tf_op jit(solution)/shard_map/ppermute | solution.py:336
  152.6 5.7 %collective-permute-done.36.refs_3_ = bf16[72,768]{1,0:T(8,128)(2,1)S(1)} collective-permute-done((bf16[72,768]{1,0:T(8,128)(2,1)S(1)}, bf16[72,768]{1,0:T(8,128)(2,1)S(1)}, u32[]{:S(2)}, u32[]{:S(2)}) %collective-permute-start.36) | collective-permute-done | bytes 110624 | tf_op jit(solution)/shard_map/ppermute | solution.py:336
  158.3 1.6 mix.1
  (59 shorter events, 10.0 us)
Async XLA Ops:
  0.0 41.1 %copy-start.2 = (bf16[512,3072]{1,0:T(8,128)(2,1)S(1)}, bf16[512,3072]{1,0:T(8,128)(2,1)}, u32[]{:S(2)}) copy-start(bf16[512,3072]{1,0:T(8,128)(2,1)} %refs_5_.1) | copy-start | bytes 9437188
  0.0 18.2 %collective-permute-start.3 = (bf16[3072,512]{1,0:T(8,128)(2,1)}, bf16[3072,512]{1,0:T(8,128)(2,1)}, u32[]{:S(2)}, u32[]{:S(2)}) collective-permute-start(bf16[3072,512]{1,0:T(8,128)(2,1)} %refs_3_.1), channel_id=1, source_target_pairs={{0,4},{4,0},{1,5},{5,1},{2,6},{6,2},{3,7},{7,3},{8,12},{12,8},{9,1... | collective-permute-start | bytes 9437192 | tf_op jit(solution)/shard_map/ppermute | solution.py:358
  1.0 11.4 %collective-permute-start = (bf16[2,128,128]{2,1,0:T(8,128)(2,1)S(1)}, bf16[2,128,128]{2,1,0:T(8,128)(2,1)S(1)}, u32[]{:S(2)}, u32[]{:S(2)}) collective-permute-start(bf16[2,128,128]{2,1,0:T(8,128)(2,1)S(1)} %get-tuple-element.177), channel_id=1, source_target_pairs={{0,32},{32,64},{64,96},{96,0},{1,33},{33,65},{65,97},{97,1},{2,34}... | collective-permute-start | bytes 196616 | tf_op jit(solution)/shard_map/ppermute | solution.py:336
  4.3 8.1 %collective-permute-start.1 = (bf16[2,128,128]{2,1,0:T(8,128)(2,1)S(1)}, bf16[2,128,128]{2,1,0:T(8,128)(2,1)S(1)}, u32[]{:S(2)}, u32[]{:S(2)}) collective-permute-start(bf16[2,128,128]{2,1,0:T(8,128)(2,1)S(1)} %get-tuple-element.176), channel_id=1, source_target_pairs={{0,96},{32,0},{64,32},{96,64},{1,97},{33,1},{65,33},{97,65},{2,98}... | collective-permute-start | bytes 196616 | tf_op jit(solution)/shard_map/ppermute | solution.py:336
  6.6 10.9 %collective-permute-start.2 = (bf16[2,128,128]{2,1,0:T(8,128)(2,1)S(1)}, bf16[2,128,128]{2,1,0:T(8,128)(2,1)S(1)}, u32[]{:S(2)}, u32[]{:S(2)}) collective-permute-start(bf16[2,128,128]{2,1,0:T(8,128)(2,1)S(1)} %get-tuple-element.175), channel_id=1, source_target_pairs={{0,64},{32,96},{64,0},{96,32},{1,65},{33,97},{65,1},{97,33},{2,66}... | collective-permute-start | bytes 196616 | tf_op jit(solution)/shard_map/ppermute | solution.py:336
  18.2 11.0 %collective-permute-start.7 = (bf16[3072,512]{1,0:T(8,128)(2,1)}, bf16[3072,512]{1,0:T(8,128)(2,1)S(1)}, u32[]{:S(2)}, u32[]{:S(2)}) collective-permute-start(bf16[3072,512]{1,0:T(8,128)(2,1)} %refs_4_.1), channel_id=1, source_target_pairs={{0,4},{4,0},{1,5},{5,1},{2,6},{6,2},{3,7},{7,3},{8,12},{12,8},{9,1... | collective-permute-start | bytes 9437192 | tf_op jit(solution)/shard_map/ppermute | solution.py:358
  18.3 7.7 %collective-permute-start.4 = (bf16[2,512,128]{2,1,0:T(8,128)(2,1)S(1)}, bf16[2,512,128]{2,1,0:T(8,128)(2,1)S(1)}, u32[]{:S(2)}, u32[]{:S(2)}) collective-permute-start(bf16[2,512,128]{2,1,0:T(8,128)(2,1)S(1)} %get-tuple-element.102.refs_0_), channel_id=1, source_target_pairs={{0,4},{4,0},{1,5},{5,1},{2,6},{6,2},{3,7},{7,3},{8,12},{12,8},{9,1... | collective-permute-start | bytes 786440 | tf_op jit(solution)/shard_map/ppermute | solution.py:358
  18.8 10.4 %collective-permute-start.5 = (bf16[2,512,128]{2,1,0:T(8,128)(2,1)S(1)}, bf16[2,512,128]{2,1,0:T(8,128)(2,1)S(1)}, u32[]{:S(2)}, u32[]{:S(2)}) collective-permute-start(bf16[2,512,128]{2,1,0:T(8,128)(2,1)S(1)} %get-tuple-element.106), channel_id=1, source_target_pairs={{0,8},{8,16},{16,24},{24,0},{1,9},{9,17},{17,25},{25,1},{2,10},{10... | collective-permute-start | bytes 786440 | tf_op jit(solution)/shard_map/ppermute | solution.py:336
  20.3 8.8 %collective-permute-start.6 = (bf16[2,512,128]{2,1,0:T(8,128)(2,1)S(1)}, bf16[2,512,128]{2,1,0:T(8,128)(2,1)S(1)}, u32[]{:S(2)}, u32[]{:S(2)}) collective-permute-start(bf16[2,512,128]{2,1,0:T(8,128)(2,1)S(1)} %get-tuple-element.107), channel_id=1, source_target_pairs={{0,24},{8,0},{16,8},{24,16},{1,25},{9,1},{17,9},{25,17},{2,26},{10... | collective-permute-start | bytes 786440 | tf_op jit(solution)/shard_map/ppermute | solution.py:336
  22.0 0.9 copy-start.3
  22.9 0.9 copy-start.4
  23.9 0.7 copy-start.6
  24.5 0.7 copy-start.7
  29.2 2.6 %collective-permute-start.8 = (bf16[2,512,128]{2,1,0:T(8,128)(2,1)S(1)}, bf16[2,512,128]{2,1,0:T(8,128)(2,1)S(1)}, u32[]{:S(2)}, u32[]{:S(2)}) collective-permute-start(bf16[2,512,128]{2,1,0:T(8,128)(2,1)S(1)} %collective-permute-done.5.refs_0_), channel_id=1, source_target_pairs={{0,4},{4,0},{1,5},{5,1},{2,6},{6,2},{3,7},{7,3},{8,12},{12,8},{9,1... | collective-permute-start | bytes 786440 | tf_op jit(solution)/shard_map/ppermute | solution.py:358
  29.3 2.6 %collective-permute-start.9 = (bf16[2,512,128]{2,1,0:T(8,128)(2,1)S(1)}, bf16[2,512,128]{2,1,0:T(8,128)(2,1)S(1)}, u32[]{:S(2)}, u32[]{:S(2)}) collective-permute-start(bf16[2,512,128]{2,1,0:T(8,128)(2,1)S(1)} %collective-permute-done.6.refs_1_), channel_id=1, source_target_pairs={{0,4},{4,0},{1,5},{5,1},{2,6},{6,2},{3,7},{7,3},{8,12},{12,8},{9,1... | collective-permute-start | bytes 786440 | tf_op jit(solution)/shard_map/ppermute | solution.py:358
  29.7 9.8 %collective-permute-start.10 = (bf16[2,512,128]{2,1,0:T(8,128)(2,1)S(1)}, bf16[2,512,128]{2,1,0:T(8,128)(2,1)S(1)}, u32[]{:S(2)}, u32[]{:S(2)}) collective-permute-start(bf16[2,512,128]{2,1,0:T(8,128)(2,1)S(1)} %get-tuple-element.118), channel_id=1, source_target_pairs={{0,16},{8,24},{16,0},{24,8},{1,17},{9,25},{17,1},{25,9},{2,18},{10... | collective-permute-start | bytes 786440 | tf_op jit(solution)/shard_map/ppermute | solution.py:336
  31.8 48.7 %copy-start.1 = (bf16[3072,512]{1,0:T(8,128)(2,1)S(1)}, bf16[3072,512]{1,0:T(8,128)(2,1)}, u32[]{:S(2)}) copy-start(bf16[3072,512]{1,0:T(8,128)(2,1)} %refs_4_.1) | copy-start | bytes 9437188
  37.5 43.1 %copy-start = (bf16[3072,512]{1,0:T(8,128)(2,1)S(1)}, bf16[3072,512]{1,0:T(8,128)(2,1)}, u32[]{:S(2)}) copy-start(bf16[3072,512]{1,0:T(8,128)(2,1)} %refs_3_.1) | copy-start | bytes 9437188
  37.5 43.1 %copy-start.5 = (f32[3072]{0:T(1024)S(1)}, f32[3072]{0:T(1024)}, u32[]{:S(2)}) copy-start(f32[3072]{0:T(1024)} %param.18) | copy-start | bytes 36868
  39.6 1.5 collective-permute-start.11
  41.1 19.4 %collective-permute-start.15 = (bf16[512,3072]{1,0:T(8,128)(2,1)S(1)}, bf16[512,3072]{1,0:T(8,128)(2,1)S(1)}, u32[]{:S(2)}, u32[]{:S(2)}) collective-permute-start(bf16[512,3072]{1,0:T(8,128)(2,1)S(1)} %copy-done.2), channel_id=1, source_target_pairs={{0,4},{4,0},{1,5},{5,1},{2,6},{6,2},{3,7},{7,3},{8,12},{12,8},{9,1... | collective-permute-start | bytes 9437192 | tf_op jit(solution)/shard_map/ppermute | solution.py:358
  44.4 8.2 %collective-permute-start.12 = (bf16[72,768]{1,0:T(8,128)(2,1)S(1)}, bf16[72,768]{1,0:T(8,128)(2,1)S(1)}, u32[]{:S(2)}, u32[]{:S(2)}) collective-permute-start(bf16[72,768]{1,0:T(8,128)(2,1)S(1)} %get-tuple-element.125), channel_id=1, source_target_pairs={{0,32},{32,64},{64,96},{96,0},{1,33},{33,65},{65,97},{97,1},{2,34}... | collective-permute-start | bytes 331784 | tf_op jit(solution)/shard_map/ppermute | solution.py:336
  44.7 11.1 %collective-permute-start.13 = (bf16[72,768]{1,0:T(8,128)(2,1)S(1)}, bf16[72,768]{1,0:T(8,128)(2,1)S(1)}, u32[]{:S(2)}, u32[]{:S(2)}) collective-permute-start(bf16[72,768]{1,0:T(8,128)(2,1)S(1)} %get-tuple-element.126), channel_id=1, source_target_pairs={{0,96},{32,0},{64,32},{96,64},{1,97},{33,1},{65,33},{97,65},{2,98}... | collective-permute-start | bytes 331784 | tf_op jit(solution)/shard_map/ppermute | solution.py:336
  48.8 11.7 %collective-permute-start.14 = (bf16[72,768]{1,0:T(8,128)(2,1)S(1)}, bf16[72,768]{1,0:T(8,128)(2,1)S(1)}, u32[]{:S(2)}, u32[]{:S(2)}) collective-permute-start(bf16[72,768]{1,0:T(8,128)(2,1)S(1)} %get-tuple-element.127), channel_id=1, source_target_pairs={{0,64},{32,96},{64,0},{96,32},{1,65},{33,97},{65,1},{97,33},{2,66}... | collective-permute-start | bytes 331784 | tf_op jit(solution)/shard_map/ppermute | solution.py:336
  60.6 8.3 %collective-permute-start.19 = (bf16[144,768]{1,0:T(8,128)(2,1)S(1)}, bf16[144,768]{1,0:T(8,128)(2,1)S(1)}, u32[]{:S(2)}, u32[]{:S(2)}) collective-permute-start(bf16[144,768]{1,0:T(8,128)(2,1)S(1)} %get-tuple-element.136), channel_id=1, source_target_pairs={{0,24},{8,16},{16,8},{24,0},{1,25},{9,17},{17,9},{25,1},{2,26},{10... | collective-permute-start | bytes 663560 | tf_op jit(solution)/shard_map/ppermute | solution.py:350
  62.6 8.6 %collective-permute-start.16 = (bf16[144,768]{1,0:T(8,128)(2,1)S(1)}, bf16[144,768]{1,0:T(8,128)(2,1)S(1)}, u32[]{:S(2)}, u32[]{:S(2)}) collective-permute-start(bf16[144,768]{1,0:T(8,128)(2,1)S(1)} %get-tuple-element.135), channel_id=1, source_target_pairs={{0,1},{1,2},{2,3},{3,0},{4,5},{5,6},{6,7},{7,4},{8,9},{9,10},{10,1... | collective-permute-start | bytes 663560 | tf_op jit(solution)/shard_map/ppermute | solution.py:336
  64.1 10.5 %collective-permute-start.17 = (bf16[144,768]{1,0:T(8,128)(2,1)S(1)}, bf16[144,768]{1,0:T(8,128)(2,1)S(1)}, u32[]{:S(2)}, u32[]{:S(2)}) collective-permute-start(bf16[144,768]{1,0:T(8,128)(2,1)S(1)} %get-tuple-element.135), channel_id=1, source_target_pairs={{0,3},{1,0},{2,1},{3,2},{4,7},{5,4},{6,5},{7,6},{8,11},{9,8},{10,9... | collective-permute-start | bytes 663560 | tf_op jit(solution)/shard_map/ppermute | solution.py:336
  65.9 10.4 %collective-permute-start.18 = (bf16[144,768]{1,0:T(8,128)(2,1)S(1)}, bf16[144,768]{1,0:T(8,128)(2,1)S(1)}, u32[]{:S(2)}, u32[]{:S(2)}) collective-permute-start(bf16[144,768]{1,0:T(8,128)(2,1)S(1)} %get-tuple-element.135), channel_id=1, source_target_pairs={{0,2},{1,3},{2,0},{3,1},{4,6},{5,7},{6,4},{7,5},{8,10},{9,11},{10,... | collective-permute-start | bytes 663560 | tf_op jit(solution)/shard_map/ppermute | solution.py:336
  68.8 7.5 %collective-permute-start.20 = (bf16[144,768]{1,0:T(8,128)(2,1)S(1)}, bf16[144,768]{1,0:T(8,128)(2,1)S(1)}, u32[]{:S(2)}, u32[]{:S(2)}) collective-permute-start(bf16[144,768]{1,0:T(8,128)(2,1)S(1)} %collective-permute-done.19), channel_id=1, source_target_pairs={{0,8},{8,0},{1,9},{9,1},{2,10},{10,2},{3,11},{11,3},{4,12},{12,4},... | collective-permute-start | bytes 663560 | tf_op jit(solution)/shard_map/ppermute | solution.py:354
  76.4 21.4 %collective-permute-start.24 = (bf16[4,144,768]{2,1,0:T(8,128)(2,1)S(1)}, bf16[4,144,768]{2,1,0:T(8,128)(2,1)S(1)}, u32[]{:S(2)}, u32[]{:S(2)}) collective-permute-start(bf16[4,144,768]{2,1,0:T(8,128)(2,1)S(1)} %pad_maximum_fusion.refs_2_), channel_id=1, source_target_pairs={{0,8},{8,0},{1,9},{9,1},{2,10},{10,2},{3,11},{11,3},{4,12},{12,4},... | collective-permute-start | bytes 2654216 | tf_op jit(solution)/shard_map/ppermute | solution.py:354
  76.5 21.3 %collective-permute-start.21 = (bf16[2,144,768]{2,1,0:T(8,128)(2,1)S(1)}, bf16[2,144,768]{2,1,0:T(8,128)(2,1)S(1)}, u32[]{:S(2)}, u32[]{:S(2)}) collective-permute-start(bf16[2,144,768]{2,1,0:T(8,128)(2,1)S(1)} %pad_maximum_fusion.1.refs_3_), channel_id=1, source_target_pairs={{0,1},{1,2},{2,3},{3,0},{4,5},{5,6},{6,7},{7,4},{8,9},{9,10},{10,1... | collective-permute-start | bytes 1327112 | tf_op jit(solution)/shard_map/ppermute | solution.py:336
  77.7 20.1 %collective-permute-start.22 = (bf16[2,144,768]{2,1,0:T(8,128)(2,1)S(1)}, bf16[2,144,768]{2,1,0:T(8,128)(2,1)S(1)}, u32[]{:S(2)}, u32[]{:S(2)}) collective-permute-start(bf16[2,144,768]{2,1,0:T(8,128)(2,1)S(1)} %pad_maximum_fusion.1.refs_3_), channel_id=1, source_target_pairs={{0,3},{1,0},{2,1},{3,2},{4,7},{5,4},{6,5},{7,6},{8,11},{9,8},{10,9... | collective-permute-start | bytes 1327112 | tf_op jit(solution)/shard_map/ppermute | solution.py:336
  79.8 18.0 %collective-permute-start.23 = (bf16[2,144,768]{2,1,0:T(8,128)(2,1)S(1)}, bf16[2,144,768]{2,1,0:T(8,128)(2,1)S(1)}, u32[]{:S(2)}, u32[]{:S(2)}) collective-permute-start(bf16[2,144,768]{2,1,0:T(8,128)(2,1)S(1)} %pad_maximum_fusion.1.refs_3_), channel_id=1, source_target_pairs={{0,2},{1,3},{2,0},{3,1},{4,6},{5,7},{6,4},{7,5},{8,10},{9,11},{10,... | collective-permute-start | bytes 1327112 | tf_op jit(solution)/shard_map/ppermute | solution.py:336
  108.7 21.9 %collective-permute-start.28 = (bf16[4,144,768]{2,1,0:T(8,128)(2,1)S(1)}, bf16[4,144,768]{2,1,0:T(8,128)(2,1)S(1)}, u32[]{:S(2)}, u32[]{:S(2)}) collective-permute-start(bf16[4,144,768]{2,1,0:T(8,128)(2,1)S(1)} %get-tuple-element.155), channel_id=1, source_target_pairs={{0,8},{8,0},{1,9},{9,1},{2,10},{10,2},{3,11},{11,3},{4,12},{12,4},... | collective-permute-start | bytes 2654216 | tf_op jit(solution)/shard_map/ppermute | solution.py:354
  110.5 14.3 %collective-permute-start.25 = (bf16[2,144,768]{2,1,0:T(8,128)(2,1)S(1)}, bf16[2,144,768]{2,1,0:T(8,128)(2,1)S(1)}, u32[]{:S(2)}, u32[]{:S(2)}) collective-permute-start(bf16[2,144,768]{2,1,0:T(8,128)(2,1)S(1)} %get-tuple-element.152), channel_id=1, source_target_pairs={{0,1},{1,2},{2,3},{3,0},{4,5},{5,6},{6,7},{7,4},{8,9},{9,10},{10,1... | collective-permute-start | bytes 1327112 | tf_op jit(solution)/shard_map/ppermute | solution.py:336
  111.3 17.1 %collective-permute-start.26 = (bf16[2,144,768]{2,1,0:T(8,128)(2,1)S(1)}, bf16[2,144,768]{2,1,0:T(8,128)(2,1)S(1)}, u32[]{:S(2)}, u32[]{:S(2)}) collective-permute-start(bf16[2,144,768]{2,1,0:T(8,128)(2,1)S(1)} %get-tuple-element.153), channel_id=1, source_target_pairs={{0,3},{1,0},{2,1},{3,2},{4,7},{5,4},{6,5},{7,6},{8,11},{9,8},{10,9... | collective-permute-start | bytes 1327112 | tf_op jit(solution)/shard_map/ppermute | solution.py:336
  113.7 16.8 %collective-permute-start.27 = (bf16[2,144,768]{2,1,0:T(8,128)(2,1)S(1)}, bf16[2,144,768]{2,1,0:T(8,128)(2,1)S(1)}, u32[]{:S(2)}, u32[]{:S(2)}) collective-permute-start(bf16[2,144,768]{2,1,0:T(8,128)(2,1)S(1)} %get-tuple-element.154), channel_id=1, source_target_pairs={{0,2},{1,3},{2,0},{3,1},{4,6},{5,7},{6,4},{7,5},{8,10},{9,11},{10,... | collective-permute-start | bytes 1327112 | tf_op jit(solution)/shard_map/ppermute | solution.py:336
  131.0 6.0 %collective-permute-start.32 = (bf16[144,768]{1,0:T(8,128)(2,1)S(1)}, bf16[144,768]{1,0:T(8,128)(2,1)S(1)}, u32[]{:S(2)}, u32[]{:S(2)}) collective-permute-start(bf16[144,768]{1,0:T(8,128)(2,1)S(1)} %get-tuple-element.166), channel_id=1, source_target_pairs={{0,8},{8,0},{1,9},{9,1},{2,10},{10,2},{3,11},{11,3},{4,12},{12,4},... | collective-permute-start | bytes 663560 | tf_op jit(solution)/shard_map/ppermute | solution.py:354
  131.1 7.2 %collective-permute-start.29 = (bf16[144,768]{1,0:T(8,128)(2,1)S(1)}, bf16[144,768]{1,0:T(8,128)(2,1)S(1)}, u32[]{:S(2)}, u32[]{:S(2)}) collective-permute-start(bf16[144,768]{1,0:T(8,128)(2,1)S(1)} %get-tuple-element.162), channel_id=1, source_target_pairs={{0,1},{1,2},{2,3},{3,0},{4,5},{5,6},{6,7},{7,4},{8,9},{9,10},{10,1... | collective-permute-start | bytes 663560 | tf_op jit(solution)/shard_map/ppermute | solution.py:336
  132.4 7.9 %collective-permute-start.30 = (bf16[144,768]{1,0:T(8,128)(2,1)S(1)}, bf16[144,768]{1,0:T(8,128)(2,1)S(1)}, u32[]{:S(2)}, u32[]{:S(2)}) collective-permute-start(bf16[144,768]{1,0:T(8,128)(2,1)S(1)} %get-tuple-element.163), channel_id=1, source_target_pairs={{0,3},{1,0},{2,1},{3,2},{4,7},{5,4},{6,5},{7,6},{8,11},{9,8},{10,9... | collective-permute-start | bytes 663560 | tf_op jit(solution)/shard_map/ppermute | solution.py:336
  134.4 7.4 %collective-permute-start.31 = (bf16[144,768]{1,0:T(8,128)(2,1)S(1)}, bf16[144,768]{1,0:T(8,128)(2,1)S(1)}, u32[]{:S(2)}, u32[]{:S(2)}) collective-permute-start(bf16[144,768]{1,0:T(8,128)(2,1)S(1)} %get-tuple-element.164), channel_id=1, source_target_pairs={{0,2},{1,3},{2,0},{3,1},{4,6},{5,7},{6,4},{7,5},{8,10},{9,11},{10,... | collective-permute-start | bytes 663560 | tf_op jit(solution)/shard_map/ppermute | solution.py:336
  137.0 7.2 %collective-permute-start.33 = (bf16[144,768]{1,0:T(8,128)(2,1)S(1)}, bf16[144,768]{1,0:T(8,128)(2,1)S(1)}, u32[]{:S(2)}, u32[]{:S(2)}) collective-permute-start(bf16[144,768]{1,0:T(8,128)(2,1)S(1)} %add_convert_fusion), channel_id=1, source_target_pairs={{0,24},{8,16},{16,8},{24,0},{1,25},{9,17},{17,9},{25,1},{2,26},{10... | collective-permute-start | bytes 663560 | tf_op jit(solution)/shard_map/ppermute | solution.py:350
  144.4 8.2 %collective-permute-start.34 = (bf16[72,768]{1,0:T(8,128)(2,1)S(1)}, bf16[72,768]{1,0:T(8,128)(2,1)S(1)}, u32[]{:S(2)}, u32[]{:S(2)}) collective-permute-start(bf16[72,768]{1,0:T(8,128)(2,1)S(1)} %get-tuple-element.172), channel_id=1, source_target_pairs={{0,32},{32,64},{64,96},{96,0},{1,33},{33,65},{65,97},{97,1},{2,34}... | collective-permute-start | bytes 331784 | tf_op jit(solution)/shard_map/ppermute | solution.py:336
  144.5 8.1 %collective-permute-start.35 = (bf16[72,768]{1,0:T(8,128)(2,1)S(1)}, bf16[72,768]{1,0:T(8,128)(2,1)S(1)}, u32[]{:S(2)}, u32[]{:S(2)}) collective-permute-start(bf16[72,768]{1,0:T(8,128)(2,1)S(1)} %get-tuple-element.173), channel_id=1, source_target_pairs={{0,96},{32,0},{64,32},{96,64},{1,97},{33,1},{65,33},{97,65},{2,98}... | collective-permute-start | bytes 331784 | tf_op jit(solution)/shard_map/ppermute | solution.py:336
  148.6 9.7 %collective-permute-start.36 = (bf16[72,768]{1,0:T(8,128)(2,1)S(1)}, bf16[72,768]{1,0:T(8,128)(2,1)S(1)}, u32[]{:S(2)}, u32[]{:S(2)}) collective-permute-start(bf16[72,768]{1,0:T(8,128)(2,1)S(1)} %get-tuple-element.174), channel_id=1, source_target_pairs={{0,64},{32,96},{64,0},{96,32},{1,65},{33,97},{65,1},{97,33},{2,66}... | collective-permute-start | bytes 331784 | tf_op jit(solution)/shard_map/ppermute | solution.py:336
